TPU v7x, 32 devices: a whole 2x2x4 slice. The times are simulated.
32 devices in a mesh: seq: 4 (over y, x), fsdp: 8 (over z, core).
Axes of the slice: x: 2, y: 2, z: 4, core: 2. Of those that a mesh axis runs over, the one named last changes fastest.
Arguments:
- hidden_in: bfloat16 [1024, 8, 2048], P('seq', 'fsdp'), may hold values from -6 to 6
- per_layer_input: bfloat16 [1024, 8, 256], P('seq', 'fsdp'), may hold values from -6 to 6
- segment_ids: int32 [1024, 8], P('seq', 'fsdp'), may hold values from 0 to 2, as said below
- positions: int32 [1024, 8], P('seq', 'fsdp'), may hold values from 0 to 513, as said below
- out_cotangent: bfloat16 [1024, 8, 2048], P('seq', 'fsdp'), may hold values from -6 to 6
- w_query: bfloat16 [2048, 2048], P(('seq', 'fsdp')), may hold values from -0.125 to 0.125
- key_matrix: bfloat16 [2048, 512], P(('seq', 'fsdp')), may hold values from -0.125 to 0.125
- value_matrix: bfloat16 [2048, 512], P(('seq', 'fsdp')), may hold values from -0.125 to 0.125
- w_out_t: bfloat16 [2048, 2048], P(('seq', 'fsdp')), may hold values from -0.125 to 0.125
- laurel_maps: bfloat16 [2048, 128], P(('seq', 'fsdp')), may hold values from -0.125 to 0.125
- per_layer_maps: bfloat16 [2048, 512], P(('seq', 'fsdp')), may hold values from -0.125 to 0.125
- norm_gains: bfloat16 [2048, 6], P(('seq', 'fsdp')), may hold values from 0.5 to 1.5
- head_gains: bfloat16 [256, 2], P(('seq', 'fsdp')), may hold values from 0.5 to 1.5
- w_mlp: bfloat16 [2048, 3, 8192], P('fsdp', None, 'seq'), may hold values from -0.125 to 0.125
Outputs:
- hidden_out: bfloat16 [1024, 8, 2048], P('seq', 'fsdp')
- input_grad: float32 [1024, 8, 2048], P('seq', 'fsdp')
- grad_query: float32 [2048, 2048], P(('seq', 'fsdp'))
- grad_key: float32 [2048, 512], P(('seq', 'fsdp'))
- grad_value: float32 [2048, 512], P(('seq', 'fsdp'))
- grad_out_t: float32 [2048, 2048], P(('seq', 'fsdp'))
- grad_laurel: float32 [2048, 128], P(('seq', 'fsdp'))
- grad_per_layer: float32 [2048, 512], P(('seq', 'fsdp'))
- grad_norm_gains: float32 [2048, 6], P(('seq', 'fsdp'))
- grad_head_gains: float32 [256, 2], P(('seq', 'fsdp'))
- grad_mlp: float32 [2048, 3, 8192], P('fsdp', None, 'seq')
Inputs may be any that keep to these rules, and one draw needn't show every extreme that they name: `segment_ids`: each sequence holds exactly three documents, numbered 0, 1, 2 in order along the sequence, each present. `positions`: within a document the position is 0 at its first token and rises by 1 or 2 from token to token until it reaches 513, where it stays; every sequence reaches that value.
All inputs are finite; a program needn't handle non-finite values.
Results may differ from a plain program's by a relative error of at most 0.025.
Values may be sent and summed in bfloat16 or wider, within the bound.
A program may use at most 320 MiB of HBM per device.

v0:
```python
import math

import jax
import jax.numpy as jnp
from jax import lax
from jax.sharding import PartitionSpec as P

QUERY_HEADS = 8
KEY_VALUE_HEADS = 2
HEAD_DIM = 256
LR = 64
PLE = 256
WIN = 512


eps = 1e-06
theta = 10000.0
root_half = 1.0 / math.sqrt(2.0)


def norm_rows(v, gain_vec):
    inverse = lax.rsqrt(jnp.mean(v * v, -1, keepdims=True) + eps)
    return (v * inverse * gain_vec, inverse)


def norm_back(v, inverse, gain_vec, incoming):
    scaled = incoming * gain_vec
    inner_mean = jnp.mean(scaled * v, -1, keepdims=True)
    return (
        inverse * (scaled - v * inverse * inverse * inner_mean),
        jnp.sum(incoming * v * inverse, axis=(0, 1)),
    )


def gelu_tanh(v):
    return jax.nn.gelu(v, approximate=True)


def rope_tables(places):
    half_width = HEAD_DIM // 2
    frequency = theta ** (-jnp.arange(half_width).astype(jnp.float32) * 2.0 / HEAD_DIM)
    angles = places.astype(jnp.float32)[..., None] * frequency
    angles = jnp.concatenate([angles, angles], -1)[..., None, :]
    return (jnp.cos(angles), jnp.sin(angles))


def rotate(v, cos_table, sin_table):
    half_width = v.shape[-1] // 2
    turned = jnp.concatenate([-v[..., half_width:], v[..., :half_width]], -1)
    return v * cos_table + turned * sin_table


def head_prep(q_lin, key_linear, value_linear, head_scale, cos_table, sin_table):
    leading_dims = q_lin.shape[:2]
    queries = rotate(
        norm_rows(q_lin.reshape(leading_dims + (-1, HEAD_DIM)), head_scale[:, 0])[0],
        cos_table,
        sin_table,
    )
    keys = rotate(
        norm_rows(key_linear.reshape(leading_dims + (-1, HEAD_DIM)), head_scale[:, 1])[0],
        cos_table,
        sin_table,
    )
    values = norm_rows(value_linear.reshape(leading_dims + (-1, HEAD_DIM)), 1.0)[0]
    return (queries, keys, values)


def allowed_mask(segments):
    indices = jnp.arange(segments.shape[0])
    offset = indices[:, None] - indices[None, :]
    nearby = (offset >= 0) & (offset < WIN)
    by_seq = segments.T
    return (by_seq[:, :, None] == by_seq[:, None, :]) & nearby


def scores_of(q_heads, k_heads, allowed):
    raw_scores = jnp.einsum("qshd,kshd->shqk", q_heads, k_heads, preferred_element_type=jnp.float32)
    return jnp.where(allowed[:, None], raw_scores * HEAD_DIM ** (-0.5), -1000000000.0)


def attend_heads(q_heads, k_heads, v_heads, allowed):
    scores = scores_of(q_heads, k_heads, allowed)
    row_peak = jnp.max(scores, -1, keepdims=True)
    exp_scores = jnp.exp(scores - row_peak)
    row_total = jnp.sum(exp_scores, -1, keepdims=True)
    attn_probs = exp_scores / row_total
    head_out = jnp.einsum(
        "shqk,kshd->qshd",
        attn_probs.astype(jnp.bfloat16),
        v_heads,
        preferred_element_type=jnp.float32,
    )
    return (head_out, row_peak + jnp.log(row_total))


def attend_back(q_heads, k_heads, v_heads, allowed, log_total, grad_heads):
    probs_again = jnp.exp(scores_of(q_heads, k_heads, allowed) - log_total)
    grad_v_heads = jnp.einsum(
        "shqk,qshd->kshd",
        probs_again.astype(jnp.bfloat16),
        grad_heads,
        preferred_element_type=jnp.float32,
    )
    grad_probs = jnp.einsum(
        "qshd,kshd->shqk", grad_heads, v_heads, preferred_element_type=jnp.float32
    )
    row_inner = jnp.sum(probs_again * grad_probs, -1, keepdims=True)
    grad_scores = (probs_again * (grad_probs - row_inner) * HEAD_DIM ** (-0.5)).astype(jnp.bfloat16)
    grad_q_heads = jnp.einsum(
        "shqk,kshd->qshd", grad_scores, k_heads, preferred_element_type=jnp.float32
    )
    grad_k_heads = jnp.einsum(
        "shqk,qshd->kshd", grad_scores, q_heads, preferred_element_type=jnp.float32
    )
    return (grad_q_heads, grad_k_heads, grad_v_heads)


def fetch_attn(
    w_query, key_matrix, value_matrix, w_out_t, laurel_maps, per_layer_maps, norm_gains, head_gains
):
    return (
        lax.all_gather(w_query, ("seq", "fsdp"), axis=0, tiled=True),
        lax.all_gather(key_matrix, ("seq", "fsdp"), axis=0, tiled=True),
        lax.all_gather(value_matrix, ("seq", "fsdp"), axis=0, tiled=True),
        lax.all_gather(w_out_t, ("seq", "fsdp"), axis=0, tiled=True),
        lax.all_gather(laurel_maps, ("seq", "fsdp"), axis=0, tiled=True),
        lax.all_gather(per_layer_maps, ("seq", "fsdp"), axis=0, tiled=True),
        lax.all_gather(norm_gains, ("seq", "fsdp"), axis=0, tiled=True),
        lax.all_gather(head_gains, ("seq", "fsdp"), axis=0, tiled=True),
    )


def fetch(
    w_query,
    key_matrix,
    value_matrix,
    w_out_t,
    laurel_maps,
    per_layer_maps,
    norm_gains,
    head_gains,
    w_mlp,
):
    attn_full = fetch_attn(
        w_query,
        key_matrix,
        value_matrix,
        w_out_t,
        laurel_maps,
        per_layer_maps,
        norm_gains,
        head_gains,
    )
    mlp_full = lax.all_gather(w_mlp, "fsdp", axis=0, tiled=True)
    return (attn_full, mlp_full)


def group_rows(source):
    return lax.all_gather(source, "seq", axis=0, tiled=True)


def body(
    hidden_in,
    per_layer_input,
    segment_ids,
    positions,
    out_cotangent,
    w_query,
    key_matrix,
    value_matrix,
    w_out_t,
    laurel_maps,
    per_layer_maps,
    norm_gains,
    head_gains,
    w_mlp,
):
    leading_dims = hidden_in.shape[:2]
    query_group_count = QUERY_HEADS // KEY_VALUE_HEADS
    attn_full, mlp_full = fetch(
        w_query,
        key_matrix,
        value_matrix,
        w_out_t,
        laurel_maps,
        per_layer_maps,
        norm_gains,
        head_gains,
        w_mlp,
    )
    full_query, full_key, full_value, full_out, full_laurel, full_ple, full_gains, full_heads = (
        attn_full
    )
    gain_table = full_gains.astype(jnp.float32)
    head_scale = full_heads.astype(jnp.float32)
    tokens = hidden_in.astype(jnp.float32)
    x_normed_f, x_inverse = norm_rows(tokens, gain_table[:, 0])
    normalized_input = x_normed_f.astype(jnp.bfloat16)
    cos_table, sin_table = rope_tables(positions)
    q_lin = jnp.einsum(
        "bsd,dn->bsn", normalized_input, full_query, preferred_element_type=jnp.float32
    )
    key_linear = jnp.einsum(
        "bsd,dn->bsn", normalized_input, full_key, preferred_element_type=jnp.float32
    )
    value_linear = jnp.einsum(
        "bsd,dn->bsn", normalized_input, full_value, preferred_element_type=jnp.float32
    )
    queries, keys, values = head_prep(
        q_lin, key_linear, value_linear, head_scale, cos_table, sin_table
    )
    q_send = queries.astype(jnp.bfloat16)
    k_send = jnp.repeat(keys.astype(jnp.bfloat16), query_group_count, axis=2)
    v_send = jnp.repeat(values.astype(jnp.bfloat16), query_group_count, axis=2)
    q_heads, k_heads, v_heads = (
        lax.all_to_all(q_send, "seq", split_axis=2, concat_axis=0, tiled=True),
        lax.all_to_all(k_send, "seq", split_axis=2, concat_axis=0, tiled=True),
        lax.all_to_all(v_send, "seq", split_axis=2, concat_axis=0, tiled=True),
    )
    all_segments = lax.all_gather(segment_ids, "seq", axis=0, tiled=True)
    allowed = allowed_mask(all_segments)
    head_out, log_total = attend_heads(q_heads, k_heads, v_heads, allowed)
    head_low = head_out.astype(jnp.bfloat16)
    back_out = lax.all_to_all(head_low, "seq", split_axis=0, concat_axis=2, tiled=True)
    attn_in = back_out.reshape(leading_dims + (QUERY_HEADS * HEAD_DIM,))
    attn_lin = jnp.einsum("bsn,dn->bsd", attn_in, full_out, preferred_element_type=jnp.float32)
    attn_normed, attn_inverse = norm_rows(attn_lin, gain_table[:, 1])
    laurel_low = jnp.einsum(
        "bsd,dr->bsr", normalized_input, full_laurel[:, :LR], preferred_element_type=jnp.float32
    ).astype(jnp.bfloat16)
    laurel_high = jnp.einsum(
        "bsr,dr->bsd", laurel_low, full_laurel[:, LR:], preferred_element_type=jnp.float32
    )
    laurel_normed, laurel_inverse = norm_rows(laurel_high, gain_table[:, 2])
    mixed = (
        tokens + attn_normed + (normalized_input.astype(jnp.float32) + laurel_normed)
    ) * root_half
    h_normed_f, h_inverse = norm_rows(mixed, gain_table[:, 3])
    h_normed = h_normed_f.astype(jnp.bfloat16)
    h_rows = group_rows(h_normed)
    gate_up = jnp.einsum(
        "tsd,dcf->tscf", h_rows, mlp_full[:, :2], preferred_element_type=jnp.float32
    )
    gate_part = gate_up[:, :, 0]
    up_part = gate_up[:, :, 1]
    hidden = (gelu_tanh(gate_part) * up_part).astype(jnp.bfloat16)
    down_map = mlp_full[:, 2]
    picked = hidden
    ffn_out = lax.psum_scatter(
        jnp.einsum("tsf,df->tsd", picked, down_map, preferred_element_type=jnp.float32),
        "seq",
        scatter_dimension=0,
        tiled=True,
    )
    ffn_normed, ffn_inverse = norm_rows(ffn_out, gain_table[:, 4])
    h_second = (mixed + ffn_normed).astype(jnp.bfloat16)
    ple_gate = jnp.einsum(
        "bsd,de->bse", h_second, full_ple[:, :PLE], preferred_element_type=jnp.float32
    )
    ple_input = per_layer_input.astype(jnp.float32)
    ple_mixed = (gelu_tanh(ple_gate) * ple_input).astype(jnp.bfloat16)
    ple_proj = jnp.einsum(
        "bse,de->bsd", ple_mixed, full_ple[:, PLE:], preferred_element_type=jnp.float32
    )
    ple_normed, ple_inverse = norm_rows(ple_proj, gain_table[:, 5])
    hidden_out = (h_second.astype(jnp.float32) + ple_normed).astype(jnp.bfloat16)
    attn_back, mlp_back = fetch(
        w_query,
        key_matrix,
        value_matrix,
        w_out_t,
        laurel_maps,
        per_layer_maps,
        norm_gains,
        head_gains,
        w_mlp,
    )
    (
        back_query,
        back_key,
        back_value,
        back_out_map,
        back_laurel,
        back_ple,
        back_gains,
        back_heads,
    ) = attn_back
    gain_back = back_gains.astype(jnp.float32)
    head_back = back_heads.astype(jnp.float32)
    grad_out = out_cotangent.astype(jnp.float32)
    grad_ple_proj, gain_grad_five = norm_back(ple_proj, ple_inverse, gain_back[:, 5], grad_out)
    grad_ple_low = grad_ple_proj.astype(jnp.bfloat16)
    grad_ple_up = jnp.einsum(
        "bsd,bse->de", grad_ple_low, ple_mixed, preferred_element_type=jnp.float32
    )
    grad_ple_mixed = jnp.einsum(
        "bsd,de->bse", grad_ple_low, back_ple[:, PLE:], preferred_element_type=jnp.float32
    )
    unused_gelu, gelu_pull = jax.vjp(gelu_tanh, ple_gate)
    grad_ple_gate = gelu_pull(grad_ple_mixed * ple_input)[0].astype(jnp.bfloat16)
    grad_ple_down = jnp.einsum(
        "bsd,bse->de", h_second, grad_ple_gate, preferred_element_type=jnp.float32
    )
    grad_second = grad_out + jnp.einsum(
        "bse,de->bsd", grad_ple_gate, back_ple[:, :PLE], preferred_element_type=jnp.float32
    )
    grad_ffn, gain_grad_four = norm_back(ffn_out, ffn_inverse, gain_back[:, 4], grad_second)
    grad_ffn_rows = group_rows(grad_ffn.astype(jnp.bfloat16))
    grad_hidden = jnp.einsum(
        "tsd,df->tsf", grad_ffn_rows, mlp_back[:, 2], preferred_element_type=jnp.float32
    )
    gate_act, act_pull = jax.vjp(gelu_tanh, gate_part)
    grad_gate_up = jnp.stack(
        [act_pull(grad_hidden * up_part)[0], grad_hidden * gate_act], 2
    ).astype(jnp.bfloat16)
    in_maps = mlp_back[:, :2]
    picked = grad_gate_up
    grad_h_normed = lax.psum_scatter(
        jnp.einsum("tscf,dcf->tsd", picked, in_maps, preferred_element_type=jnp.float32).astype(
            jnp.bfloat16
        ),
        "seq",
        scatter_dimension=0,
        tiled=True,
    ).astype(jnp.float32)
    first_pair = jnp.einsum(
        "tsd,tscf->dcf", h_rows, grad_gate_up, preferred_element_type=jnp.float32
    )
    down_grad = jnp.einsum("tsd,tsf->df", grad_ffn_rows, hidden, preferred_element_type=jnp.float32)
    grad_mlp = lax.psum_scatter(
        jnp.concatenate([first_pair, down_grad[:, None]], 1).astype(jnp.bfloat16),
        "fsdp",
        scatter_dimension=0,
        tiled=True,
    ).astype(jnp.float32)
    grad_mixed_norm, gain_grad_three = norm_back(mixed, h_inverse, gain_back[:, 3], grad_h_normed)
    grad_mixed = grad_second + grad_mixed_norm
    grad_branch = grad_mixed * root_half
    grad_laurel_high, gain_grad_two = norm_back(
        laurel_high, laurel_inverse, gain_back[:, 2], grad_branch
    )
    grad_high_low = grad_laurel_high.astype(jnp.bfloat16)
    grad_laurel_up = jnp.einsum(
        "bsd,bsr->dr", grad_high_low, laurel_low, preferred_element_type=jnp.float32
    )
    grad_laurel_low = jnp.einsum(
        "bsd,dr->bsr", grad_high_low, back_laurel[:, LR:], preferred_element_type=jnp.float32
    ).astype(jnp.bfloat16)
    grad_laurel_down = jnp.einsum(
        "bsd,bsr->dr", normalized_input, grad_laurel_low, preferred_element_type=jnp.float32
    )
    grad_x_normed = grad_branch + jnp.einsum(
        "bsr,dr->bsd", grad_laurel_low, back_laurel[:, :LR], preferred_element_type=jnp.float32
    )
    grad_attn, gain_grad_one = norm_back(attn_lin, attn_inverse, gain_back[:, 1], grad_branch)
    grad_attn_low = grad_attn.astype(jnp.bfloat16)
    grad_out_map = jnp.einsum(
        "bsd,bsn->dn", grad_attn_low, attn_in, preferred_element_type=jnp.float32
    )
    grad_heads_seq = (
        jnp.einsum("bsd,dn->bsn", grad_attn_low, back_out_map, preferred_element_type=jnp.float32)
        .astype(jnp.bfloat16)
        .reshape(leading_dims + (QUERY_HEADS, HEAD_DIM))
    )
    grad_heads = lax.all_to_all(grad_heads_seq, "seq", split_axis=2, concat_axis=0, tiled=True)
    grad_q_heads, grad_k_heads, grad_v_heads = attend_back(
        q_heads, k_heads, v_heads, allowed, log_total, grad_heads
    )
    grad_q_seq, key_gradient_sequence, value_gradient_sequence = (
        lax.all_to_all(
            grad_q_heads.astype(jnp.bfloat16), "seq", split_axis=0, concat_axis=2, tiled=True
        ),
        lax.all_to_all(
            grad_k_heads.astype(jnp.bfloat16), "seq", split_axis=0, concat_axis=2, tiled=True
        ),
        lax.all_to_all(
            grad_v_heads.astype(jnp.bfloat16), "seq", split_axis=0, concat_axis=2, tiled=True
        ),
    )
    grad_keys = jnp.sum(
        key_gradient_sequence.astype(jnp.float32).reshape(
            leading_dims + (KEY_VALUE_HEADS, query_group_count, HEAD_DIM)
        ),
        3,
    )
    grad_values = jnp.sum(
        value_gradient_sequence.astype(jnp.float32).reshape(
            leading_dims + (KEY_VALUE_HEADS, query_group_count, HEAD_DIM)
        ),
        3,
    )
    unused_heads, head_pull = jax.vjp(
        head_prep, q_lin, key_linear, value_linear, head_back, cos_table, sin_table
    )
    grad_q_lin, grad_k_lin, grad_v_lin, grad_head_scale, unused_cos, unused_sin = head_pull(
        (grad_q_seq.astype(jnp.float32), grad_keys, grad_values)
    )
    grad_q_low = grad_q_lin.astype(jnp.bfloat16)
    grad_k_low = grad_k_lin.astype(jnp.bfloat16)
    grad_v_low = grad_v_lin.astype(jnp.bfloat16)
    grad_query_map = jnp.einsum(
        "bsd,bsn->dn", normalized_input, grad_q_low, preferred_element_type=jnp.float32
    )
    grad_key_map = jnp.einsum(
        "bsd,bsn->dn", normalized_input, grad_k_low, preferred_element_type=jnp.float32
    )
    grad_value_map = jnp.einsum(
        "bsd,bsn->dn", normalized_input, grad_v_low, preferred_element_type=jnp.float32
    )
    grad_x_normed = grad_x_normed + jnp.einsum(
        "bsn,dn->bsd", grad_q_low, back_query, preferred_element_type=jnp.float32
    )
    grad_x_normed = grad_x_normed + jnp.einsum(
        "bsn,dn->bsd", grad_k_low, back_key, preferred_element_type=jnp.float32
    )
    grad_x_normed = grad_x_normed + jnp.einsum(
        "bsn,dn->bsd", grad_v_low, back_value, preferred_element_type=jnp.float32
    )
    grad_tokens_norm, gain_grad_zero = norm_back(tokens, x_inverse, gain_back[:, 0], grad_x_normed)
    input_grad = grad_mixed * root_half + grad_tokens_norm
    gain_grads = jnp.stack(
        [
            gain_grad_zero,
            gain_grad_one,
            gain_grad_two,
            gain_grad_three,
            gain_grad_four,
            gain_grad_five,
        ],
        1,
    )
    laurel_grad = jnp.concatenate([grad_laurel_down, grad_laurel_up], 1)
    ple_grad = jnp.concatenate([grad_ple_down, grad_ple_up], 1)
    summed = (
        lax.psum_scatter(grad_query_map, ("seq", "fsdp"), scatter_dimension=0, tiled=True),
        lax.psum_scatter(grad_key_map, ("seq", "fsdp"), scatter_dimension=0, tiled=True),
        lax.psum_scatter(grad_value_map, ("seq", "fsdp"), scatter_dimension=0, tiled=True),
        lax.psum_scatter(grad_out_map, ("seq", "fsdp"), scatter_dimension=0, tiled=True),
        lax.psum_scatter(laurel_grad, ("seq", "fsdp"), scatter_dimension=0, tiled=True),
        lax.psum_scatter(ple_grad, ("seq", "fsdp"), scatter_dimension=0, tiled=True),
        lax.psum_scatter(gain_grads, ("seq", "fsdp"), scatter_dimension=0, tiled=True),
        lax.psum_scatter(grad_head_scale, ("seq", "fsdp"), scatter_dimension=0, tiled=True),
    )
    return (
        hidden_out,
        input_grad,
        summed[0],
        summed[1],
        summed[2],
        summed[3],
        summed[4],
        summed[5],
        summed[6],
        summed[7],
        grad_mlp,
    )


def solution(mesh):
    placed = (
        P("seq", "fsdp", None),
        P("seq", "fsdp", None),
        P("seq", "fsdp"),
        P("seq", "fsdp"),
        P("seq", "fsdp", None),
        P(("seq", "fsdp"), None),
        P(("seq", "fsdp"), None),
        P(("seq", "fsdp"), None),
        P(("seq", "fsdp"), None),
        P(("seq", "fsdp"), None),
        P(("seq", "fsdp"), None),
        P(("seq", "fsdp"), None),
        P(("seq", "fsdp"), None),
        P("fsdp", None, "seq"),
    )
    return jax.shard_map(
        body,
        mesh=mesh,
        in_specs=placed,
        out_specs=(
            P("seq", "fsdp", None),
            P("seq", "fsdp", None),
            P(("seq", "fsdp"), None),
            P(("seq", "fsdp"), None),
            P(("seq", "fsdp"), None),
            P(("seq", "fsdp"), None),
            P(("seq", "fsdp"), None),
            P(("seq", "fsdp"), None),
            P(("seq", "fsdp"), None),
            P(("seq", "fsdp"), None),
            P("fsdp", None, "seq"),
        ),
        check_vma=False,
    )
```

profile of v0, /device:TPU:20, one launch (start us, length us, event | category | flops | bytes accessed | tf_op | source)
XLA Modules:
  0.0 2441.9 jit_solution(9380614354438782766)
XLA Ops:
  10.7 36.0 %all-gather.1 = bf16[32,8,2]{1,2,0:T(2,128)(2,1)S(1)} all-gather(bf16[1,8,2]{1,2,0:T(2,128)(2,1)} %bitcast.465), channel_id=1, replica_groups=mesh['seq'=4,'fsdp'=8] {'seq','fsdp'}, dimensions={0}, use_global_device_ids=true | all-gather | bytes 1056 | tf_op jit(solution)/shard_map/all_gather | solution.py:130
  46.9 37.4 %all-gather = bf16[32,64,6]{1,2,0:T(8,128)(2,1)S(1)} all-gather(bf16[1,64,6]{1,2,0:T(8,128)(2,1)} %bitcast.464), channel_id=1, replica_groups=mesh['seq'=4,'fsdp'=8] {'seq','fsdp'}, dimensions={0}, use_global_device_ids=true | all-gather | bytes 25344 | tf_op jit(solution)/shard_map/all_gather | solution.py:129
  92.2 33.3 %all-gather.15.cloned.1.call-done = bf16[2048,512]{1,0:T(8,128)(2,1)} async-done(((bf16[64,512]{1,0:T(8,128)(2,1)}), bf16[2048,512]{1,0:T(8,128)(2,1)}) %all-gather.15.cloned.1.call-update) | async-done | bytes 2097168 | tf_op jit(solution)/shard_map/all_gather | solution.py:124
  132.6 4.8 all-to-all-start
  139.3 72.7 %all-gather.13.cloned.1.call-done = bf16[2048,2048]{1,0:T(8,128)(2,1)} async-done(((bf16[64,2048]{1,0:T(8,128)(2,1)}), bf16[2048,2048]{1,0:T(8,128)(2,1)}) %all-gather.13.cloned.1.call-update) | async-done | bytes 8388624 | tf_op jit(solution)/shard_map/all_gather | solution.py:123
  212.0 5.8 fusion.164
  228.1 4.8 all-to-all-start.2
  237.8 13.6 all-to-all-done.2
  251.4 4.8 all-to-all-start.1
  256.2 13.9 all_gather.47
  293.4 4.4 all-to-all-start.3
  297.8 37.3 %all_gather.52 = bf16[2048,128]{1,0:T(8,128)(2,1)S(1)} all-gather(bf16[64,128]{1,0:T(8,128)(2,1)S(1)} %copy-done.109), channel_id=1, replica_groups=mesh['seq'=4,'fsdp'=8] {'seq','fsdp'}, dimensions={0}, use_global_device_ids=true | all-gather | bytes 540672 | tf_op jit(solution)/shard_map/all_gather | solution.py:127
  338.4 6.2 multiply_reduce_fusion.9
  349.0 53.8 %all-gather.19.cloned.1.call-done = bf16[1024,1,2048]{2,0,1:T(8,128)(2,1)} async-done(((bf16[256,1,2048]{2,0,1:T(8,128)(2,1)}), bf16[1024,1,2048]{2,0,1:T(8,128)(2,1)}) %all-gather.19.cloned.1.call-update) | async-done | bytes 4194320 | tf_op jit(solution)/shard_map/all_gather | solution.py:160
  402.8 219.6 %all-gather.21.cloned.1.call-done = bf16[2048,3,2048]{2,0,1:T(8,128)(2,1)} async-done(((bf16[256,3,2048]{2,0,1:T(8,128)(2,1)}), bf16[2048,3,2048]{2,0,1:T(8,128)(2,1)}) %all-gather.21.cloned.1.call-update) | async-done | bytes 25165840 | tf_op jit(solution)/shard_map/all_gather | solution.py:155
  622.3 21.5 fusion.29
  643.8 5.8 copy-done.13
  654.7 13.6 fusion.42
  669.0 85.7 %reduce-scatter.18.cloned.1.call-done = f32[256,1,2048]{2,0,1:T(8,128)} async-done(((f32[1024,1,2048]{2,0,1:T(8,128)}), f32[256,1,2048]{2,0,1:T(8,128)}) %reduce-scatter.18.cloned.1.call-update) | async-done | bytes 2097168 | tf_op jit(solution)/shard_map/reduce_scatter | solution.py:250
  757.4 55.7 %all-gather.23.cloned.1.call-done = bf16[2048,512]{1,0:T(8,128)(2,1)} async-done(((bf16[64,512]{1,0:T(8,128)(2,1)}), bf16[2048,512]{1,0:T(8,128)(2,1)}) %all-gather.23.cloned.1.call-update) | async-done | bytes 2097168 | tf_op jit(solution)/shard_map/all_gather | solution.py:128
  826.1 53.0 %all-gather.25.cloned.1.call-done = bf16[1024,1,2048]{2,0,1:T(8,128)(2,1)} async-done(((bf16[256,1,2048]{2,0,1:T(8,128)(2,1)}), bf16[1024,1,2048]{2,0,1:T(8,128)(2,1)}) %all-gather.25.cloned.1.call-update) | async-done | bytes 4194320 | tf_op jit(solution)/shard_map/all_gather | solution.py:160
  879.1 22.6 fusion.78
  903.7 22.6 fusion.45
  928.6 25.0 %convolution_convert_fusion = bf16[2048,2,2048]{2,0,1:T(8,128)(2,1)} fusion(bf16[1024,1,2048]{2,0,1:T(8,128)(2,1)} %get-tuple-element.145, bf16[1024,1,2048]{2,0,1:T(8,128)(2,1)} %copy-done.116, bf16[1024,1,2048]{2,0,1:T(8,128)(2,1)} %all-gather.19.cloned.1.call-done), kind=kOutput, calls=%fused_computation.9 | convolution fusion | flops 17205035008 | bytes 29360128 | tf_op jit(solution)/shard_map/tsd,tscf->dcf/dot_general | solution.py:327
  953.6 25.5 %reduce-scatter.20.cloned.1.call-done = bf16[256,1,2048]{2,0,1:T(8,128)(2,1)} async-done(((bf16[1024,1,2048]{2,0,1:T(8,128)(2,1)}), bf16[256,1,2048]{2,0,1:T(8,128)(2,1)}) %reduce-scatter.20.cloned.1.call-update) | async-done | bytes 1048592 | tf_op jit(solution)/shard_map/reduce_scatter | solution.py:319
  981.8 5.0 fusion.123
  988.1 6.5 convolution_convert_fusion.1
  1000.2 14.1 convert_bitcast_fusion
  1017.9 7.1 fusion.141
  1028.8 4.4 all-to-all-start.7
  1033.3 4.6 fusion.247
  1037.9 14.9 fusion.135
  1059.1 15.1 fusion.138
  1112.7 5.9 convolution_bitcast_fusion.3
  1123.1 20.9 pad_maximum_fusion
  1149.0 5.4 copy.441
  1167.6 9.7 fusion.248
  1177.6 9.5 fusion.159
  1193.0 40.9 %all-reduce.6 = f32[256,2]{0,1:T(2,128)S(1)} all-reduce(f32[256,2]{0,1:T(2,128)S(1)} %pad_add_fusion.1), channel_id=11, replica_groups=mesh['seq'=4,'fsdp'=8] {'seq','fsdp'}, use_global_device_ids=true, to_apply=%region_42.43.clone | all-reduce | flops 512 | bytes 4096
  1234.5 12.4 reduce-scatter.36.cloned.1.call-done
  1248.3 253.6 %reduce-scatter.30.cloned.1.call-done = bf16[256,3,2048]{2,0,1:T(8,128)(2,1)} async-done(((bf16[2048,3,2048]{2,0,1:T(8,128)(2,1)}), bf16[256,3,2048]{2,0,1:T(8,128)(2,1)}) %reduce-scatter.30.cloned.1.call-update) | async-done | bytes 3145744 | tf_op jit(solution)/shard_map/reduce_scatter | solution.py:331
  1501.9 5.4 convert_element_type.302
  1507.3 129.5 %reduce-scatter.34.cloned.1.call-done = f32[64,512]{1,0:T(8,128)} async-done(((f32[2048,512]{1,0:T(8,128)}), f32[64,512]{1,0:T(8,128)}) %reduce-scatter.34.cloned.1.call-update) | async-done | bytes 131088
  1636.8 134.5 %reduce-scatter.32.cloned.1.call-done = f32[64,128]{1,0:T(8,128)} async-done(((f32[2048,128]{1,0:T(8,128)}), f32[64,128]{1,0:T(8,128)}) %reduce-scatter.32.cloned.1.call-update) | async-done | bytes 32784
  1771.3 141.4 %reduce-scatter.26.cloned.1.call-done = f32[64,512]{1,0:T(8,128)} async-done(((f32[2048,512]{1,0:T(8,128)}), f32[64,512]{1,0:T(8,128)}) %reduce-scatter.26.cloned.1.call-update) | async-done | bytes 131088 | tf_op jit(solution)/shard_map/reduce_scatter | solution.py:438
  1912.7 142.1 %reduce-scatter.24.cloned.1.call-done = f32[64,512]{1,0:T(8,128)} async-done(((f32[2048,512]{1,0:T(8,128)}), f32[64,512]{1,0:T(8,128)}) %reduce-scatter.24.cloned.1.call-update) | async-done | bytes 131088 | tf_op jit(solution)/shard_map/reduce_scatter | solution.py:437
  2054.8 192.9 %reduce-scatter.28.cloned.1.call-done = f32[64,2048]{1,0:T(8,128)} async-done(((f32[2048,2048]{1,0:T(8,128)}), f32[64,2048]{1,0:T(8,128)}) %reduce-scatter.28.cloned.1.call-update) | async-done | bytes 524304 | tf_op jit(solution)/shard_map/reduce_scatter | solution.py:439
  2247.7 187.1 %reduce-scatter.22.cloned.1.call-done = f32[64,2048]{1,0:T(8,128)} async-done(((f32[2048,2048]{1,0:T(8,128)}), f32[64,2048]{1,0:T(8,128)}) %reduce-scatter.22.cloned.1.call-update) | async-done | bytes 524304 | tf_op jit(solution)/shard_map/reduce_scatter | solution.py:436
  (421 shorter events, 183.6 us)
Async XLA Ops:
  7.2 79.4 %copy-start = (bf16[256,1,2048]{2,0,1:T(8,128)(2,1)S(1)}, bf16[256,1,2048]{2,0,1:T(8,128)(2,1)}, u32[]{:S(2)}) copy-start(bf16[256,1,2048]{2,0,1:T(8,128)(2,1)} %param.14) | copy-start | bytes 3145732
  7.2 80.9 %all-gather.11.cloned.1.call-start = ((), (), s32[]{:S(2)}) async-start(), calls=%async_computation.18 | async-start | bytes 2162688 | tf_op jit(solution)/shard_map/all_gather | solution.py:125
  7.9 117.6 %all-gather.15.cloned.1.call-start = ((), (), s32[]{:S(2)}) async-start(), calls=%async_computation.20 | async-start | bytes 2162688 | tf_op jit(solution)/shard_map/all_gather | solution.py:124
  8.7 203.4 %all-gather.13.cloned.1.call-start = ((), (), s32[]{:S(2)}) async-start(), calls=%async_computation.19 | async-start | bytes 8650752 | tf_op jit(solution)/shard_map/all_gather | solution.py:123
  9.4 328.9 %all-gather.17.cloned.1.call-start = ((), (), s32[]{:S(2)}) async-start(), calls=%async_computation.21 | async-start | bytes 8650752 | tf_op jit(solution)/shard_map/all_gather | solution.py:126
  85.5 52.1 %copy-start.39 = (f32[256,256]{1,0:T(8,128)}, f32[256,256]{1,0:T(8,128)S(1)}, u32[]{:S(2)}) copy-start(f32[256,256]{1,0:T(8,128)S(1)} %get-tuple-element.159) | copy-start | bytes 786436
  85.5 52.1 %copy-start.41 = (f32[256,256]{1,0:T(8,128)}, f32[256,256]{1,0:T(8,128)S(1)}, u32[]{:S(2)}) copy-start(f32[256,256]{1,0:T(8,128)S(1)} %get-tuple-element.158) | copy-start | bytes 786436
  85.7 147.6 %copy-start.44 = (f32[256,256]{0,1:T(8,128)}, f32[256,256]{0,1:T(8,128)S(1)}, u32[]{:S(2)}) copy-start(f32[256,256]{0,1:T(8,128)S(1)} %copy.380) | copy-start | bytes 786436
  86.8 125.2 %copy-start.78 = (f32[256]{0:T(256)}, f32[256]{0:T(256)S(1)}, u32[]{:S(2)}) copy-start(f32[256]{0:T(256)S(1)} %add_rsqrt_fusion.5) | copy-start | bytes 3076
  87.4 50.3 %copy-start.95 = (f32[256,1]{0,1:T(1,128)}, f32[256,1]{0,1:T(1,128)S(1)}, u32[]{:S(2)}) copy-start(f32[256,1]{0,1:T(1,128)S(1)} %get-tuple-element.166) | copy-start | bytes 3076
  88.1 256.6 %copy-start.59 = (f32[2048,1]{0,1:T(1,128)}, f32[2048,1]{0,1:T(1,128)S(1)}, u32[]{:S(2)}) copy-start(f32[2048,1]{0,1:T(1,128)S(1)} %get-tuple-element.165) | copy-start | bytes 24580
  90.4 37.7 %copy-start.23 = (f32[256,512]{1,0:T(8,128)}, f32[256,512]{1,0:T(8,128)S(1)}, u32[]{:S(2)}) copy-start(f32[256,512]{1,0:T(8,128)S(1)} %fusion.166) | copy-start | bytes 1572868
  90.8 37.4 %copy-start.25 = (f32[256,1,2,256]{3,2,0,1:T(2,128)}, f32[256,1,2,256]{3,2,0,1:T(2,128)S(1)}, u32[]{:S(2)}) copy-start(f32[256,1,2,256]{3,2,0,1:T(2,128)S(1)} %reshape.1014) | copy-start | bytes 1572868
  92.2 38.2 %copy-start.107 = (f32[256,2]{0,1:T(2,128)}, f32[256,2]{0,1:T(2,128)S(1)}, u32[]{:S(2)}) copy-start(f32[256,2]{0,1:T(2,128)S(1)} %copy.373) | copy-start | bytes 6148
  132.6 93.5 %all-to-all-start = ((bf16[256,1,8,256]{3,0,1,2:T(8,128)(2,1)}), bf16[256,1,8,256]{3,0,1,2:T(8,128)(2,1)}, u32[]{:S(2)}, u32[]{:S(2)}) async-start(bf16[256,1,8,256]{3,0,1,2:T(8,128)(2,1)} %bitcast.400), calls=%async_computation | async-start | bytes 2097152 | tf_op jit(solution)/shard_map/all_to_all | solution.py:219
  137.4 80.4 %copy-start.105 = (f32[256,2]{0,1:T(2,128)}, f32[256,2]{0,1:T(2,128)S(1)}, u32[]{:S(2)}) copy-start(f32[256,2]{0,1:T(2,128)S(1)} %multiply_reduce_fusion.13) | copy-start | bytes 6148
  137.5 80.3 %copy-start.84 = (f32[256,2]{0,1:T(2,128)}, f32[256,2]{0,1:T(2,128)S(1)}, u32[]{:S(2)}) copy-start(f32[256,2]{0,1:T(2,128)S(1)} %fusion.211) | copy-start | bytes 6148
  228.1 23.3 all-to-all-start.2
  235.6 20.7 copy-start.115
  251.4 27.6 %all-to-all-start.1 = ((bf16[256,1,8,256]{3,0,1,2:T(8,128)(2,1)}), bf16[256,1,8,256]{3,0,1,2:T(8,128)(2,1)}, u32[]{:S(2)}, u32[]{:S(2)}) async-start(bf16[256,1,8,256]{3,0,1,2:T(8,128)(2,1)} %copy.382), calls=%async_computation.1 | async-start | bytes 2097152 | tf_op jit(solution)/shard_map/all_to_all | solution.py:217
  289.7 45.4 %copy-start.79 = (f32[256]{0:T(256)S(1)}, f32[256]{0:T(256)}, u32[]{:S(2)}) copy-start(f32[256]{0:T(256)} %copy-done.78) | copy-start | bytes 3076
  293.4 44.2 %all-to-all-start.3 = ((bf16[1024,1,2,256]{3,2,1,0:T(2,128)(2,1)}), bf16[1024,1,2,256]{3,2,1,0:T(2,128)(2,1)S(1)}, u32[]{:S(2)}, u32[]{:S(2)}) async-start(bf16[1024,1,2,256]{3,2,1,0:T(2,128)(2,1)} %copy.392), calls=%async_computation.3 | async-start | bytes 2097152 | tf_op jit(solution)/shard_map/all_to_all | solution.py:225
  297.8 105.0 %all-gather.19.cloned.1.call-start = ((), (), s32[]{:S(2)}) async-start(), calls=%async_computation.22 | async-start | bytes 5242880 | tf_op jit(solution)/shard_map/all_gather | solution.py:160
  347.9 274.4 %all-gather.21.cloned.1.call-start = ((), (), s32[]{:S(2)}) async-start(), calls=%async_computation.23 | async-start | bytes 28311552 | tf_op jit(solution)/shard_map/all_gather | solution.py:155
  348.5 406.2 %reduce-scatter.18.cloned.1.call-start = ((), (), s32[]{:S(2)}) async-start(), calls=%async_computation.24 | async-start | bytes 10485760 | tf_op jit(solution)/shard_map/reduce_scatter | solution.py:250
  668.2 144.9 %all-gather.23.cloned.1.call-start = ((), (), s32[]{:S(2)}) async-start(), calls=%async_computation.25 | async-start | bytes 2162688 | tf_op jit(solution)/shard_map/all_gather | solution.py:128
  669.0 210.1 %all-gather.25.cloned.1.call-start = ((), (), s32[]{:S(2)}) async-start(), calls=%async_computation.26 | async-start | bytes 5242880 | tf_op jit(solution)/shard_map/all_gather | solution.py:160
  757.4 60.2 %copy-start.14 = (bf16[256,1,2048]{2,0,1:T(8,128)(2,1)}, bf16[256,1,2048]{2,0,1:T(8,128)(2,1)S(1)}, u32[]{:S(2)}) copy-start(bf16[256,1,2048]{2,0,1:T(8,128)(2,1)S(1)} %add_convert_fusion) | copy-start | bytes 3145732
  757.4 57.5 %copy-start.66 = (bf16[256,1,256]{2,0,1:T(8,128)(2,1)S(1)}, bf16[256,1,256]{2,0,1:T(8,128)(2,1)}, u32[]{:S(2)}) copy-start(bf16[256,1,256]{2,0,1:T(8,128)(2,1)} %param.15) | copy-start | bytes 393220
  825.9 153.3 %reduce-scatter.20.cloned.1.call-start = ((), (), s32[]{:S(2)}) async-start(), calls=%async_computation.27 | async-start | bytes 5242880 | tf_op jit(solution)/shard_map/reduce_scatter | solution.py:319
  928.5 50.6 %copy-start.77 = (f32[2048,1]{0,1:T(1,128)S(1)}, f32[2048,1]{0,1:T(1,128)}, u32[]{:S(2)}) copy-start(f32[2048,1]{0,1:T(1,128)} %get-tuple-element.162) | copy-start | bytes 24580
  928.6 50.6 %copy-start.110 = (f32[256]{0:T(256)S(1)}, f32[256]{0:T(256)}, u32[]{:S(2)}) copy-start(f32[256]{0:T(256)} %get-tuple-element.168) | copy-start | bytes 3076
  953.6 28.1 %copy-start.100 = (f32[256]{0:T(256)S(1)}, f32[256]{0:T(256)}, u32[]{:S(2)}) copy-start(f32[256]{0:T(256)} %copy-done.99) | copy-start | bytes 3076
  953.6 28.1 %copy-start.102 = (f32[256]{0:T(256)S(1)}, f32[256]{0:T(256)}, u32[]{:S(2)}) copy-start(f32[256]{0:T(256)} %copy-done.101) | copy-start | bytes 3076
  953.6 28.1 %copy-start.112 = (f32[256]{0:T(256)S(1)}, f32[256]{0:T(256)}, u32[]{:S(2)}) copy-start(f32[256]{0:T(256)} %copy-done.111) | copy-start | bytes 3076
  988.1 26.3 %copy-start.15 = (bf16[256,2048]{1,0:T(8,128)(2,1)}, bf16[256,2048]{1,0:T(8,128)(2,1)S(1)}, u32[]{:S(2)}) copy-start(bf16[256,2048]{1,0:T(8,128)(2,1)S(1)} %get-tuple-element.148) | copy-start | bytes 3145732
  996.1 19.5 all-to-all-start.4
  1028.8 26.1 %all-to-all-start.7 = ((bf16[1024,1,2,256]{3,2,1,0:T(2,128)(2,1)}), bf16[1024,1,2,256]{3,2,1,0:T(2,128)(2,1)}, u32[]{:S(2)}, u32[]{:S(2)}) async-start(bf16[1024,1,2,256]{3,2,1,0:T(2,128)(2,1)} %copy.416), calls=%async_computation.9 | async-start | bytes 2097152 | tf_op jit(solution)/shard_map/all_to_all | solution.py:377
  1054.9 31.0 %all-to-all-start.6 = ((bf16[1024,1,2,256]{3,2,1,0:T(2,128)(2,1)}), bf16[1024,1,2,256]{3,2,1,0:T(2,128)(2,1)S(1)}, u32[]{:S(2)}, u32[]{:S(2)}) async-start(bf16[1024,1,2,256]{3,2,1,0:T(2,128)(2,1)} %copy.406), calls=%async_computation.8 | async-start | bytes 2097152 | tf_op jit(solution)/shard_map/all_to_all | solution.py:374
  1086.9 17.2 all-to-all-start.5
  1091.1 155.8 %reduce-scatter.36.cloned.1.call-start = ((), (), s32[]{:S(2)}) async-start(), calls=%async_computation.35 | async-start | bytes 1081344
  1122.7 379.2 %reduce-scatter.30.cloned.1.call-start = ((), (), s32[]{:S(2)}) async-start(), calls=%async_computation.32 | async-start | bytes 28311552 | tf_op jit(solution)/shard_map/reduce_scatter | solution.py:331
  1144.1 492.8 %reduce-scatter.34.cloned.1.call-start = ((), (), s32[]{:S(2)}) async-start(), calls=%async_computation.34 | async-start | bytes 4325376
  1154.4 616.9 %reduce-scatter.32.cloned.1.call-start = ((), (), s32[]{:S(2)}) async-start(), calls=%async_computation.33 | async-start | bytes 1081344
  1160.8 751.9 %reduce-scatter.26.cloned.1.call-start = ((), (), s32[]{:S(2)}) async-start(), calls=%async_computation.30 | async-start | bytes 4325376 | tf_op jit(solution)/shard_map/reduce_scatter | solution.py:438
  1163.7 891.1 %reduce-scatter.24.cloned.1.call-start = ((), (), s32[]{:S(2)}) async-start(), calls=%async_computation.29 | async-start | bytes 4325376 | tf_op jit(solution)/shard_map/reduce_scatter | solution.py:437
  1167.5 1080.2 %reduce-scatter.28.cloned.1.call-start = ((), (), s32[]{:S(2)}) async-start(), calls=%async_computation.31 | async-start | bytes 17301504 | tf_op jit(solution)/shard_map/reduce_scatter | solution.py:439
  1177.3 1257.5 %reduce-scatter.22.cloned.1.call-start = ((), (), s32[]{:S(2)}) async-start(), calls=%async_computation.28 | async-start | bytes 17301504 | tf_op jit(solution)/shard_map/reduce_scatter | solution.py:436
  (95 other events, 335.0 us)
Sparse Core Ops, SparseCore 0:
  11.0 56.0 all-gather.10
  70.1 55.4 all-gather.14
  128.5 83.4 all-gather.12
  214.9 80.6 all-gather.16
  348.1 54.6 all-gather.18
  404.2 218.0 all-gather.20
  668.4 86.2 reduce-scatter.17
  758.1 54.9 all-gather.22
  826.0 53.1 all-gather.24
  926.5 52.6 reduce-scatter.19
  1122.8 124.0 reduce-scatter.35
  1249.2 252.6 reduce-scatter.29
  1504.8 131.9 reduce-scatter.33
  1639.6 131.6 reduce-scatter.31
  1774.0 138.6 reduce-scatter.25
  1915.4 139.3 reduce-scatter.23
  2057.5 190.1 reduce-scatter.27
  2250.4 184.3 reduce-scatter.21
where the time goes:
time: 2460 us; the launch traced here: 2440 us
  waiting for transfers between devices  1810 us (74%)
  matrix products  238 us (10%)
  blocking collectives  166 us (7%)
  local copies, waits for them, and re-layouts  94.2 us (4%)
  other arithmetic  80.5 us (3%)
  starting transfers between devices  37.7 us (2%)
    unnamed x21, waiting for transfers between devices  280 us
    reduce_scatter x1, waiting for transfers between devices, body(): lax.psum_scatter(jnp.concatenate([first_pair, down_grad[:, None]], 1).ast...  254 us
    all_gather x1, waiting for transfers between devices, fetch(): mlp_full = lax.all_gather(w_mlp, 'fsdp', axis=0, tiled=True)  220 us
    reduce_scatter x1, waiting for transfers between devices, body(): lax.psum_scatter(grad_out_map, ('seq', 'fsdp'), scatter_dimension=0, tile...  193 us
    reduce_scatter x1, waiting for transfers between devices, body(): lax.psum_scatter(grad_query_map, ('seq', 'fsdp'), scatter_dimension=0, ti...  187 us
    reduce_scatter x1, waiting for transfers between devices, body(): lax.psum_scatter(grad_key_map, ('seq', 'fsdp'), scatter_dimension=0, tile...  142 us
    reduce_scatter x1, waiting for transfers between devices, body(): lax.psum_scatter(grad_value_map, ('seq', 'fsdp'), scatter_dimension=0, ti...  141 us
    all_gather x2, waiting for transfers between devices, group_rows(): return lax.all_gather(source, 'seq', axis=0, tiled=True)  107 us
  transfers between devices with their start and end apart: 26, of which 17 were waited for; matrix products, arithmetic and copies ran while one was open for 10% of the time, Pallas kernels for 0%

commit v1 on v0

--- a/solution.py
+++ b/solution.py
@@ -114,46 +114,6 @@
         "shqk,qshd->kshd", grad_scores, q_heads, preferred_element_type=jnp.float32
     )
     return (grad_q_heads, grad_k_heads, grad_v_heads)
-
-
-def fetch_attn(
-    w_query, key_matrix, value_matrix, w_out_t, laurel_maps, per_layer_maps, norm_gains, head_gains
-):
-    return (
-        lax.all_gather(w_query, ("seq", "fsdp"), axis=0, tiled=True),
-        lax.all_gather(key_matrix, ("seq", "fsdp"), axis=0, tiled=True),
-        lax.all_gather(value_matrix, ("seq", "fsdp"), axis=0, tiled=True),
-        lax.all_gather(w_out_t, ("seq", "fsdp"), axis=0, tiled=True),
-        lax.all_gather(laurel_maps, ("seq", "fsdp"), axis=0, tiled=True),
-        lax.all_gather(per_layer_maps, ("seq", "fsdp"), axis=0, tiled=True),
-        lax.all_gather(norm_gains, ("seq", "fsdp"), axis=0, tiled=True),
-        lax.all_gather(head_gains, ("seq", "fsdp"), axis=0, tiled=True),
-    )
-
-
-def fetch(
-    w_query,
-    key_matrix,
-    value_matrix,
-    w_out_t,
-    laurel_maps,
-    per_layer_maps,
-    norm_gains,
-    head_gains,
-    w_mlp,
-):
-    attn_full = fetch_attn(
-        w_query,
-        key_matrix,
-        value_matrix,
-        w_out_t,
-        laurel_maps,
-        per_layer_maps,
-        norm_gains,
-        head_gains,
-    )
-    mlp_full = lax.all_gather(w_mlp, "fsdp", axis=0, tiled=True)
-    return (attn_full, mlp_full)
 
 
 def group_rows(source):
@@ -178,19 +138,19 @@
 ):
     leading_dims = hidden_in.shape[:2]
     query_group_count = QUERY_HEADS // KEY_VALUE_HEADS
-    attn_full, mlp_full = fetch(
-        w_query,
-        key_matrix,
-        value_matrix,
-        w_out_t,
-        laurel_maps,
-        per_layer_maps,
-        norm_gains,
-        head_gains,
-        w_mlp,
-    )
-    full_query, full_key, full_value, full_out, full_laurel, full_ple, full_gains, full_heads = (
-        attn_full
+    packed = jnp.concatenate(
+        [w_query, key_matrix, value_matrix, w_out_t, laurel_maps, per_layer_maps, norm_gains], 1
+    )
+    packed_full = lax.all_gather(packed, ("seq", "fsdp"), axis=0, tiled=True)
+    full_heads = lax.all_gather(head_gains, ("seq", "fsdp"), axis=0, tiled=True)
+    mlp_full = lax.all_gather(w_mlp, "fsdp", axis=0, tiled=True)
+    widths = [
+        w.shape[1]
+        for w in (w_query, key_matrix, value_matrix, w_out_t, laurel_maps, per_layer_maps)
+    ]
+    cuts = [sum(widths[: i + 1]) for i in range(len(widths))]
+    full_query, full_key, full_value, full_out, full_laurel, full_ple, full_gains = jnp.split(
+        packed_full, cuts, axis=1
     )
     gain_table = full_gains.astype(jnp.float32)
     head_scale = full_heads.astype(jnp.float32)
@@ -248,11 +208,13 @@
     down_map = mlp_full[:, 2]
     picked = hidden
     ffn_out = lax.psum_scatter(
-        jnp.einsum("tsf,df->tsd", picked, down_map, preferred_element_type=jnp.float32),
+        jnp.einsum("tsf,df->tsd", picked, down_map, preferred_element_type=jnp.float32).astype(
+            jnp.bfloat16
+        ),
         "seq",
         scatter_dimension=0,
         tiled=True,
-    )
+    ).astype(jnp.float32)
     ffn_normed, ffn_inverse = norm_rows(ffn_out, gain_table[:, 4])
     h_second = (mixed + ffn_normed).astype(jnp.bfloat16)
     ple_gate = jnp.einsum(
@@ -265,29 +227,11 @@
     )
     ple_normed, ple_inverse = norm_rows(ple_proj, gain_table[:, 5])
     hidden_out = (h_second.astype(jnp.float32) + ple_normed).astype(jnp.bfloat16)
-    attn_back, mlp_back = fetch(
-        w_query,
-        key_matrix,
-        value_matrix,
-        w_out_t,
-        laurel_maps,
-        per_layer_maps,
-        norm_gains,
-        head_gains,
-        w_mlp,
-    )
-    (
-        back_query,
-        back_key,
-        back_value,
-        back_out_map,
-        back_laurel,
-        back_ple,
-        back_gains,
-        back_heads,
-    ) = attn_back
-    gain_back = back_gains.astype(jnp.float32)
-    head_back = back_heads.astype(jnp.float32)
+    mlp_back = mlp_full
+    back_query, back_key, back_value, back_out_map = full_query, full_key, full_value, full_out
+    back_laurel, back_ple = full_laurel, full_ple
+    gain_back = gain_table
+    head_back = head_scale
     grad_out = out_cotangent.astype(jnp.float32)
     grad_ple_proj, gain_grad_five = norm_back(ple_proj, ple_inverse, gain_back[:, 5], grad_out)
     grad_ple_low = grad_ple_proj.astype(jnp.bfloat16)
@@ -432,16 +376,24 @@
     )
     laurel_grad = jnp.concatenate([grad_laurel_down, grad_laurel_up], 1)
     ple_grad = jnp.concatenate([grad_ple_down, grad_ple_up], 1)
-    summed = (
-        lax.psum_scatter(grad_query_map, ("seq", "fsdp"), scatter_dimension=0, tiled=True),
-        lax.psum_scatter(grad_key_map, ("seq", "fsdp"), scatter_dimension=0, tiled=True),
-        lax.psum_scatter(grad_value_map, ("seq", "fsdp"), scatter_dimension=0, tiled=True),
-        lax.psum_scatter(grad_out_map, ("seq", "fsdp"), scatter_dimension=0, tiled=True),
-        lax.psum_scatter(laurel_grad, ("seq", "fsdp"), scatter_dimension=0, tiled=True),
-        lax.psum_scatter(ple_grad, ("seq", "fsdp"), scatter_dimension=0, tiled=True),
-        lax.psum_scatter(gain_grads, ("seq", "fsdp"), scatter_dimension=0, tiled=True),
-        lax.psum_scatter(grad_head_scale, ("seq", "fsdp"), scatter_dimension=0, tiled=True),
-    )
+    packed_grads = jnp.concatenate(
+        [
+            grad_query_map,
+            grad_key_map,
+            grad_value_map,
+            grad_out_map,
+            laurel_grad,
+            ple_grad,
+            gain_grads,
+        ],
+        1,
+    ).astype(jnp.bfloat16)
+    packed_sum = lax.psum_scatter(
+        packed_grads, ("seq", "fsdp"), scatter_dimension=0, tiled=True
+    ).astype(jnp.float32)
+    summed = jnp.split(packed_sum, cuts, axis=1) + [
+        lax.psum_scatter(grad_head_scale, ("seq", "fsdp"), scatter_dimension=0, tiled=True)
+    ]
     return (
         hidden_out,
         input_grad,

time: 2460 us -> 1350 us (0.55)
  waiting for transfers between devices: 1810 us -> 590 us
  local copies, waits for them, and re-layouts: 94.2 us -> 254 us
  blocking collectives: 166 us -> 93.8 us
    reduce_scatter x4 -> x0, waiting for transfers between devices: 664 us -> none  [the longest x1 193 us: body(): lax.psum_scatter(grad_out_map, ('seq', 'fsdp'), scatter_dimension=0, tile...]
    reduce_scatter x1, waiting for transfers between devices: 254 us -> 0.01 us  [body(): lax.psum_scatter(jnp.concatenate([first_pair, down_grad[:, None]], 1).ast...]
    all_gather x6 -> x2, waiting for transfers between devices: 381 us -> 204 us  [the longest x1 110 us: body(): packed_full = lax.all_gather(packed, ('seq', 'fsdp'), axis=0, tiled=True)]
    concatenate x0 -> x2, local copies, waits for them, and re-layouts: none -> 102 us  [the longest x1 102 us: body(): jnp.concatenate([grad_query_map, grad_key_map, grad_value_map, grad_out_m...]
    all_gather x3 -> x1, blocking collectives: 111 us -> 35.9 us  [body(): full_heads = lax.all_gather(head_gains, ('seq', 'fsdp'), axis=0, tiled=True)]
    unnamed x21 -> x9, waiting for transfers between devices: 280 us -> 207 us
    reduce_scatter x1, waiting for transfers between devices: 85.7 us -> 52.6 us  [body(): lax.psum_scatter(jnp.einsum('tsf,df->tsd', picked, down_map, preferred_el...]
    unnamed x243 -> x230, local copies, waits for them, and re-layouts: 44 us -> 74.7 us
  transfers between devices with their start and end apart: 26 -> 16, of which waited for: 17 -> 9; matrix products, arithmetic and copies ran while one was open for 10% -> 34% of each run, Pallas kernels for 0% -> 0%
where the time goes in v1:
time: 1350 us; the launch traced here: 1330 us
  waiting for transfers between devices  590 us (44%)
  local copies, waits for them, and re-layouts  254 us (19%)
  matrix products  249 us (18%)
  blocking collectives  93.8 us (7%)
  other arithmetic  86 us (6%)
  starting transfers between devices  39.3 us (3%)
  between operations  15.8 us (1%)
    unnamed x9, waiting for transfers between devices  207 us
    all_gather x1, waiting for transfers between devices, body(): packed_full = lax.all_gather(packed, ('seq', 'fsdp'), axis=0, tiled=True)  110 us
    all_gather x2, waiting for transfers between devices, group_rows(): return lax.all_gather(source, 'seq', axis=0, tiled=True)  108 us
    concatenate x1, local copies, waits for them, and re-layouts, body(): jnp.concatenate([grad_query_map, grad_key_map, grad_value_map, grad_out_m...  102 us
    all_gather x1, waiting for transfers between devices, body(): mlp_full = lax.all_gather(w_mlp, 'fsdp', axis=0, tiled=True)  93.8 us
    unnamed x230, local copies, waits for them, and re-layouts  74.7 us
    reduce_scatter x1, waiting for transfers between devices, body(): lax.psum_scatter(jnp.einsum('tsf,df->tsd', picked, down_map, preferred_el...  52.6 us
    unnamed x1, blocking collectives  42.7 us
  transfers between devices with their start and end apart: 16, of which 9 were waited for; matrix products, arithmetic and copies ran while one was open for 34% of the time, Pallas kernels for 0%

profile of v1, /device:TPU:20, one launch (start us, length us, event | category | flops | bytes accessed | tf_op | source)
XLA Modules:
  0.0 1326.9 jit_solution(17616267589059849791)
XLA Ops:
  14.9 35.9 %all-gather = bf16[32,8,2]{1,2,0:T(2,128)(2,1)S(1)} all-gather(bf16[1,8,2]{1,2,0:T(2,128)(2,1)S(1)} %bitcast.409), channel_id=1, replica_groups=mesh['seq'=4,'fsdp'=8] {'seq','fsdp'}, dimensions={0}, use_global_device_ids=true | all-gather | bytes 1056 | tf_op jit(solution)/shard_map/all_gather | solution.py:145
  54.3 109.8 %all-gather.6.cloned.1.call-done = bf16[2048,5766]{1,0:T(8,128)(2,1)} async-done(((bf16[64,5766]{1,0:T(8,128)(2,1)}), bf16[2048,5766]{1,0:T(8,128)(2,1)}) %all-gather.6.cloned.1.call-update) | async-done | bytes 23617552 | tf_op jit(solution)/shard_map/all_gather | solution.py:144
  173.1 4.8 all-to-all-start
  177.9 7.2 fusion.35
  200.8 4.9 all-to-all-start.2
  210.8 8.8 all-to-all-done.2
  219.6 4.8 all-to-all-start.1
  224.3 15.2 %all_gather.19 = s32[1024,1]{0,1:T(1,128)S(1)} all-gather(s32[256,1]{0,1:T(1,128)S(1)} %copy-done.101), channel_id=1, replica_groups=mesh['seq'=4,'fsdp'=8] {'seq'}, dimensions={0}, use_global_device_ids=true | all-gather | bytes 5120 | tf_op jit(solution)/shard_map/all_gather | solution.py:181
  255.2 3.9 fusion.183
  259.1 3.7 copy.429
  262.8 4.3 all-to-all-start.3
  271.6 6.7 all-to-all-done.3
  279.0 6.5 multiply_reduce_fusion.6
  289.1 93.8 %all-gather.10.cloned.1.call-done = bf16[2048,3,2048]{2,0,1:T(8,128)(2,1)} async-done(((bf16[256,3,2048]{2,0,1:T(8,128)(2,1)}), bf16[2048,3,2048]{2,0,1:T(8,128)(2,1)}) %all-gather.10.cloned.1.call-update) | async-done | bytes 25165840 | tf_op jit(solution)/shard_map/all_gather | solution.py:146
  382.9 55.1 %all-gather.8.cloned.1.call-done = bf16[1024,1,2048]{2,0,1:T(8,128)(2,1)} async-done(((bf16[256,1,2048]{2,0,1:T(8,128)(2,1)}), bf16[1024,1,2048]{2,0,1:T(8,128)(2,1)}) %all-gather.8.cloned.1.call-update) | async-done | bytes 4194320 | tf_op jit(solution)/shard_map/all_gather | solution.py:120
  438.0 21.5 %fusion.37 = f32[1024,1,2,2048]{3,0,2,1:T(8,128)S(1)} fusion(bf16[2048,3,2048]{2,0,1:T(8,128)(2,1)} %all-gather.10.cloned.1.call-done, bf16[1024,1,2048]{2,0,1:T(8,128)(2,1)} %all-gather.8.cloned.1.call-done), kind=kOutput, calls=%fused_computation.57 | convolution fusion | flops 17179869184 | bytes 37748736 | tf_op jit(solution)/shard_map/tsd,dcf->tscf/dot_general | solution.py:202
  459.5 5.7 copy-done.12
  470.1 12.8 convert_bitcast_fusion.1
  483.2 52.6 %reduce-scatter.8.cloned.1.call-done = bf16[256,1,2048]{2,0,1:T(8,128)(2,1)} async-done(((bf16[1024,1,2048]{2,0,1:T(8,128)(2,1)}), bf16[256,1,2048]{2,0,1:T(8,128)(2,1)}) %reduce-scatter.8.cloned.1.call-update) | async-done | bytes 1048592 | tf_op jit(solution)/shard_map/reduce_scatter | solution.py:210
  554.0 52.7 %all-gather.12.cloned.1.call-done = bf16[1024,1,2048]{2,0,1:T(8,128)(2,1)} async-done(((bf16[256,1,2048]{2,0,1:T(8,128)(2,1)}), bf16[1024,1,2048]{2,0,1:T(8,128)(2,1)}) %all-gather.12.cloned.1.call-update) | async-done | bytes 4194320 | tf_op jit(solution)/shard_map/all_gather | solution.py:120
  606.6 22.6 %fusion.85 = (bf16[1024,1,2048]{2,0,1:T(8,128)(2,1)S(1)}, bf16[1024,1,2048]{2,0,1:T(8,128)(2,1)}) fusion(f32[1024,1,2,2048]{3,0,2,1:T(8,128)} %copy-done.12, bf16[2048,3,2048]{2,0,1:T(8,128)(2,1)} %all-gather.10.cloned.1.call-done, bf16[1024,1,2048]{2,0,1:T(8,128)(2,1)} %all-gather.12.cloned.1.call-done), kind=kOutput, calls=%fused_computation.95 | convolution fusion | flops 8640266240 | bytes 37748736 | tf_op jit(solution)/shard_map/tsd,df->tsf/dot_general | solution.py:254
  631.2 22.6 %fusion.52 = bf16[1024,1,2048]{2,0,1:T(8,128)(2,1)} fusion(bf16[2048,3,2048]{2,0,1:T(8,128)(2,1)} %all-gather.10.cloned.1.call-done, bf16[1024,1,2048]{2,0,1:T(8,128)(2,1)} %get-tuple-element.151, bf16[1024,1,2048]{2,0,1:T(8,128)(2,1)S(1)} %get-tuple-element.150), kind=kOutput, calls=%fused_computation.63 | convolution fusion | flops 17186160640 | bytes 29360128 | tf_op jit(solution)/shard_map/tscf,dcf->tsd/dot_general | solution.py:264
  654.4 14.1 %convert_bitcast_fusion = bf16[2048,1,2048]{2,0,1:T(8,128)(2,1)} fusion(bf16[1024,1,2048]{2,0,1:T(8,128)(2,1)} %all-gather.12.cloned.1.call-done, bf16[1024,1,1,2048]{3,0,2,1:T(8,128)(2,1)} %copy-done.24), kind=kOutput, calls=%fused_computation.36 | convolution fusion | flops 8594128896 | bytes 16777216 | tf_op jit(solution)/shard_map/tsd,tsf->df/dot_general | solution.py:274
  668.5 25.1 %convolution_convert_fusion = bf16[2048,2,2048]{2,0,1:T(8,128)(2,1)} fusion(bf16[1024,1,2048]{2,0,1:T(8,128)(2,1)} %get-tuple-element.151, bf16[1024,1,2048]{2,0,1:T(8,128)(2,1)} %copy-done.104, bf16[1024,1,2048]{2,0,1:T(8,128)(2,1)} %all-gather.8.cloned.1.call-done), kind=kOutput, calls=%fused_computation.9 | convolution fusion | flops 17205035008 | bytes 29360128 | tf_op jit(solution)/shard_map/tsd,tscf->dcf/dot_general | solution.py:271
  693.6 20.9 %pad_maximum_fusion = bf16[2048,3,2048]{2,0,1:T(8,128)(2,1)} fusion(bf16[2048,1,2048]{2,0,1:T(8,128)(2,1)} %convert_bitcast_fusion, bf16[2048,2,2048]{2,0,1:T(8,128)(2,1)} %convolution_convert_fusion), kind=kLoop, calls=%fused_computation.1 | loop fusion | flops 12582912 | bytes 50331648 | tf_op jit(solution)/shard_map/concatenate | solution.py:276
  727.3 4.2 fusion.156
  732.8 6.6 fusion.103
  740.9 4.9 all-to-all-start.4
  750.5 5.7 convolution_convert_fusion.1
  761.5 7.3 fusion.180
  768.8 3.7 copy.453
  772.5 5.2 all-to-all-start.7
  777.7 6.1 fusion.278
  783.7 15.9 %fusion.174 = bf16[1024,1,2,256]{0,3,2,1:T(8,128)(2,1)} fusion(bf16[1024,2,256]{2,0,1:T(8,128)(2,1)} %bitcast.395, f32[2,1024,1024]{1,2,0:T(8,128)} %fusion.278, f32[2,1024,1024]{1,2,0:T(8,128)} %copy-done.15, f32[2,1024]{1,0:T(2,128)S(1)} %copy-done.100, pred[1024,1024]{0,1:T(8,128)(4,1)S(1)} %copy-done.27), kind=kOutput, calls=%fused_computation.205 | convolution fusion | flops 1097337856 | bytes 19931136 | tf_op jit(solution)/shard_map/shqk,qshd->kshd/dot_general | solution.py:113
  799.6 3.7 copy.443
  803.2 4.4 all-to-all-start.6
  812.9 16.0 %fusion.177 = bf16[1024,1,2,256]{0,3,2,1:T(8,128)(2,1)} fusion(bf16[1024,2,256]{2,0,1:T(8,128)(2,1)} %bitcast.392, f32[2,1024,1024]{1,2,0:T(8,128)} %fusion.278, f32[2,1024,1024]{1,2,0:T(8,128)} %copy-done.15, f32[2,1024]{1,0:T(2,128)S(1)} %copy-done.100, pred[1024,1024]{0,1:T(8,128)(4,1)} %copy-done.26), kind=kOutput, calls=%fused_computation.206 | convolution fusion | flops 1097337856 | bytes 19931136 | tf_op jit(solution)/shard_map/shqk,kshd->qshd/dot_general | solution.py:110
  828.9 3.7 copy.437
  840.6 3.7 reduce_sum.356
  846.4 4.5 all-to-all-start.5
  880.3 4.0 copy.438
  896.2 8.2 fusion.144
  908.8 5.7 convolution_convert_fusion.2
  914.5 101.5 %concatenate.46 = bf16[2048,5766]{0,1:T(8,128)(2,1)} concatenate(bf16[2048,2048]{0,1:T(8,128)(2,1)} %convolution_convert_fusion.2, bf16[2048,512]{0,1:T(8,128)(2,1)} %convolution_convert_fusion.3, bf16[2048,512]{0,1:T(8,128)(2,1)} %convolution_convert_fusion.4, bf16[2048,2048]{0,1:T(8,128)(2,1)} %convolution_convert_fusion.1, bf16[2048,64]{0,1:T(8,128)(2,1)} %convolution_convert_fusion.8, ...), dimensions={1} | concatenate | bytes 47235072 | tf_op jit(solution)/shard_map/concatenate | solution.py:379
  1016.1 32.4 %copy.480 = bf16[2048,5766]{1,0:T(8,128)(2,1)} copy(bf16[2048,5766]{0,1:T(8,128)(2,1)} %concatenate.46) | data formatting | bytes 47235072
  1054.3 42.7 %all-reduce.6 = f32[256,2]{0,1:T(2,128)S(1)} all-reduce(f32[256,2]{0,1:T(2,128)S(1)} %pad_add_fusion.1), channel_id=5, replica_groups=mesh['seq'=4,'fsdp'=8] {'seq','fsdp'}, use_global_device_ids=true, to_apply=%region_36.37.clone | all-reduce | flops 512 | bytes 4096
  1097.7 5.5 convert_element_type.317
  1103.2 206.2 %reduce-scatter.14.cloned.1.call-done = bf16[64,5766]{1,0:T(8,128)(2,1)} async-done(((bf16[2048,5766]{1,0:T(8,128)(2,1)}), bf16[64,5766]{1,0:T(8,128)(2,1)}) %reduce-scatter.14.cloned.1.call-update) | async-done | bytes 738064
  (383 shorter events, 193.7 us)
Async XLA Ops:
  7.2 156.9 %all-gather.6.cloned.1.call-start = ((), (), s32[]{:S(2)}) async-start(), calls=%async_computation.12 | async-start | bytes 24870912 | tf_op jit(solution)/shard_map/all_gather | solution.py:144
  14.2 39.8 %copy-start.2 = (bf16[256,1,2048]{2,0,1:T(8,128)(2,1)S(1)}, bf16[256,1,2048]{2,0,1:T(8,128)(2,1)}, u32[]{:S(2)}) copy-start(bf16[256,1,2048]{2,0,1:T(8,128)(2,1)} %param.14) | copy-start | bytes 3145732
  14.2 368.7 %all-gather.10.cloned.1.call-start = ((), (), s32[]{:S(2)}) async-start(), calls=%async_computation.14 | async-start | bytes 28311552 | tf_op jit(solution)/shard_map/all_gather | solution.py:146
  52.2 116.1 %copy-start.37 = (f32[256,256]{1,0:T(8,128)}, f32[256,256]{1,0:T(8,128)S(1)}, u32[]{:S(2)}) copy-start(f32[256,256]{1,0:T(8,128)S(1)} %get-tuple-element.169) | copy-start | bytes 786436
  52.2 145.7 %copy-start.33 = (f32[256,256]{1,0:T(8,128)}, f32[256,256]{1,0:T(8,128)S(1)}, u32[]{:S(2)}) copy-start(f32[256,256]{1,0:T(8,128)S(1)} %get-tuple-element.170) | copy-start | bytes 786436
  54.2 231.3 %copy-start.74 = (f32[256]{0:T(256)}, f32[256]{0:T(256)S(1)}, u32[]{:S(2)}) copy-start(f32[256]{0:T(256)S(1)} %add_rsqrt_fusion.5) | copy-start | bytes 3076
  54.2 143.7 %copy-start.83 = (f32[256,1]{0,1:T(1,128)}, f32[256,1]{0,1:T(1,128)S(1)}, u32[]{:S(2)}) copy-start(f32[256,1]{0,1:T(1,128)S(1)} %get-tuple-element.171) | copy-start | bytes 3076
  54.2 151.9 %copy-start.85 = (f32[256,1]{0,1:T(1,128)}, f32[256,1]{0,1:T(1,128)S(1)}, u32[]{:S(2)}) copy-start(f32[256,1]{0,1:T(1,128)S(1)} %get-tuple-element.172) | copy-start | bytes 3076
  168.3 117.2 %copy-start.55 = (f32[2048]{0:T(1024)}, f32[2048]{0:T(1024)S(1)}, u32[]{:S(2)}) copy-start(f32[2048]{0:T(1024)S(1)} %get-tuple-element.144) | copy-start | bytes 24580
  168.3 117.2 %copy-start.66 = (f32[2048]{0:T(1024)}, f32[2048]{0:T(1024)S(1)}, u32[]{:S(2)}) copy-start(f32[2048]{0:T(1024)S(1)} %get-tuple-element.142) | copy-start | bytes 24580
  168.3 117.2 %copy-start.68 = (f32[2048]{0:T(1024)}, f32[2048]{0:T(1024)S(1)}, u32[]{:S(2)}) copy-start(f32[2048]{0:T(1024)S(1)} %get-tuple-element.143) | copy-start | bytes 24580
  168.3 119.0 %copy-start.59 = (f32[2048]{0:T(1024)}, f32[2048]{0:T(1024)S(1)}, u32[]{:S(2)}) copy-start(f32[2048]{0:T(1024)S(1)} %get-tuple-element.141) | copy-start | bytes 24580
  173.1 25.7 %all-to-all-start = ((bf16[256,1,8,256]{3,0,1,2:T(8,128)(2,1)}), bf16[256,1,8,256]{3,0,1,2:T(8,128)(2,1)}, u32[]{:S(2)}, u32[]{:S(2)}) async-start(bf16[256,1,8,256]{3,0,1,2:T(8,128)(2,1)} %bitcast.2), calls=%async_computation | async-start | bytes 2097152 | tf_op jit(solution)/shard_map/all_to_all | solution.py:179
  190.5 15.6 %copy-start.57 = (f32[256,8]{0,1:T(8,128)}, f32[256,8]{0,1:T(8,128)S(1)}, u32[]{:S(2)}) copy-start(f32[256,8]{0,1:T(8,128)S(1)} %fusion.239) | copy-start | bytes 24580
  191.2 6.7 copy-start.72
  194.2 12.0 copy-start
  200.8 18.8 %all-to-all-start.2 = ((bf16[256,1,8,256]{3,0,1,2:T(8,128)(2,1)}), bf16[256,1,8,256]{3,0,1,2:T(8,128)(2,1)}, u32[]{:S(2)}, u32[]{:S(2)}) async-start(bf16[256,1,8,256]{3,0,1,2:T(8,128)(2,1)} %bitcast.378), calls=%async_computation.2 | async-start | bytes 2097152 | tf_op jit(solution)/shard_map/all_to_all | solution.py:178
  208.5 15.8 %copy-start.101 = (s32[256,1]{0,1:T(1,128)S(1)}, s32[256,1]{0,1:T(1,128)}, u32[]{:S(2)}) copy-start(s32[256,1]{0,1:T(1,128)} %param.16) | copy-start | bytes 3076
  219.6 28.8 %all-to-all-start.1 = ((bf16[256,1,8,256]{3,0,1,2:T(8,128)(2,1)}), bf16[256,1,8,256]{3,0,1,2:T(8,128)(2,1)}, u32[]{:S(2)}, u32[]{:S(2)}) async-start(bf16[256,1,8,256]{3,0,1,2:T(8,128)(2,1)} %copy.419), calls=%async_computation.1 | async-start | bytes 2097152 | tf_op jit(solution)/shard_map/all_to_all | solution.py:177
  241.2 12.7 copy-start.26
  245.8 8.1 copy-start.28
  262.8 15.5 %all-to-all-start.3 = ((bf16[1024,1,2,256]{3,2,1,0:T(2,128)(2,1)}), bf16[1024,1,2,256]{3,2,1,0:T(2,128)(2,1)S(1)}, u32[]{:S(2)}, u32[]{:S(2)}) async-start(bf16[1024,1,2,256]{3,2,1,0:T(2,128)(2,1)} %copy.429), calls=%async_computation.3 | async-start | bytes 2097152 | tf_op jit(solution)/shard_map/all_to_all | solution.py:185
  267.0 171.0 %all-gather.8.cloned.1.call-start = ((), (), s32[]{:S(2)}) async-start(), calls=%async_computation.13 | async-start | bytes 5242880 | tf_op jit(solution)/shard_map/all_gather | solution.py:120
  268.6 9.8 copy-start.62
  279.0 6.5 copy-start.18
  279.0 6.6 copy-start.6
  288.6 247.1 %reduce-scatter.8.cloned.1.call-start = ((), (), s32[]{:S(2)}) async-start(), calls=%async_computation.15 | async-start | bytes 5242880 | tf_op jit(solution)/shard_map/reduce_scatter | solution.py:210
  482.9 123.7 %all-gather.12.cloned.1.call-start = ((), (), s32[]{:S(2)}) async-start(), calls=%async_computation.16 | async-start | bytes 5242880 | tf_op jit(solution)/shard_map/all_gather | solution.py:120
  553.7 171.4 %reduce-scatter.10.cloned.1.call-start = ((), (), s32[]{:S(2)}) async-start(), calls=%async_computation.17 | async-start | bytes 5242880 | tf_op jit(solution)/shard_map/reduce_scatter | solution.py:263
  653.9 443.8 %reduce-scatter.12.cloned.1.call-start = ((), (), s32[]{:S(2)}) async-start(), calls=%async_computation.18 | async-start | bytes 28311552 | tf_op jit(solution)/shard_map/reduce_scatter | solution.py:275
  716.5 7.0 copy-start.30
  732.8 6.6 copy-start.35
  732.8 13.1 copy-start.13
  740.9 6.6 copy-start.5
  740.9 18.3 %all-to-all-start.4 = ((bf16[256,1,8,256]{3,0,1,2:T(8,128)(2,1)}), bf16[256,1,8,256]{3,0,1,2:T(8,128)(2,1)}, u32[]{:S(2)}, u32[]{:S(2)}) async-start(bf16[256,1,8,256]{3,0,1,2:T(8,128)(2,1)} %copy.432), calls=%async_computation.6 | async-start | bytes 2097152 | tf_op jit(solution)/shard_map/all_to_all | solution.py:310
  772.5 30.8 %all-to-all-start.7 = ((bf16[1024,1,2,256]{3,2,1,0:T(2,128)(2,1)}), bf16[1024,1,2,256]{3,2,1,0:T(2,128)(2,1)}, u32[]{:S(2)}, u32[]{:S(2)}) async-start(bf16[1024,1,2,256]{3,2,1,0:T(2,128)(2,1)} %copy.453), calls=%async_computation.9 | async-start | bytes 2097152 | tf_op jit(solution)/shard_map/all_to_all | solution.py:321
  799.6 8.0 copy-start.63
  803.2 8.4 copy-start.3
  803.2 8.4 copy-start.56
  803.2 8.4 copy-start.75
  803.2 43.1 %all-to-all-start.6 = ((bf16[1024,1,2,256]{3,2,1,0:T(2,128)(2,1)}), bf16[1024,1,2,256]{3,2,1,0:T(2,128)(2,1)}, u32[]{:S(2)}, u32[]{:S(2)}) async-start(bf16[1024,1,2,256]{3,2,1,0:T(2,128)(2,1)} %copy.443), calls=%async_computation.8 | async-start | bytes 2097152 | tf_op jit(solution)/shard_map/all_to_all | solution.py:318
  846.4 33.9 %all-to-all-start.5 = ((bf16[1024,1,2,256]{3,2,1,0:T(2,128)(2,1)}), bf16[1024,1,2,256]{3,2,1,0:T(2,128)(2,1)}, u32[]{:S(2)}, u32[]{:S(2)}) async-start(bf16[1024,1,2,256]{3,2,1,0:T(2,128)(2,1)} %copy.437), calls=%async_computation.7 | async-start | bytes 2097152 | tf_op jit(solution)/shard_map/all_to_all | solution.py:315
  850.9 458.5 %reduce-scatter.14.cloned.1.call-start = ((), (), s32[]{:S(2)}) async-start(), calls=%async_computation.19 | async-start | bytes 24870912
  859.1 7.2 copy-start.34
  869.2 6.7 copy-start.39
  869.2 6.7 copy-start.73
  878.5 5.8 copy-start.43
  880.3 6.0 copy-start.58
  (73 other events, 194.1 us)
Sparse Core Ops, SparseCore 0:
  14.3 149.7 all-gather.5
  165.7 217.1 all-gather.9
  385.3 52.6 all-gather.7
  483.1 52.6 reduce-scatter.7
  553.8 52.7 all-gather.11
  654.0 52.6 reduce-scatter.9
  714.7 244.5 reduce-scatter.11
  1048.6 260.7 reduce-scatter.13

commit v2 on v1

v2 whole, which is shorter than its diff:
```python
import functools
import math

import jax
import jax.numpy as jnp
from jax import lax
from jax.experimental import pallas as pl
from jax.experimental.pallas import tpu as pltpu
from jax.sharding import PartitionSpec as P

QUERY_HEADS = 8
KEY_VALUE_HEADS = 2
HEAD_DIM = 256
LR = 64
PLE = 256
WIN = 512

MESH = pl.DeviceIdType.MESH
eps = 1e-06
theta = 10000.0
root_half = 1.0 / math.sqrt(2.0)
low = jnp.bfloat16
full = jnp.float32


def gather_kernel(sizes, head_ref, rest_ref, mark_ref, head_out, rest_out, mark_out, *sems):
    (local, head_s1, head_r1, head_s2, head_r2, head_s3, head_r3) = sems[:7]
    (rest_s1, rest_r1, rest_s2, rest_r2, rest_s3, rest_r3, mark_s, mark_r) = sems[7:]
    ranks, pairs = sizes["seq"], sizes["pair"]
    rank = lax.axis_index("seq")
    fsdp_index = lax.axis_index("fsdp")
    pair, core = fsdp_index // 2, fsdp_index % 2
    sibling = (rank, pair * 2 + 1 - core)

    def on_seq(step):
        return ((rank + step) % ranks, fsdp_index)

    def on_pair(step):
        return (rank, ((pair + step) % pairs) * 2 + core)

    def remote(source, target, send, recv, device):
        return pltpu.make_async_remote_copy(
            src_ref=source,
            dst_ref=target,
            send_sem=send,
            recv_sem=recv,
            device_id=device,
            device_id_type=MESH,
        )

    barrier = pltpu.get_barrier_semaphore()
    devices = [on_seq(i) for i in range(1, ranks)] + [on_pair(i) for i in range(1, pairs)]
    for device in devices + [sibling]:
        pl.semaphore_signal(barrier, inc=1, device_id=device, device_id_type=MESH)
    pl.semaphore_wait(barrier, len(devices) + 1)

    sent = []

    def go(copy):
        copy.start()
        sent.append(copy)
        return copy

    head_seq = [
        go(
            remote(
                head_ref.at[on_seq(i)[0]],
                head_out.at[rank, pair, core],
                head_s1.at[i - 1],
                head_r1.at[i - 1],
                on_seq(i),
            )
        )
        for i in range(1, ranks)
    ]
    rest_pair = [
        go(
            remote(
                rest_ref,
                rest_out.at[rank, pair, core],
                rest_s1.at[i - 1],
                rest_r1.at[i - 1],
                on_pair(i),
            )
        )
        for i in range(1, pairs)
    ]
    own_head = pltpu.make_async_copy(head_ref.at[rank], head_out.at[rank, pair, core], local.at[0])
    own_head.start()
    own_rest = pltpu.make_async_copy(rest_ref, rest_out.at[rank, pair, core], local.at[1])
    own_rest.start()
    marks = [
        go(remote(mark_ref, mark_out.at[rank], mark_s.at[i - 1], mark_r.at[i - 1], on_seq(i)))
        for i in range(1, ranks)
    ]
    own_mark = pltpu.make_async_copy(mark_ref, mark_out.at[rank], local.at[2])
    own_mark.start()

    own_head.wait()
    for copy in head_seq:
        copy.wait_recv()
    mine = head_out.at[:, pair, core]
    head_pair = [
        go(remote(mine, mine, head_s2.at[i - 1], head_r2.at[i - 1], on_pair(i)))
        for i in range(1, pairs)
    ]
    head_core = [go(remote(mine, mine, head_s3.at[0], head_r3.at[0], sibling))]

    own_rest.wait()
    for copy in rest_pair:
        copy.wait_recv()
    row = rest_out.at[rank, :, core]
    rest_seq = [
        go(remote(row, row, rest_s2.at[i - 1], rest_r2.at[i - 1], on_seq(i)))
        for i in range(1, ranks)
    ]
    rest_core = [go(remote(row, row, rest_s3.at[0], rest_r3.at[0], sibling))]
    for i in range(1, ranks):
        rest_seq[i - 1].wait_recv()
        row = rest_out.at[(rank + ranks - i) % ranks, :, core]
        rest_core.append(go(remote(row, row, rest_s3.at[i], rest_r3.at[i], sibling)))
    for i in range(1, pairs):
        head_pair[i - 1].wait_recv()
        part = head_out.at[:, (pair + pairs - i) % pairs, core]
        head_core.append(go(remote(part, part, head_s3.at[i], head_r3.at[i], sibling)))
    own_mark.wait()
    for copy in marks + head_core + rest_core:
        copy.wait_recv()
    for copy in sent:
        copy.wait_send()


def gather_weights(sizes, head, rest, marks):
    ranks, pairs = sizes["seq"], sizes["pair"]
    dma = lambda n: pltpu.SemaphoreType.DMA((n,))
    anywhere = pl.BlockSpec(memory_space=pl.ANY)
    return pl.pallas_call(
        functools.partial(gather_kernel, sizes),
        out_shape=(
            jax.ShapeDtypeStruct((ranks, pairs, 2) + head.shape[1:], head.dtype),
            jax.ShapeDtypeStruct((ranks, pairs, 2) + rest.shape, rest.dtype),
            jax.ShapeDtypeStruct((ranks,) + marks.shape, marks.dtype),
        ),
        in_specs=[anywhere] * 3,
        out_specs=(anywhere,) * 3,
        scratch_shapes=[
            dma(3),
            *[dma(ranks - 1)] * 2,
            *[dma(pairs - 1)] * 2,
            *[dma(pairs)] * 2,
            *[dma(pairs - 1)] * 2,
            *[dma(ranks - 1)] * 2,
            *[dma(ranks)] * 2,
            *[dma(ranks - 1)] * 2,
        ],
        compiler_params=pltpu.CompilerParams(collective_id=0, has_side_effects=True),
    )(head, rest, marks)


def permute(v, axis, offset):
    size = lax.axis_size(axis)
    return lax.ppermute(v, axis, [(i, i ^ offset) for i in range(size)])


def gather_seq(v, ranks):
    if ranks != 4:
        return [v] + [permute(v, "seq", k) for k in range(1, ranks)]
    half = v.shape[1] // 2
    first, second = permute(v, "seq", 1), permute(v, "seq", 2)
    left = permute(first[:, :half], "seq", 2)
    right = permute(second[:, half:], "seq", 1)
    return [v, first, second, jnp.concatenate([left, right], 1)]


def sum_seq(blocks, ranks):
    up = lambda v: v.astype(full)
    if ranks != 4:
        return sum((up(permute(blocks[k], "seq", k)) for k in range(1, ranks)), up(blocks[0]))
    half = blocks[0].shape[1] // 2
    left = [b[:, :half] for b in blocks]
    right = [b[:, half:] for b in blocks]
    left_far, right_far = permute(left[3], "seq", 1), permute(right[3], "seq", 2)
    left_near, right_near = permute(left[1], "seq", 1), permute(right[2], "seq", 2)
    left_far = permute((up(left[2]) + up(left_far)).astype(low), "seq", 2)
    right_far = permute((up(right[1]) + up(right_far)).astype(low), "seq", 1)
    return jnp.concatenate(
        [
            up(left[0]) + up(left_near) + up(left_far),
            up(right[0]) + up(right_near) + up(right_far),
        ],
        1,
    )


def take(v, axis, index):
    return lax.dynamic_index_in_dim(v, index, axis, keepdims=False)


def scatter_fsdp(v, pair_axis, pairs):
    index = lax.axis_index("fsdp")
    pair, core = index // 2, index % 2
    other = permute(take(v, pair_axis + 1, 1 - core), "fsdp", 1)
    v = (take(v, pair_axis + 1, core).astype(full) + other.astype(full)).astype(low)
    parts = [take(v, pair_axis, pair).astype(full)]
    for k in range(1, pairs):
        parts.append(permute(take(v, pair_axis, pair ^ k), "fsdp", 2 * k).astype(full))
    return sum(parts[1:], parts[0])


def dot(left, right, over):
    return lax.dot_general(left, right, (over, ((), ())), preferred_element_type=full)


def mm(left, right):
    return dot(left, right, ((1,), (0,)))


def mm_nt(left, right):
    return dot(left, right, ((1,), (1,)))


def mm_tn(left, right):
    return dot(left, right, ((0,), (0,)))


def norm_rows(v, gain_vec):
    inverse = lax.rsqrt(jnp.mean(v * v, -1, keepdims=True) + eps)
    return (v * inverse * gain_vec, inverse)


def norm_back(v, inverse, gain_vec, incoming):
    scaled = incoming * gain_vec
    inner_mean = jnp.mean(scaled * v, -1, keepdims=True)
    return (
        inverse * (scaled - v * inverse * inverse * inner_mean),
        jnp.sum(incoming * v * inverse, axis=0),
    )


def gelu_tanh(v):
    return jax.nn.gelu(v, approximate=True)


def rope_tables(places):
    half_width = HEAD_DIM // 2
    frequency = theta ** (-jnp.arange(half_width).astype(full) * 2.0 / HEAD_DIM)
    angles = places.astype(full)[:, None] * frequency
    angles = jnp.concatenate([angles, angles], -1)[:, None, :]
    return (jnp.cos(angles), jnp.sin(angles))


def rotate(v, cos_table, sin_table):
    half_width = v.shape[-1] // 2
    turned = jnp.concatenate([-v[..., half_width:], v[..., :half_width]], -1)
    return v * cos_table + turned * sin_table


def head_prep(qkv, head_scale, cos_table, sin_table):
    per_head = qkv.reshape(qkv.shape[0], -1, HEAD_DIM)
    queries = rotate(norm_rows(per_head[:, :-2], head_scale[:, 0])[0], cos_table, sin_table)
    keys = rotate(norm_rows(per_head[:, -2:-1], head_scale[:, 1])[0], cos_table, sin_table)
    values = norm_rows(per_head[:, -1:], 1.0)[0]
    return (queries, keys, values)


def allowed_mask(segments, indices):
    offset = indices[:, None] - indices[None, :]
    nearby = (offset >= 0) & (offset < WIN)
    return (segments[:, None] == segments[None, :]) & nearby


def scores_of(q_heads, keys, allowed):
    raw_scores = jnp.einsum("qhd,kd->hqk", q_heads, keys, preferred_element_type=full)
    return jnp.where(allowed[None], raw_scores * HEAD_DIM ** (-0.5), -1000000000.0)


def attend_heads(q_heads, keys, values, allowed):
    scores = scores_of(q_heads, keys, allowed)
    row_peak = jnp.max(scores, -1, keepdims=True)
    exp_scores = jnp.exp(scores - row_peak)
    row_total = jnp.sum(exp_scores, -1, keepdims=True)
    attn_probs = exp_scores / row_total
    head_out = jnp.einsum(
        "hqk,kd->qhd", attn_probs.astype(low), values, preferred_element_type=full
    )
    return (head_out, row_peak + jnp.log(row_total))


def attend_back(q_heads, keys, values, allowed, log_total, grad_heads):
    probs_again = jnp.exp(scores_of(q_heads, keys, allowed) - log_total)
    grad_values = jnp.einsum(
        "hqk,qhd->kd", probs_again.astype(low), grad_heads, preferred_element_type=full
    )
    grad_probs = jnp.einsum("qhd,kd->hqk", grad_heads, values, preferred_element_type=full)
    row_inner = jnp.sum(probs_again * grad_probs, -1, keepdims=True)
    grad_scores = (probs_again * (grad_probs - row_inner) * HEAD_DIM ** (-0.5)).astype(low)
    grad_queries = jnp.einsum("hqk,kd->qhd", grad_scores, keys, preferred_element_type=full)
    grad_keys = jnp.einsum("hqk,qhd->kd", grad_scores, q_heads, preferred_element_type=full)
    return (grad_queries, grad_keys, grad_values)


def body(
    sizes,
    hidden_in,
    per_layer_input,
    segment_ids,
    positions,
    out_cotangent,
    w_query,
    key_matrix,
    value_matrix,
    w_out_t,
    laurel_maps,
    per_layer_maps,
    norm_gains,
    head_gains,
    w_mlp,
):
    ranks, pairs = sizes["seq"], sizes["pair"]
    block, _, width = hidden_in.shape
    rows = w_query.shape[0]
    q_width = QUERY_HEADS // ranks * HEAD_DIM
    share = QUERY_HEADS // KEY_VALUE_HEADS
    kv_of = [rank * (QUERY_HEADS // ranks) // share for rank in range(ranks)]
    length = block * ranks
    rank = lax.axis_index("seq")
    relative = [rank ^ k for k in range(ranks)]
    cut = lambda v: [v[k * block : (k + 1) * block] for k in range(ranks)]
    join = lambda blocks: jnp.concatenate(blocks, 0)

    in_maps = lax.all_gather(w_mlp[:, :2], "fsdp", axis=0, tiled=True)
    down_map = lax.all_gather(w_mlp[:, 2], "fsdp", axis=0, tiled=True)

    by_rank = lambda m: m.reshape(rows, ranks, q_width).transpose(1, 0, 2)
    by_kv = lambda m: jnp.stack([m[:, j * HEAD_DIM : (j + 1) * HEAD_DIM] for j in kv_of])
    head_pack = jnp.concatenate(
        [by_rank(w_query), by_kv(key_matrix), by_kv(value_matrix), by_rank(w_out_t)], 2
    )
    head_rows = head_gains.shape[0]
    small = jnp.concatenate(
        [norm_gains, jnp.pad(head_gains, ((0, rows - head_rows), (0, 0)))], 1
    )
    small = jnp.pad(small, ((0, 0), (0, 128 - small.shape[1])))
    rest_pack = jnp.concatenate([laurel_maps, per_layer_maps, small], 1)
    marks = jnp.pad(jnp.concatenate([segment_ids.T, positions.T], 0), ((0, 6), (0, 0)))
    x_local = hidden_in.reshape(block, width)

    head_all, rest_all, marks_all = gather_weights(sizes, head_pack, rest_pack, marks)
    x_all = join(gather_seq(x_local, ranks))
    marks_all = jnp.concatenate([take(marks_all, 0, r) for r in relative], 1)
    head_all = head_all.reshape(width, -1)
    rest_all = rest_all.reshape(width, -1)
    qkv_map, out_map = head_all[:, :-q_width], head_all[:, -q_width:]
    laurel = rest_all[:, : 2 * LR]
    ple = rest_all[:, 2 * LR : 2 * LR + 2 * PLE]
    gains = rest_all[:, 2 * LR + 2 * PLE :].astype(full)
    gain = [gains[:, i] for i in range(6)]
    head_scale = gains[:, 6:8].reshape(-1, rows, 2)[:, :head_rows].reshape(HEAD_DIM, 2)

    tokens_all = x_all.astype(full)
    normed_all_f, all_inverse = norm_rows(tokens_all, gain[0])
    normed_all = normed_all_f.astype(low)
    tokens = x_local.astype(full)
    x_normed_f, x_inverse = norm_rows(tokens, gain[0])
    normed = x_normed_f.astype(low)
    indices = jnp.concatenate([r * block + jnp.arange(block) for r in relative])
    cos_table, sin_table = rope_tables(marks_all[1])
    allowed = allowed_mask(marks_all[0], indices)

    qkv = mm(normed_all, qkv_map)
    queries, keys, values = head_prep(qkv, head_scale, cos_table, sin_table)
    q_heads = queries.astype(low)
    k_head = keys[:, 0].astype(low)
    v_head = values[:, 0].astype(low)
    head_out, log_total = attend_heads(q_heads, k_head, v_head, allowed)
    attn_in = head_out.astype(low).reshape(length, q_width)
    attn_lin = sum_seq(cut(mm_nt(attn_in, out_map).astype(low)), ranks)

    attn_normed, attn_inverse = norm_rows(attn_lin, gain[1])
    laurel_low = mm(normed, laurel[:, :LR]).astype(low)
    laurel_high = mm_nt(laurel_low, laurel[:, LR:])
    laurel_normed, laurel_inverse = norm_rows(laurel_high, gain[2])
    mixed = (tokens + attn_normed + (normed.astype(full) + laurel_normed)) * root_half
    h_normed_f, h_inverse = norm_rows(mixed, gain[3])
    h_rows = join(gather_seq(h_normed_f.astype(low), ranks))

    gate_up = dot(h_rows, in_maps, ((1,), (0,)))
    gate_part, up_part = gate_up[:, 0], gate_up[:, 1]
    hidden = (gelu_tanh(gate_part) * up_part).astype(low)
    ffn_out = sum_seq(cut(mm_nt(hidden, down_map).astype(low)), ranks)

    ffn_normed, ffn_inverse = norm_rows(ffn_out, gain[4])
    h_second = (mixed + ffn_normed).astype(low)
    ple_gate = mm(h_second, ple[:, :PLE])
    ple_input = per_layer_input.reshape(block, PLE).astype(full)
    ple_mixed = (gelu_tanh(ple_gate) * ple_input).astype(low)
    ple_proj = mm_nt(ple_mixed, ple[:, PLE:])
    ple_normed, ple_inverse = norm_rows(ple_proj, gain[5])
    hidden_out = (h_second.astype(full) + ple_normed).astype(low)

    grad_out = out_cotangent.reshape(block, width).astype(full)
    grad_ple_proj, gain_grad_five = norm_back(ple_proj, ple_inverse, gain[5], grad_out)
    grad_ple_low = grad_ple_proj.astype(low)
    grad_ple_mixed = mm(grad_ple_low, ple[:, PLE:])
    unused_gelu, gelu_pull = jax.vjp(gelu_tanh, ple_gate)
    grad_ple_gate = gelu_pull(grad_ple_mixed * ple_input)[0].astype(low)
    grad_second = grad_out + mm_nt(grad_ple_gate, ple[:, :PLE])
    grad_ffn, gain_grad_four = norm_back(ffn_out, ffn_inverse, gain[4], grad_second)
    grad_ffn_rows = join(gather_seq(grad_ffn.astype(low), ranks))

    down_grad = mm_tn(grad_ffn_rows, hidden).astype(low)
    down_sum = lax.psum_scatter(down_grad, "fsdp", scatter_dimension=0, tiled=True)
    grad_hidden = mm(grad_ffn_rows, down_map)
    gate_act, act_pull = jax.vjp(gelu_tanh, gate_part)
    grad_gate_up = jnp.stack(
        [act_pull(grad_hidden * up_part)[0], grad_hidden * gate_act], 1
    ).astype(low)
    in_grad = dot(h_rows, grad_gate_up, ((0,), (0,))).astype(low)
    in_sum = lax.psum_scatter(in_grad, "fsdp", scatter_dimension=0, tiled=True)
    h_part = dot(grad_gate_up, in_maps, ((1, 2), (1, 2))).astype(low)
    grad_h_normed = sum_seq(cut(h_part), ranks)

    grad_ple_up = mm_tn(grad_ple_low, ple_mixed)
    grad_ple_down = mm_tn(h_second, grad_ple_gate)
    grad_mixed_norm, gain_grad_three = norm_back(mixed, h_inverse, gain[3], grad_h_normed)
    grad_mixed = grad_second + grad_mixed_norm
    grad_branch = grad_mixed * root_half
    grad_attn, gain_grad_one = norm_back(attn_lin, attn_inverse, gain[1], grad_branch)
    grad_attn_rows = join(gather_seq(grad_attn.astype(low), ranks))
    grad_out_map = mm_tn(grad_attn_rows, attn_in)
    grad_heads = mm(grad_attn_rows, out_map).astype(low).reshape(length, -1, HEAD_DIM)
    grad_queries, grad_keys, grad_values = attend_back(
        q_heads, k_head, v_head, allowed, log_total, grad_heads
    )
    unused_heads, head_pull = jax.vjp(head_prep, qkv, head_scale, cos_table, sin_table)
    grad_qkv, grad_head_scale, unused_cos, unused_sin = head_pull(
        (grad_queries, grad_keys[:, None], grad_values[:, None])
    )
    grad_qkv = grad_qkv.astype(low)
    grad_qkv_map = mm_tn(normed_all, grad_qkv)
    x_part = mm_nt(grad_qkv, qkv_map)

    grad_laurel_high, gain_grad_two = norm_back(
        laurel_high, laurel_inverse, gain[2], grad_branch
    )
    grad_high_low = grad_laurel_high.astype(low)
    grad_laurel_up = mm_tn(grad_high_low, laurel_low)
    grad_laurel_low = mm(grad_high_low, laurel[:, LR:]).astype(low)
    grad_laurel_down = mm_tn(normed, grad_laurel_low)

    head_grad = jnp.concatenate([grad_qkv_map, grad_out_map], 1).astype(low)
    head_sum = scatter_fsdp(head_grad.reshape(ranks, pairs, 2, rows, -1), 1, pairs).astype(low)
    head_ranks = [take(head_sum, 0, rank)] + [
        permute(take(head_sum, 0, relative[k]), "seq", k) for k in range(1, ranks)
    ]
    stacked = jnp.stack(head_ranks)
    head_ranks = jnp.stack([take(stacked, 0, r ^ rank) for r in range(ranks)]).astype(full)

    x_here = grad_branch + mm_nt(grad_laurel_low, laurel[:, :LR])
    grad_x_normed = x_here + sum_seq(cut(x_part.astype(low)), ranks)
    grad_tokens_norm = norm_back(tokens, x_inverse, gain[0], grad_x_normed)[0]
    input_grad = grad_mixed * root_half + grad_tokens_norm
    gain_grad_zero = jnp.sum(x_here * tokens * x_inverse, 0) + jnp.sum(
        x_part * tokens_all * all_inverse, 0
    )

    gain_grads = jnp.stack(
        [
            gain_grad_zero,
            gain_grad_one,
            gain_grad_two,
            gain_grad_three,
            gain_grad_four,
            gain_grad_five,
        ],
        1,
    )
    head_scale_grad = jnp.pad(
        grad_head_scale.reshape(-1, head_rows, 2), ((0, 0), (0, rows - head_rows), (0, 0))
    ).reshape(width, 2)
    small_grad = jnp.concatenate([gain_grads, head_scale_grad], 1)
    small_grad = jnp.pad(small_grad, ((0, 0), (0, 128 - small_grad.shape[1])))
    rest_grad = jnp.concatenate(
        [grad_laurel_down, grad_laurel_up, grad_ple_down, grad_ple_up, small_grad], 1
    ).astype(low)
    rest_grad = rest_grad.reshape(ranks, -1, rest_grad.shape[1])
    rest_own = take(rest_grad, 0, rank).astype(full) + sum(
        permute(take(rest_grad, 0, relative[k]), "seq", k).astype(full) for k in range(1, ranks)
    )
    rest_sum = scatter_fsdp(rest_own.astype(low).reshape(pairs, 2, rows, -1), 0, pairs)

    whole = lambda part: part.transpose(1, 0, 2).reshape(rows, -1)

    def of_kv(part):
        return jnp.concatenate(
            [
                sum(part[rank] for rank in range(ranks) if kv_of[rank] == j)
                for j in range(KEY_VALUE_HEADS)
            ],
            1,
        )

    ple_end = 2 * LR + 2 * PLE
    scale_sum = rest_sum[:head_rows, ple_end + 6 : ple_end + 8]
    grad_mlp = jnp.concatenate([in_sum, down_sum[:, None]], 1).astype(full)
    lead = (block, 1, width)
    return (
        hidden_out.reshape(lead),
        input_grad.reshape(lead),
        whole(head_ranks[:, :, :q_width]),
        of_kv(head_ranks[:, :, q_width : q_width + HEAD_DIM]),
        of_kv(head_ranks[:, :, q_width + HEAD_DIM : q_width + 2 * HEAD_DIM]),
        whole(head_ranks[:, :, -q_width:]),
        rest_sum[:, : 2 * LR],
        rest_sum[:, 2 * LR : ple_end],
        rest_sum[:, ple_end : ple_end + 6],
        scale_sum,
        grad_mlp,
    )


def solution(mesh):
    sizes = {"seq": mesh.shape["seq"], "pair": mesh.shape["fsdp"] // 2, "core": 2}
    spread = P(("seq", "fsdp"), None)
    tokens = P("seq", "fsdp", None)
    return jax.shard_map(
        functools.partial(body, sizes),
        mesh=mesh,
        in_specs=(tokens, tokens, P("seq", "fsdp"), P("seq", "fsdp"), tokens)
        + (spread,) * 8
        + (P("fsdp", None, "seq"),),
        out_specs=(tokens, tokens) + (spread,) * 8 + (P("fsdp", None, "seq"),),
        check_vma=False,
    )
```

time: 1350 us -> 943 us (0.70)
  waiting for transfers between devices: 590 us -> 266 us
  local copies, waits for them, and re-layouts: 254 us -> 69.4 us
  Pallas kernels: 0 us -> 172 us
  blocking collectives: 93.8 us -> 0 us
  starting transfers between devices: 39.3 us -> 67.2 us
    all_gather x4 -> x2, waiting for transfers between devices: 311 us -> 0.01 us  [the longest x1 0.01 us: body(): down_map = lax.all_gather(w_mlp[:, 2], 'fsdp', axis=0, tiled=True)]
    ppermute x0 -> x54, waiting for transfers between devices: none -> 266 us  [permute(): return lax.ppermute(v, axis, [(i, i ^ offset) for i in range(size)])]
    unnamed x9 -> x4, waiting for transfers between devices: 207 us -> 0.07 us
    pallas_call x0 -> x1, Pallas kernels: none -> 172 us  [gather_weights(): pl.pallas_call(functools.partial(gather_kernel, sizes), out_shape=(jax.Sh...]
    concatenate x2 -> x4, local copies, waits for them, and re-layouts: 102 us -> 7.17 us  [the longest x2 6.3 us: body(): jnp.concatenate([grad_laurel_down, grad_laurel_up, grad_ple_down, grad_pl...]
    ppermute x0 -> x54, starting transfers between devices: none -> 67 us  [permute(): return lax.ppermute(v, axis, [(i, i ^ offset) for i in range(size)])]
    unnamed x230 -> x232, local copies, waits for them, and re-layouts: 74.7 us -> 20.5 us
    reduce_scatter x3 -> x2, waiting for transfers between devices: 52.6 us -> 0.01 us  [the longest x1 0.01 us: body(): lax.psum_scatter(down_grad, 'fsdp', scatter_dimension=0, tiled=True)]
  transfers between devices with their start and end apart: 16 -> 58, of which waited for: 9 -> 35; matrix products, arithmetic and copies ran while one was open for 34% -> 37% of each run, Pallas kernels for 0% -> 18%
where the time goes in v2:
time: 943 us; the launch traced here: 930 us
  waiting for transfers between devices  266 us (28%)
  matrix products  246 us (26%)
  Pallas kernels  172 us (18%)
  other arithmetic  93.4 us (10%)
  local copies, waits for them, and re-layouts  69.4 us (7%)
  starting transfers between devices  67.2 us (7%)
  between operations  16.2 us (2%)
    ppermute x54, waiting for transfers between devices, permute(): return lax.ppermute(v, axis, [(i, i ^ offset) for i in range(size)])  266 us
    dot_general x24, matrix products, dot(): lax.dot_general(left, right, (over, ((), ())), preferred_element_type=full)  196 us
    pallas_call x1, Pallas kernels, gather_weights(): pl.pallas_call(functools.partial(gather_kernel, sizes), out_shape=(jax.Sh...  172 us
    ppermute x54, starting transfers between devices, permute(): return lax.ppermute(v, axis, [(i, i ^ offset) for i in range(size)])  67 us
    unnamed x232, local copies, waits for them, and re-layouts  20.5 us
  transfers between devices with their start and end apart: 58, of which 35 were waited for; matrix products, arithmetic and copies ran while one was open for 37% of the time, Pallas kernels for 18%

profile of v2, /device:TPU:20, one launch (start us, length us, event | category | flops | bytes accessed | tf_op | source)
XLA Modules:
  0.0 930.2 jit_solution(9053810465451173441)
XLA Ops:
  21.9 171.5 %shard_map.221 = (bf16[4,4,2,64,1536]{4,3,2,1,0:T(8,128)(2,1)}, bf16[4,4,2,64,768]{4,3,2,1,0:T(8,128)(2,1)}, s32[4,8,256]{2,1,0:T(8,128)}) custom-call(bf16[4,64,1536]{2,1,0:T(8,128)(2,1)} %pad_maximum_fusion.10.head_ref, bf16[64,768]{1,0:T(8,128)(2,1)} %fusion.132.rest_ref, s32[8,256]{1,0:T(8,128)} %pad.51.mark_ref), custom_call_target="tpu_custom_call" | custom-call | tf_op jit(solution)/shard_map/pallas_call | solution.py:137
  201.1 6.9 collective-permute-start.3
  217.3 8.4 fusion.8
  225.7 7.2 fusion.37
  233.8 4.8 fusion.91
  247.1 4.9 convolution_convert_fusion.2
  254.9 9.4 %collective-permute-done.5 = bf16[256,1024]{1,0:T(8,128)(2,1)S(1)} collective-permute-done((bf16[256,1024]{1,0:T(8,128)(2,1)S(1)}, bf16[256,1024]{1,0:T(8,128)(2,1)S(1)}, u32[]{:S(2)}, u32[]{:S(2)}) %collective-permute-start.5) | collective-permute-done | bytes 524320 | tf_op jit(solution)/shard_map/ppermute | solution.py:162
  270.8 7.8 collective-permute-done.6
  286.0 8.0 collective-permute-done.9
  296.9 20.2 %collective-permute-done.11 = bf16[256,2048]{1,0:T(8,128)(2,1)S(1)} collective-permute-done((bf16[256,2048]{1,0:T(8,128)(2,1)S(1)}, bf16[256,2048]{1,0:T(8,128)(2,1)S(1)}, u32[]{:S(2)}, u32[]{:S(2)}) %collective-permute-start.11) | collective-permute-done | bytes 1048608 | tf_op jit(solution)/shard_map/ppermute | solution.py:162
  318.2 8.2 collective-permute-done.13
  327.5 25.2 %fusion.83 = f32[1024,2,2048]{2,0,1:T(8,128)} fusion(bf16[2048,2,2048]{2,0,1:T(8,128)(2,1)} %all-gather.4.cloned.1.call-done, bf16[256,1024]{1,0:T(8,128)(2,1)} %copy-done.108, bf16[256,1024]{1,0:T(8,128)(2,1)} %collective-permute-done.12, bf16[256,2048]{1,0:T(8,128)(2,1)} %copy-done.53, bf16[256,2048]{1,0:T(8,128)(2,1)} %copy-done.54, ...), kind=kOutput, calls=%fused_computation.162 | convolution fusion | flops 17200840704 | bytes 37748736 | tf_op jit(solution)/shard_map/dot_general | solution.py:211
  352.7 8.6 multiply_convert_fusion.1
  361.3 12.8 %fusion.32 = bf16[1024,2048]{1,0:T(8,128)(2,1)S(1)} fusion(bf16[1024,2048]{1,0:T(8,128)(2,1)} %multiply_convert_fusion.1, bf16[2048,1,2048]{2,0,1:T(8,128)(2,1)} %all-gather.6.cloned.1.call-done), kind=kOutput, calls=%fused_computation.68 | convolution fusion | flops 8592031744 | bytes 16777216 | tf_op jit(solution)/shard_map/dot_general | solution.py:211
  376.4 10.4 %collective-permute-done.15 = bf16[256,1024]{1,0:T(8,128)(2,1)S(1)} collective-permute-done((bf16[256,1024]{1,0:T(8,128)(2,1)S(1)}, bf16[256,1024]{1,0:T(8,128)(2,1)S(1)}, u32[]{:S(2)}, u32[]{:S(2)}) %collective-permute-start.15) | collective-permute-done | bytes 524320 | tf_op jit(solution)/shard_map/ppermute | solution.py:162
  389.1 5.7 collective-permute-done.14
  401.8 6.9 collective-permute-done.19
  421.1 15.5 %collective-permute-done.21 = bf16[256,2048]{1,0:T(8,128)(2,1)S(1)} collective-permute-done((bf16[256,2048]{1,0:T(8,128)(2,1)S(1)}, bf16[256,2048]{1,0:T(8,128)(2,1)S(1)}, u32[]{:S(2)}, u32[]{:S(2)}) %collective-permute-start.21) | collective-permute-done | bytes 1048608 | tf_op jit(solution)/shard_map/ppermute | solution.py:162
  439.1 6.8 collective-permute-done.23
  448.8 21.1 %convolution_convert_fusion.1 = bf16[2048,2048]{1,0:T(8,128)(2,1)} fusion(bf16[1024,2048]{1,0:T(8,128)(2,1)S(1)} %copy-done.20, bf16[256,1024]{1,0:T(8,128)(2,1)S(1)} %collective-permute-done.23, bf16[256,1024]{1,0:T(8,128)(2,1)S(1)} %collective-permute-done.22, bf16[256,2048]{1,0:T(8,128)(2,1)S(1)} %collective-permute-done.21, ...), kind=kOutput, calls=%fused_computation.41 | convolution fusion | flops 8615100416 | bytes 16777216 | tf_op jit(solution)/shard_map/dot_general | solution.py:211
  470.0 25.0 %fusion.31 = (bf16[1024,1,2048]{2,0,1:T(8,128)(2,1)}, bf16[1024,1,2048]{2,0,1:T(8,128)(2,1)}) fusion(f32[1024,2,2048]{2,0,1:T(8,128)} %fusion.83, bf16[2048,1,2048]{2,0,1:T(8,128)(2,1)} %all-gather.6.cloned.1.call-done, bf16[256,1024]{1,0:T(8,128)(2,1)} %copy-done.109, bf16[256,1024]{1,0:T(8,128)(2,1)} %copy-done.110, bf16[256,2048]{1,0:T(8,128)(2,1)} %copy-done.55, ...), kind=kOutput, calls=%fused_computation.67 | convolution fusion | flops 8661237760 | bytes 37748736 | tf_op jit(solution)/shard_map/dot_general | solution.py:211
  495.0 24.9 %convolution_convert_fusion = bf16[2048,2,2048]{2,0,1:T(8,128)(2,1)} fusion(bf16[1024,1,2048]{2,0,1:T(8,128)(2,1)} %get-tuple-element.88, bf16[1024,1,2048]{2,0,1:T(8,128)(2,1)} %get-tuple-element.87, bf16[256,1024]{1,0:T(8,128)(2,1)} %copy-done.108, bf16[256,1024]{1,0:T(8,128)(2,1)} %collective-permute-done.12, bf16[256,2048]{1,0:T(8,128)(2,1)} %copy-done.53, ...), kind=kOutput, calls=%fused_computation.6 | convolution fusion | flops 17226006528 | bytes 29360128 | tf_op jit(solution)/shard_map/dot_general | solution.py:211
  519.9 23.2 %bitcast_convert_fusion = bf16[1024,2048]{1,0:T(8,128)(2,1)S(1)} fusion(bf16[2048,2,2048]{2,0,1:T(8,128)(2,1)} %all-gather.4.cloned.1.call-done, bf16[1024,1,2048]{2,0,1:T(8,128)(2,1)} %get-tuple-element.88, bf16[1024,1,2048]{2,0,1:T(8,128)(2,1)} %get-tuple-element.87), kind=kOutput, calls=%fused_computation.27 | convolution fusion | flops 17186160640 | bytes 29360128 | tf_op jit(solution)/shard_map/dot_general | solution.py:211
  545.7 9.7 %collective-permute-done.25 = bf16[256,1024]{1,0:T(8,128)(2,1)S(1)} collective-permute-done((bf16[256,1024]{1,0:T(8,128)(2,1)S(1)}, bf16[256,1024]{1,0:T(8,128)(2,1)S(1)}, u32[]{:S(2)}, u32[]{:S(2)}) %collective-permute-start.25) | collective-permute-done | bytes 524320 | tf_op jit(solution)/shard_map/ppermute | solution.py:162
  561.1 7.3 collective-permute-done.26
  569.6 10.0 %collective-permute-done.27 = bf16[256,1024]{1,0:T(8,128)(2,1)S(1)} collective-permute-done((bf16[256,1024]{1,0:T(8,128)(2,1)S(1)}, bf16[256,1024]{1,0:T(8,128)(2,1)S(1)}, u32[]{:S(2)}, u32[]{:S(2)}) %collective-permute-start.27) | collective-permute-done | bytes 524320 | tf_op jit(solution)/shard_map/ppermute | solution.py:162
  593.9 11.2 %collective-permute-done.31 = bf16[256,2048]{1,0:T(8,128)(2,1)} collective-permute-done((bf16[256,2048]{1,0:T(8,128)(2,1)S(1)}, bf16[256,2048]{1,0:T(8,128)(2,1)}, u32[]{:S(2)}, u32[]{:S(2)}) %collective-permute-start.31) | collective-permute-done | bytes 1048608 | tf_op jit(solution)/shard_map/ppermute | solution.py:162
  617.0 4.8 fusion.79
  622.8 5.9 fusion.129
  628.7 15.9 %fusion.82 = f32[1024,256]{0,1:T(8,128)S(1)} fusion(bf16[1024,2,256]{0,2,1:T(8,128)(2,1)} %copy-done.42, f32[1024,1024,2]{1,0,2:T(8,128)} %fusion.129, f32[2,1024,1024]{1,2,0:T(8,128)} %copy-done.4, f32[2,1024]{1,0:T(2,128)S(1)} %log_add_fusion), kind=kOutput, calls=%fused_computation.161 | convolution fusion | flops 1088424960 | bytes 18882560 | tf_op jit(solution)/shard_map/hqk,qhd->kd/dot_general | solution.py:298
  648.3 9.0 multiply_reduce_fusion.16
  657.4 15.8 %bitcast_multiply_fusion.6 = (f32[1024,2,256]{0,2,1:T(8,128)}, f32[256,2,1024]{2,0,1:T(8,128)}) fusion(f32[1024,256]{0,1:T(8,128)S(1)} %copy-done.22, f32[1024,1024,2]{1,0,2:T(8,128)} %fusion.129, f32[2,1024,1024]{1,2,0:T(8,128)} %copy-done.4, f32[2,1024]{1,0:T(2,128)S(1)} %log_add_fusion, bf16[1024,1,256]{0,2,1:T(8,128)(2,1)} %copy-done.52), kind=kOutput, calls=%fused_computation.119 | convolution fusion | flops 1088949248 | bytes 22552576 | tf_op jit(solution)/shard_map/hqk,kd->qhd/dot_general | solution.py:297
  682.7 19.7 %fusion.12 = (f32[2048]{0:T(1024)S(1)}, bf16[1024,2048]{1,0:T(8,128)(2,1)S(1)}, bf16[2048,1024]{0,1:T(8,128)(2,1)}) fusion(f32[1024]{0:T(1024)S(1)} %copy-done.104, bf16[256,1024]{1,0:T(8,128)(2,1)S(1)} %copy-done.47, bf16[256,1024]{1,0:T(8,128)(2,1)S(1)} %copy-done.49, bf16[256,2048]{1,0:T(8,128)(2,1)S(1)} %copy-done.37, ...), kind=kOutput, calls=%fused_computation.18 | convolution fusion | flops 4330616832 | bytes 18894848 | tf_op jit(solution)/shard_map/dot_general | solution.py:211
  706.8 8.1 fusion.154
  714.9 6.4 copy.120
  724.4 6.6 copy.118
  733.0 8.4 convolution_convert_fusion.3
  750.0 4.0 fusion.40
  763.7 5.3 concatenate.155
  774.0 17.2 %collective-permute-done.47 = bf16[512,768]{1,0:T(8,128)(2,1)} collective-permute-done((bf16[512,768]{1,0:T(8,128)(2,1)}, bf16[512,768]{1,0:T(8,128)(2,1)}, u32[]{:S(2)}, u32[]{:S(2)}) %collective-permute-start.47) | collective-permute-done | bytes 786464 | tf_op jit(solution)/shard_map/ppermute | solution.py:162
  791.2 16.8 %collective-permute-done.49 = bf16[512,768]{1,0:T(8,128)(2,1)} collective-permute-done((bf16[512,768]{1,0:T(8,128)(2,1)}, bf16[512,768]{1,0:T(8,128)(2,1)}, u32[]{:S(2)}, u32[]{:S(2)}) %collective-permute-start.49) | collective-permute-done | bytes 786464 | tf_op jit(solution)/shard_map/ppermute | solution.py:162
  811.3 3.9 fusion.22
  816.7 14.5 %collective-permute-start.41 = (bf16[4,64,1536]{2,1,0:T(8,128)(2,1)}, bf16[4,64,1536]{2,1,0:T(8,128)(2,1)}, u32[]{:S(2)}, u32[]{:S(2)}) collective-permute-start(bf16[4,64,1536]{2,1,0:T(8,128)(2,1)} %get-tuple-element.121), channel_id=1, source_target_pairs={{0,2},{1,3},{2,0},{3,1},{4,6},{5,7},{6,4},{7,5},{8,10},{9,11},{10,... | collective-permute-start | bytes 2359304 | tf_op jit(solution)/shard_map/ppermute | solution.py:162
  834.3 5.1 copy.129
  840.8 24.4 %collective-permute-done.41 = bf16[4,64,1536]{2,1,0:T(8,128)(2,1)} collective-permute-done((bf16[4,64,1536]{2,1,0:T(8,128)(2,1)}, bf16[4,64,1536]{2,1,0:T(8,128)(2,1)}, u32[]{:S(2)}, u32[]{:S(2)}) %collective-permute-start.41) | collective-permute-done | bytes 786464 | tf_op jit(solution)/shard_map/ppermute | solution.py:162
  865.1 24.7 %collective-permute-done.43 = bf16[4,64,1536]{2,1,0:T(8,128)(2,1)} collective-permute-done((bf16[4,64,1536]{2,1,0:T(8,128)(2,1)}, bf16[4,64,1536]{2,1,0:T(8,128)(2,1)}, u32[]{:S(2)}, u32[]{:S(2)}) %collective-permute-start.43) | collective-permute-done | bytes 786464 | tf_op jit(solution)/shard_map/ppermute | solution.py:162
  889.9 14.4 %collective-permute-done.42 = bf16[4,64,1536]{2,1,0:T(8,128)(2,1)} collective-permute-done((bf16[4,64,1536]{2,1,0:T(8,128)(2,1)}, bf16[4,64,1536]{2,1,0:T(8,128)(2,1)}, u32[]{:S(2)}, u32[]{:S(2)}) %collective-permute-start.42) | collective-permute-done | bytes 786464 | tf_op jit(solution)/shard_map/ppermute | solution.py:162
  918.2 5.0 maximum_convert_fusion
  (483 shorter events, 196.7 us)
Async XLA Ops:
  7.2 320.2 %all-gather.4.cloned.1.call-start = ((), (), s32[]{:S(2)}) async-start(), calls=%async_computation.2 | async-start | bytes 18874368 | tf_op jit(solution)/shard_map/all_gather | solution.py:331
  10.6 350.8 %all-gather.6.cloned.1.call-start = ((), (), s32[]{:S(2)}) async-start(), calls=%async_computation.5 | async-start | bytes 9437184 | tf_op jit(solution)/shard_map/all_gather | solution.py:332
  10.6 190.4 %collective-permute-start.1 = (bf16[256,2048]{1,0:T(8,128)(2,1)S(1)}, bf16[256,2048]{1,0:T(8,128)(2,1)S(1)}, u32[]{:S(2)}, u32[]{:S(2)}) collective-permute-start(bf16[256,2048]{1,0:T(8,128)(2,1)S(1)} %bitcast.335), channel_id=1, source_target_pairs={{0,16},{8,24},{16,0},{24,8},{1,17},{9,25},{17,1},{25,9},{2,18},{10... | collective-permute-start | bytes 3145736 | tf_op jit(solution)/shard_map/ppermute | solution.py:162
  11.2 196.8 %collective-permute-start = (bf16[256,2048]{1,0:T(8,128)(2,1)S(1)}, bf16[256,2048]{1,0:T(8,128)(2,1)S(1)}, u32[]{:S(2)}, u32[]{:S(2)}) collective-permute-start(bf16[256,2048]{1,0:T(8,128)(2,1)S(1)} %bitcast.336), channel_id=1, source_target_pairs={{0,8},{8,0},{16,24},{24,16},{1,9},{9,1},{17,25},{25,17},{2,10},{10... | collective-permute-start | bytes 3145736 | tf_op jit(solution)/shard_map/ppermute | solution.py:162
  15.0 903.1 %reduce-scatter.5.cloned.1.call-start = ((), (), s32[]{:S(2)}) async-start(), calls=%async_computation.4 | async-start | bytes 9437184 | tf_op jit(solution)/shard_map/reduce_scatter | solution.py:412
  201.1 14.1 %collective-permute-start.3 = (bf16[256,1024]{1,0:T(8,128)(2,1)S(1)}, bf16[256,1024]{1,0:T(8,128)(2,1)S(1)}, u32[]{:S(2)}, u32[]{:S(2)}) collective-permute-start(bf16[256,1024]{1,0:T(8,128)(2,1)S(1)} %slice.430), channel_id=1, source_target_pairs={{0,8},{8,0},{16,24},{24,16},{1,9},{9,1},{17,25},{25,17},{2,10},{10... | collective-permute-start | bytes 1572872 | tf_op jit(solution)/shard_map/ppermute | solution.py:162
  208.0 9.2 collective-permute-start.2
  252.2 12.1 %collective-permute-start.5 = (bf16[256,1024]{1,0:T(8,128)(2,1)S(1)}, bf16[256,1024]{1,0:T(8,128)(2,1)S(1)}, u32[]{:S(2)}, u32[]{:S(2)}) collective-permute-start(bf16[256,1024]{1,0:T(8,128)(2,1)S(1)} %get-tuple-element.117), channel_id=1, source_target_pairs={{0,8},{8,0},{16,24},{24,16},{1,9},{9,1},{17,25},{25,17},{2,10},{10... | collective-permute-start | bytes 1572872 | tf_op jit(solution)/shard_map/ppermute | solution.py:162
  252.3 18.5 %collective-permute-start.4 = (bf16[256,1024]{1,0:T(8,128)(2,1)S(1)}, bf16[256,1024]{1,0:T(8,128)(2,1)S(1)}, u32[]{:S(2)}, u32[]{:S(2)}) collective-permute-start(bf16[256,1024]{1,0:T(8,128)(2,1)S(1)} %get-tuple-element.114), channel_id=1, source_target_pairs={{0,8},{8,0},{16,24},{24,16},{1,9},{9,1},{17,25},{25,17},{2,10},{10... | collective-permute-start | bytes 1572872 | tf_op jit(solution)/shard_map/ppermute | solution.py:162
  254.3 16.5 %collective-permute-start.8 = (bf16[256,1024]{1,0:T(8,128)(2,1)S(1)}, bf16[256,1024]{1,0:T(8,128)(2,1)S(1)}, u32[]{:S(2)}, u32[]{:S(2)}) collective-permute-start(bf16[256,1024]{1,0:T(8,128)(2,1)S(1)} %get-tuple-element.115), channel_id=1, source_target_pairs={{0,16},{8,24},{16,0},{24,8},{1,17},{9,25},{17,1},{25,9},{2,18},{10... | collective-permute-start | bytes 1572872 | tf_op jit(solution)/shard_map/ppermute | solution.py:162
  264.5 14.1 %collective-permute-start.6 = (bf16[256,1024]{1,0:T(8,128)(2,1)S(1)}, bf16[256,1024]{1,0:T(8,128)(2,1)S(1)}, u32[]{:S(2)}, u32[]{:S(2)}) collective-permute-start(bf16[256,1024]{1,0:T(8,128)(2,1)S(1)} %add_convert_fusion.10), channel_id=1, source_target_pairs={{0,16},{8,24},{16,0},{24,8},{1,17},{9,25},{17,1},{25,9},{2,18},{10... | collective-permute-start | bytes 1572872 | tf_op jit(solution)/shard_map/ppermute | solution.py:162
  265.4 20.6 %collective-permute-start.7 = (bf16[256,1024]{1,0:T(8,128)(2,1)S(1)}, bf16[256,1024]{1,0:T(8,128)(2,1)S(1)}, u32[]{:S(2)}, u32[]{:S(2)}) collective-permute-start(bf16[256,1024]{1,0:T(8,128)(2,1)S(1)} %get-tuple-element.116), channel_id=1, source_target_pairs={{0,16},{8,24},{16,0},{24,8},{1,17},{9,25},{17,1},{25,9},{2,18},{10... | collective-permute-start | bytes 1572872 | tf_op jit(solution)/shard_map/ppermute | solution.py:162
  279.1 14.9 %collective-permute-start.9 = (bf16[256,1024]{1,0:T(8,128)(2,1)S(1)}, bf16[256,1024]{1,0:T(8,128)(2,1)S(1)}, u32[]{:S(2)}, u32[]{:S(2)}) collective-permute-start(bf16[256,1024]{1,0:T(8,128)(2,1)S(1)} %get-tuple-element.113), channel_id=1, source_target_pairs={{0,8},{8,0},{16,24},{24,16},{1,9},{9,1},{17,25},{25,17},{2,10},{10... | collective-permute-start | bytes 1572872 | tf_op jit(solution)/shard_map/ppermute | solution.py:162
  296.6 20.5 %collective-permute-start.11 = (bf16[256,2048]{1,0:T(8,128)(2,1)S(1)}, bf16[256,2048]{1,0:T(8,128)(2,1)S(1)}, u32[]{:S(2)}, u32[]{:S(2)}) collective-permute-start(bf16[256,2048]{1,0:T(8,128)(2,1)S(1)} %multiply_convert_fusion.5), channel_id=1, source_target_pairs={{0,16},{8,24},{16,0},{24,8},{1,17},{9,25},{17,1},{25,9},{2,18},{10... | collective-permute-start | bytes 3145736 | tf_op jit(solution)/shard_map/ppermute | solution.py:162
  296.7 21.4 %collective-permute-start.10 = (bf16[256,2048]{1,0:T(8,128)(2,1)S(1)}, bf16[256,2048]{1,0:T(8,128)(2,1)S(1)}, u32[]{:S(2)}, u32[]{:S(2)}) collective-permute-start(bf16[256,2048]{1,0:T(8,128)(2,1)S(1)} %multiply_convert_fusion.5), channel_id=1, source_target_pairs={{0,8},{8,0},{16,24},{24,16},{1,9},{9,1},{17,25},{25,17},{2,10},{10... | collective-permute-start | bytes 3145736 | tf_op jit(solution)/shard_map/ppermute | solution.py:162
  317.1 9.2 collective-permute-start.13
  318.1 9.4 %collective-permute-start.12 = (bf16[256,1024]{1,0:T(8,128)(2,1)S(1)}, bf16[256,1024]{1,0:T(8,128)(2,1)}, u32[]{:S(2)}, u32[]{:S(2)}) collective-permute-start(bf16[256,1024]{1,0:T(8,128)(2,1)S(1)} %slice.459), channel_id=1, source_target_pairs={{0,16},{8,24},{16,0},{24,8},{1,17},{9,25},{17,1},{25,9},{2,18},{10... | collective-permute-start | bytes 1572872 | tf_op jit(solution)/shard_map/ppermute | solution.py:162
  374.3 12.5 %collective-permute-start.15 = (bf16[256,1024]{1,0:T(8,128)(2,1)S(1)}, bf16[256,1024]{1,0:T(8,128)(2,1)S(1)}, u32[]{:S(2)}, u32[]{:S(2)}) collective-permute-start(bf16[256,1024]{1,0:T(8,128)(2,1)S(1)} %get-tuple-element.111), channel_id=1, source_target_pairs={{0,8},{8,0},{16,24},{24,16},{1,9},{9,1},{17,25},{25,17},{2,10},{10... | collective-permute-start | bytes 1572872 | tf_op jit(solution)/shard_map/ppermute | solution.py:162
  375.5 19.3 %collective-permute-start.14 = (bf16[256,1024]{1,0:T(8,128)(2,1)S(1)}, bf16[256,1024]{1,0:T(8,128)(2,1)S(1)}, u32[]{:S(2)}, u32[]{:S(2)}) collective-permute-start(bf16[256,1024]{1,0:T(8,128)(2,1)S(1)} %get-tuple-element.108), channel_id=1, source_target_pairs={{0,8},{8,0},{16,24},{24,16},{1,9},{9,1},{17,25},{25,17},{2,10},{10... | collective-permute-start | bytes 1572872 | tf_op jit(solution)/shard_map/ppermute | solution.py:162
  376.4 18.4 %collective-permute-start.18 = (bf16[256,1024]{1,0:T(8,128)(2,1)S(1)}, bf16[256,1024]{1,0:T(8,128)(2,1)S(1)}, u32[]{:S(2)}, u32[]{:S(2)}) collective-permute-start(bf16[256,1024]{1,0:T(8,128)(2,1)S(1)} %get-tuple-element.109), channel_id=1, source_target_pairs={{0,16},{8,24},{16,0},{24,8},{1,17},{9,25},{17,1},{25,9},{2,18},{10... | collective-permute-start | bytes 1572872 | tf_op jit(solution)/shard_map/ppermute | solution.py:162
  387.1 14.8 %collective-permute-start.17 = (bf16[256,1024]{1,0:T(8,128)(2,1)S(1)}, bf16[256,1024]{1,0:T(8,128)(2,1)S(1)}, u32[]{:S(2)}, u32[]{:S(2)}) collective-permute-start(bf16[256,1024]{1,0:T(8,128)(2,1)S(1)} %get-tuple-element.110), channel_id=1, source_target_pairs={{0,16},{8,24},{16,0},{24,8},{1,17},{9,25},{17,1},{25,9},{2,18},{10... | collective-permute-start | bytes 1572872 | tf_op jit(solution)/shard_map/ppermute | solution.py:162
  396.7 12.1 %collective-permute-start.19 = (bf16[256,1024]{1,0:T(8,128)(2,1)S(1)}, bf16[256,1024]{1,0:T(8,128)(2,1)S(1)}, u32[]{:S(2)}, u32[]{:S(2)}) collective-permute-start(bf16[256,1024]{1,0:T(8,128)(2,1)S(1)} %get-tuple-element.107), channel_id=1, source_target_pairs={{0,8},{8,0},{16,24},{24,16},{1,9},{9,1},{17,25},{25,17},{2,10},{10... | collective-permute-start | bytes 1572872 | tf_op jit(solution)/shard_map/ppermute | solution.py:162
  418.6 18.0 %collective-permute-start.21 = (bf16[256,2048]{1,0:T(8,128)(2,1)S(1)}, bf16[256,2048]{1,0:T(8,128)(2,1)S(1)}, u32[]{:S(2)}, u32[]{:S(2)}) collective-permute-start(bf16[256,2048]{1,0:T(8,128)(2,1)S(1)} %multiply_convert_fusion.4), channel_id=1, source_target_pairs={{0,16},{8,24},{16,0},{24,8},{1,17},{9,25},{17,1},{25,9},{2,18},{10... | collective-permute-start | bytes 3145736 | tf_op jit(solution)/shard_map/ppermute | solution.py:162
  418.6 20.1 %collective-permute-start.20 = (bf16[256,2048]{1,0:T(8,128)(2,1)S(1)}, bf16[256,2048]{1,0:T(8,128)(2,1)S(1)}, u32[]{:S(2)}, u32[]{:S(2)}) collective-permute-start(bf16[256,2048]{1,0:T(8,128)(2,1)S(1)} %multiply_convert_fusion.4), channel_id=1, source_target_pairs={{0,8},{8,0},{16,24},{24,16},{1,9},{9,1},{17,25},{25,17},{2,10},{10... | collective-permute-start | bytes 3145736 | tf_op jit(solution)/shard_map/ppermute | solution.py:162
  469.9 448.2 %reduce-scatter.3.cloned.1.call-start = ((), (), s32[]{:S(2)}) async-start(), calls=%async_computation.3 | async-start | bytes 18874368 | tf_op jit(solution)/shard_map/reduce_scatter | solution.py:419
  543.3 12.1 %collective-permute-start.25 = (bf16[256,1024]{1,0:T(8,128)(2,1)S(1)}, bf16[256,1024]{1,0:T(8,128)(2,1)S(1)}, u32[]{:S(2)}, u32[]{:S(2)}) collective-permute-start(bf16[256,1024]{1,0:T(8,128)(2,1)S(1)} %get-tuple-element.105), channel_id=1, source_target_pairs={{0,8},{8,0},{16,24},{24,16},{1,9},{9,1},{17,25},{25,17},{2,10},{10... | collective-permute-start | bytes 1572872 | tf_op jit(solution)/shard_map/ppermute | solution.py:162
  544.0 17.0 %collective-permute-start.24 = (bf16[256,1024]{1,0:T(8,128)(2,1)S(1)}, bf16[256,1024]{1,0:T(8,128)(2,1)S(1)}, u32[]{:S(2)}, u32[]{:S(2)}) collective-permute-start(bf16[256,1024]{1,0:T(8,128)(2,1)S(1)} %get-tuple-element.102), channel_id=1, source_target_pairs={{0,8},{8,0},{16,24},{24,16},{1,9},{9,1},{17,25},{25,17},{2,10},{10... | collective-permute-start | bytes 1572872 | tf_op jit(solution)/shard_map/ppermute | solution.py:162
  545.4 15.6 %collective-permute-start.28 = (bf16[256,1024]{1,0:T(8,128)(2,1)S(1)}, bf16[256,1024]{1,0:T(8,128)(2,1)S(1)}, u32[]{:S(2)}, u32[]{:S(2)}) collective-permute-start(bf16[256,1024]{1,0:T(8,128)(2,1)S(1)} %get-tuple-element.103), channel_id=1, source_target_pairs={{0,16},{8,24},{16,0},{24,8},{1,17},{9,25},{17,1},{25,9},{2,18},{10... | collective-permute-start | bytes 1572872 | tf_op jit(solution)/shard_map/ppermute | solution.py:162
  555.6 12.7 %collective-permute-start.26 = (bf16[256,1024]{1,0:T(8,128)(2,1)S(1)}, bf16[256,1024]{1,0:T(8,128)(2,1)S(1)}, u32[]{:S(2)}, u32[]{:S(2)}) collective-permute-start(bf16[256,1024]{1,0:T(8,128)(2,1)S(1)} %add_convert_fusion.6), channel_id=1, source_target_pairs={{0,16},{8,24},{16,0},{24,8},{1,17},{9,25},{17,1},{25,9},{2,18},{10... | collective-permute-start | bytes 1572872 | tf_op jit(solution)/shard_map/ppermute | solution.py:162
  556.3 23.3 %collective-permute-start.27 = (bf16[256,1024]{1,0:T(8,128)(2,1)S(1)}, bf16[256,1024]{1,0:T(8,128)(2,1)S(1)}, u32[]{:S(2)}, u32[]{:S(2)}) collective-permute-start(bf16[256,1024]{1,0:T(8,128)(2,1)S(1)} %get-tuple-element.104), channel_id=1, source_target_pairs={{0,16},{8,24},{16,0},{24,8},{1,17},{9,25},{17,1},{25,9},{2,18},{10... | collective-permute-start | bytes 1572872 | tf_op jit(solution)/shard_map/ppermute | solution.py:162
  568.9 10.7 %collective-permute-start.29 = (bf16[256,1024]{1,0:T(8,128)(2,1)S(1)}, bf16[256,1024]{1,0:T(8,128)(2,1)S(1)}, u32[]{:S(2)}, u32[]{:S(2)}) collective-permute-start(bf16[256,1024]{1,0:T(8,128)(2,1)S(1)} %get-tuple-element.101), channel_id=1, source_target_pairs={{0,8},{8,0},{16,24},{24,16},{1,9},{9,1},{17,25},{25,17},{2,10},{10... | collective-permute-start | bytes 1572872 | tf_op jit(solution)/shard_map/ppermute | solution.py:162
  585.5 19.6 %collective-permute-start.31 = (bf16[256,2048]{1,0:T(8,128)(2,1)S(1)}, bf16[256,2048]{1,0:T(8,128)(2,1)}, u32[]{:S(2)}, u32[]{:S(2)}) collective-permute-start(bf16[256,2048]{1,0:T(8,128)(2,1)S(1)} %get-tuple-element.128), channel_id=1, source_target_pairs={{0,16},{8,24},{16,0},{24,8},{1,17},{9,25},{17,1},{25,9},{2,18},{10... | collective-permute-start | bytes 3145736 | tf_op jit(solution)/shard_map/ppermute | solution.py:162
  586.6 20.1 %collective-permute-start.30 = (bf16[256,2048]{1,0:T(8,128)(2,1)S(1)}, bf16[256,2048]{1,0:T(8,128)(2,1)}, u32[]{:S(2)}, u32[]{:S(2)}) collective-permute-start(bf16[256,2048]{1,0:T(8,128)(2,1)S(1)} %get-tuple-element.128), channel_id=1, source_target_pairs={{0,8},{8,0},{16,24},{24,16},{1,9},{9,1},{17,25},{25,17},{2,10},{10... | collective-permute-start | bytes 3145736 | tf_op jit(solution)/shard_map/ppermute | solution.py:162
  703.8 27.2 %collective-permute-start.35 = (bf16[256,1024]{1,0:T(8,128)(2,1)}, bf16[256,1024]{1,0:T(8,128)(2,1)}, u32[]{:S(2)}, u32[]{:S(2)}) collective-permute-start(bf16[256,1024]{1,0:T(8,128)(2,1)} %get-tuple-element.97), channel_id=1, source_target_pairs={{0,8},{8,0},{16,24},{24,16},{1,9},{9,1},{17,25},{25,17},{2,10},{10... | collective-permute-start | bytes 1572872 | tf_op jit(solution)/shard_map/ppermute | solution.py:162
  721.4 20.0 %collective-permute-start.34 = (bf16[256,1024]{1,0:T(8,128)(2,1)}, bf16[256,1024]{1,0:T(8,128)(2,1)}, u32[]{:S(2)}, u32[]{:S(2)}) collective-permute-start(bf16[256,1024]{1,0:T(8,128)(2,1)} %get-tuple-element.94), channel_id=1, source_target_pairs={{0,8},{8,0},{16,24},{24,16},{1,9},{9,1},{17,25},{25,17},{2,10},{10... | collective-permute-start | bytes 1572872 | tf_op jit(solution)/shard_map/ppermute | solution.py:162
  722.3 19.0 %collective-permute-start.38 = (bf16[256,1024]{1,0:T(8,128)(2,1)}, bf16[256,1024]{1,0:T(8,128)(2,1)}, u32[]{:S(2)}, u32[]{:S(2)}) collective-permute-start(bf16[256,1024]{1,0:T(8,128)(2,1)} %get-tuple-element.95), channel_id=1, source_target_pairs={{0,16},{8,24},{16,0},{24,8},{1,17},{9,25},{17,1},{25,9},{2,18},{10... | collective-permute-start | bytes 1572872 | tf_op jit(solution)/shard_map/ppermute | solution.py:162
  722.9 31.1 %collective-permute-start.37 = (bf16[256,1024]{1,0:T(8,128)(2,1)}, bf16[256,1024]{1,0:T(8,128)(2,1)}, u32[]{:S(2)}, u32[]{:S(2)}) collective-permute-start(bf16[256,1024]{1,0:T(8,128)(2,1)} %get-tuple-element.96), channel_id=1, source_target_pairs={{0,16},{8,24},{16,0},{24,8},{1,17},{9,25},{17,1},{25,9},{2,18},{10... | collective-permute-start | bytes 1572872 | tf_op jit(solution)/shard_map/ppermute | solution.py:162
  732.3 10.6 %collective-permute-start.36 = (bf16[256,1024]{1,0:T(8,128)(2,1)S(1)}, bf16[256,1024]{1,0:T(8,128)(2,1)S(1)}, u32[]{:S(2)}, u32[]{:S(2)}) collective-permute-start(bf16[256,1024]{1,0:T(8,128)(2,1)S(1)} %add_convert_fusion.4), channel_id=1, source_target_pairs={{0,16},{8,24},{16,0},{24,8},{1,17},{9,25},{17,1},{25,9},{2,18},{10... | collective-permute-start | bytes 1572872 | tf_op jit(solution)/shard_map/ppermute | solution.py:162
  754.0 57.3 %collective-permute-start.40 = (bf16[4,4,64,1536]{3,2,1,0:T(8,128)(2,1)}, bf16[4,4,64,1536]{3,2,1,0:T(8,128)(2,1)}, u32[]{:S(2)}, u32[]{:S(2)}) collective-permute-start(bf16[4,4,64,1536]{3,2,1,0:T(8,128)(2,1)} %fusion.40), channel_id=1, source_target_pairs={{0,1},{1,0},{2,3},{3,2},{4,5},{5,4},{6,7},{7,6},{8,9},{9,8},{10,11... | collective-permute-start | bytes 9437192 | tf_op jit(solution)/shard_map/ppermute | solution.py:162
  770.5 20.7 %collective-permute-start.47 = (bf16[512,768]{1,0:T(8,128)(2,1)}, bf16[512,768]{1,0:T(8,128)(2,1)}, u32[]{:S(2)}, u32[]{:S(2)}) collective-permute-start(bf16[512,768]{1,0:T(8,128)(2,1)} %get-tuple-element.118), channel_id=1, source_target_pairs={{0,8},{8,0},{16,24},{24,16},{1,9},{9,1},{17,25},{25,17},{2,10},{10... | collective-permute-start | bytes 2359304 | tf_op jit(solution)/shard_map/ppermute | solution.py:162
  771.5 36.4 %collective-permute-start.49 = (bf16[512,768]{1,0:T(8,128)(2,1)}, bf16[512,768]{1,0:T(8,128)(2,1)}, u32[]{:S(2)}, u32[]{:S(2)}) collective-permute-start(bf16[512,768]{1,0:T(8,128)(2,1)} %get-tuple-element.119), channel_id=1, source_target_pairs={{0,24},{8,16},{16,8},{24,0},{1,25},{9,17},{17,9},{25,1},{2,26},{10... | collective-permute-start | bytes 2359304 | tf_op jit(solution)/shard_map/ppermute | solution.py:162
  772.9 36.4 %collective-permute-start.48 = (bf16[512,768]{1,0:T(8,128)(2,1)}, bf16[512,768]{1,0:T(8,128)(2,1)}, u32[]{:S(2)}, u32[]{:S(2)}) collective-permute-start(bf16[512,768]{1,0:T(8,128)(2,1)} %get-tuple-element.120), channel_id=1, source_target_pairs={{0,16},{8,24},{16,0},{24,8},{1,17},{9,25},{17,1},{25,9},{2,18},{10... | collective-permute-start | bytes 2359304 | tf_op jit(solution)/shard_map/ppermute | solution.py:162
  816.7 48.5 %collective-permute-start.41 = (bf16[4,64,1536]{2,1,0:T(8,128)(2,1)}, bf16[4,64,1536]{2,1,0:T(8,128)(2,1)}, u32[]{:S(2)}, u32[]{:S(2)}) collective-permute-start(bf16[4,64,1536]{2,1,0:T(8,128)(2,1)} %get-tuple-element.121), channel_id=1, source_target_pairs={{0,2},{1,3},{2,0},{3,1},{4,6},{5,7},{6,4},{7,5},{8,10},{9,11},{10,... | collective-permute-start | bytes 2359304 | tf_op jit(solution)/shard_map/ppermute | solution.py:162
  831.1 58.7 %collective-permute-start.43 = (bf16[4,64,1536]{2,1,0:T(8,128)(2,1)}, bf16[4,64,1536]{2,1,0:T(8,128)(2,1)}, u32[]{:S(2)}, u32[]{:S(2)}) collective-permute-start(bf16[4,64,1536]{2,1,0:T(8,128)(2,1)} %get-tuple-element.122), channel_id=1, source_target_pairs={{0,6},{1,7},{2,4},{3,5},{4,2},{5,3},{6,0},{7,1},{8,14},{9,15},{10,... | collective-permute-start | bytes 2359304 | tf_op jit(solution)/shard_map/ppermute | solution.py:162
  831.2 73.1 %collective-permute-start.42 = (bf16[4,64,1536]{2,1,0:T(8,128)(2,1)}, bf16[4,64,1536]{2,1,0:T(8,128)(2,1)}, u32[]{:S(2)}, u32[]{:S(2)}) collective-permute-start(bf16[4,64,1536]{2,1,0:T(8,128)(2,1)} %get-tuple-element.123), channel_id=1, source_target_pairs={{0,4},{1,5},{2,6},{3,7},{4,0},{5,1},{6,2},{7,3},{8,12},{9,13},{10,... | collective-permute-start | bytes 2359304 | tf_op jit(solution)/shard_map/ppermute | solution.py:162
  839.6 68.4 %collective-permute-start.51 = (bf16[64,768]{1,0:T(8,128)(2,1)S(1)}, bf16[64,768]{1,0:T(8,128)(2,1)S(1)}, u32[]{:S(2)}, u32[]{:S(2)}) collective-permute-start(bf16[64,768]{1,0:T(8,128)(2,1)S(1)} %get-tuple-element.158), channel_id=1, source_target_pairs={{0,2},{1,3},{2,0},{3,1},{4,6},{5,7},{6,4},{7,5},{8,10},{9,11},{10,... | collective-permute-start | bytes 294920 | tf_op jit(solution)/shard_map/ppermute | solution.py:162
  840.8 69.1 %collective-permute-start.53 = (bf16[64,768]{1,0:T(8,128)(2,1)S(1)}, bf16[64,768]{1,0:T(8,128)(2,1)S(1)}, u32[]{:S(2)}, u32[]{:S(2)}) collective-permute-start(bf16[64,768]{1,0:T(8,128)(2,1)S(1)} %get-tuple-element.159), channel_id=1, source_target_pairs={{0,6},{1,7},{2,4},{3,5},{4,2},{5,3},{6,0},{7,1},{8,14},{9,15},{10,... | collective-permute-start | bytes 294920 | tf_op jit(solution)/shard_map/ppermute | solution.py:162
  865.1 44.7 %collective-permute-start.52 = (bf16[64,768]{1,0:T(8,128)(2,1)S(1)}, bf16[64,768]{1,0:T(8,128)(2,1)S(1)}, u32[]{:S(2)}, u32[]{:S(2)}) collective-permute-start(bf16[64,768]{1,0:T(8,128)(2,1)S(1)} %get-tuple-element.160), channel_id=1, source_target_pairs={{0,4},{1,5},{2,6},{3,7},{4,0},{5,1},{6,2},{7,3},{8,12},{9,13},{10,... | collective-permute-start | bytes 294920 | tf_op jit(solution)/shard_map/ppermute | solution.py:162
  (123 other events, 1609.0 us)
Sparse Core Ops, SparseCore 0:
  10.7 222.9 all-gather.3
  235.8 83.3 all-gather.5
  470.1 99.9 reduce-scatter.4
  572.2 166.6 reduce-scatter.2

commit v3 on v2

--- a/solution.py
+++ b/solution.py
@@ -23,9 +23,20 @@
 full = jnp.float32
 
 
-def gather_kernel(sizes, head_ref, rest_ref, mark_ref, head_out, rest_out, mark_out, *sems):
-    (local, head_s1, head_r1, head_s2, head_r2, head_s3, head_r3) = sems[:7]
-    (rest_s1, rest_r1, rest_s2, rest_r2, rest_s3, rest_r3, mark_s, mark_r) = sems[7:]
+def flip(index, offset, size):
+    value, bit = 0, 1
+    while bit < size:
+        has = (index // bit) % 2
+        value = value + bit * ((1 - has) if offset & bit else has)
+        bit *= 2
+    return value
+
+
+def gather_kernel(
+    sizes, head_ref, rest_ref, mark_ref, x_ref, head_out, rest_out, mark_out, x_out, *sems
+):
+    (local, head_s1, head_r1, right_s, right_r, left_s, left_r, head_s3, head_r3) = sems[:9]
+    (rest_s1, rest_r1, rest_s2, rest_r2, rest_s3, rest_r3, mark_s, mark_r, x_s, x_r) = sems[9:]
     ranks, pairs = sizes["seq"], sizes["pair"]
     rank = lax.axis_index("seq")
     fsdp_index = lax.axis_index("fsdp")
@@ -33,7 +44,7 @@
     sibling = (rank, pair * 2 + 1 - core)
 
     def on_seq(step):
-        return ((rank + step) % ranks, fsdp_index)
+        return (flip(rank, step, ranks), fsdp_index)
 
     def on_pair(step):
         return (rank, ((pair + step) % pairs) * 2 + core)
@@ -85,28 +96,46 @@
         )
         for i in range(1, pairs)
     ]
-    own_head = pltpu.make_async_copy(head_ref.at[rank], head_out.at[rank, pair, core], local.at[0])
-    own_head.start()
-    own_rest = pltpu.make_async_copy(rest_ref, rest_out.at[rank, pair, core], local.at[1])
-    own_rest.start()
+    owns = [
+        pltpu.make_async_copy(head_ref.at[rank], head_out.at[rank, pair, core], local.at[0]),
+        pltpu.make_async_copy(rest_ref, rest_out.at[rank, pair, core], local.at[1]),
+        pltpu.make_async_copy(mark_ref, mark_out.at[0], local.at[2]),
+        pltpu.make_async_copy(x_ref, x_out.at[0], local.at[3]),
+    ]
+    for copy in owns:
+        copy.start()
     marks = [
-        go(remote(mark_ref, mark_out.at[rank], mark_s.at[i - 1], mark_r.at[i - 1], on_seq(i)))
+        go(remote(mark_ref, mark_out.at[i], mark_s.at[i - 1], mark_r.at[i - 1], on_seq(i)))
         for i in range(1, ranks)
     ]
-    own_mark = pltpu.make_async_copy(mark_ref, mark_out.at[rank], local.at[2])
-    own_mark.start()
-
-    own_head.wait()
+
+    owns[0].wait()
     for copy in head_seq:
         copy.wait_recv()
-    mine = head_out.at[:, pair, core]
-    head_pair = [
-        go(remote(mine, mine, head_s2.at[i - 1], head_r2.at[i - 1], on_pair(i)))
-        for i in range(1, pairs)
+
+    def right(t):
+        part = head_out.at[:, pair - (t - 1), core]
+        return remote(part, part, right_s.at[t - 1], right_r.at[t - 1], (rank, fsdp_index + 2))
+
+    def left(t):
+        part = head_out.at[:, pair + (t - 1), core]
+        return remote(part, part, left_s.at[t - 1], left_r.at[t - 1], (rank, fsdp_index - 2))
+
+    def to_sibling(at, slot):
+        part = head_out.at[:, at, core]
+        return remote(part, part, head_s3.at[slot], head_r3.at[slot], sibling)
+
+    sends_right = lambda t: (pair - (t - 1) >= 0) & (pair + 1 < pairs)
+    sends_left = lambda t: (pair + (t - 1) < pairs) & (pair - 1 >= 0)
+    pl.when(sends_right(1))(lambda: right(1).start())
+    pl.when(sends_left(1))(lambda: left(1).start())
+    to_sibling(pair, 0).start()
+
+    x_seq = [
+        go(remote(x_ref, x_out.at[i], x_s.at[i - 1], x_r.at[i - 1], on_seq(i)))
+        for i in range(1, ranks)
     ]
-    head_core = [go(remote(mine, mine, head_s3.at[0], head_r3.at[0], sibling))]
-
-    own_rest.wait()
+    owns[1].wait()
     for copy in rest_pair:
         copy.wait_recv()
     row = rest_out.at[rank, :, core]
@@ -115,22 +144,45 @@
         for i in range(1, ranks)
     ]
     rest_core = [go(remote(row, row, rest_s3.at[0], rest_r3.at[0], sibling))]
+
+    for t in range(1, pairs):
+
+        def from_left(t=t):
+            part = head_out.at[:, pair - t, core]
+            remote(part, part, right_s.at[t - 1], right_r.at[t - 1], sibling).wait_recv()
+            if t + 1 < pairs:
+                pl.when(pair + 1 < pairs)(lambda: right(t + 1).start())
+            to_sibling(pair - t, t).start()
+
+        def from_right(t=t):
+            part = head_out.at[:, pair + t, core]
+            remote(part, part, left_s.at[t - 1], left_r.at[t - 1], sibling).wait_recv()
+            if t + 1 < pairs:
+                pl.when(pair - 1 >= 0)(lambda: left(t + 1).start())
+            to_sibling(pair + t, pairs - 1 + t).start()
+
+        pl.when(pair - t >= 0)(from_left)
+        pl.when(pair + t < pairs)(from_right)
+
     for i in range(1, ranks):
         rest_seq[i - 1].wait_recv()
-        row = rest_out.at[(rank + ranks - i) % ranks, :, core]
+        row = rest_out.at[flip(rank, i, ranks), :, core]
         rest_core.append(go(remote(row, row, rest_s3.at[i], rest_r3.at[i], sibling)))
-    for i in range(1, pairs):
-        head_pair[i - 1].wait_recv()
-        part = head_out.at[:, (pair + pairs - i) % pairs, core]
-        head_core.append(go(remote(part, part, head_s3.at[i], head_r3.at[i], sibling)))
-    own_mark.wait()
-    for copy in marks + head_core + rest_core:
+    for copy in owns[2:]:
+        copy.wait()
+    for copy in marks + x_seq + rest_core:
         copy.wait_recv()
+    to_sibling(pair, 0).wait()
+    for t in range(1, pairs):
+        pl.when(pair - t >= 0)(lambda t=t: to_sibling(pair - t, t).wait())
+        pl.when(pair + t < pairs)(lambda t=t: to_sibling(pair + t, pairs - 1 + t).wait())
+        pl.when(sends_right(t))(lambda t=t: right(t).wait_send())
+        pl.when(sends_left(t))(lambda t=t: left(t).wait_send())
     for copy in sent:
         copy.wait_send()
 
 
-def gather_weights(sizes, head, rest, marks):
+def gather_weights(sizes, head, rest, marks, x):
     ranks, pairs = sizes["seq"], sizes["pair"]
     dma = lambda n: pltpu.SemaphoreType.DMA((n,))
     anywhere = pl.BlockSpec(memory_space=pl.ANY)
@@ -140,21 +192,22 @@
             jax.ShapeDtypeStruct((ranks, pairs, 2) + head.shape[1:], head.dtype),
             jax.ShapeDtypeStruct((ranks, pairs, 2) + rest.shape, rest.dtype),
             jax.ShapeDtypeStruct((ranks,) + marks.shape, marks.dtype),
+            jax.ShapeDtypeStruct((ranks,) + x.shape, x.dtype),
         ),
-        in_specs=[anywhere] * 3,
-        out_specs=(anywhere,) * 3,
+        in_specs=[anywhere] * 4,
+        out_specs=(anywhere,) * 4,
         scratch_shapes=[
-            dma(3),
+            dma(4),
             *[dma(ranks - 1)] * 2,
-            *[dma(pairs - 1)] * 2,
-            *[dma(pairs)] * 2,
+            *[dma(pairs - 1)] * 4,
+            *[dma(2 * pairs - 1)] * 2,
             *[dma(pairs - 1)] * 2,
             *[dma(ranks - 1)] * 2,
             *[dma(ranks)] * 2,
-            *[dma(ranks - 1)] * 2,
+            *[dma(ranks - 1)] * 4,
         ],
         compiler_params=pltpu.CompilerParams(collective_id=0, has_side_effects=True),
-    )(head, rest, marks)
+    )(head, rest, marks, x)
 
 
 def permute(v, axis, offset):
@@ -169,7 +222,13 @@
     first, second = permute(v, "seq", 1), permute(v, "seq", 2)
     left = permute(first[:, :half], "seq", 2)
     right = permute(second[:, half:], "seq", 1)
-    return [v, first, second, jnp.concatenate([left, right], 1)]
+    return [v, first, second, left, right]
+
+
+def whole_rows(blocks):
+    if blocks[-1].shape[1] < blocks[0].shape[1]:
+        blocks = blocks[:-2] + [jnp.concatenate(blocks[-2:], 1)]
+    return jnp.concatenate(blocks, 0)
 
 
 def sum_seq(blocks, ranks):
@@ -196,17 +255,6 @@
     return lax.dynamic_index_in_dim(v, index, axis, keepdims=False)
 
 
-def scatter_fsdp(v, pair_axis, pairs):
-    index = lax.axis_index("fsdp")
-    pair, core = index // 2, index % 2
-    other = permute(take(v, pair_axis + 1, 1 - core), "fsdp", 1)
-    v = (take(v, pair_axis + 1, core).astype(full) + other.astype(full)).astype(low)
-    parts = [take(v, pair_axis, pair).astype(full)]
-    for k in range(1, pairs):
-        parts.append(permute(take(v, pair_axis, pair ^ k), "fsdp", 2 * k).astype(full))
-    return sum(parts[1:], parts[0])
-
-
 def dot(left, right, over):
     return lax.dot_general(left, right, (over, ((), ())), preferred_element_type=full)
 
@@ -286,17 +334,206 @@
     return (head_out, row_peak + jnp.log(row_total))
 
 
-def attend_back(q_heads, keys, values, allowed, log_total, grad_heads):
-    probs_again = jnp.exp(scores_of(q_heads, keys, allowed) - log_total)
-    grad_values = jnp.einsum(
-        "hqk,qhd->kd", probs_again.astype(low), grad_heads, preferred_element_type=full
-    )
-    grad_probs = jnp.einsum("qhd,kd->hqk", grad_heads, values, preferred_element_type=full)
-    row_inner = jnp.sum(probs_again * grad_probs, -1, keepdims=True)
-    grad_scores = (probs_again * (grad_probs - row_inner) * HEAD_DIM ** (-0.5)).astype(low)
-    grad_queries = jnp.einsum("hqk,kd->qhd", grad_scores, keys, preferred_element_type=full)
-    grad_keys = jnp.einsum("hqk,qhd->kd", grad_scores, q_heads, preferred_element_type=full)
-    return (grad_queries, grad_keys, grad_values)
+def norm_rope_back(lin, gain, incoming):
+    inverse = lax.rsqrt(jnp.mean(lin * lin, -1, keepdims=True) + eps)
+    scaled = incoming * gain
+    inner_mean = jnp.mean(scaled * lin, -1, keepdims=True)
+    return (
+        inverse * (scaled - lin * inverse * inverse * inner_mean),
+        jnp.sum(incoming * lin * inverse, 0, keepdims=True),
+    )
+
+
+def attend_back_kernel(
+    ranks,
+    block,
+    qkv_ref,
+    q_ref,
+    k_ref,
+    v_ref,
+    grad_ref,
+    total_ref,
+    code_col_ref,
+    code_row_ref,
+    cos_ref,
+    sin_ref,
+    gain_ref,
+    out_ref,
+    gain_out_ref,
+    key_acc,
+    value_acc,
+    query_acc,
+    row_acc,
+    probs_ref,
+    grad_probs_ref,
+):
+    head, mine = pl.program_id(0), pl.program_id(1)
+    heads = pl.num_programs(0)
+    rank = lax.axis_index("seq")
+    scale = HEAD_DIM ** (-0.5)
+    half = HEAD_DIM // 2
+
+    @pl.when((head == 0) & (mine == 0))
+    def _():
+        key_acc[...] = jnp.zeros_like(key_acc)
+        value_acc[...] = jnp.zeros_like(value_acc)
+        gain_out_ref[...] = jnp.zeros_like(gain_out_ref)
+
+    rows = pl.ds(pl.multiple_of(mine * block, block), block)
+    columns = pl.ds(pl.multiple_of(head * HEAD_DIM, HEAD_DIM), HEAD_DIM)
+    q, grad = q_ref[rows, columns], grad_ref[rows, columns]
+    code = code_col_ref[rows, :]
+    peaks = total_ref[head, rows, :]
+    row_acc[...] = jnp.zeros_like(row_acc)
+    query_acc[...] = jnp.zeros_like(query_acc)
+
+    def reaches(other):
+        apart = (rank ^ mine) - (rank ^ other)
+        return (apart >= 0) & (apart * block - (block - 1) < WIN)
+
+    for other in range(ranks):
+        span = slice(other * block, (other + 1) * block)
+
+        @pl.when(reaches(other))
+        def _():
+            scores = mm_nt(q, k_ref[span, :]) * scale
+            offset = code - code_row_ref[:, span]
+            probs = jnp.where((offset >= 0) & (offset < WIN), jnp.exp(scores - peaks), 0.0)
+            grad_probs = mm_nt(grad, v_ref[span, :])
+            probs_ref[other] = probs
+            grad_probs_ref[other] = grad_probs
+            row_acc[...] += jnp.sum(probs * grad_probs, -1, keepdims=True)
+
+    inner = row_acc[...]
+    for other in range(ranks):
+        span = slice(other * block, (other + 1) * block)
+
+        @pl.when(reaches(other))
+        def _():
+            probs = probs_ref[other]
+            grad_scores = (probs * (grad_probs_ref[other] - inner) * scale).astype(low)
+            query_acc[...] += mm(grad_scores, k_ref[span, :])
+            key_acc[span, :] += mm_tn(grad_scores, q)
+            value_acc[span, :] += mm_tn(probs.astype(low), grad)
+
+    def turned_back(v, cos_table, sin_table):
+        first, second = v[:, :half], v[:, half:]
+        return jnp.concatenate(
+            [
+                first * cos_table + second * sin_table,
+                second * cos_table - first * sin_table,
+            ],
+            1,
+        )
+
+    incoming = turned_back(query_acc[...].astype(low).astype(full), cos_ref[rows, :], sin_ref[rows, :])
+    grad_lin, grad_gain = norm_rope_back(qkv_ref[rows, columns], gain_ref[0:1, :], incoming)
+    out_ref[rows, columns] = grad_lin.astype(low)
+    gain_out_ref[0:1, :] += grad_gain
+
+    @pl.when((head == heads - 1) & (mine == ranks - 1))
+    def _():
+        base = out_ref.shape[1] - 2 * HEAD_DIM
+        for other in range(ranks):
+            span = slice(other * block, (other + 1) * block)
+            incoming = turned_back(key_acc[span, :], cos_ref[span, :], sin_ref[span, :])
+            grad_lin, grad_gain = norm_rope_back(
+                qkv_ref[span, base : base + HEAD_DIM], gain_ref[1:2, :], incoming
+            )
+            out_ref[span, base : base + HEAD_DIM] = grad_lin.astype(low)
+            gain_out_ref[1:2, :] += grad_gain
+            grad_lin = norm_rope_back(qkv_ref[span, base + HEAD_DIM :], 1.0, value_acc[span, :])[0]
+            out_ref[span, base + HEAD_DIM :] = grad_lin.astype(low)
+
+
+def attend_back(ranks, qkv, q, k, v, grad, total, codes, cos_table, sin_table, gains):
+    length = qkv.shape[0]
+    block = length // ranks
+    heads = q.shape[1] // HEAD_DIM
+    whole = lambda v: pl.BlockSpec(
+        v.shape, lambda i, j, n=len(v.shape): (0,) * n, pipeline_mode=pl.Buffered(1)
+    )
+    operands = (qkv, q, k, v, grad, total, codes[:, None], codes[None], cos_table, sin_table, gains)
+    results = (
+        jax.ShapeDtypeStruct(qkv.shape, low),
+        jax.ShapeDtypeStruct((8, HEAD_DIM), full),
+    )
+    return pl.pallas_call(
+        functools.partial(attend_back_kernel, ranks, block),
+        grid=(heads, ranks),
+        out_shape=results,
+        in_specs=[whole(v) for v in operands],
+        out_specs=tuple(whole(v) for v in results),
+        scratch_shapes=[
+            pltpu.VMEM((length, HEAD_DIM), full),
+            pltpu.VMEM((length, HEAD_DIM), full),
+            pltpu.VMEM((block, HEAD_DIM), full),
+            pltpu.VMEM((block, 1), full),
+            pltpu.VMEM((ranks, block, block), full),
+            pltpu.VMEM((ranks, block, block), full),
+        ],
+        compiler_params=pltpu.CompilerParams(vmem_limit_bytes=40 << 20),
+        cost_estimate=pl.CostEstimate(
+            flops=10 * heads * length * length * HEAD_DIM * 9 // 16,
+            bytes_accessed=16 * length * HEAD_DIM * (heads + 2),
+            transcendentals=heads * length * length,
+        ),
+    )(*operands)
+
+
+def weight_grad_kernel(count, half_tiles, *refs):
+    lefts, right_ref, out_ref = refs[:count], refs[count], refs[-1]
+    pieces = [ref[...] for ref in lefts]
+    if half_tiles:
+        pieces[-2:] = [jnp.where(pl.program_id(0) < half_tiles, pieces[-2], pieces[-1])]
+    result, start = None, 0
+    for piece in pieces:
+        part = mm_tn(piece, right_ref[start : start + piece.shape[0], :])
+        result = part if result is None else result + part
+        start += piece.shape[0]
+    if len(refs) > count + 2:
+        map_ref, gain_ref, late_ref = refs[count + 1 : count + 4]
+        maps = map_ref[:, : result.shape[1]].astype(full)
+        of_gain = jnp.sum(maps * result, -1, keepdims=True) / gain_ref[...]
+        late = late_ref[...]
+        lane = lax.broadcasted_iota(jnp.int32, late.shape, 1)
+        result = jnp.concatenate([result, jnp.where(lane == 0, of_gain, late)], 1)
+    out_ref[...] = result.astype(low).reshape(out_ref.shape)
+
+
+def weight_grad(ranks, parts, lefts, right, *extras):
+    width = lefts[0].shape[1]
+    length, columns = right.shape
+    rows = width // (ranks * parts)
+    tile = max(min(256, rows * parts), rows)
+    each = tile // rows
+    wide = columns + (128 if extras else 0)
+    half_tiles = lefts[-1].shape[1] // tile if lefts[-1].shape[1] < width else 0
+
+    def place(i):
+        return (((i * each) % parts) // each, (i * each) // parts, 0, 0)
+
+    left_specs = [pl.BlockSpec((v.shape[0], tile), lambda i: (0, i)) for v in lefts]
+    if half_tiles:
+        left_specs[-2:] = [
+            pl.BlockSpec((lefts[-1].shape[0], tile), lambda i: (0, jnp.minimum(i, half_tiles - 1))),
+            pl.BlockSpec((lefts[-1].shape[0], tile), lambda i: (0, jnp.maximum(i - half_tiles, 0))),
+        ]
+    return pl.pallas_call(
+        functools.partial(weight_grad_kernel, len(lefts), half_tiles),
+        grid=(width // tile,),
+        out_shape=jax.ShapeDtypeStruct((parts, ranks, rows, wide), low),
+        in_specs=left_specs
+        + [pl.BlockSpec((length, columns), lambda i: (0, 0))]
+        + [pl.BlockSpec((tile, v.shape[1]), lambda i: (i, 0)) for v in extras],
+        out_specs=pl.BlockSpec((each, 1, rows, wide), place),
+        compiler_params=pltpu.CompilerParams(vmem_limit_bytes=32 << 20),
+        cost_estimate=pl.CostEstimate(
+            flops=2 * length * width * columns,
+            bytes_accessed=2 * (length * (width + columns) + width * columns),
+            transcendentals=0,
+        ),
+    )(*lefts, right, *extras)
 
 
 def body(
@@ -326,10 +563,6 @@
     rank = lax.axis_index("seq")
     relative = [rank ^ k for k in range(ranks)]
     cut = lambda v: [v[k * block : (k + 1) * block] for k in range(ranks)]
-    join = lambda blocks: jnp.concatenate(blocks, 0)
-
-    in_maps = lax.all_gather(w_mlp[:, :2], "fsdp", axis=0, tiled=True)
-    down_map = lax.all_gather(w_mlp[:, 2], "fsdp", axis=0, tiled=True)
 
     by_rank = lambda m: m.reshape(rows, ranks, q_width).transpose(1, 0, 2)
     by_kv = lambda m: jnp.stack([m[:, j * HEAD_DIM : (j + 1) * HEAD_DIM] for j in kv_of])
@@ -345,9 +578,15 @@
     marks = jnp.pad(jnp.concatenate([segment_ids.T, positions.T], 0), ((0, 6), (0, 0)))
     x_local = hidden_in.reshape(block, width)
 
-    head_all, rest_all, marks_all = gather_weights(sizes, head_pack, rest_pack, marks)
-    x_all = join(gather_seq(x_local, ranks))
-    marks_all = jnp.concatenate([take(marks_all, 0, r) for r in relative], 1)
+    head_all, rest_all, marks_all, x_all = gather_weights(
+        sizes, head_pack, rest_pack, marks, x_local
+    )
+    in_rows, down_rows, head_all = lax.optimization_barrier(
+        (w_mlp[:, :2], w_mlp[:, 2], head_all)
+    )
+    in_maps = lax.all_gather(in_rows, "fsdp", axis=0, tiled=True)
+    down_map = lax.all_gather(down_rows, "fsdp", axis=0, tiled=True)
+    x_all = x_all.reshape(length, width)
     head_all = head_all.reshape(width, -1)
     rest_all = rest_all.reshape(width, -1)
     qkv_map, out_map = head_all[:, :-q_width], head_all[:, -q_width:]
@@ -358,14 +597,13 @@
     head_scale = gains[:, 6:8].reshape(-1, rows, 2)[:, :head_rows].reshape(HEAD_DIM, 2)
 
     tokens_all = x_all.astype(full)
-    normed_all_f, all_inverse = norm_rows(tokens_all, gain[0])
-    normed_all = normed_all_f.astype(low)
+    normed_all = norm_rows(tokens_all, gain[0])[0].astype(low)
     tokens = x_local.astype(full)
     x_normed_f, x_inverse = norm_rows(tokens, gain[0])
     normed = x_normed_f.astype(low)
     indices = jnp.concatenate([r * block + jnp.arange(block) for r in relative])
-    cos_table, sin_table = rope_tables(marks_all[1])
-    allowed = allowed_mask(marks_all[0], indices)
+    cos_table, sin_table = rope_tables(marks_all[:, 1].reshape(length))
+    allowed = allowed_mask(marks_all[:, 0].reshape(length), indices)
 
     qkv = mm(normed_all, qkv_map)
     queries, keys, values = head_prep(qkv, head_scale, cos_table, sin_table)
@@ -382,11 +620,11 @@
     laurel_normed, laurel_inverse = norm_rows(laurel_high, gain[2])
     mixed = (tokens + attn_normed + (normed.astype(full) + laurel_normed)) * root_half
     h_normed_f, h_inverse = norm_rows(mixed, gain[3])
-    h_rows = join(gather_seq(h_normed_f.astype(low), ranks))
-
-    gate_up = dot(h_rows, in_maps, ((1,), (0,)))
+    h_blocks = gather_seq(h_normed_f.astype(low), ranks)
+    gate_up = dot(whole_rows(h_blocks), in_maps, ((1,), (0,)))
     gate_part, up_part = gate_up[:, 0], gate_up[:, 1]
     hidden = (gelu_tanh(gate_part) * up_part).astype(low)
+    hidden, down_map = lax.optimization_barrier((hidden, down_map))
     ffn_out = sum_seq(cut(mm_nt(hidden, down_map).astype(low)), ranks)
 
     ffn_normed, ffn_inverse = norm_rows(ffn_out, gain[4])
@@ -406,19 +644,21 @@
     grad_ple_gate = gelu_pull(grad_ple_mixed * ple_input)[0].astype(low)
     grad_second = grad_out + mm_nt(grad_ple_gate, ple[:, :PLE])
     grad_ffn, gain_grad_four = norm_back(ffn_out, ffn_inverse, gain[4], grad_second)
-    grad_ffn_rows = join(gather_seq(grad_ffn.astype(low), ranks))
-
-    down_grad = mm_tn(grad_ffn_rows, hidden).astype(low)
+    grad_ffn_blocks = gather_seq(grad_ffn.astype(low), ranks)
+
+    down_grad = mm_tn(whole_rows(grad_ffn_blocks), hidden).astype(low)
     down_sum = lax.psum_scatter(down_grad, "fsdp", scatter_dimension=0, tiled=True)
-    grad_hidden = mm(grad_ffn_rows, down_map)
+    grad_ffn_blocks, down_grad = lax.optimization_barrier((grad_ffn_blocks, down_grad))
+    grad_hidden = mm(whole_rows(grad_ffn_blocks), down_map)
     gate_act, act_pull = jax.vjp(gelu_tanh, gate_part)
     grad_gate_up = jnp.stack(
         [act_pull(grad_hidden * up_part)[0], grad_hidden * gate_act], 1
     ).astype(low)
-    in_grad = dot(h_rows, grad_gate_up, ((0,), (0,))).astype(low)
-    in_sum = lax.psum_scatter(in_grad, "fsdp", scatter_dimension=0, tiled=True)
     h_part = dot(grad_gate_up, in_maps, ((1, 2), (1, 2))).astype(low)
     grad_h_normed = sum_seq(cut(h_part), ranks)
+    h_blocks, h_part = lax.optimization_barrier((h_blocks, h_part))
+    in_grad = dot(whole_rows(h_blocks), grad_gate_up, ((0,), (0,))).astype(low)
+    in_sum = lax.psum_scatter(in_grad, "fsdp", scatter_dimension=0, tiled=True)
 
     grad_ple_up = mm_tn(grad_ple_low, ple_mixed)
     grad_ple_down = mm_tn(h_second, grad_ple_gate)
@@ -426,20 +666,7 @@
     grad_mixed = grad_second + grad_mixed_norm
     grad_branch = grad_mixed * root_half
     grad_attn, gain_grad_one = norm_back(attn_lin, attn_inverse, gain[1], grad_branch)
-    grad_attn_rows = join(gather_seq(grad_attn.astype(low), ranks))
-    grad_out_map = mm_tn(grad_attn_rows, attn_in)
-    grad_heads = mm(grad_attn_rows, out_map).astype(low).reshape(length, -1, HEAD_DIM)
-    grad_queries, grad_keys, grad_values = attend_back(
-        q_heads, k_head, v_head, allowed, log_total, grad_heads
-    )
-    unused_heads, head_pull = jax.vjp(head_prep, qkv, head_scale, cos_table, sin_table)
-    grad_qkv, grad_head_scale, unused_cos, unused_sin = head_pull(
-        (grad_queries, grad_keys[:, None], grad_values[:, None])
-    )
-    grad_qkv = grad_qkv.astype(low)
-    grad_qkv_map = mm_tn(normed_all, grad_qkv)
-    x_part = mm_nt(grad_qkv, qkv_map)
-
+    grad_attn_blocks = gather_seq(grad_attn.astype(low), ranks)
     grad_laurel_high, gain_grad_two = norm_back(
         laurel_high, laurel_inverse, gain[2], grad_branch
     )
@@ -448,72 +675,110 @@
     grad_laurel_low = mm(grad_high_low, laurel[:, LR:]).astype(low)
     grad_laurel_down = mm_tn(normed, grad_laurel_low)
 
-    head_grad = jnp.concatenate([grad_qkv_map, grad_out_map], 1).astype(low)
-    head_sum = scatter_fsdp(head_grad.reshape(ranks, pairs, 2, rows, -1), 1, pairs).astype(low)
-    head_ranks = [take(head_sum, 0, rank)] + [
-        permute(take(head_sum, 0, relative[k]), "seq", k) for k in range(1, ranks)
-    ]
-    stacked = jnp.stack(head_ranks)
-    head_ranks = jnp.stack([take(stacked, 0, r ^ rank) for r in range(ranks)]).astype(full)
-
     x_here = grad_branch + mm_nt(grad_laurel_low, laurel[:, :LR])
-    grad_x_normed = x_here + sum_seq(cut(x_part.astype(low)), ranks)
-    grad_tokens_norm = norm_back(tokens, x_inverse, gain[0], grad_x_normed)[0]
-    input_grad = grad_mixed * root_half + grad_tokens_norm
-    gain_grad_zero = jnp.sum(x_here * tokens * x_inverse, 0) + jnp.sum(
-        x_part * tokens_all * all_inverse, 0
-    )
-
-    gain_grads = jnp.stack(
-        [
-            gain_grad_zero,
-            gain_grad_one,
-            gain_grad_two,
-            gain_grad_three,
-            gain_grad_four,
-            gain_grad_five,
-        ],
-        1,
-    )
+    gain_grad_zero = jnp.sum(x_here * tokens * x_inverse, 0)
+    small_grad = jnp.stack(
+        [gain_grad_zero, gain_grad_one, gain_grad_two, gain_grad_three, gain_grad_four, gain_grad_five], 1
+    )
+    small_grad = jnp.pad(small_grad, ((0, 0), (0, 128 - small_grad.shape[1])))
+    rest_grad = jnp.concatenate(
+        [grad_ple_down, grad_ple_up, grad_laurel_down, grad_laurel_up, small_grad], 1
+    ).astype(low)
+    rest_grad = rest_grad.reshape(ranks, -1, rest_grad.shape[1])
+    rest_grad, grad_attn_blocks = lax.optimization_barrier((rest_grad, grad_attn_blocks))
+    rest_own = take(rest_grad, 0, rank).astype(full) + sum(
+        permute(take(rest_grad, 0, relative[k]), "seq", k).astype(full) for k in range(1, ranks)
+    )
+    rest_own = rest_own.astype(low).reshape(pairs * 2, rows, -1)
+    out_grad = weight_grad(ranks, pairs * 2, grad_attn_blocks, attn_in)
+    grad_heads = mm(whole_rows(grad_attn_blocks), out_map).astype(low)
+    codes = marks_all[:, 0].reshape(length) * (4 * length) + indices
+    grad_qkv, grad_gains = attend_back(
+        ranks,
+        qkv,
+        q_heads.reshape(length, q_width),
+        k_head,
+        v_head,
+        grad_heads,
+        log_total,
+        codes,
+        cos_table[:, 0, : HEAD_DIM // 2],
+        sin_table[:, 0, : HEAD_DIM // 2],
+        head_scale.T,
+    )
+    grad_head_scale = grad_gains[:2].T
     head_scale_grad = jnp.pad(
         grad_head_scale.reshape(-1, head_rows, 2), ((0, 0), (0, rows - head_rows), (0, 0))
     ).reshape(width, 2)
-    small_grad = jnp.concatenate([gain_grads, head_scale_grad], 1)
-    small_grad = jnp.pad(small_grad, ((0, 0), (0, 128 - small_grad.shape[1])))
-    rest_grad = jnp.concatenate(
-        [grad_laurel_down, grad_laurel_up, grad_ple_down, grad_ple_up, small_grad], 1
-    ).astype(low)
-    rest_grad = rest_grad.reshape(ranks, -1, rest_grad.shape[1])
-    rest_own = take(rest_grad, 0, rank).astype(full) + sum(
-        permute(take(rest_grad, 0, relative[k]), "seq", k).astype(full) for k in range(1, ranks)
-    )
-    rest_sum = scatter_fsdp(rest_own.astype(low).reshape(pairs, 2, rows, -1), 0, pairs)
-
-    whole = lambda part: part.transpose(1, 0, 2).reshape(rows, -1)
-
-    def of_kv(part):
+    late_grad = jnp.pad(head_scale_grad, ((0, 0), (1, 125)))
+    last = weight_grad(
+        ranks, pairs * 2, [normed_all], grad_qkv, head_all, gain[0][:, None], late_grad
+    )
+    last, grad_qkv = lax.optimization_barrier((last, grad_qkv))
+    x_part = mm_nt(grad_qkv, qkv_map).astype(low)
+
+    half = rows // 2
+    folded = jnp.concatenate(
+        [rest_own[:, :half, 2 * PLE :], rest_own[:, half:, 2 * PLE :]], 2
+    )
+    out_grad = out_grad.reshape(pairs * 2, ranks * rows, q_width)
+    first = [out_grad, rest_own[:, :, : 2 * PLE], folded]
+    if q_width != 2 * PLE:
+        first[0] = out_grad.reshape(pairs * 2, -1, 2 * PLE)
+    first = jnp.concatenate(first, 1)
+    first, last, x_part, in_sum, down_sum = lax.optimization_barrier(
+        (first, last, x_part, in_sum, down_sum)
+    )
+    first_sum = lax.psum_scatter(first, "fsdp", scatter_dimension=0, tiled=False).astype(low)
+    last = last.reshape(width, -1)
+    last_sum = lax.psum_scatter(last, "fsdp", scatter_dimension=0, tiled=True)
+    last_sum = last_sum.reshape(ranks, rows, -1)
+
+    out_end = first.shape[1] - rows - half
+    out_sum = first_sum[:out_end].reshape(ranks, rows, q_width)
+    ple_sum = first_sum[out_end : out_end + rows].astype(full)
+    folded = first_sum[out_end + rows :].astype(full)
+    other_sum = jnp.concatenate([folded[:, : folded.shape[1] // 2], folded[:, folded.shape[1] // 2 :]], 0)
+
+    def across(part):
+        got = jnp.stack(
+            [take(part, 0, rank)]
+            + [permute(take(part, 0, relative[k]), "seq", k) for k in range(1, ranks)]
+        )
+        return [take(got, 0, r ^ rank).astype(full) for r in range(ranks)]
+
+    out_ranks, last_ranks = across(out_sum), across(last_sum)
+
+    grad_x_normed = x_here + sum_seq(cut(x_part), ranks)
+    grad_tokens_norm = norm_back(tokens, x_inverse, gain[0], grad_x_normed)[0]
+    input_grad = grad_mixed * root_half + grad_tokens_norm
+
+    late_sum = sum(part[:, q_width + 2 * HEAD_DIM :] for part in last_ranks)
+    gain_sum = other_sum[:, 2 * LR : 2 * LR + 6]
+    gain_sum = jnp.concatenate([gain_sum[:, :1] + late_sum[:, :1], gain_sum[:, 1:]], 1)
+    scale_sum = late_sum[:head_rows, 1:3]
+
+    def of_kv(parts):
         return jnp.concatenate(
             [
-                sum(part[rank] for rank in range(ranks) if kv_of[rank] == j)
+                sum(parts[r] for r in range(ranks) if kv_of[r] == j)
                 for j in range(KEY_VALUE_HEADS)
             ],
             1,
         )
 
-    ple_end = 2 * LR + 2 * PLE
-    scale_sum = rest_sum[:head_rows, ple_end + 6 : ple_end + 8]
     grad_mlp = jnp.concatenate([in_sum, down_sum[:, None]], 1).astype(full)
     lead = (block, 1, width)
     return (
         hidden_out.reshape(lead),
         input_grad.reshape(lead),
-        whole(head_ranks[:, :, :q_width]),
-        of_kv(head_ranks[:, :, q_width : q_width + HEAD_DIM]),
-        of_kv(head_ranks[:, :, q_width + HEAD_DIM : q_width + 2 * HEAD_DIM]),
-        whole(head_ranks[:, :, -q_width:]),
-        rest_sum[:, : 2 * LR],
-        rest_sum[:, 2 * LR : ple_end],
-        rest_sum[:, ple_end : ple_end + 6],
+        jnp.concatenate([part[:, :q_width] for part in last_ranks], 1),
+        of_kv([part[:, q_width : q_width + HEAD_DIM] for part in last_ranks]),
+        of_kv([part[:, q_width + HEAD_DIM : q_width + 2 * HEAD_DIM] for part in last_ranks]),
+        jnp.concatenate(out_ranks, 1),
+        other_sum[:, : 2 * LR],
+        ple_sum,
+        gain_sum,
         scale_sum,
         grad_mlp,
     )

time: 943 us -> 832 us (0.88)
  matrix products: 246 us -> 177 us
  Pallas kernels: 172 us -> 111 us
  waiting for transfers between devices: 266 us -> 303 us
  other arithmetic: 93.4 us -> 75.7 us
  local copies, waits for them, and re-layouts: 69.4 us -> 83 us
  starting transfers between devices: 67.2 us -> 54.5 us
    pallas_call x1, Pallas kernels: 172 us -> 78 us  [gather_weights(): pl.pallas_call(functools.partial(gather_kernel, sizes), out_shape=(jax.Sh...]
    ppermute x54 -> x45, waiting for transfers between devices: 266 us -> 192 us  [permute(): return lax.ppermute(v, axis, [(i, i ^ offset) for i in range(size)])]
    all_gather x2, waiting for transfers between devices: 0.01 us -> 63.6 us  [the longest x1 47.8 us: body(): down_map = lax.all_gather(down_rows, 'fsdp', axis=0, tiled=True)]
    dot_general x4 -> x0, matrix products: 46.6 us -> none  [the longest x1 15.9 us: attend_back(): jnp.einsum('hqk,qhd->kd', grad_scores, q_heads, preferred_element_type=full)]
    reduce_scatter x0 -> x2, waiting for transfers between devices: none -> 35.7 us  [the longest x1 35.7 us: body(): last_sum = lax.psum_scatter(last, 'fsdp', scatter_dimension=0, tiled=True)]
    pallas_call x0 -> x3, Pallas kernels: none -> 32.6 us  [the longest x1 16.7 us: attend_back(): pl.pallas_call(functools.partial(attend_back_kernel, ranks, block), grid=...]
    dot_general x24 -> x22, matrix products: 196 us -> 172 us  [dot(): lax.dot_general(left, right, (over, ((), ())), preferred_element_type=full)]
    ppermute x54 -> x45, starting transfers between devices: 67 us -> 54 us  [permute(): return lax.ppermute(v, axis, [(i, i ^ offset) for i in range(size)])]
  transfers between devices with their start and end apart: 58 -> 51, of which waited for: 35 -> 36; matrix products, arithmetic and copies ran while one was open for 37% -> 32% of each run, Pallas kernels for 18% -> 4%
where the time goes in v3:
time: 832 us; the launch traced here: 820 us
  waiting for transfers between devices  303 us (36%)
  matrix products  177 us (21%)
  Pallas kernels  111 us (13%)
  local copies, waits for them, and re-layouts  83 us (10%)
  other arithmetic  75.7 us (9%)
  starting transfers between devices  54.5 us (7%)
  between operations  16.3 us (2%)
    ppermute x45, waiting for transfers between devices, permute(): return lax.ppermute(v, axis, [(i, i ^ offset) for i in range(size)])  192 us
    dot_general x22, matrix products, dot(): lax.dot_general(left, right, (over, ((), ())), preferred_element_type=full)  172 us
    pallas_call x1, Pallas kernels, gather_weights(): pl.pallas_call(functools.partial(gather_kernel, sizes), out_shape=(jax.Sh...  78 us
    ppermute x45, starting transfers between devices, permute(): return lax.ppermute(v, axis, [(i, i ^ offset) for i in range(size)])  54 us
    all_gather x1, waiting for transfers between devices, body(): down_map = lax.all_gather(down_rows, 'fsdp', axis=0, tiled=True)  47.8 us
    reduce_scatter x1, waiting for transfers between devices, body(): last_sum = lax.psum_scatter(last, 'fsdp', scatter_dimension=0, tiled=True)  35.7 us
    unnamed x267, local copies, waits for them, and re-layouts  26.6 us
    pallas_call x1, Pallas kernels, attend_back(): pl.pallas_call(functools.partial(attend_back_kernel, ranks, block), grid=...  16.7 us
  transfers between devices with their start and end apart: 51, of which 36 were waited for; matrix products, arithmetic and copies ran while one was open for 32% of the time, Pallas kernels for 4%

profile of v3, /device:TPU:20, one launch (start us, length us, event | category | flops | bytes accessed | tf_op | source)
XLA Modules:
  0.0 819.7 jit_solution(4626442147645963908)
XLA Ops:
  9.7 3.2 slice.387
  15.3 78.0 %shard_map.221 = (bf16[4,4,2,64,1536]{4,3,2,1,0:T(8,128)(2,1)}, bf16[4,4,2,64,768]{4,3,2,1,0:T(8,128)(2,1)}, s32[4,8,256]{2,1,0:T(8,128)}, bf16[4,256,2048]{2,1,0:T(8,128)(2,1)}) custom-call(bf16[4,64,1536]{2,1,0:T(8,128)(2,1)} %pad_maximum_fusion.10.head_ref, bf16[64,768]{1,0:T(8,128)(2,1)} %fusion.134.rest_ref, s32[8,256]{1,0:T(8,128)} %pad.27.mark_ref, ...), custom_call_target="tpu_custom_call" | custom-call | tf_op jit(solution)/shard_map/pallas_call | solution.py:189
  102.2 4.6 fusion.64
  112.9 3.9 fusion.104
  126.4 5.6 fusion.99
  138.9 3.1 fusion.92
  142.0 4.4 convolution_convert_fusion.3
  151.0 10.4 %collective-permute-done.1 = bf16[256,1024]{1,0:T(8,128)(2,1)S(1)} collective-permute-done((bf16[256,1024]{1,0:T(8,128)(2,1)S(1)}, bf16[256,1024]{1,0:T(8,128)(2,1)S(1)}, u32[]{:S(2)}, u32[]{:S(2)}) %collective-permute-start.1) | collective-permute-done | bytes 524320 | tf_op jit(solution)/shard_map/ppermute | solution.py:215
  164.3 8.1 collective-permute-done
  172.4 4.3 collective-permute-done.2
  181.8 5.0 collective-permute-done.3
  195.0 19.9 %collective-permute-done.7 = bf16[256,2048]{1,0:T(8,128)(2,1)S(1)} collective-permute-done((bf16[256,2048]{1,0:T(8,128)(2,1)S(1)}, bf16[256,2048]{1,0:T(8,128)(2,1)S(1)}, u32[]{:S(2)}, u32[]{:S(2)}) %collective-permute-start.7) | collective-permute-done | bytes 1048608 | tf_op jit(solution)/shard_map/ppermute | solution.py:215
  218.8 8.3 %collective-permute-done.9 = bf16[256,1024]{1,0:T(8,128)(2,1)S(1)} collective-permute-done((bf16[256,1024]{1,0:T(8,128)(2,1)S(1)}, bf16[256,1024]{1,0:T(8,128)(2,1)S(1)}, u32[]{:S(2)}, u32[]{:S(2)}) %collective-permute-start.9) | collective-permute-done | bytes 524320 | tf_op jit(solution)/shard_map/ppermute | solution.py:215
  227.9 15.8 %all-gather.3.cloned.1.call-done = bf16[2048,2,2048]{2,0,1:T(8,128)(2,1)} async-done(((bf16[256,2,2048]{2,0,1:T(8,128)(2,1)}), bf16[2048,2,2048]{2,0,1:T(8,128)(2,1)}) %all-gather.3.cloned.1.call-update) | async-done | bytes 16777232 | tf_op jit(solution)/shard_map/all_gather | solution.py:587
  243.7 25.7 %fusion.13 = f32[1024,2,2048]{2,0,1:T(8,128)} fusion(bf16[2048,2,2048]{2,0,1:T(8,128)(2,1)} %all-gather.3.cloned.1.call-done, bf16[256,1024]{1,0:T(8,128)(2,1)} %copy-done.123, bf16[256,1024]{1,0:T(8,128)(2,1)} %collective-permute-done.8, bf16[256,2048]{1,0:T(8,128)(2,1)} %copy-done.63, bf16[256,2048]{1,0:T(8,128)(2,1)} %copy-done.64, ...), kind=kOutput, calls=%fused_computation.32 | convolution fusion | flops 17200840704 | bytes 37748736 | tf_op jit(solution)/shard_map/dot_general | solution.py:259
  269.4 8.8 %multiply_convert_fusion.1 = bf16[1024,2048]{1,0:T(8,128)(2,1)} fusion(f32[1024,2,2048]{2,0,1:T(8,128)} %fusion.13), kind=kLoop, calls=%fused_computation.19 | loop fusion | flops 20971520 | bytes 20971520 | tf_op jit(solution)/shard_map/convert_element_type | solution.py:626
  278.2 47.8 %all-gather.5.cloned.1.call-done = bf16[2048,2048]{1,0:T(8,128)(2,1)} async-done(((bf16[256,2048]{1,0:T(8,128)(2,1)}), bf16[2048,2048]{1,0:T(8,128)(2,1)}) %all-gather.5.cloned.1.call-update) | async-done | bytes 8388624 | tf_op jit(solution)/shard_map/all_gather | solution.py:588
  325.9 12.8 %convolution_convert_fusion.2 = bf16[1024,2048]{1,0:T(8,128)(2,1)S(1)} fusion(bf16[1024,2048]{1,0:T(8,128)(2,1)} %multiply_convert_fusion.1, bf16[2048,2048]{1,0:T(8,128)(2,1)} %all-gather.5.cloned.1.call-done), kind=kOutput, calls=%fused_computation.88 | convolution fusion | flops 8592031744 | bytes 16777216 | tf_op jit(solution)/shard_map/dot_general | solution.py:259
  341.6 12.2 %collective-permute-done.11 = bf16[256,1024]{1,0:T(8,128)(2,1)S(1)} collective-permute-done((bf16[256,1024]{1,0:T(8,128)(2,1)S(1)}, bf16[256,1024]{1,0:T(8,128)(2,1)S(1)}, u32[]{:S(2)}, u32[]{:S(2)}) %collective-permute-start.11) | collective-permute-done | bytes 524320 | tf_op jit(solution)/shard_map/ppermute | solution.py:215
  356.0 8.3 %collective-permute-done.10 = bf16[256,1024]{1,0:T(8,128)(2,1)S(1)} collective-permute-done((bf16[256,1024]{1,0:T(8,128)(2,1)S(1)}, bf16[256,1024]{1,0:T(8,128)(2,1)S(1)}, u32[]{:S(2)}, u32[]{:S(2)}) %collective-permute-start.10) | collective-permute-done | bytes 524320 | tf_op jit(solution)/shard_map/ppermute | solution.py:215
  364.3 4.6 collective-permute-done.12
  370.9 7.0 collective-permute-done.13
  390.5 19.9 %collective-permute-done.17 = bf16[256,2048]{1,0:T(8,128)(2,1)S(1)} collective-permute-done((bf16[256,2048]{1,0:T(8,128)(2,1)S(1)}, bf16[256,2048]{1,0:T(8,128)(2,1)S(1)}, u32[]{:S(2)}, u32[]{:S(2)}) %collective-permute-start.17) | collective-permute-done | bytes 1048608 | tf_op jit(solution)/shard_map/ppermute | solution.py:215
  414.7 7.2 collective-permute-done.19
  423.6 21.3 %convolution_convert_fusion.1 = bf16[2048,2048]{1,0:T(8,128)(2,1)} fusion(bf16[1024,2048]{1,0:T(8,128)(2,1)S(1)} %copy-done.45, bf16[256,1024]{1,0:T(8,128)(2,1)S(1)} %collective-permute-done.19, bf16[256,1024]{1,0:T(8,128)(2,1)S(1)} %collective-permute-done.18, bf16[256,2048]{1,0:T(8,128)(2,1)S(1)} %collective-permute-done.17, ...), kind=kOutput, calls=%fused_computation.24 | convolution fusion | flops 8615100416 | bytes 16777216 | tf_op jit(solution)/shard_map/dot_general | solution.py:259
  444.9 25.0 %fusion.62 = (bf16[1024,1,2048]{2,0,1:T(8,128)(2,1)}, bf16[1024,1,2048]{2,0,1:T(8,128)(2,1)}) fusion(f32[1024,2,2048]{2,0,1:T(8,128)} %fusion.13, bf16[2048,2048]{1,0:T(8,128)(2,1)} %all-gather.5.cloned.1.call-done, bf16[256,1024]{1,0:T(8,128)(2,1)} %copy-done.124, bf16[256,1024]{1,0:T(8,128)(2,1)} %copy-done.125, bf16[256,2048]{1,0:T(8,128)(2,1)} %copy-done.65, ...), kind=kOutput, calls=%fused_computation.87 | convolution fusion | flops 8661237760 | bytes 37748736 | tf_op jit(solution)/shard_map/dot_general | solution.py:259
  469.9 24.0 %bitcast_convert_fusion = bf16[1024,2048]{1,0:T(8,128)(2,1)} fusion(bf16[2048,2,2048]{2,0,1:T(8,128)(2,1)} %all-gather.3.cloned.1.call-done, bf16[1024,1,2048]{2,0,1:T(8,128)(2,1)} %get-tuple-element.145, bf16[1024,1,2048]{2,0,1:T(8,128)(2,1)} %get-tuple-element.144), kind=kOutput, calls=%fused_computation.13 | convolution fusion | flops 17186160640 | bytes 29360128 | tf_op jit(solution)/shard_map/dot_general | solution.py:259
  493.9 24.9 %convolution_convert_fusion = bf16[2048,2,2048]{2,0,1:T(8,128)(2,1)} fusion(bf16[1024,1,2048]{2,0,1:T(8,128)(2,1)} %get-tuple-element.145, bf16[1024,1,2048]{2,0,1:T(8,128)(2,1)} %get-tuple-element.144, bf16[256,1024]{1,0:T(8,128)(2,1)} %copy-done.123, bf16[256,1024]{1,0:T(8,128)(2,1)} %collective-permute-done.8, bf16[256,2048]{1,0:T(8,128)(2,1)} %copy-done.63, ...), kind=kOutput, calls=%fused_computation.2 | convolution fusion | flops 17226006528 | bytes 29360128 | tf_op jit(solution)/shard_map/dot_general | solution.py:259
  526.3 10.2 %collective-permute-done.21 = bf16[256,1024]{1,0:T(8,128)(2,1)S(1)} collective-permute-done((bf16[256,1024]{1,0:T(8,128)(2,1)S(1)}, bf16[256,1024]{1,0:T(8,128)(2,1)S(1)}, u32[]{:S(2)}, u32[]{:S(2)}) %collective-permute-start.21) | collective-permute-done | bytes 524320 | tf_op jit(solution)/shard_map/ppermute | solution.py:215
  542.9 8.7 %collective-permute-done.22 = bf16[256,1024]{1,0:T(8,128)(2,1)S(1)} collective-permute-done((bf16[256,1024]{1,0:T(8,128)(2,1)S(1)}, bf16[256,1024]{1,0:T(8,128)(2,1)S(1)}, u32[]{:S(2)}, u32[]{:S(2)}) %collective-permute-start.22) | collective-permute-done | bytes 524320 | tf_op jit(solution)/shard_map/ppermute | solution.py:215
  555.6 5.9 copy.116.qkv_ref
  597.1 6.1 collective-permute-done.27.refs_2_
  618.8 6.3 concatenate.198
  625.3 4.7 fusion.93.grad_ref
  630.1 16.7 %shard_map.223 = (bf16[1024,1024]{1,0:T(8,128)(2,1)S(1)}, f32[8,256]{1,0:T(8,128)S(1)}) custom-call(f32[1024,1024]{1,0:T(8,128)S(1)} %copy-done.4, bf16[1024,512]{1,0:T(8,128)(2,1)S(1)} %copy-done.8, bf16[1024,256]{1,0:T(8,128)(2,1)S(1)} %bitcast.264, bf16[1024,256]{1,0:T(8,128)(2,1)S(1)} %copy-done.14, bf16[1024,512]{1,0:T(8,128)(2,1)S(1)} %fusion.93.grad_ref, ...), custom_call_target="tpu_custom_call" | custom-call | flops 3019898880 | bytes 16777216 | tf_op jit(solution)/shard_map/pallas_call | solution.py:461
  655.0 8.9 %shard_map.224 = bf16[8,4,64,1152]{3,2,1,0:T(8,128)(2,1)S(1)} custom-call(bf16[1024,2048]{1,0:T(8,128)(2,1)S(1)} %copy-done.2, bf16[1024,1024]{1,0:T(8,128)(2,1)S(1)} %copy-done.6, bf16[2048,1536]{1,0:T(8,128)(2,1)S(1)} %bitcast.259, f32[2048,1]{1,0:T(8,128)S(1)} %get-tuple-element.182.refs_3_, f32[2048,128]{1,0:T(8,128)S(1)} %pad.30.refs_4_), custom_call_target="tpu_custom_call" | custom-call | flops 4294967296 | bytes 10485760 | tf_op jit(solution)/shard_map/pallas_call | solution.py:522
  669.9 6.9 shard_map.222
  676.8 6.1 convolution_convert_fusion.4
  682.9 3.8 collective-permute-done.32
  690.9 10.0 %reduce-scatter.5.cloned.1.call-done = bf16[256,2,2048]{2,0,1:T(8,128)(2,1)} async-done(((bf16[2048,2,2048]{2,0,1:T(8,128)(2,1)}), bf16[256,2,2048]{2,0,1:T(8,128)(2,1)}) %reduce-scatter.5.cloned.1.call-update) | async-done | bytes 2097168 | tf_op jit(solution)/shard_map/reduce_scatter | solution.py:661
  706.1 12.2 %collective-permute-done.34 = bf16[256,1024]{1,0:T(8,128)(2,1)S(1)} collective-permute-done((bf16[256,1024]{1,0:T(8,128)(2,1)S(1)}, bf16[256,1024]{1,0:T(8,128)(2,1)S(1)}, u32[]{:S(2)}, u32[]{:S(2)}) %collective-permute-start.34) | collective-permute-done | bytes 524320 | tf_op jit(solution)/shard_map/ppermute | solution.py:215
  720.5 8.8 %collective-permute-done.33 = bf16[256,1024]{1,0:T(8,128)(2,1)S(1)} collective-permute-done((bf16[256,1024]{1,0:T(8,128)(2,1)S(1)}, bf16[256,1024]{1,0:T(8,128)(2,1)S(1)}, u32[]{:S(2)}, u32[]{:S(2)}) %collective-permute-start.33) | collective-permute-done | bytes 524320 | tf_op jit(solution)/shard_map/ppermute | solution.py:215
  729.3 4.0 collective-permute-done.35
  735.3 3.1 maximum_convert_fusion
  738.5 5.0 collective-permute-done.36
  748.5 3.5 copy.124
  761.2 35.7 %reduce-scatter.9.cloned.1.call-done = bf16[256,1152]{1,0:T(8,128)(2,1)} async-done(((bf16[2048,1152]{1,0:T(8,128)(2,1)}), bf16[256,1152]{1,0:T(8,128)(2,1)}) %reduce-scatter.9.cloned.1.call-update) | async-done | bytes 589840 | tf_op jit(solution)/shard_map/reduce_scatter | solution.py:734
  802.4 3.3 collective-permute-done.41
  (511 shorter events, 209.7 us)
Async XLA Ops:
  7.3 236.4 %all-gather.3.cloned.1.call-start = ((), (), s32[]{:S(2)}) async-start(), calls=%async_computation.4 | async-start | bytes 18874368 | tf_op jit(solution)/shard_map/all_gather | solution.py:587
  93.3 232.6 %all-gather.5.cloned.1.call-start = ((), (), s32[]{:S(2)}) async-start(), calls=%async_computation.5 | async-start | bytes 9437184 | tf_op jit(solution)/shard_map/all_gather | solution.py:588
  94.1 596.8 %reduce-scatter.7.cloned.1.call-start = ((), (), s32[]{:S(2)}) async-start(), calls=%async_computation.7 | async-start | bytes 9437184 | tf_op jit(solution)/shard_map/reduce_scatter | solution.py:650
  146.7 14.8 %collective-permute-start.1 = (bf16[256,1024]{1,0:T(8,128)(2,1)S(1)}, bf16[256,1024]{1,0:T(8,128)(2,1)S(1)}, u32[]{:S(2)}, u32[]{:S(2)}) collective-permute-start(bf16[256,1024]{1,0:T(8,128)(2,1)S(1)} %get-tuple-element.169), channel_id=1, source_target_pairs={{0,8},{8,0},{16,24},{24,16},{1,9},{9,1},{17,25},{25,17},{2,10},{10... | collective-permute-start | bytes 1572872 | tf_op jit(solution)/shard_map/ppermute | solution.py:215
  148.1 24.2 %collective-permute-start = (bf16[256,1024]{1,0:T(8,128)(2,1)S(1)}, bf16[256,1024]{1,0:T(8,128)(2,1)S(1)}, u32[]{:S(2)}, u32[]{:S(2)}) collective-permute-start(bf16[256,1024]{1,0:T(8,128)(2,1)S(1)} %get-tuple-element.166), channel_id=1, source_target_pairs={{0,8},{8,0},{16,24},{24,16},{1,9},{9,1},{17,25},{25,17},{2,10},{10... | collective-permute-start | bytes 1572872 | tf_op jit(solution)/shard_map/ppermute | solution.py:215
  148.8 23.6 %collective-permute-start.4 = (bf16[256,1024]{1,0:T(8,128)(2,1)S(1)}, bf16[256,1024]{1,0:T(8,128)(2,1)S(1)}, u32[]{:S(2)}, u32[]{:S(2)}) collective-permute-start(bf16[256,1024]{1,0:T(8,128)(2,1)S(1)} %get-tuple-element.167), channel_id=1, source_target_pairs={{0,16},{8,24},{16,0},{24,8},{1,17},{9,25},{17,1},{25,9},{2,18},{10... | collective-permute-start | bytes 1572872 | tf_op jit(solution)/shard_map/ppermute | solution.py:215
  161.6 15.1 %collective-permute-start.2 = (bf16[256,1024]{1,0:T(8,128)(2,1)S(1)}, bf16[256,1024]{1,0:T(8,128)(2,1)S(1)}, u32[]{:S(2)}, u32[]{:S(2)}) collective-permute-start(bf16[256,1024]{1,0:T(8,128)(2,1)S(1)} %add_convert_fusion.9), channel_id=1, source_target_pairs={{0,16},{8,24},{16,0},{24,8},{1,17},{9,25},{17,1},{25,9},{2,18},{10... | collective-permute-start | bytes 1572872 | tf_op jit(solution)/shard_map/ppermute | solution.py:215
  163.9 22.9 %collective-permute-start.3 = (bf16[256,1024]{1,0:T(8,128)(2,1)S(1)}, bf16[256,1024]{1,0:T(8,128)(2,1)S(1)}, u32[]{:S(2)}, u32[]{:S(2)}) collective-permute-start(bf16[256,1024]{1,0:T(8,128)(2,1)S(1)} %get-tuple-element.168), channel_id=1, source_target_pairs={{0,16},{8,24},{16,0},{24,8},{1,17},{9,25},{17,1},{25,9},{2,18},{10... | collective-permute-start | bytes 1572872 | tf_op jit(solution)/shard_map/ppermute | solution.py:215
  177.2 11.9 %collective-permute-start.5 = (bf16[256,1024]{1,0:T(8,128)(2,1)S(1)}, bf16[256,1024]{1,0:T(8,128)(2,1)S(1)}, u32[]{:S(2)}, u32[]{:S(2)}) collective-permute-start(bf16[256,1024]{1,0:T(8,128)(2,1)S(1)} %get-tuple-element.165), channel_id=1, source_target_pairs={{0,8},{8,0},{16,24},{24,16},{1,9},{9,1},{17,25},{25,17},{2,10},{10... | collective-permute-start | bytes 1572872 | tf_op jit(solution)/shard_map/ppermute | solution.py:215
  192.6 22.3 %collective-permute-start.7 = (bf16[256,2048]{1,0:T(8,128)(2,1)S(1)}, bf16[256,2048]{1,0:T(8,128)(2,1)S(1)}, u32[]{:S(2)}, u32[]{:S(2)}) collective-permute-start(bf16[256,2048]{1,0:T(8,128)(2,1)S(1)} %multiply_convert_fusion.5), channel_id=1, source_target_pairs={{0,16},{8,24},{16,0},{24,8},{1,17},{9,25},{17,1},{25,9},{2,18},{10... | collective-permute-start | bytes 3145736 | tf_op jit(solution)/shard_map/ppermute | solution.py:215
  194.1 23.5 %collective-permute-start.6 = (bf16[256,2048]{1,0:T(8,128)(2,1)S(1)}, bf16[256,2048]{1,0:T(8,128)(2,1)S(1)}, u32[]{:S(2)}, u32[]{:S(2)}) collective-permute-start(bf16[256,2048]{1,0:T(8,128)(2,1)S(1)} %multiply_convert_fusion.5), channel_id=1, source_target_pairs={{0,8},{8,0},{16,24},{24,16},{1,9},{9,1},{17,25},{25,17},{2,10},{10... | collective-permute-start | bytes 3145736 | tf_op jit(solution)/shard_map/ppermute | solution.py:215
  215.0 12.1 %collective-permute-start.9 = (bf16[256,1024]{1,0:T(8,128)(2,1)S(1)}, bf16[256,1024]{1,0:T(8,128)(2,1)S(1)}, u32[]{:S(2)}, u32[]{:S(2)}) collective-permute-start(bf16[256,1024]{1,0:T(8,128)(2,1)S(1)} %slice.514), channel_id=1, source_target_pairs={{0,8},{8,0},{16,24},{24,16},{1,9},{9,1},{17,25},{25,17},{2,10},{10... | collective-permute-start | bytes 1572872 | tf_op jit(solution)/shard_map/ppermute | solution.py:215
  217.6 10.2 %collective-permute-start.8 = (bf16[256,1024]{1,0:T(8,128)(2,1)S(1)}, bf16[256,1024]{1,0:T(8,128)(2,1)}, u32[]{:S(2)}, u32[]{:S(2)}) collective-permute-start(bf16[256,1024]{1,0:T(8,128)(2,1)S(1)} %slice.513), channel_id=1, source_target_pairs={{0,16},{8,24},{16,0},{24,8},{1,17},{9,25},{17,1},{25,9},{2,18},{10... | collective-permute-start | bytes 1572872 | tf_op jit(solution)/shard_map/ppermute | solution.py:215
  338.9 14.8 %collective-permute-start.11 = (bf16[256,1024]{1,0:T(8,128)(2,1)S(1)}, bf16[256,1024]{1,0:T(8,128)(2,1)S(1)}, u32[]{:S(2)}, u32[]{:S(2)}) collective-permute-start(bf16[256,1024]{1,0:T(8,128)(2,1)S(1)} %get-tuple-element.163), channel_id=1, source_target_pairs={{0,8},{8,0},{16,24},{24,16},{1,9},{9,1},{17,25},{25,17},{2,10},{10... | collective-permute-start | bytes 1572872 | tf_op jit(solution)/shard_map/ppermute | solution.py:215
  340.4 23.8 %collective-permute-start.10 = (bf16[256,1024]{1,0:T(8,128)(2,1)S(1)}, bf16[256,1024]{1,0:T(8,128)(2,1)S(1)}, u32[]{:S(2)}, u32[]{:S(2)}) collective-permute-start(bf16[256,1024]{1,0:T(8,128)(2,1)S(1)} %get-tuple-element.160), channel_id=1, source_target_pairs={{0,8},{8,0},{16,24},{24,16},{1,9},{9,1},{17,25},{25,17},{2,10},{10... | collective-permute-start | bytes 1572872 | tf_op jit(solution)/shard_map/ppermute | solution.py:215
  341.0 23.3 %collective-permute-start.14 = (bf16[256,1024]{1,0:T(8,128)(2,1)S(1)}, bf16[256,1024]{1,0:T(8,128)(2,1)S(1)}, u32[]{:S(2)}, u32[]{:S(2)}) collective-permute-start(bf16[256,1024]{1,0:T(8,128)(2,1)S(1)} %get-tuple-element.161), channel_id=1, source_target_pairs={{0,16},{8,24},{16,0},{24,8},{1,17},{9,25},{17,1},{25,9},{2,18},{10... | collective-permute-start | bytes 1572872 | tf_op jit(solution)/shard_map/ppermute | solution.py:215
  353.9 14.9 %collective-permute-start.12 = (bf16[256,1024]{1,0:T(8,128)(2,1)S(1)}, bf16[256,1024]{1,0:T(8,128)(2,1)S(1)}, u32[]{:S(2)}, u32[]{:S(2)}) collective-permute-start(bf16[256,1024]{1,0:T(8,128)(2,1)S(1)} %add_convert_fusion.7), channel_id=1, source_target_pairs={{0,16},{8,24},{16,0},{24,8},{1,17},{9,25},{17,1},{25,9},{2,18},{10... | collective-permute-start | bytes 1572872 | tf_op jit(solution)/shard_map/ppermute | solution.py:215
  354.6 23.3 %collective-permute-start.13 = (bf16[256,1024]{1,0:T(8,128)(2,1)S(1)}, bf16[256,1024]{1,0:T(8,128)(2,1)S(1)}, u32[]{:S(2)}, u32[]{:S(2)}) collective-permute-start(bf16[256,1024]{1,0:T(8,128)(2,1)S(1)} %get-tuple-element.162), channel_id=1, source_target_pairs={{0,16},{8,24},{16,0},{24,8},{1,17},{9,25},{17,1},{25,9},{2,18},{10... | collective-permute-start | bytes 1572872 | tf_op jit(solution)/shard_map/ppermute | solution.py:215
  369.3 9.5 %collective-permute-start.15 = (bf16[256,1024]{1,0:T(8,128)(2,1)S(1)}, bf16[256,1024]{1,0:T(8,128)(2,1)S(1)}, u32[]{:S(2)}, u32[]{:S(2)}) collective-permute-start(bf16[256,1024]{1,0:T(8,128)(2,1)S(1)} %get-tuple-element.159), channel_id=1, source_target_pairs={{0,8},{8,0},{16,24},{24,16},{1,9},{9,1},{17,25},{25,17},{2,10},{10... | collective-permute-start | bytes 1572872 | tf_op jit(solution)/shard_map/ppermute | solution.py:215
  388.4 22.0 %collective-permute-start.17 = (bf16[256,2048]{1,0:T(8,128)(2,1)S(1)}, bf16[256,2048]{1,0:T(8,128)(2,1)S(1)}, u32[]{:S(2)}, u32[]{:S(2)}) collective-permute-start(bf16[256,2048]{1,0:T(8,128)(2,1)S(1)} %multiply_convert_fusion.4), channel_id=1, source_target_pairs={{0,16},{8,24},{16,0},{24,8},{1,17},{9,25},{17,1},{25,9},{2,18},{10... | collective-permute-start | bytes 3145736 | tf_op jit(solution)/shard_map/ppermute | solution.py:215
  389.1 23.8 %collective-permute-start.16 = (bf16[256,2048]{1,0:T(8,128)(2,1)S(1)}, bf16[256,2048]{1,0:T(8,128)(2,1)S(1)}, u32[]{:S(2)}, u32[]{:S(2)}) collective-permute-start(bf16[256,2048]{1,0:T(8,128)(2,1)S(1)} %multiply_convert_fusion.4), channel_id=1, source_target_pairs={{0,8},{8,0},{16,24},{24,16},{1,9},{9,1},{17,25},{25,17},{2,10},{10... | collective-permute-start | bytes 3145736 | tf_op jit(solution)/shard_map/ppermute | solution.py:215
  410.5 11.5 %collective-permute-start.19 = (bf16[256,1024]{1,0:T(8,128)(2,1)S(1)}, bf16[256,1024]{1,0:T(8,128)(2,1)S(1)}, u32[]{:S(2)}, u32[]{:S(2)}) collective-permute-start(bf16[256,1024]{1,0:T(8,128)(2,1)S(1)} %slice.530), channel_id=1, source_target_pairs={{0,8},{8,0},{16,24},{24,16},{1,9},{9,1},{17,25},{25,17},{2,10},{10... | collective-permute-start | bytes 1572872 | tf_op jit(solution)/shard_map/ppermute | solution.py:215
  412.9 9.2 %collective-permute-start.18 = (bf16[256,1024]{1,0:T(8,128)(2,1)S(1)}, bf16[256,1024]{1,0:T(8,128)(2,1)S(1)}, u32[]{:S(2)}, u32[]{:S(2)}) collective-permute-start(bf16[256,1024]{1,0:T(8,128)(2,1)S(1)} %slice.529), channel_id=1, source_target_pairs={{0,16},{8,24},{16,0},{24,8},{1,17},{9,25},{17,1},{25,9},{2,18},{10... | collective-permute-start | bytes 1572872 | tf_op jit(solution)/shard_map/ppermute | solution.py:215
  444.9 256.0 %reduce-scatter.5.cloned.1.call-start = ((), (), s32[]{:S(2)}) async-start(), calls=%async_computation.6 | async-start | bytes 18874368 | tf_op jit(solution)/shard_map/reduce_scatter | solution.py:661
  518.9 233.1 %reduce-scatter.11.cloned.1.call-start = ((), (), s32[]{:S(2)}) async-start(), calls=%async_computation.9 | async-start | bytes 3244032 | tf_op jit(solution)/shard_map/reduce_scatter | solution.py:732
  521.6 14.9 %collective-permute-start.21 = (bf16[256,1024]{1,0:T(8,128)(2,1)S(1)}, bf16[256,1024]{1,0:T(8,128)(2,1)S(1)}, u32[]{:S(2)}, u32[]{:S(2)}) collective-permute-start(bf16[256,1024]{1,0:T(8,128)(2,1)S(1)} %get-tuple-element.157), channel_id=1, source_target_pairs={{0,8},{8,0},{16,24},{24,16},{1,9},{9,1},{17,25},{25,17},{2,10},{10... | collective-permute-start | bytes 1572872 | tf_op jit(solution)/shard_map/ppermute | solution.py:215
  523.7 19.2 %collective-permute-start.20 = (bf16[256,1024]{1,0:T(8,128)(2,1)S(1)}, bf16[256,1024]{1,0:T(8,128)(2,1)S(1)}, u32[]{:S(2)}, u32[]{:S(2)}) collective-permute-start(bf16[256,1024]{1,0:T(8,128)(2,1)S(1)} %get-tuple-element.154), channel_id=1, source_target_pairs={{0,8},{8,0},{16,24},{24,16},{1,9},{9,1},{17,25},{25,17},{2,10},{10... | collective-permute-start | bytes 1572872 | tf_op jit(solution)/shard_map/ppermute | solution.py:215
  524.3 18.6 %collective-permute-start.24 = (bf16[256,1024]{1,0:T(8,128)(2,1)S(1)}, bf16[256,1024]{1,0:T(8,128)(2,1)S(1)}, u32[]{:S(2)}, u32[]{:S(2)}) collective-permute-start(bf16[256,1024]{1,0:T(8,128)(2,1)S(1)} %get-tuple-element.155), channel_id=1, source_target_pairs={{0,16},{8,24},{16,0},{24,8},{1,17},{9,25},{17,1},{25,9},{2,18},{10... | collective-permute-start | bytes 1572872 | tf_op jit(solution)/shard_map/ppermute | solution.py:215
  537.7 13.8 %collective-permute-start.22 = (bf16[256,1024]{1,0:T(8,128)(2,1)S(1)}, bf16[256,1024]{1,0:T(8,128)(2,1)S(1)}, u32[]{:S(2)}, u32[]{:S(2)}) collective-permute-start(bf16[256,1024]{1,0:T(8,128)(2,1)S(1)} %add_convert_fusion.5), channel_id=1, source_target_pairs={{0,16},{8,24},{16,0},{24,8},{1,17},{9,25},{17,1},{25,9},{2,18},{10... | collective-permute-start | bytes 1572872 | tf_op jit(solution)/shard_map/ppermute | solution.py:215
  541.8 31.6 %collective-permute-start.23 = (bf16[256,1024]{1,0:T(8,128)(2,1)}, bf16[256,1024]{1,0:T(8,128)(2,1)}, u32[]{:S(2)}, u32[]{:S(2)}) collective-permute-start(bf16[256,1024]{1,0:T(8,128)(2,1)} %get-tuple-element.156), channel_id=1, source_target_pairs={{0,16},{8,24},{16,0},{24,8},{1,17},{9,25},{17,1},{25,9},{2,18},{10... | collective-permute-start | bytes 1572872 | tf_op jit(solution)/shard_map/ppermute | solution.py:215
  554.4 19.1 %collective-permute-start.25 = (bf16[256,1024]{1,0:T(8,128)(2,1)}, bf16[256,1024]{1,0:T(8,128)(2,1)}, u32[]{:S(2)}, u32[]{:S(2)}) collective-permute-start(bf16[256,1024]{1,0:T(8,128)(2,1)} %get-tuple-element.153), channel_id=1, source_target_pairs={{0,8},{8,0},{16,24},{24,16},{1,9},{9,1},{17,25},{25,17},{2,10},{10... | collective-permute-start | bytes 1572872 | tf_op jit(solution)/shard_map/ppermute | solution.py:215
  582.8 20.4 %collective-permute-start.27 = (bf16[256,2048]{1,0:T(8,128)(2,1)S(1)}, bf16[256,2048]{1,0:T(8,128)(2,1)S(1)}, u32[]{:S(2)}, u32[]{:S(2)}) collective-permute-start(bf16[256,2048]{1,0:T(8,128)(2,1)S(1)} %get-tuple-element.59.refs_0_), channel_id=1, source_target_pairs={{0,16},{8,24},{16,0},{24,8},{1,17},{9,25},{17,1},{25,9},{2,18},{10... | collective-permute-start | bytes 3145736 | tf_op jit(solution)/shard_map/ppermute | solution.py:215
  584.4 20.5 %collective-permute-start.26 = (bf16[256,2048]{1,0:T(8,128)(2,1)S(1)}, bf16[256,2048]{1,0:T(8,128)(2,1)}, u32[]{:S(2)}, u32[]{:S(2)}) collective-permute-start(bf16[256,2048]{1,0:T(8,128)(2,1)S(1)} %get-tuple-element.59.refs_0_), channel_id=1, source_target_pairs={{0,8},{8,0},{16,24},{24,16},{1,9},{9,1},{17,25},{25,17},{2,10},{10... | collective-permute-start | bytes 3145736 | tf_op jit(solution)/shard_map/ppermute | solution.py:215
  604.1 21.1 %collective-permute-start.29 = (bf16[256,1024]{1,0:T(8,128)(2,1)}, bf16[256,1024]{1,0:T(8,128)(2,1)}, u32[]{:S(2)}, u32[]{:S(2)}) collective-permute-start(bf16[256,1024]{1,0:T(8,128)(2,1)} %slice.540), channel_id=1, source_target_pairs={{0,8},{8,0},{16,24},{24,16},{1,9},{9,1},{17,25},{25,17},{2,10},{10... | collective-permute-start | bytes 1572872 | tf_op jit(solution)/shard_map/ppermute | solution.py:215
  606.8 18.4 %collective-permute-start.28 = (bf16[256,1024]{1,0:T(8,128)(2,1)}, bf16[256,1024]{1,0:T(8,128)(2,1)}, u32[]{:S(2)}, u32[]{:S(2)}) collective-permute-start(bf16[256,1024]{1,0:T(8,128)(2,1)} %slice.539), channel_id=1, source_target_pairs={{0,16},{8,24},{16,0},{24,8},{1,17},{9,25},{17,1},{25,9},{2,18},{10... | collective-permute-start | bytes 1572872 | tf_op jit(solution)/shard_map/ppermute | solution.py:215
  666.3 16.6 %collective-permute-start.30 = (bf16[512,768]{1,0:T(8,128)(2,1)S(1)}, bf16[512,768]{1,0:T(8,128)(2,1)S(1)}, u32[]{:S(2)}, u32[]{:S(2)}) collective-permute-start(bf16[512,768]{1,0:T(8,128)(2,1)S(1)} %get-tuple-element.172), channel_id=1, source_target_pairs={{0,8},{8,0},{16,24},{24,16},{1,9},{9,1},{17,25},{25,17},{2,10},{10... | collective-permute-start | bytes 2359304 | tf_op jit(solution)/shard_map/ppermute | solution.py:215
  667.8 19.0 %collective-permute-start.32 = (bf16[512,768]{1,0:T(8,128)(2,1)S(1)}, bf16[512,768]{1,0:T(8,128)(2,1)S(1)}, u32[]{:S(2)}, u32[]{:S(2)}) collective-permute-start(bf16[512,768]{1,0:T(8,128)(2,1)S(1)} %get-tuple-element.173), channel_id=1, source_target_pairs={{0,24},{8,16},{16,8},{24,0},{1,25},{9,17},{17,9},{25,1},{2,26},{10... | collective-permute-start | bytes 2359304 | tf_op jit(solution)/shard_map/ppermute | solution.py:215
  668.3 20.4 %collective-permute-start.31 = (bf16[512,768]{1,0:T(8,128)(2,1)S(1)}, bf16[512,768]{1,0:T(8,128)(2,1)S(1)}, u32[]{:S(2)}, u32[]{:S(2)}) collective-permute-start(bf16[512,768]{1,0:T(8,128)(2,1)S(1)} %get-tuple-element.174), channel_id=1, source_target_pairs={{0,16},{8,24},{16,0},{24,8},{1,17},{9,25},{17,1},{25,9},{2,18},{10... | collective-permute-start | bytes 2359304 | tf_op jit(solution)/shard_map/ppermute | solution.py:215
  700.9 96.0 %reduce-scatter.9.cloned.1.call-start = ((), (), s32[]{:S(2)}) async-start(), calls=%async_computation.8 | async-start | bytes 5308416 | tf_op jit(solution)/shard_map/reduce_scatter | solution.py:734
  703.4 14.9 %collective-permute-start.34 = (bf16[256,1024]{1,0:T(8,128)(2,1)S(1)}, bf16[256,1024]{1,0:T(8,128)(2,1)S(1)}, u32[]{:S(2)}, u32[]{:S(2)}) collective-permute-start(bf16[256,1024]{1,0:T(8,128)(2,1)S(1)} %get-tuple-element.151), channel_id=1, source_target_pairs={{0,8},{8,0},{16,24},{24,16},{1,9},{9,1},{17,25},{25,17},{2,10},{10... | collective-permute-start | bytes 1572872 | tf_op jit(solution)/shard_map/ppermute | solution.py:215
  704.9 24.4 %collective-permute-start.33 = (bf16[256,1024]{1,0:T(8,128)(2,1)S(1)}, bf16[256,1024]{1,0:T(8,128)(2,1)S(1)}, u32[]{:S(2)}, u32[]{:S(2)}) collective-permute-start(bf16[256,1024]{1,0:T(8,128)(2,1)S(1)} %get-tuple-element.148), channel_id=1, source_target_pairs={{0,8},{8,0},{16,24},{24,16},{1,9},{9,1},{17,25},{25,17},{2,10},{10... | collective-permute-start | bytes 1572872 | tf_op jit(solution)/shard_map/ppermute | solution.py:215
  705.5 23.8 %collective-permute-start.37 = (bf16[256,1024]{1,0:T(8,128)(2,1)S(1)}, bf16[256,1024]{1,0:T(8,128)(2,1)S(1)}, u32[]{:S(2)}, u32[]{:S(2)}) collective-permute-start(bf16[256,1024]{1,0:T(8,128)(2,1)S(1)} %get-tuple-element.149), channel_id=1, source_target_pairs={{0,16},{8,24},{16,0},{24,8},{1,17},{9,25},{17,1},{25,9},{2,18},{10... | collective-permute-start | bytes 1572872 | tf_op jit(solution)/shard_map/ppermute | solution.py:215
  718.4 14.9 %collective-permute-start.35 = (bf16[256,1024]{1,0:T(8,128)(2,1)S(1)}, bf16[256,1024]{1,0:T(8,128)(2,1)S(1)}, u32[]{:S(2)}, u32[]{:S(2)}) collective-permute-start(bf16[256,1024]{1,0:T(8,128)(2,1)S(1)} %add_convert_fusion.3), channel_id=1, source_target_pairs={{0,16},{8,24},{16,0},{24,8},{1,17},{9,25},{17,1},{25,9},{2,18},{10... | collective-permute-start | bytes 1572872 | tf_op jit(solution)/shard_map/ppermute | solution.py:215
  719.1 24.3 %collective-permute-start.36 = (bf16[256,1024]{1,0:T(8,128)(2,1)S(1)}, bf16[256,1024]{1,0:T(8,128)(2,1)S(1)}, u32[]{:S(2)}, u32[]{:S(2)}) collective-permute-start(bf16[256,1024]{1,0:T(8,128)(2,1)S(1)} %get-tuple-element.150), channel_id=1, source_target_pairs={{0,16},{8,24},{16,0},{24,8},{1,17},{9,25},{17,1},{25,9},{2,18},{10... | collective-permute-start | bytes 1572872 | tf_op jit(solution)/shard_map/ppermute | solution.py:215
  733.8 11.9 %collective-permute-start.38 = (bf16[256,1024]{1,0:T(8,128)(2,1)S(1)}, bf16[256,1024]{1,0:T(8,128)(2,1)S(1)}, u32[]{:S(2)}, u32[]{:S(2)}) collective-permute-start(bf16[256,1024]{1,0:T(8,128)(2,1)S(1)} %get-tuple-element.147), channel_id=1, source_target_pairs={{0,8},{8,0},{16,24},{24,16},{1,9},{9,1},{17,25},{25,17},{2,10},{10... | collective-permute-start | bytes 1572872 | tf_op jit(solution)/shard_map/ppermute | solution.py:215
  798.0 7.7 collective-permute-start.41
  799.6 9.1 %collective-permute-start.40 = (bf16[64,1152]{1,0:T(8,128)(2,1)S(1)}, bf16[64,1152]{1,0:T(8,128)(2,1)S(1)}, u32[]{:S(2)}, u32[]{:S(2)}) collective-permute-start(bf16[64,1152]{1,0:T(8,128)(2,1)S(1)} %get-tuple-element.197), channel_id=1, source_target_pairs={{0,16},{8,24},{16,0},{24,8},{1,17},{9,25},{17,1},{25,9},{2,18},{10... | collective-permute-start | bytes 442376 | tf_op jit(solution)/shard_map/ppermute | solution.py:215
  801.1 7.7 collective-permute-start.39
  (133 other events, 1603.7 us)
Sparse Core Ops, SparseCore 0:
  93.5 150.1 all-gather.2
  245.3 80.5 all-gather.4
  445.0 86.9 reduce-scatter.6
  534.3 166.5 reduce-scatter.4
  703.0 34.6 reduce-scatter.10
  739.9 56.8 reduce-scatter.8

commit v4 on v3

--- a/solution.py
+++ b/solution.py
@@ -72,6 +72,35 @@
         sent.append(copy)
         return copy
 
+    def part(at, k):
+        return head_out.at[flip(rank, k, ranks), at, core]
+
+    def right(t, k):
+        source = head_ref.at[rank] if t == 1 and k == 0 else part(pair - (t - 1), k)
+        slot = (t - 1) * ranks + k
+        target = part(pair - (t - 1), k)
+        return remote(source, target, right_s.at[slot], right_r.at[slot], (rank, fsdp_index + 2))
+
+    def left(t, k):
+        source = head_ref.at[rank] if t == 1 and k == 0 else part(pair + (t - 1), k)
+        slot = (t - 1) * ranks + k
+        target = part(pair + (t - 1), k)
+        return remote(source, target, left_s.at[slot], left_r.at[slot], (rank, fsdp_index - 2))
+
+    def to_sibling(t, k):
+        source = head_ref.at[rank] if t == 0 and k == 0 else part(pair - t, k)
+        slot = (t + pairs - 1) * ranks + k
+        return remote(source, part(pair - t, k), head_s3.at[slot], head_r3.at[slot], sibling)
+
+    sends_right = lambda t: (pair - (t - 1) >= 0) & (pair + 1 < pairs)
+    sends_left = lambda t: (pair + (t - 1) < pairs) & (pair - 1 >= 0)
+
+    def begin(k):
+        pl.when(sends_right(1))(lambda: right(1, k).start())
+        pl.when(sends_left(1))(lambda: left(1, k).start())
+        to_sibling(0, k).start()
+
+    begin(0)
     head_seq = [
         go(
             remote(
@@ -108,33 +137,34 @@
         go(remote(mark_ref, mark_out.at[i], mark_s.at[i - 1], mark_r.at[i - 1], on_seq(i)))
         for i in range(1, ranks)
     ]
-
-    owns[0].wait()
-    for copy in head_seq:
-        copy.wait_recv()
-
-    def right(t):
-        part = head_out.at[:, pair - (t - 1), core]
-        return remote(part, part, right_s.at[t - 1], right_r.at[t - 1], (rank, fsdp_index + 2))
-
-    def left(t):
-        part = head_out.at[:, pair + (t - 1), core]
-        return remote(part, part, left_s.at[t - 1], left_r.at[t - 1], (rank, fsdp_index - 2))
-
-    def to_sibling(at, slot):
-        part = head_out.at[:, at, core]
-        return remote(part, part, head_s3.at[slot], head_r3.at[slot], sibling)
-
-    sends_right = lambda t: (pair - (t - 1) >= 0) & (pair + 1 < pairs)
-    sends_left = lambda t: (pair + (t - 1) < pairs) & (pair - 1 >= 0)
-    pl.when(sends_right(1))(lambda: right(1).start())
-    pl.when(sends_left(1))(lambda: left(1).start())
-    to_sibling(pair, 0).start()
-
-    x_seq = [
-        go(remote(x_ref, x_out.at[i], x_s.at[i - 1], x_r.at[i - 1], on_seq(i)))
-        for i in range(1, ranks)
-    ]
+    for k in range(1, ranks):
+        head_seq[k - 1].wait_recv()
+        begin(k)
+
+    half = x_ref.shape[1] // 2
+    first, second = slice(0, half), slice(half, 2 * half)
+    x_seq, relays = [], []
+    if ranks == 4:
+        for order in range(2):
+            for i, columns in ((1, (first, second)[order]), (2, (second, first)[order])):
+                slot = (i - 1) * 2 + order
+                x_seq.append(
+                    go(
+                        remote(
+                            x_ref.at[:, columns],
+                            x_out.at[i, :, columns],
+                            x_s.at[slot],
+                            x_r.at[slot],
+                            on_seq(i),
+                        )
+                    )
+                )
+    else:
+        for i in range(1, ranks):
+            x_seq.append(
+                go(remote(x_ref, x_out.at[i], x_s.at[i - 1], x_r.at[i - 1], on_seq(i)))
+            )
+
     owns[1].wait()
     for copy in rest_pair:
         copy.wait_recv()
@@ -146,38 +176,58 @@
     rest_core = [go(remote(row, row, rest_s3.at[0], rest_r3.at[0], sibling))]
 
     for t in range(1, pairs):
-
-        def from_left(t=t):
-            part = head_out.at[:, pair - t, core]
-            remote(part, part, right_s.at[t - 1], right_r.at[t - 1], sibling).wait_recv()
-            if t + 1 < pairs:
-                pl.when(pair + 1 < pairs)(lambda: right(t + 1).start())
-            to_sibling(pair - t, t).start()
-
-        def from_right(t=t):
-            part = head_out.at[:, pair + t, core]
-            remote(part, part, left_s.at[t - 1], left_r.at[t - 1], sibling).wait_recv()
-            if t + 1 < pairs:
-                pl.when(pair - 1 >= 0)(lambda: left(t + 1).start())
-            to_sibling(pair + t, pairs - 1 + t).start()
-
-        pl.when(pair - t >= 0)(from_left)
-        pl.when(pair + t < pairs)(from_right)
+        for k in range(ranks):
+
+            def from_left(t=t, k=k):
+                slot = (t - 1) * ranks + k
+                target = part(pair - t, k)
+                remote(target, target, right_s.at[slot], right_r.at[slot], sibling).wait_recv()
+                if t + 1 < pairs:
+                    pl.when(pair + 1 < pairs)(lambda: right(t + 1, k).start())
+                to_sibling(t, k).start()
+
+            def from_right(t=t, k=k):
+                slot = (t - 1) * ranks + k
+                target = part(pair + t, k)
+                remote(target, target, left_s.at[slot], left_r.at[slot], sibling).wait_recv()
+                if t + 1 < pairs:
+                    pl.when(pair - 1 >= 0)(lambda: left(t + 1, k).start())
+                to_sibling(-t, k).start()
+
+            pl.when(pair - t >= 0)(from_left)
+            pl.when(pair + t < pairs)(from_right)
+        if t == 1 and ranks == 4:
+            x_seq[0].wait_recv()
+            x_seq[1].wait_recv()
+            for slot, i, columns, to in ((4, 1, first, 2), (5, 2, second, 1)):
+                relays.append(
+                    go(
+                        remote(
+                            x_out.at[i, :, columns],
+                            x_out.at[3, :, columns],
+                            x_s.at[slot],
+                            x_r.at[slot],
+                            on_seq(to),
+                        )
+                    )
+                )
 
     for i in range(1, ranks):
         rest_seq[i - 1].wait_recv()
         row = rest_out.at[flip(rank, i, ranks), :, core]
         rest_core.append(go(remote(row, row, rest_s3.at[i], rest_r3.at[i], sibling)))
+    owns[0].wait()
     for copy in owns[2:]:
         copy.wait()
-    for copy in marks + x_seq + rest_core:
+    for copy in marks + x_seq[2 if ranks == 4 else 0 :] + relays + rest_core:
         copy.wait_recv()
-    to_sibling(pair, 0).wait()
-    for t in range(1, pairs):
-        pl.when(pair - t >= 0)(lambda t=t: to_sibling(pair - t, t).wait())
-        pl.when(pair + t < pairs)(lambda t=t: to_sibling(pair + t, pairs - 1 + t).wait())
-        pl.when(sends_right(t))(lambda t=t: right(t).wait_send())
-        pl.when(sends_left(t))(lambda t=t: left(t).wait_send())
+    for k in range(ranks):
+        to_sibling(0, k).wait()
+        for t in range(1, pairs):
+            pl.when(pair - t >= 0)(lambda t=t, k=k: to_sibling(t, k).wait())
+            pl.when(pair + t < pairs)(lambda t=t, k=k: to_sibling(-t, k).wait())
+            pl.when(sends_right(t))(lambda t=t, k=k: right(t, k).wait_send())
+            pl.when(sends_left(t))(lambda t=t, k=k: left(t, k).wait_send())
     for copy in sent:
         copy.wait_send()
 
@@ -199,12 +249,13 @@
         scratch_shapes=[
             dma(4),
             *[dma(ranks - 1)] * 2,
-            *[dma(pairs - 1)] * 4,
-            *[dma(2 * pairs - 1)] * 2,
+            *[dma((pairs - 1) * ranks)] * 4,
+            *[dma((2 * pairs - 1) * ranks)] * 2,
             *[dma(pairs - 1)] * 2,
             *[dma(ranks - 1)] * 2,
             *[dma(ranks)] * 2,
-            *[dma(ranks - 1)] * 4,
+            *[dma(ranks - 1)] * 2,
+            *[dma(2 * ranks - 2)] * 2,
         ],
         compiler_params=pltpu.CompilerParams(collective_id=0, has_side_effects=True),
     )(head, rest, marks, x)
@@ -253,6 +304,21 @@
 
 def take(v, axis, index):
     return lax.dynamic_index_in_dim(v, index, axis, keepdims=False)
+
+
+def gather_everywhere(v, after, ranks, pairs):
+    v, after = lax.optimization_barrier((v, after))
+    index, rank = lax.axis_index("fsdp"), lax.axis_index("seq")
+    pair, core = index // 2, index % 2
+
+    def spread(part, axis, offsets, mine):
+        got = jnp.stack([part] + [permute(part, axis, k) for k in offsets])
+        return jnp.stack([take(got, 0, mine ^ i) for i in range(len(offsets) + 1)])
+
+    v = spread(v, "fsdp", [2 * k for k in range(1, pairs)], pair)
+    v = spread(v, "seq", range(1, ranks), rank)
+    v = spread(v, "fsdp", [1], core)
+    return jnp.moveaxis(v, 0, 2).reshape(-1, v.shape[-1])
 
 
 def dot(left, right, over):
@@ -536,6 +602,350 @@
     )(*lefts, right, *extras)
 
 
+def middle_kernel(
+    block,
+    parts,
+    hidden_ref,
+    map_ref,
+    mixed_ref,
+    gain_ref,
+    ple_gate_ref,
+    ple_proj_ref,
+    ple_input_ref,
+    cotangent_ref,
+    rows_ref,
+    grad_map_ref,
+    out_ref,
+    second_ref,
+    grad_second_ref,
+    grad_ple_ref,
+    ple_mixed_ref,
+    grad_gate_ref,
+    gain_out_ref,
+    maps,
+    own,
+    keep_left,
+    keep_right,
+    send_x,
+    send_y,
+    got_x,
+    got_y,
+    relay_x,
+    relay_y,
+    far_x,
+    far_y,
+    stage,
+    map_sem,
+    stage_sem,
+    *sems,
+):
+    (sx_s, sx_r, sy_s, sy_r, rx_s, rx_r, ry_s, ry_r) = sems[:8]
+    (gx_s, gx_r, gy_s, gy_r, fx_s, fx_r, fy_s, fy_r) = sems[8:]
+    rank = lax.axis_index("seq")
+    fsdp_index = lax.axis_index("fsdp")
+    by_x, by_y = (flip(rank, 1, 4), fsdp_index), (flip(rank, 2, 4), fsdp_index)
+    size = block // parts
+    width = map_ref.shape[0]
+    half = width // 2
+    tile = 256
+    tiles = width // tile
+    left, right = slice(0, half), slice(half, width)
+    up = lambda v: v.astype(full)
+
+    def remote(source, target, send, recv, device):
+        return pltpu.make_async_remote_copy(
+            src_ref=source,
+            dst_ref=target,
+            send_sem=send,
+            recv_sem=recv,
+            device_id=device,
+            device_id_type=MESH,
+        )
+
+    def map_copy(i):
+        at = pl.ds(pl.multiple_of(i * tile, tile), tile)
+        return pltpu.make_async_copy(map_ref.at[at, :], maps.at[at, :], map_sem.at[i])
+
+    for i in range(tiles):
+        map_copy(i).start()
+
+    barrier = pltpu.get_barrier_semaphore()
+    for device in (by_x, by_y):
+        pl.semaphore_signal(barrier, inc=1, device_id=device, device_id_type=MESH)
+    pl.semaphore_wait(barrier, 2)
+
+    sent = []
+
+    def go(copy):
+        copy.start()
+        sent.append(copy)
+        return copy
+
+    def rows_of(u):
+        return pl.ds(u * size, size)
+
+    near_x, near_y = [], []
+    for u in range(parts):
+        at = rows_of(u)
+
+        def product(i):
+            if u == 0:
+                map_copy(i).wait()
+            rows = pl.ds(pl.multiple_of(i * tile, tile), tile)
+            v = hidden_ref[:, at, :].reshape(4 * size, hidden_ref.shape[2])
+            return mm_nt(v, maps[rows, :]).reshape(4, size, tile)
+
+        def left_tile(i, carry):
+            v = product(i)
+            columns = pl.ds(pl.multiple_of(i * tile, tile), tile)
+            own[at, columns] = v[0]
+            keep_left[at, columns] = v[2]
+            send_x[u, 0, :, columns] = v[3].astype(low)
+            send_x[u, 1, :, columns] = v[1].astype(low)
+            return carry
+
+        def right_tile(i, carry):
+            v = product(i + tiles // 2)
+            columns = pl.ds(pl.multiple_of(i * tile, tile), tile)
+            own[at, pl.ds(pl.multiple_of(half + i * tile, tile), tile)] = v[0]
+            keep_right[at, columns] = v[1]
+            send_y[u, 0, :, columns] = v[3].astype(low)
+            send_y[u, 1, :, columns] = v[2].astype(low)
+            return carry
+
+        lax.fori_loop(0, tiles // 2, left_tile, 0)
+        near_x.append(go(remote(send_x.at[u], got_x.at[u], sx_s.at[u], sx_r.at[u], by_x)))
+        lax.fori_loop(0, tiles // 2, right_tile, 0)
+        near_y.append(go(remote(send_y.at[u], got_y.at[u], sy_s.at[u], sy_r.at[u], by_y)))
+
+    last_x, last_y = [], []
+    for u in range(parts):
+        at = rows_of(u)
+        near_x[u].wait_recv()
+        relay_y[u] = (keep_left[at, :] + up(got_x[u, 0])).astype(low)
+        last_y.append(go(remote(relay_y.at[u], far_y.at[u], ry_s.at[u], ry_r.at[u], by_y)))
+        near_y[u].wait_recv()
+        relay_x[u] = (keep_right[at, :] + up(got_y[u, 0])).astype(low)
+        last_x.append(go(remote(relay_x.at[u], far_x.at[u], rx_s.at[u], rx_r.at[u], by_x)))
+
+    gain_out_ref[...] = jnp.zeros_like(gain_out_ref)
+    ffn_gain, ple_gain = gain_ref[0:1, :], gain_ref[1:2, :]
+    mean = lambda v: jnp.mean(v, -1, keepdims=True)
+    total = lambda v: jnp.sum(v, 0, keepdims=True)
+    slope, cubic = math.sqrt(2.0 / math.pi), 0.044715
+    rows_x, rows_y = [], []
+    for u in range(parts):
+        at = rows_of(u)
+        last_y[u].wait_recv()
+        last_x[u].wait_recv()
+        own[at, left] = own[at, left] + up(got_x[u, 1]) + up(far_y[u])
+        own[at, right] = own[at, right] + up(got_y[u, 1]) + up(far_x[u])
+        f = own[at, :]
+        f_inverse = lax.rsqrt(mean(f * f) + eps)
+        second = (mixed_ref[at, :] + f * f_inverse * ffn_gain).astype(low)
+        second_ref[at, :] = second
+        gate = mm(second, ple_gate_ref[...])
+        bend = jnp.tanh(slope * (gate + cubic * gate * gate * gate))
+        gate_slope = 0.5 * (1.0 + bend) + 0.5 * gate * (1.0 - bend * bend) * slope * (
+            1.0 + 3.0 * cubic * gate * gate
+        )
+        given = up(ple_input_ref[at, :])
+        ple_mixed = (0.5 * gate * (1.0 + bend) * given).astype(low)
+        ple_mixed_ref[at, :] = ple_mixed
+        proj = mm_nt(ple_mixed, ple_proj_ref[...])
+        proj_inverse = lax.rsqrt(mean(proj * proj) + eps)
+        out_ref[at, :] = (up(second) + proj * proj_inverse * ple_gain).astype(low)
+        incoming = up(cotangent_ref[at, :])
+        gain_out_ref[1:2, :] += total(incoming * proj * proj_inverse)
+        scaled = incoming * ple_gain
+        grad_proj = proj_inverse * (
+            scaled - proj * (proj_inverse * proj_inverse * mean(scaled * proj))
+        )
+        grad_ple = grad_proj.astype(low)
+        grad_ple_ref[at, :] = grad_ple
+        grad_gate = (mm(grad_ple, ple_proj_ref[...]) * given * gate_slope).astype(low)
+        grad_gate_ref[at, :] = grad_gate
+        grad_second = incoming + mm_nt(grad_gate, ple_gate_ref[...])
+        grad_second_ref[at, :] = grad_second
+        f = own[at, :]
+        gain_out_ref[0:1, :] += total(grad_second * f * f_inverse)
+        scaled = grad_second * ffn_gain
+        grad_f = f_inverse * (scaled - f * (f_inverse * f_inverse * mean(scaled * f)))
+        rows_ref[0, at, :] = grad_f.astype(low)
+        pair_x, pair_y = [], []
+        for order in range(2):
+            for pairs, device, send, recv, index, part in (
+                (pair_x, by_x, gx_s, gx_r, 1, (left, right)[order]),
+                (pair_y, by_y, gy_s, gy_r, 2, (right, left)[order]),
+            ):
+                pairs.append(
+                    go(
+                        remote(
+                            rows_ref.at[0, at, part],
+                            rows_ref.at[index, at, part],
+                            send.at[u, order],
+                            recv.at[u, order],
+                            device,
+                        )
+                    )
+                )
+        rows_x.append(pair_x)
+        rows_y.append(pair_y)
+
+    far = []
+    for u in range(parts):
+        at = rows_of(u)
+        rows_x[u][0].wait_recv()
+        far.append(
+            go(
+                remote(
+                    rows_ref.at[1, at, left],
+                    rows_ref.at[3, at, left],
+                    fy_s.at[u],
+                    fy_r.at[u],
+                    by_y,
+                )
+            )
+        )
+        rows_y[u][0].wait_recv()
+        far.append(
+            go(
+                remote(
+                    rows_ref.at[2, at, right],
+                    rows_ref.at[3, at, right],
+                    fx_s.at[u],
+                    fx_r.at[u],
+                    by_x,
+                )
+            )
+        )
+    for u in range(parts):
+        rows_x[u][1].wait_recv()
+        rows_y[u][1].wait_recv()
+    for copy in far:
+        copy.wait_recv()
+
+    def stage_copy(i, slot):
+        at = pl.ds(pl.multiple_of(i * tile, tile), tile)
+        return pltpu.make_async_copy(stage.at[slot], grad_map_ref.at[at, :], stage_sem.at[slot])
+
+    span = hidden_ref.shape[2]
+
+    def grad_tile(i, carry):
+        slot = i % 2
+
+        @pl.when(i >= 2)
+        def _():
+            stage_copy(i - 2, slot).wait()
+
+        columns = pl.ds(pl.multiple_of(i * tile, tile), tile)
+        v = rows_ref[:, :, columns].reshape(4 * block, tile)
+        for j in range(0, span, span // 2):
+            w = hidden_ref[:, :, j : j + span // 2].reshape(4 * block, span // 2)
+            stage[slot, :, j : j + span // 2] = mm_tn(v, w).astype(low)
+        stage_copy(i, slot).start()
+        return carry
+
+    lax.fori_loop(0, tiles, grad_tile, 0)
+    stage_copy(tiles - 2, 0).wait()
+    stage_copy(tiles - 1, 1).wait()
+    for copy in sent:
+        copy.wait_send()
+
+
+def middle(hidden, down_map, mixed, gains, ple, ple_input, cotangent):
+    block, width = mixed.shape
+    span = hidden.shape[1]
+    parts, half = 2, width // 2
+    size = block // parts
+    hidden = hidden.reshape(4, block, span)
+    dma = pltpu.SemaphoreType.DMA
+    vmem = pl.BlockSpec(memory_space=pltpu.VMEM)
+    anywhere = pl.BlockSpec(memory_space=pl.ANY)
+    pieces = pltpu.VMEM((parts, 2, size, half), low)
+    singles = pltpu.VMEM((parts, size, half), low)
+    shapes = (
+        ((4, block, width), low),
+        ((width, span), low),
+        ((block, width), low),
+        ((block, width), low),
+        ((block, width), full),
+        ((block, width), low),
+        ((block, PLE), low),
+        ((block, PLE), low),
+        ((8, width), full),
+    )
+    return pl.pallas_call(
+        functools.partial(middle_kernel, block, parts),
+        out_shape=tuple(jax.ShapeDtypeStruct(*v) for v in shapes),
+        in_specs=[vmem, anywhere] + [vmem] * 6,
+        out_specs=tuple(anywhere if i == 1 else vmem for i in range(len(shapes))),
+        scratch_shapes=[
+            pltpu.VMEM((width, span), low),
+            pltpu.VMEM((block, width), full),
+            pltpu.VMEM((block, half), full),
+            pltpu.VMEM((block, half), full),
+            *[pieces] * 4,
+            *[singles] * 4,
+            pltpu.VMEM((2, 256, span), low),
+            dma((width // 256,)),
+            dma((2,)),
+            *[dma((parts,))] * 8,
+            *[dma((parts, 2))] * 4,
+            *[dma((parts,))] * 4,
+        ],
+        compiler_params=pltpu.CompilerParams(
+            collective_id=1, has_side_effects=True, vmem_limit_bytes=56 << 20
+        ),
+        cost_estimate=pl.CostEstimate(
+            flops=16 * block * width * span, bytes_accessed=100 << 20, transcendentals=0
+        ),
+    )(
+        hidden,
+        down_map,
+        mixed,
+        jnp.pad(jnp.stack(gains), ((0, 6), (0, 0))),
+        ple[:, :PLE],
+        ple[:, PLE:],
+        ple_input,
+        cotangent,
+    )
+
+
+def middle_plain(ranks, hidden, down_map, mixed, gains, ple, ple_input, cotangent):
+    block = mixed.shape[0]
+    parts = mm_nt(hidden, down_map).astype(low)
+    ffn_out = sum_seq([parts[k * block : (k + 1) * block] for k in range(ranks)], ranks)
+    ffn_normed, ffn_inverse = norm_rows(ffn_out, gains[0])
+    h_second = (mixed + ffn_normed).astype(low)
+    ple_gate = mm(h_second, ple[:, :PLE])
+    ple_input = ple_input.astype(full)
+    ple_mixed = (gelu_tanh(ple_gate) * ple_input).astype(low)
+    ple_proj = mm_nt(ple_mixed, ple[:, PLE:])
+    ple_normed, ple_inverse = norm_rows(ple_proj, gains[1])
+    hidden_out = (h_second.astype(full) + ple_normed).astype(low)
+    grad_out = cotangent.astype(full)
+    grad_ple_proj, gain_grad_five = norm_back(ple_proj, ple_inverse, gains[1], grad_out)
+    grad_ple_low = grad_ple_proj.astype(low)
+    grad_ple_mixed = mm(grad_ple_low, ple[:, PLE:])
+    unused_gelu, gelu_pull = jax.vjp(gelu_tanh, ple_gate)
+    grad_ple_gate = gelu_pull(grad_ple_mixed * ple_input)[0].astype(low)
+    grad_second = grad_out + mm_nt(grad_ple_gate, ple[:, :PLE])
+    grad_ffn, gain_grad_four = norm_back(ffn_out, ffn_inverse, gains[0], grad_second)
+    rows = whole_rows(gather_seq(grad_ffn.astype(low), ranks))
+    return (
+        rows,
+        mm_tn(rows, hidden).astype(low),
+        hidden_out,
+        h_second,
+        grad_second,
+        grad_ple_low,
+        ple_mixed,
+        grad_ple_gate,
+        jnp.stack([gain_grad_four, gain_grad_five]),
+    )
+
+
 def body(
     sizes,
     hidden_in,
@@ -574,7 +984,7 @@
         [norm_gains, jnp.pad(head_gains, ((0, rows - head_rows), (0, 0)))], 1
     )
     small = jnp.pad(small, ((0, 0), (0, 128 - small.shape[1])))
-    rest_pack = jnp.concatenate([laurel_maps, per_layer_maps, small], 1)
+    rest_pack = jnp.concatenate([laurel_maps, small], 1)
     marks = jnp.pad(jnp.concatenate([segment_ids.T, positions.T], 0), ((0, 6), (0, 0)))
     x_local = hidden_in.reshape(block, width)
 
@@ -587,12 +997,12 @@
     in_maps = lax.all_gather(in_rows, "fsdp", axis=0, tiled=True)
     down_map = lax.all_gather(down_rows, "fsdp", axis=0, tiled=True)
     x_all = x_all.reshape(length, width)
+    ple = gather_everywhere(per_layer_maps, head_all, ranks, pairs)
     head_all = head_all.reshape(width, -1)
     rest_all = rest_all.reshape(width, -1)
     qkv_map, out_map = head_all[:, :-q_width], head_all[:, -q_width:]
     laurel = rest_all[:, : 2 * LR]
-    ple = rest_all[:, 2 * LR : 2 * LR + 2 * PLE]
-    gains = rest_all[:, 2 * LR + 2 * PLE :].astype(full)
+    gains = rest_all[:, 2 * LR :].astype(full)
     gain = [gains[:, i] for i in range(6)]
     head_scale = gains[:, 6:8].reshape(-1, rows, 2)[:, :head_rows].reshape(HEAD_DIM, 2)
 
@@ -625,31 +1035,31 @@
     gate_part, up_part = gate_up[:, 0], gate_up[:, 1]
     hidden = (gelu_tanh(gate_part) * up_part).astype(low)
     hidden, down_map = lax.optimization_barrier((hidden, down_map))
-    ffn_out = sum_seq(cut(mm_nt(hidden, down_map).astype(low)), ranks)
-
-    ffn_normed, ffn_inverse = norm_rows(ffn_out, gain[4])
-    h_second = (mixed + ffn_normed).astype(low)
-    ple_gate = mm(h_second, ple[:, :PLE])
-    ple_input = per_layer_input.reshape(block, PLE).astype(full)
-    ple_mixed = (gelu_tanh(ple_gate) * ple_input).astype(low)
-    ple_proj = mm_nt(ple_mixed, ple[:, PLE:])
-    ple_normed, ple_inverse = norm_rows(ple_proj, gain[5])
-    hidden_out = (h_second.astype(full) + ple_normed).astype(low)
-
-    grad_out = out_cotangent.reshape(block, width).astype(full)
-    grad_ple_proj, gain_grad_five = norm_back(ple_proj, ple_inverse, gain[5], grad_out)
-    grad_ple_low = grad_ple_proj.astype(low)
-    grad_ple_mixed = mm(grad_ple_low, ple[:, PLE:])
-    unused_gelu, gelu_pull = jax.vjp(gelu_tanh, ple_gate)
-    grad_ple_gate = gelu_pull(grad_ple_mixed * ple_input)[0].astype(low)
-    grad_second = grad_out + mm_nt(grad_ple_gate, ple[:, :PLE])
-    grad_ffn, gain_grad_four = norm_back(ffn_out, ffn_inverse, gain[4], grad_second)
-    grad_ffn_blocks = gather_seq(grad_ffn.astype(low), ranks)
-
-    down_grad = mm_tn(whole_rows(grad_ffn_blocks), hidden).astype(low)
+    run_middle = middle if ranks == 4 else functools.partial(middle_plain, ranks)
+    (
+        grad_ffn_rows,
+        down_grad,
+        hidden_out,
+        h_second,
+        grad_second,
+        grad_ple_low,
+        ple_mixed,
+        grad_ple_gate,
+        ffn_gain_grads,
+    ) = run_middle(
+        hidden,
+        down_map,
+        mixed,
+        gain[4:6],
+        ple,
+        per_layer_input.reshape(block, PLE),
+        out_cotangent.reshape(block, width),
+    )
+    gain_grad_four, gain_grad_five = ffn_gain_grads[0], ffn_gain_grads[1]
+    grad_ffn_rows = grad_ffn_rows.reshape(length, width)
     down_sum = lax.psum_scatter(down_grad, "fsdp", scatter_dimension=0, tiled=True)
-    grad_ffn_blocks, down_grad = lax.optimization_barrier((grad_ffn_blocks, down_grad))
-    grad_hidden = mm(whole_rows(grad_ffn_blocks), down_map)
+    grad_ffn_rows, down_grad = lax.optimization_barrier((grad_ffn_rows, down_grad))
+    grad_hidden = mm(grad_ffn_rows, down_map)
     gate_act, act_pull = jax.vjp(gelu_tanh, gate_part)
     grad_gate_up = jnp.stack(
         [act_pull(grad_hidden * up_part)[0], grad_hidden * gate_act], 1
@@ -678,7 +1088,15 @@
     x_here = grad_branch + mm_nt(grad_laurel_low, laurel[:, :LR])
     gain_grad_zero = jnp.sum(x_here * tokens * x_inverse, 0)
     small_grad = jnp.stack(
-        [gain_grad_zero, gain_grad_one, gain_grad_two, gain_grad_three, gain_grad_four, gain_grad_five], 1
+        [
+            gain_grad_zero,
+            gain_grad_one,
+            gain_grad_two,
+            gain_grad_three,
+            gain_grad_four,
+            gain_grad_five,
+        ],
+        1,
     )
     small_grad = jnp.pad(small_grad, ((0, 0), (0, 128 - small_grad.shape[1])))
     rest_grad = jnp.concatenate(

time: 832 us -> 791 us (0.951)
  waiting for transfers between devices: 303 us -> 220 us
  Pallas kernels: 111 us -> 185 us
  matrix products: 177 us -> 142 us
    pallas_call x0 -> x1, Pallas kernels: none -> 95.6 us  [middle(): pl.pallas_call(functools.partial(middle_kernel, block, parts), out_shape=...]
    dot_general x22 -> x16, matrix products: 172 us -> 137 us  [dot(): lax.dot_general(left, right, (over, ((), ())), preferred_element_type=full)]
    all_gather x1, waiting for transfers between devices: 47.8 us -> 13.8 us  [body(): down_map = lax.all_gather(down_rows, 'fsdp', axis=0, tiled=True)]
    ppermute x45 -> x42, waiting for transfers between devices: 192 us -> 168 us  [permute(): return lax.ppermute(v, axis, [(i, i ^ offset) for i in range(size)])]
    pallas_call x1, Pallas kernels: 78 us -> 56.5 us  [gather_weights(): pl.pallas_call(functools.partial(gather_kernel, sizes), out_shape=(jax.Sh...]
    all_gather x1, waiting for transfers between devices: 15.8 us -> 0.01 us  [body(): in_maps = lax.all_gather(in_rows, 'fsdp', axis=0, tiled=True)]
    reduce_scatter x1, waiting for transfers between devices: 10 us -> 0.01 us  [body(): in_sum = lax.psum_scatter(in_grad, 'fsdp', scatter_dimension=0, tiled=True)]
    unnamed x267 -> x232, local copies, waits for them, and re-layouts: 26.6 us -> 30.5 us
  transfers between devices with their start and end apart: 51 -> 48, of which waited for: 36 -> 25; matrix products, arithmetic and copies ran while one was open for 32% -> 35% of each run, Pallas kernels for 4% -> 4%
where the time goes in v4:
time: 791 us; the launch traced here: 778 us
  waiting for transfers between devices  220 us (28%)
  Pallas kernels  185 us (23%)
  matrix products  142 us (18%)
  local copies, waits for them, and re-layouts  87.4 us (11%)
  other arithmetic  77.1 us (10%)
  starting transfers between devices  50.9 us (6%)
  between operations  16.2 us (2%)
    ppermute x42, waiting for transfers between devices, permute(): return lax.ppermute(v, axis, [(i, i ^ offset) for i in range(size)])  168 us
    dot_general x16, matrix products, dot(): lax.dot_general(left, right, (over, ((), ())), preferred_element_type=full)  137 us
    pallas_call x1, Pallas kernels, middle(): pl.pallas_call(functools.partial(middle_kernel, block, parts), out_shape=...  95.6 us
    pallas_call x1, Pallas kernels, gather_weights(): pl.pallas_call(functools.partial(gather_kernel, sizes), out_shape=(jax.Sh...  56.5 us
    ppermute x42, starting transfers between devices, permute(): return lax.ppermute(v, axis, [(i, i ^ offset) for i in range(size)])  50.5 us
    reduce_scatter x1, waiting for transfers between devices, body(): last_sum = lax.psum_scatter(last, 'fsdp', scatter_dimension=0, tiled=True)  37.2 us
    unnamed x232, local copies, waits for them, and re-layouts  30.5 us
    pallas_call x1, Pallas kernels, attend_back(): pl.pallas_call(functools.partial(attend_back_kernel, ranks, block), grid=...  17 us
  transfers between devices with their start and end apart: 48, of which 25 were waited for; matrix products, arithmetic and copies ran while one was open for 35% of the time, Pallas kernels for 4%

profile of v4, /device:TPU:20, one launch (start us, length us, event | category | flops | bytes accessed | tf_op | source)
XLA Modules:
  0.0 778.3 jit_solution(1233937049989301625)
XLA Ops:
  9.7 3.2 slice.348
  15.3 56.5 %shard_map.221 = (bf16[4,4,2,64,1536]{4,3,2,1,0:T(8,128)(2,1)}, bf16[4,4,2,64,256]{4,3,2,1,0:T(8,128)(2,1)}, s32[4,8,256]{2,1,0:T(8,128)}, bf16[4,256,2048]{2,1,0:T(8,128)(2,1)}) custom-call(bf16[4,64,1536]{2,1,0:T(8,128)(2,1)} %pad_maximum_fusion.11.head_ref, bf16[64,256]{1,0:T(8,128)(2,1)} %fusion.94.rest_ref, s32[8,256]{1,0:T(8,128)} %pad.31.mark_ref, ...), custom_call_target="tpu_custom_call" | custom-call | tf_op jit(solution)/shard_map/pallas_call | solution.py:239
  72.8 5.8 collective-permute-start.11
  79.2 3.1 slice_reduce_fusion.1
  87.3 4.6 fusion.45
  98.1 3.8 fusion.79
  113.0 2.8 fusion.61
  115.9 5.5 fusion.74
  127.3 3.1 fusion.66
  130.4 4.4 convolution_convert_fusion.1
  138.9 22.3 %collective-permute-done.1 = bf16[256,1024]{1,0:T(8,128)(2,1)S(1)} collective-permute-done((bf16[256,1024]{1,0:T(8,128)(2,1)S(1)}, bf16[256,1024]{1,0:T(8,128)(2,1)S(1)}, u32[]{:S(2)}, u32[]{:S(2)}) %collective-permute-start.1) | collective-permute-done | bytes 524320 | tf_op jit(solution)/shard_map/ppermute | solution.py:266
  169.3 7.1 collective-permute-done.4
  177.8 15.5 %collective-permute-done.2 = bf16[256,1024]{1,0:T(8,128)(2,1)} collective-permute-done((bf16[256,1024]{1,0:T(8,128)(2,1)S(1)}, bf16[256,1024]{1,0:T(8,128)(2,1)}, u32[]{:S(2)}, u32[]{:S(2)}) %collective-permute-start.2) | collective-permute-done | bytes 524320 | tf_op jit(solution)/shard_map/ppermute | solution.py:266
  193.2 2.9 convert_add_fusion.7
  197.2 11.1 %collective-permute-done.14 = bf16[4,64,512]{2,1,0:T(8,128)(2,1)} collective-permute-done((bf16[4,64,512]{2,1,0:T(8,128)(2,1)}, bf16[4,64,512]{2,1,0:T(8,128)(2,1)}, u32[]{:S(2)}, u32[]{:S(2)}) %collective-permute-start.14) | collective-permute-done | bytes 262176 | tf_op jit(solution)/shard_map/ppermute | solution.py:266
  222.6 20.6 %collective-permute-done.7 = bf16[256,2048]{1,0:T(8,128)(2,1)} collective-permute-done((bf16[256,2048]{1,0:T(8,128)(2,1)S(1)}, bf16[256,2048]{1,0:T(8,128)(2,1)}, u32[]{:S(2)}, u32[]{:S(2)}) %collective-permute-start.7) | collective-permute-done | bytes 1048608 | tf_op jit(solution)/shard_map/ppermute | solution.py:266
  249.0 9.0 %collective-permute-done.9 = bf16[256,1024]{1,0:T(8,128)(2,1)S(1)} collective-permute-done((bf16[256,1024]{1,0:T(8,128)(2,1)S(1)}, bf16[256,1024]{1,0:T(8,128)(2,1)S(1)}, u32[]{:S(2)}, u32[]{:S(2)}) %collective-permute-start.9) | collective-permute-done | bytes 524320 | tf_op jit(solution)/shard_map/ppermute | solution.py:266
  259.4 24.9 %fusion.13 = f32[1024,2,2048]{2,0,1:T(8,128)} fusion(bf16[2048,2,2048]{2,0,1:T(8,128)(2,1)} %all-gather.3.cloned.1.call-done, bf16[256,1024]{1,0:T(8,128)(2,1)S(1)} %collective-permute-done.9, bf16[256,1024]{1,0:T(8,128)(2,1)S(1)} %collective-permute-done.8, bf16[256,2048]{1,0:T(8,128)(2,1)} %collective-permute-done.7, ...), kind=kOutput, calls=%fused_computation.31 | convolution fusion | flops 17200840704 | bytes 37748736 | tf_op jit(solution)/shard_map/dot_general | solution.py:325
  284.4 8.8 %multiply_convert_fusion.1 = bf16[1024,2048]{1,0:T(8,128)(2,1)} fusion(f32[1024,2,2048]{2,0,1:T(8,128)} %fusion.13), kind=kLoop, calls=%fused_computation.19 | loop fusion | flops 20971520 | bytes 20971520 | tf_op jit(solution)/shard_map/convert_element_type | solution.py:1036
  293.1 13.8 %all-gather.5.cloned.1.call-done.map_ref = bf16[2048,2048]{1,0:T(8,128)(2,1)} async-done(((bf16[256,2048]{1,0:T(8,128)(2,1)}), bf16[2048,2048]{1,0:T(8,128)(2,1)}) %all-gather.5.cloned.1.call-update) | async-done | bytes 8388624 | tf_op jit(solution)/shard_map/all_gather | solution.py:998
  306.9 95.6 %shard_map.222 = (bf16[4,256,2048]{2,1,0:T(8,128)(2,1)}, bf16[2048,2048]{1,0:T(8,128)(2,1)}, bf16[256,2048]{1,0:T(8,128)(2,1)}, bf16[256,2048]{1,0:T(8,128)(2,1)...) custom-call(bf16[4,256,2048]{2,1,0:T(8,128)(2,1)} %bitcast.278, ...), custom_call_target="tpu_custom_call" | custom-call | flops 17179869184 | bytes 104857600 | tf_op jit(solution)/shard_map/pallas_call | solution.py:878
  402.6 22.4 %fusion.43 = (bf16[1024,1,2048]{2,0,1:T(8,128)(2,1)S(1)}, bf16[1024,1,2048]{2,0,1:T(8,128)(2,1)S(1)}) fusion(f32[1024,2,2048]{2,0,1:T(8,128)} %fusion.13, bf16[1024,2048]{1,0:T(8,128)(2,1)} %bitcast.336, bf16[2048,2048]{1,0:T(8,128)(2,1)} %all-gather.5.cloned.1.call-done.map_ref), kind=kOutput, calls=%fused_computation.67 | convolution fusion | flops 8640266240 | bytes 37748736 | tf_op jit(solution)/shard_map/dot_general | solution.py:325
  428.5 21.5 %bitcast_convert_fusion = bf16[1024,2048]{1,0:T(8,128)(2,1)} fusion(bf16[2048,2,2048]{2,0,1:T(8,128)(2,1)} %all-gather.3.cloned.1.call-done, bf16[1024,1,2048]{2,0,1:T(8,128)(2,1)S(1)} %get-tuple-element.153, bf16[1024,1,2048]{2,0,1:T(8,128)(2,1)S(1)} %get-tuple-element.152), kind=kOutput, calls=%fused_computation.13 | convolution fusion | flops 17186160640 | bytes 29360128 | tf_op jit(solution)/shard_map/dot_general | solution.py:325
  450.0 34.8 %convolution_convert_fusion = bf16[2048,2,2048]{2,0,1:T(8,128)(2,1)} fusion(bf16[1024,1,2048]{2,0,1:T(8,128)(2,1)} %copy-done.107, bf16[1024,1,2048]{2,0,1:T(8,128)(2,1)} %copy-done.106, bf16[256,1024]{1,0:T(8,128)(2,1)S(1)} %collective-permute-done.9, bf16[256,1024]{1,0:T(8,128)(2,1)S(1)} %collective-permute-done.8, ...), kind=kOutput, calls=%fused_computation.2 | convolution fusion | flops 17226006528 | bytes 29360128 | tf_op jit(solution)/shard_map/dot_general | solution.py:325
  491.3 11.2 %collective-permute-done.18 = bf16[256,1024]{1,0:T(8,128)(2,1)S(1)} collective-permute-done((bf16[256,1024]{1,0:T(8,128)(2,1)S(1)}, bf16[256,1024]{1,0:T(8,128)(2,1)S(1)}, u32[]{:S(2)}, u32[]{:S(2)}) %collective-permute-start.18) | collective-permute-done | bytes 524320 | tf_op jit(solution)/shard_map/ppermute | solution.py:266
  506.0 5.4 copy.120.qkv_ref
  521.2 3.3 convert_add_fusion.5
  529.2 2.8 convolution_convert_fusion.4
  532.1 3.0 collective-permute-done.22
  548.1 13.7 %collective-permute-done.24.refs_2_ = bf16[256,2048]{1,0:T(8,128)(2,1)S(1)} collective-permute-done((bf16[256,2048]{1,0:T(8,128)(2,1)S(1)}, bf16[256,2048]{1,0:T(8,128)(2,1)S(1)}, u32[]{:S(2)}, u32[]{:S(2)}) %collective-permute-start.24) | collective-permute-done | bytes 1048608 | tf_op jit(solution)/shard_map/ppermute | solution.py:266
  570.8 4.3 fusion.58
  578.3 6.2 concatenate.178
  584.6 4.8 fusion.67.grad_ref
  589.5 17.0 %shard_map.224 = (bf16[1024,1024]{1,0:T(8,128)(2,1)S(1)}, f32[8,256]{1,0:T(8,128)S(1)}) custom-call(f32[1024,1024]{1,0:T(8,128)S(1)} %copy-done.4, bf16[1024,512]{1,0:T(8,128)(2,1)S(1)} %copy-done.8, bf16[1024,256]{1,0:T(8,128)(2,1)S(1)} %bitcast.270, bf16[1024,256]{1,0:T(8,128)(2,1)S(1)} %copy-done.14, bf16[1024,512]{1,0:T(8,128)(2,1)S(1)} %fusion.67.grad_ref, ...), custom_call_target="tpu_custom_call" | custom-call | flops 3019898880 | bytes 16777216 | tf_op jit(solution)/shard_map/pallas_call | solution.py:527
  611.7 2.8 copy-done.3
  614.6 8.9 %shard_map.225 = bf16[8,4,64,1152]{3,2,1,0:T(8,128)(2,1)S(1)} custom-call(bf16[1024,2048]{1,0:T(8,128)(2,1)S(1)} %copy-done.2, bf16[1024,1024]{1,0:T(8,128)(2,1)S(1)} %copy-done.6, bf16[2048,1536]{1,0:T(8,128)(2,1)S(1)} %bitcast.265, f32[2048,1]{1,0:T(8,128)S(1)} %get-tuple-element.186.refs_3_, f32[2048,128]{1,0:T(8,128)S(1)} %pad.35.refs_4_), custom_call_target="tpu_custom_call" | custom-call | flops 4294967296 | bytes 10485760 | tf_op jit(solution)/shard_map/pallas_call | solution.py:588
  629.4 7.0 shard_map.223
  636.4 6.1 convolution_convert_fusion.2
  642.5 3.9 collective-permute-done.27
  646.4 10.3 %collective-permute-done.29 = bf16[512,768]{1,0:T(8,128)(2,1)S(1)} collective-permute-done((bf16[512,768]{1,0:T(8,128)(2,1)S(1)}, bf16[512,768]{1,0:T(8,128)(2,1)S(1)}, u32[]{:S(2)}, u32[]{:S(2)}) %collective-permute-start.29) | collective-permute-done | bytes 786464 | tf_op jit(solution)/shard_map/ppermute | solution.py:266
  666.6 11.1 %collective-permute-done.31 = bf16[256,1024]{1,0:T(8,128)(2,1)S(1)} collective-permute-done((bf16[256,1024]{1,0:T(8,128)(2,1)S(1)}, bf16[256,1024]{1,0:T(8,128)(2,1)S(1)}, u32[]{:S(2)}, u32[]{:S(2)}) %collective-permute-start.31) | collective-permute-done | bytes 524320 | tf_op jit(solution)/shard_map/ppermute | solution.py:266
  680.0 7.1 collective-permute-done.30
  687.1 5.8 collective-permute-done.32
  694.1 3.1 maximum_convert_fusion
  705.3 3.5 copy.128
  717.3 37.2 %reduce-scatter.9.cloned.1.call-done = bf16[256,1152]{1,0:T(8,128)(2,1)} async-done(((bf16[2048,1152]{1,0:T(8,128)(2,1)}), bf16[256,1152]{1,0:T(8,128)(2,1)}) %reduce-scatter.9.cloned.1.call-update) | async-done | bytes 589840 | tf_op jit(solution)/shard_map/reduce_scatter | solution.py:1152
  760.1 3.3 collective-permute-done.38
  763.5 2.9 collective-permute-done.37
  (462 shorter events, 174.3 us)
Async XLA Ops:
  7.3 252.2 %all-gather.3.cloned.1.call-start = ((), (), s32[]{:S(2)}) async-start(), calls=%async_computation.4 | async-start | bytes 18874368 | tf_op jit(solution)/shard_map/all_gather | solution.py:997
  71.8 235.1 %all-gather.5.cloned.1.call-start = ((), (), s32[]{:S(2)}) async-start(), calls=%async_computation.5 | async-start | bytes 9437184 | tf_op jit(solution)/shard_map/all_gather | solution.py:998
  71.8 90.3 %collective-permute-start.12 = (bf16[64,512]{1,0:T(8,128)(2,1)S(1)}, bf16[64,512]{1,0:T(8,128)(2,1)S(1)}, u32[]{:S(2)}, u32[]{:S(2)}) collective-permute-start(bf16[64,512]{1,0:T(8,128)(2,1)S(1)} %copy-done.76), channel_id=1, source_target_pairs={{0,6},{1,7},{2,4},{3,5},{4,2},{5,3},{6,0},{7,1},{8,14},{9,15},{10,... | collective-permute-start | bytes 196616 | tf_op jit(solution)/shard_map/ppermute | solution.py:266
  72.8 92.6 %collective-permute-start.11 = (bf16[64,512]{1,0:T(8,128)(2,1)S(1)}, bf16[64,512]{1,0:T(8,128)(2,1)S(1)}, u32[]{:S(2)}, u32[]{:S(2)}) collective-permute-start(bf16[64,512]{1,0:T(8,128)(2,1)S(1)} %copy-done.76), channel_id=1, source_target_pairs={{0,4},{1,5},{2,6},{3,7},{4,0},{5,1},{6,2},{7,3},{8,12},{9,13},{10,... | collective-permute-start | bytes 196616 | tf_op jit(solution)/shard_map/ppermute | solution.py:266
  78.7 87.5 %collective-permute-start.10 = (bf16[64,512]{1,0:T(8,128)(2,1)S(1)}, bf16[64,512]{1,0:T(8,128)(2,1)S(1)}, u32[]{:S(2)}, u32[]{:S(2)}) collective-permute-start(bf16[64,512]{1,0:T(8,128)(2,1)S(1)} %copy-done.76), channel_id=1, source_target_pairs={{0,2},{1,3},{2,0},{3,1},{4,6},{5,7},{6,4},{7,5},{8,10},{9,11},{10,... | collective-permute-start | bytes 196616 | tf_op jit(solution)/shard_map/ppermute | solution.py:266
  78.7 581.5 %reduce-scatter.7.cloned.1.call-start = ((), (), s32[]{:S(2)}) async-start(), calls=%async_computation.7 | async-start | bytes 9437184 | tf_op jit(solution)/shard_map/reduce_scatter | solution.py:1060
  136.0 32.3 %collective-permute-start = (bf16[256,1024]{1,0:T(8,128)(2,1)}, bf16[256,1024]{1,0:T(8,128)(2,1)S(1)}, u32[]{:S(2)}, u32[]{:S(2)}) collective-permute-start(bf16[256,1024]{1,0:T(8,128)(2,1)} %get-tuple-element.168), channel_id=1, source_target_pairs={{0,8},{8,0},{16,24},{24,16},{1,9},{9,1},{17,25},{25,17},{2,10},{10... | collective-permute-start | bytes 1572872 | tf_op jit(solution)/shard_map/ppermute | solution.py:266
  137.1 24.1 %collective-permute-start.1 = (bf16[256,1024]{1,0:T(8,128)(2,1)S(1)}, bf16[256,1024]{1,0:T(8,128)(2,1)S(1)}, u32[]{:S(2)}, u32[]{:S(2)}) collective-permute-start(bf16[256,1024]{1,0:T(8,128)(2,1)S(1)} %get-tuple-element.171), channel_id=1, source_target_pairs={{0,8},{8,0},{16,24},{24,16},{1,9},{9,1},{17,25},{25,17},{2,10},{10... | collective-permute-start | bytes 1572872 | tf_op jit(solution)/shard_map/ppermute | solution.py:266
  161.2 15.2 %collective-permute-start.4 = (bf16[256,1024]{1,0:T(8,128)(2,1)}, bf16[256,1024]{1,0:T(8,128)(2,1)}, u32[]{:S(2)}, u32[]{:S(2)}) collective-permute-start(bf16[256,1024]{1,0:T(8,128)(2,1)} %get-tuple-element.169), channel_id=1, source_target_pairs={{0,16},{8,24},{16,0},{24,8},{1,17},{9,25},{17,1},{25,9},{2,18},{10... | collective-permute-start | bytes 1572872 | tf_op jit(solution)/shard_map/ppermute | solution.py:266
  162.2 31.1 %collective-permute-start.2 = (bf16[256,1024]{1,0:T(8,128)(2,1)S(1)}, bf16[256,1024]{1,0:T(8,128)(2,1)}, u32[]{:S(2)}, u32[]{:S(2)}) collective-permute-start(bf16[256,1024]{1,0:T(8,128)(2,1)S(1)} %add_convert_fusion.5), channel_id=1, source_target_pairs={{0,16},{8,24},{16,0},{24,8},{1,17},{9,25},{17,1},{25,9},{2,18},{10... | collective-permute-start | bytes 1572872 | tf_op jit(solution)/shard_map/ppermute | solution.py:266
  165.4 45.7 %collective-permute-start.3 = (bf16[256,1024]{1,0:T(8,128)(2,1)}, bf16[256,1024]{1,0:T(8,128)(2,1)}, u32[]{:S(2)}, u32[]{:S(2)}) collective-permute-start(bf16[256,1024]{1,0:T(8,128)(2,1)} %get-tuple-element.170), channel_id=1, source_target_pairs={{0,16},{8,24},{16,0},{24,8},{1,17},{9,25},{17,1},{25,9},{2,18},{10... | collective-permute-start | bytes 1572872 | tf_op jit(solution)/shard_map/ppermute | solution.py:266
  167.0 41.3 %collective-permute-start.14 = (bf16[4,64,512]{2,1,0:T(8,128)(2,1)}, bf16[4,64,512]{2,1,0:T(8,128)(2,1)}, u32[]{:S(2)}, u32[]{:S(2)}) collective-permute-start(bf16[4,64,512]{2,1,0:T(8,128)(2,1)} %get-tuple-element.223), channel_id=1, source_target_pairs={{0,16},{8,24},{16,0},{24,8},{1,17},{9,25},{17,1},{25,9},{2,18},{10... | collective-permute-start | bytes 786440 | tf_op jit(solution)/shard_map/ppermute | solution.py:266
  168.3 40.0 %collective-permute-start.13 = (bf16[4,64,512]{2,1,0:T(8,128)(2,1)}, bf16[4,64,512]{2,1,0:T(8,128)(2,1)}, u32[]{:S(2)}, u32[]{:S(2)}) collective-permute-start(bf16[4,64,512]{2,1,0:T(8,128)(2,1)} %get-tuple-element.223), channel_id=1, source_target_pairs={{0,8},{8,0},{16,24},{24,16},{1,9},{9,1},{17,25},{25,17},{2,10},{10... | collective-permute-start | bytes 786440 | tf_op jit(solution)/shard_map/ppermute | solution.py:266
  176.4 31.9 %collective-permute-start.15 = (bf16[4,64,512]{2,1,0:T(8,128)(2,1)}, bf16[4,64,512]{2,1,0:T(8,128)(2,1)}, u32[]{:S(2)}, u32[]{:S(2)}) collective-permute-start(bf16[4,64,512]{2,1,0:T(8,128)(2,1)} %get-tuple-element.223), channel_id=1, source_target_pairs={{0,24},{8,16},{16,8},{24,0},{1,25},{9,17},{17,9},{25,1},{2,26},{10... | collective-permute-start | bytes 786440 | tf_op jit(solution)/shard_map/ppermute | solution.py:266
  196.2 15.0 %collective-permute-start.5 = (bf16[256,1024]{1,0:T(8,128)(2,1)}, bf16[256,1024]{1,0:T(8,128)(2,1)}, u32[]{:S(2)}, u32[]{:S(2)}) collective-permute-start(bf16[256,1024]{1,0:T(8,128)(2,1)} %get-tuple-element.167), channel_id=1, source_target_pairs={{0,8},{8,0},{16,24},{24,16},{1,9},{9,1},{17,25},{25,17},{2,10},{10... | collective-permute-start | bytes 1572872 | tf_op jit(solution)/shard_map/ppermute | solution.py:266
  211.1 9.0 %collective-permute-start.16 = (bf16[4,4,64,512]{3,2,1,0:T(8,128)(2,1)}, bf16[4,4,64,512]{3,2,1,0:T(8,128)(2,1)}, u32[]{:S(2)}, u32[]{:S(2)}) collective-permute-start(bf16[4,4,64,512]{3,2,1,0:T(8,128)(2,1)} %get-tuple-element.187), channel_id=1, source_target_pairs={{0,1},{1,0},{2,3},{3,2},{4,5},{5,4},{6,7},{7,6},{8,9},{9,8},{10,11... | collective-permute-start | bytes 3145736 | tf_op jit(solution)/shard_map/ppermute | solution.py:266
  217.5 25.7 %collective-permute-start.7 = (bf16[256,2048]{1,0:T(8,128)(2,1)S(1)}, bf16[256,2048]{1,0:T(8,128)(2,1)}, u32[]{:S(2)}, u32[]{:S(2)}) collective-permute-start(bf16[256,2048]{1,0:T(8,128)(2,1)S(1)} %multiply_convert_fusion.4), channel_id=1, source_target_pairs={{0,16},{8,24},{16,0},{24,8},{1,17},{9,25},{17,1},{25,9},{2,18},{10... | collective-permute-start | bytes 3145736 | tf_op jit(solution)/shard_map/ppermute | solution.py:266
  218.0 27.2 %collective-permute-start.6 = (bf16[256,2048]{1,0:T(8,128)(2,1)S(1)}, bf16[256,2048]{1,0:T(8,128)(2,1)}, u32[]{:S(2)}, u32[]{:S(2)}) collective-permute-start(bf16[256,2048]{1,0:T(8,128)(2,1)S(1)} %multiply_convert_fusion.4), channel_id=1, source_target_pairs={{0,8},{8,0},{16,24},{24,16},{1,9},{9,1},{17,25},{25,17},{2,10},{10... | collective-permute-start | bytes 3145736 | tf_op jit(solution)/shard_map/ppermute | solution.py:266
  244.4 13.5 %collective-permute-start.9 = (bf16[256,1024]{1,0:T(8,128)(2,1)S(1)}, bf16[256,1024]{1,0:T(8,128)(2,1)S(1)}, u32[]{:S(2)}, u32[]{:S(2)}) collective-permute-start(bf16[256,1024]{1,0:T(8,128)(2,1)S(1)} %slice.467), channel_id=1, source_target_pairs={{0,8},{8,0},{16,24},{24,16},{1,9},{9,1},{17,25},{25,17},{2,10},{10... | collective-permute-start | bytes 1572872 | tf_op jit(solution)/shard_map/ppermute | solution.py:266
  246.3 13.2 %collective-permute-start.8 = (bf16[256,1024]{1,0:T(8,128)(2,1)S(1)}, bf16[256,1024]{1,0:T(8,128)(2,1)S(1)}, u32[]{:S(2)}, u32[]{:S(2)}) collective-permute-start(bf16[256,1024]{1,0:T(8,128)(2,1)S(1)} %slice.466), channel_id=1, source_target_pairs={{0,16},{8,24},{16,0},{24,8},{1,17},{9,25},{17,1},{25,9},{2,18},{10... | collective-permute-start | bytes 1572872 | tf_op jit(solution)/shard_map/ppermute | solution.py:266
  402.5 257.7 %reduce-scatter.5.cloned.1.call-start = ((), (), s32[]{:S(2)}) async-start(), calls=%async_computation.6 | async-start | bytes 18874368 | tf_op jit(solution)/shard_map/reduce_scatter | solution.py:1071
  484.9 223.9 %reduce-scatter.11.cloned.1.call-start = ((), (), s32[]{:S(2)}) async-start(), calls=%async_computation.9 | async-start | bytes 3244032 | tf_op jit(solution)/shard_map/reduce_scatter | solution.py:1150
  487.7 14.9 %collective-permute-start.18 = (bf16[256,1024]{1,0:T(8,128)(2,1)S(1)}, bf16[256,1024]{1,0:T(8,128)(2,1)S(1)}, u32[]{:S(2)}, u32[]{:S(2)}) collective-permute-start(bf16[256,1024]{1,0:T(8,128)(2,1)S(1)} %get-tuple-element.165), channel_id=1, source_target_pairs={{0,8},{8,0},{16,24},{24,16},{1,9},{9,1},{17,25},{25,17},{2,10},{10... | collective-permute-start | bytes 1572872 | tf_op jit(solution)/shard_map/ppermute | solution.py:266
  489.2 32.0 %collective-permute-start.17 = (bf16[256,1024]{1,0:T(8,128)(2,1)}, bf16[256,1024]{1,0:T(8,128)(2,1)}, u32[]{:S(2)}, u32[]{:S(2)}) collective-permute-start(bf16[256,1024]{1,0:T(8,128)(2,1)} %get-tuple-element.162), channel_id=1, source_target_pairs={{0,8},{8,0},{16,24},{24,16},{1,9},{9,1},{17,25},{25,17},{2,10},{10... | collective-permute-start | bytes 1572872 | tf_op jit(solution)/shard_map/ppermute | solution.py:266
  489.9 31.3 %collective-permute-start.21 = (bf16[256,1024]{1,0:T(8,128)(2,1)}, bf16[256,1024]{1,0:T(8,128)(2,1)}, u32[]{:S(2)}, u32[]{:S(2)}) collective-permute-start(bf16[256,1024]{1,0:T(8,128)(2,1)} %get-tuple-element.163), channel_id=1, source_target_pairs={{0,16},{8,24},{16,0},{24,8},{1,17},{9,25},{17,1},{25,9},{2,18},{10... | collective-permute-start | bytes 1572872 | tf_op jit(solution)/shard_map/ppermute | solution.py:266
  504.6 16.6 %collective-permute-start.19 = (bf16[256,1024]{1,0:T(8,128)(2,1)}, bf16[256,1024]{1,0:T(8,128)(2,1)}, u32[]{:S(2)}, u32[]{:S(2)}) collective-permute-start(bf16[256,1024]{1,0:T(8,128)(2,1)} %add_convert_fusion.3), channel_id=1, source_target_pairs={{0,16},{8,24},{16,0},{24,8},{1,17},{9,25},{17,1},{25,9},{2,18},{10... | collective-permute-start | bytes 1572872 | tf_op jit(solution)/shard_map/ppermute | solution.py:266
  520.6 11.5 %collective-permute-start.20 = (bf16[256,1024]{1,0:T(8,128)(2,1)}, bf16[256,1024]{1,0:T(8,128)(2,1)}, u32[]{:S(2)}, u32[]{:S(2)}) collective-permute-start(bf16[256,1024]{1,0:T(8,128)(2,1)} %get-tuple-element.164), channel_id=1, source_target_pairs={{0,16},{8,24},{16,0},{24,8},{1,17},{9,25},{17,1},{25,9},{2,18},{10... | collective-permute-start | bytes 1572872 | tf_op jit(solution)/shard_map/ppermute | solution.py:266
  524.5 10.5 %collective-permute-start.22 = (bf16[256,1024]{1,0:T(8,128)(2,1)}, bf16[256,1024]{1,0:T(8,128)(2,1)}, u32[]{:S(2)}, u32[]{:S(2)}) collective-permute-start(bf16[256,1024]{1,0:T(8,128)(2,1)} %get-tuple-element.161), channel_id=1, source_target_pairs={{0,8},{8,0},{16,24},{24,16},{1,9},{9,1},{17,25},{25,17},{2,10},{10... | collective-permute-start | bytes 1572872 | tf_op jit(solution)/shard_map/ppermute | solution.py:266
  540.9 20.8 %collective-permute-start.24 = (bf16[256,2048]{1,0:T(8,128)(2,1)S(1)}, bf16[256,2048]{1,0:T(8,128)(2,1)S(1)}, u32[]{:S(2)}, u32[]{:S(2)}) collective-permute-start(bf16[256,2048]{1,0:T(8,128)(2,1)S(1)} %get-tuple-element.71.refs_0_), channel_id=1, source_target_pairs={{0,16},{8,24},{16,0},{24,8},{1,17},{9,25},{17,1},{25,9},{2,18},{10... | collective-permute-start | bytes 3145736 | tf_op jit(solution)/shard_map/ppermute | solution.py:266
  542.7 23.4 %collective-permute-start.23 = (bf16[256,2048]{1,0:T(8,128)(2,1)S(1)}, bf16[256,2048]{1,0:T(8,128)(2,1)}, u32[]{:S(2)}, u32[]{:S(2)}) collective-permute-start(bf16[256,2048]{1,0:T(8,128)(2,1)S(1)} %get-tuple-element.71.refs_0_), channel_id=1, source_target_pairs={{0,8},{8,0},{16,24},{24,16},{1,9},{9,1},{17,25},{25,17},{2,10},{10... | collective-permute-start | bytes 3145736 | tf_op jit(solution)/shard_map/ppermute | solution.py:266
  562.6 21.9 %collective-permute-start.26 = (bf16[256,1024]{1,0:T(8,128)(2,1)}, bf16[256,1024]{1,0:T(8,128)(2,1)}, u32[]{:S(2)}, u32[]{:S(2)}) collective-permute-start(bf16[256,1024]{1,0:T(8,128)(2,1)} %slice.485), channel_id=1, source_target_pairs={{0,8},{8,0},{16,24},{24,16},{1,9},{9,1},{17,25},{25,17},{2,10},{10... | collective-permute-start | bytes 1572872 | tf_op jit(solution)/shard_map/ppermute | solution.py:266
  568.0 16.6 %collective-permute-start.25 = (bf16[256,1024]{1,0:T(8,128)(2,1)}, bf16[256,1024]{1,0:T(8,128)(2,1)}, u32[]{:S(2)}, u32[]{:S(2)}) collective-permute-start(bf16[256,1024]{1,0:T(8,128)(2,1)} %slice.484), channel_id=1, source_target_pairs={{0,16},{8,24},{16,0},{24,8},{1,17},{9,25},{17,1},{25,9},{2,18},{10... | collective-permute-start | bytes 1572872 | tf_op jit(solution)/shard_map/ppermute | solution.py:266
  625.9 20.5 %collective-permute-start.27 = (bf16[512,768]{1,0:T(8,128)(2,1)S(1)}, bf16[512,768]{1,0:T(8,128)(2,1)S(1)}, u32[]{:S(2)}, u32[]{:S(2)}) collective-permute-start(bf16[512,768]{1,0:T(8,128)(2,1)S(1)} %get-tuple-element.174), channel_id=1, source_target_pairs={{0,8},{8,0},{16,24},{24,16},{1,9},{9,1},{17,25},{25,17},{2,10},{10... | collective-permute-start | bytes 2359304 | tf_op jit(solution)/shard_map/ppermute | solution.py:266
  627.3 29.4 %collective-permute-start.29 = (bf16[512,768]{1,0:T(8,128)(2,1)S(1)}, bf16[512,768]{1,0:T(8,128)(2,1)S(1)}, u32[]{:S(2)}, u32[]{:S(2)}) collective-permute-start(bf16[512,768]{1,0:T(8,128)(2,1)S(1)} %get-tuple-element.175), channel_id=1, source_target_pairs={{0,24},{8,16},{16,8},{24,0},{1,25},{9,17},{17,9},{25,1},{2,26},{10... | collective-permute-start | bytes 2359304 | tf_op jit(solution)/shard_map/ppermute | solution.py:266
  629.0 29.1 %collective-permute-start.28 = (bf16[512,768]{1,0:T(8,128)(2,1)S(1)}, bf16[512,768]{1,0:T(8,128)(2,1)S(1)}, u32[]{:S(2)}, u32[]{:S(2)}) collective-permute-start(bf16[512,768]{1,0:T(8,128)(2,1)S(1)} %get-tuple-element.176), channel_id=1, source_target_pairs={{0,16},{8,24},{16,0},{24,8},{1,17},{9,25},{17,1},{25,9},{2,18},{10... | collective-permute-start | bytes 2359304 | tf_op jit(solution)/shard_map/ppermute | solution.py:266
  660.3 94.3 %reduce-scatter.9.cloned.1.call-start = ((), (), s32[]{:S(2)}) async-start(), calls=%async_computation.8 | async-start | bytes 5308416 | tf_op jit(solution)/shard_map/reduce_scatter | solution.py:1152
  662.8 14.9 %collective-permute-start.31 = (bf16[256,1024]{1,0:T(8,128)(2,1)S(1)}, bf16[256,1024]{1,0:T(8,128)(2,1)S(1)}, u32[]{:S(2)}, u32[]{:S(2)}) collective-permute-start(bf16[256,1024]{1,0:T(8,128)(2,1)S(1)} %get-tuple-element.159), channel_id=1, source_target_pairs={{0,8},{8,0},{16,24},{24,16},{1,9},{9,1},{17,25},{25,17},{2,10},{10... | collective-permute-start | bytes 1572872 | tf_op jit(solution)/shard_map/ppermute | solution.py:266
  663.6 23.5 %collective-permute-start.30 = (bf16[256,1024]{1,0:T(8,128)(2,1)S(1)}, bf16[256,1024]{1,0:T(8,128)(2,1)S(1)}, u32[]{:S(2)}, u32[]{:S(2)}) collective-permute-start(bf16[256,1024]{1,0:T(8,128)(2,1)S(1)} %get-tuple-element.156), channel_id=1, source_target_pairs={{0,8},{8,0},{16,24},{24,16},{1,9},{9,1},{17,25},{25,17},{2,10},{10... | collective-permute-start | bytes 1572872 | tf_op jit(solution)/shard_map/ppermute | solution.py:266
  664.9 22.2 %collective-permute-start.34 = (bf16[256,1024]{1,0:T(8,128)(2,1)S(1)}, bf16[256,1024]{1,0:T(8,128)(2,1)S(1)}, u32[]{:S(2)}, u32[]{:S(2)}) collective-permute-start(bf16[256,1024]{1,0:T(8,128)(2,1)S(1)} %get-tuple-element.157), channel_id=1, source_target_pairs={{0,16},{8,24},{16,0},{24,8},{1,17},{9,25},{17,1},{25,9},{2,18},{10... | collective-permute-start | bytes 1572872 | tf_op jit(solution)/shard_map/ppermute | solution.py:266
  677.9 14.9 %collective-permute-start.32 = (bf16[256,1024]{1,0:T(8,128)(2,1)S(1)}, bf16[256,1024]{1,0:T(8,128)(2,1)S(1)}, u32[]{:S(2)}, u32[]{:S(2)}) collective-permute-start(bf16[256,1024]{1,0:T(8,128)(2,1)S(1)} %add_convert_fusion.1), channel_id=1, source_target_pairs={{0,16},{8,24},{16,0},{24,8},{1,17},{9,25},{17,1},{25,9},{2,18},{10... | collective-permute-start | bytes 1572872 | tf_op jit(solution)/shard_map/ppermute | solution.py:266
  679.7 20.1 %collective-permute-start.33 = (bf16[256,1024]{1,0:T(8,128)(2,1)S(1)}, bf16[256,1024]{1,0:T(8,128)(2,1)S(1)}, u32[]{:S(2)}, u32[]{:S(2)}) collective-permute-start(bf16[256,1024]{1,0:T(8,128)(2,1)S(1)} %get-tuple-element.158), channel_id=1, source_target_pairs={{0,16},{8,24},{16,0},{24,8},{1,17},{9,25},{17,1},{25,9},{2,18},{10... | collective-permute-start | bytes 1572872 | tf_op jit(solution)/shard_map/ppermute | solution.py:266
  693.3 9.2 %collective-permute-start.35 = (bf16[256,1024]{1,0:T(8,128)(2,1)S(1)}, bf16[256,1024]{1,0:T(8,128)(2,1)S(1)}, u32[]{:S(2)}, u32[]{:S(2)}) collective-permute-start(bf16[256,1024]{1,0:T(8,128)(2,1)S(1)} %get-tuple-element.155), channel_id=1, source_target_pairs={{0,8},{8,0},{16,24},{24,16},{1,9},{9,1},{17,25},{25,17},{2,10},{10... | collective-permute-start | bytes 1572872 | tf_op jit(solution)/shard_map/ppermute | solution.py:266
  710.7 5.7 collective-permute-start.41
  712.4 4.3 collective-permute-start.40
  713.0 4.3 collective-permute-start.39
  755.7 7.7 collective-permute-start.38
  757.3 9.1 %collective-permute-start.37 = (bf16[64,1152]{1,0:T(8,128)(2,1)S(1)}, bf16[64,1152]{1,0:T(8,128)(2,1)S(1)}, u32[]{:S(2)}, u32[]{:S(2)}) collective-permute-start(bf16[64,1152]{1,0:T(8,128)(2,1)S(1)} %get-tuple-element.207), channel_id=1, source_target_pairs={{0,16},{8,24},{16,0},{24,8},{1,17},{9,25},{17,1},{25,9},{2,18},{10... | collective-permute-start | bytes 442376 | tf_op jit(solution)/shard_map/ppermute | solution.py:266
  758.7 7.7 collective-permute-start.36
  (112 other events, 1244.3 us)
Sparse Core Ops, SparseCore 0:
  71.9 152.7 all-gather.2
  226.3 80.5 all-gather.4
  402.7 86.9 reduce-scatter.6
  491.9 166.6 reduce-scatter.4
  660.7 34.7 reduce-scatter.10
  697.6 56.8 reduce-scatter.8

commit v5 on v4

--- a/solution.py
+++ b/solution.py
@@ -306,8 +306,7 @@
     return lax.dynamic_index_in_dim(v, index, axis, keepdims=False)
 
 
-def gather_everywhere(v, after, ranks, pairs):
-    v, after = lax.optimization_barrier((v, after))
+def gather_everywhere(v, ranks, pairs):
     index, rank = lax.axis_index("fsdp"), lax.axis_index("seq")
     pair, core = index // 2, index % 2
 
@@ -946,6 +945,281 @@
     )
 
 
+def finish_kernel(sizes, with_x, *refs):
+    ranks, pairs = sizes["seq"], sizes["pair"]
+    refs = list(refs)
+
+    def some(count):
+        head = refs[:count]
+        del refs[:count]
+        return head
+
+    owns = some(3)
+    x_ref, branch_ref, tokens_ref, base_ref, gain_ref = some(5) if with_x else [None] * 5
+    query_ref, key_ref, value_ref, out_ref, ple_ref, laurel_ref, small_ref = some(7)
+    (input_ref,) = some(1) if with_x else [None]
+    sums, from_left, from_right = some(3), some(3), some(3)
+    got_last, got_out = some(2)
+    if with_x:
+        got_x, got_y, relay_x, relay_y, far_x, far_y = some(6)
+    core_s, core_r, right_s, right_r, left_s, left_r, last_s, last_r, out_s, out_r = some(10)
+    if with_x:
+        x_s, x_r = some(2)
+
+    rank = lax.axis_index("seq")
+    fsdp_index = lax.axis_index("fsdp")
+    pair, core = fsdp_index // 2, fsdp_index % 2
+    sibling = (rank, pair * 2 + 1 - core)
+    on_seq = lambda k: (flip(rank, k, ranks), fsdp_index)
+    up = lambda v: v.astype(full)
+
+    def remote(source, target, send, recv, device):
+        return pltpu.make_async_remote_copy(
+            src_ref=source,
+            dst_ref=target,
+            send_sem=send,
+            recv_sem=recv,
+            device_id=device,
+            device_id_type=MESH,
+        )
+
+    barrier = pltpu.get_barrier_semaphore()
+    devices = [on_seq(k) for k in range(1, ranks)]
+    devices += [(rank, ((pair + i) % pairs) * 2 + core) for i in range(1, pairs)]
+    for device in devices + [sibling]:
+        pl.semaphore_signal(barrier, inc=1, device_id=device, device_id_type=MESH)
+    pl.semaphore_wait(barrier, len(devices) + 1)
+
+    sent = []
+
+    def go(copy):
+        copy.start()
+        sent.append(copy)
+        return copy
+
+    half_ranks = ranks // 2
+    pieces = [
+        (1, slice(0, ranks)),
+        (2, None),
+        (0, slice(0, half_ranks)),
+        (0, slice(half_ranks, ranks)),
+    ]
+    count = len(pieces)
+
+    def view(group, lead, piece):
+        number, rows = pieces[piece]
+        ref = group[number]
+        return ref.at[lead] if rows is None else ref.at[lead, rows]
+
+    order = [i // 2 if i % 2 else pairs - 1 - i // 2 for i in range(pairs)]
+
+    def swap(chip, piece):
+        slot = chip * count + piece
+        return remote(
+            view(owns, chip * 2 + 1 - core, piece),
+            view(sums, chip, piece),
+            core_s.at[slot],
+            core_r.at[slot],
+            sibling,
+        )
+
+    for chip in order:
+        for piece in range(count):
+            go(swap(chip, piece))
+    if with_x:
+        half = x_ref.shape[2] // 2
+        left, right = slice(0, half), slice(half, 2 * half)
+        by_x, by_y = on_seq(1), on_seq(2)
+        near = []
+        for slot, block, columns, target, device in (
+            (0, 3, left, got_x.at[0], by_x),
+            (1, 3, right, got_y.at[0], by_y),
+            (2, 1, left, got_x.at[1], by_x),
+            (3, 2, right, got_y.at[1], by_y),
+        ):
+            near.append(
+                go(remote(x_ref.at[block, :, columns], target, x_s.at[slot], x_r.at[slot], device))
+            )
+
+    def whole_chip(chip, piece):
+        target = view(sums, chip, piece)
+        remote(
+            target, target, core_s.at[0], core_r.at[chip * count + piece], sibling
+        ).wait_recv()
+        target[...] = (up(target[...]) + up(view(owns, chip * 2 + core, piece)[...])).astype(low)
+
+    def pass_right(t, piece):
+        slot = (t - 1) * count + piece
+        return remote(
+            view(sums, pair + pairs - t, piece),
+            view(from_left, t - 1, piece),
+            right_s.at[slot],
+            right_r.at[slot],
+            (rank, fsdp_index + 2),
+        )
+
+    def pass_left(t, piece):
+        slot = (t - 1) * count + piece
+        return remote(
+            view(sums, pair - (pairs - t), piece),
+            view(from_right, t - 1, piece),
+            left_s.at[slot],
+            left_r.at[slot],
+            (rank, fsdp_index - 2),
+        )
+
+    def add_left(t, piece, target):
+        got = view(from_left, t - 1, piece)
+        slot = (t - 1) * count + piece
+        remote(got, got, right_s.at[slot], right_r.at[slot], sibling).wait_recv()
+        target[...] = (up(target[...]) + up(got[...])).astype(low)
+
+    def add_right(t, piece, target):
+        got = view(from_right, t - 1, piece)
+        slot = (t - 1) * count + piece
+        remote(got, got, left_s.at[slot], left_r.at[slot], sibling).wait_recv()
+        target[...] = (up(target[...]) + up(got[...])).astype(low)
+
+    mirrored = pairs - 1 - pair
+    relays = []
+    for t in range(1, pairs):
+        for piece in range(count):
+
+            def to_right(t=t, piece=piece):
+                chip = pair + pairs - t
+                whole_chip(chip, piece)
+                if t > 1:
+                    pl.when(pair > 0)(lambda: add_left(t - 1, piece, view(sums, chip, piece)))
+                pass_right(t, piece).start()
+
+            def to_left(t=t, piece=piece):
+                chip = pair - (pairs - t)
+                whole_chip(chip, piece)
+                if t > 1:
+                    pl.when(mirrored > 0)(lambda: add_right(t - 1, piece, view(sums, chip, piece)))
+                pass_left(t, piece).start()
+
+            pl.when(t >= pair + 1)(to_right)
+            pl.when(t >= mirrored + 1)(to_left)
+        if with_x and t == 1:
+            near[0].wait_recv()
+            relay_y[...] = (up(x_ref[2, :, left]) + up(got_x[0])).astype(low)
+            relays.append(go(remote(relay_y, far_y, x_s.at[4], x_r.at[4], by_y)))
+            near[1].wait_recv()
+            relay_x[...] = (up(x_ref[1, :, right]) + up(got_y[0])).astype(low)
+            relays.append(go(remote(relay_x, far_x, x_s.at[5], x_r.at[5], by_x)))
+            for piece in range(count):
+                whole_chip(pair, piece)
+    if with_x:
+        for copy in near[2:] + relays:
+            copy.wait_recv()
+        mean = lambda v: jnp.mean(v, -1, keepdims=True)
+        step = x_ref.shape[1] // 2
+        for i in range(2):
+            at = slice(i * step, (i + 1) * step)
+            incoming = branch_ref[at, :] + jnp.concatenate(
+                [
+                    up(x_ref[0, at, left]) + up(got_x[1, at, :]) + up(far_y[at, :]),
+                    up(x_ref[0, at, right]) + up(got_y[1, at, :]) + up(far_x[at, :]),
+                ],
+                1,
+            )
+            v = up(tokens_ref[at, :])
+            inverse = lax.rsqrt(mean(v * v) + eps)
+            scaled = incoming * gain_ref[0:1, :]
+            input_ref[at, 0, :] = base_ref[at, :] * root_half + inverse * (
+                scaled - v * (inverse * inverse * mean(scaled * v))
+            )
+    else:
+        for piece in range(count):
+            whole_chip(pair, piece)
+
+    for piece in range(count):
+        target = view(sums, pair, piece)
+        pl.when(pair > 0)(lambda: add_left(pairs - 1, piece, target))
+        pl.when(mirrored > 0)(lambda: add_right(pairs - 1, piece, target))
+
+    last_sum, out_sum, rest_sum = [ref.at[pair] for ref in sums]
+    across = []
+    for k in range(1, ranks):
+        peer = flip(rank, k, ranks)
+        across.append(
+            (
+                go(remote(last_sum.at[peer], got_last.at[k], last_s.at[k], last_r.at[k], on_seq(k))),
+                go(remote(out_sum.at[peer], got_out.at[k], out_s.at[k], out_r.at[k], on_seq(k))),
+            )
+        )
+    ple_ref[...] = up(rest_sum[:, : 2 * PLE])
+    laurel_ref[...] = up(rest_sum[:, 2 * PLE : 2 * PLE + 2 * LR])
+    small_ref[...] = up(rest_sum[:, 2 * PLE + 2 * LR :])
+    key_ref[...] = jnp.zeros_like(key_ref)
+    value_ref[...] = jnp.zeros_like(value_ref)
+    q_width = out_sum.shape[2]
+    for k in range(ranks):
+        if k:
+            for copy in across[k - 1]:
+                copy.wait_recv()
+            last, out = up(got_last[k]), up(got_out[k])
+        else:
+            last, out = up(last_sum[rank]), up(out_sum[rank])
+        sender = flip(rank, k, ranks)
+        columns = pl.ds(pl.multiple_of(sender * q_width, q_width), q_width)
+        group = sender * (QUERY_HEADS // ranks) // (QUERY_HEADS // KEY_VALUE_HEADS)
+        head = pl.ds(pl.multiple_of(group * HEAD_DIM, HEAD_DIM), HEAD_DIM)
+        query_ref[:, columns] = last[:, :q_width]
+        out_ref[:, columns] = out
+        key_ref[:, head] += last[:, q_width : q_width + HEAD_DIM]
+        value_ref[:, head] += last[:, q_width + HEAD_DIM : q_width + 2 * HEAD_DIM]
+        small_ref[...] += last[:, q_width + 2 * HEAD_DIM :]
+
+    for t in range(1, pairs):
+        for piece in range(count):
+            pl.when(t >= pair + 1)(lambda t=t, piece=piece: pass_right(t, piece).wait_send())
+            pl.when(t >= mirrored + 1)(lambda t=t, piece=piece: pass_left(t, piece).wait_send())
+    for copy in sent:
+        copy.wait_send()
+
+
+def finish(sizes, last, out, rest, x=None):
+    ranks, pairs = sizes["seq"], sizes["pair"]
+    rows = last.shape[2]
+    arrays = [last, out, rest]
+    vmem = pl.BlockSpec(memory_space=pltpu.VMEM)
+    dma = lambda n: pltpu.SemaphoreType.DMA((n,))
+    width = KEY_VALUE_HEADS * HEAD_DIM
+    shapes = [
+        (rows, QUERY_HEADS * HEAD_DIM),
+        (rows, width),
+        (rows, width),
+        (rows, QUERY_HEADS * HEAD_DIM),
+        (rows, 2 * PLE),
+        (rows, 2 * LR),
+        (rows, rest.shape[-1] - 2 * PLE - 2 * LR),
+    ]
+    scratch = [pltpu.VMEM((pairs,) + v.shape[1:], low) for v in arrays]
+    scratch += [pltpu.VMEM((pairs - 1,) + v.shape[1:], low) for v in arrays] * 2
+    scratch += [pltpu.VMEM((ranks,) + v.shape[2:], low) for v in arrays[:2]]
+    if x is not None:
+        block, columns = x[0].shape[1], x[0].shape[2] // 2
+        shapes.append((block, 1, 2 * columns))
+        scratch += [pltpu.VMEM((2, block, columns), low)] * 2
+        scratch += [pltpu.VMEM((block, columns), low)] * 4
+    scratch += [dma(4 * pairs)] * 2 + [dma(4 * (pairs - 1))] * 4 + [dma(ranks)] * 4
+    if x is not None:
+        scratch += [dma(6)] * 2
+    operands = arrays + list(x or ())
+    return pl.pallas_call(
+        functools.partial(finish_kernel, sizes, x is not None),
+        out_shape=tuple(jax.ShapeDtypeStruct(v, full) for v in shapes),
+        in_specs=[vmem] * len(operands),
+        out_specs=(vmem,) * len(shapes),
+        scratch_shapes=scratch,
+        compiler_params=pltpu.CompilerParams(
+            collective_id=2, has_side_effects=True, vmem_limit_bytes=56 << 20
+        ),
+    )(*operands)
+
+
 def body(
     sizes,
     hidden_in,
@@ -997,7 +1271,6 @@
     in_maps = lax.all_gather(in_rows, "fsdp", axis=0, tiled=True)
     down_map = lax.all_gather(down_rows, "fsdp", axis=0, tiled=True)
     x_all = x_all.reshape(length, width)
-    ple = gather_everywhere(per_layer_maps, head_all, ranks, pairs)
     head_all = head_all.reshape(width, -1)
     rest_all = rest_all.reshape(width, -1)
     qkv_map, out_map = head_all[:, :-q_width], head_all[:, -q_width:]
@@ -1031,6 +1304,8 @@
     mixed = (tokens + attn_normed + (normed.astype(full) + laurel_normed)) * root_half
     h_normed_f, h_inverse = norm_rows(mixed, gain[3])
     h_blocks = gather_seq(h_normed_f.astype(low), ranks)
+    h_blocks, per_layer_maps = lax.optimization_barrier((h_blocks, per_layer_maps))
+    ple = gather_everywhere(per_layer_maps, ranks, pairs)
     gate_up = dot(whole_rows(h_blocks), in_maps, ((1,), (0,)))
     gate_part, up_part = gate_up[:, 0], gate_up[:, 1]
     hidden = (gelu_tanh(gate_part) * up_part).astype(low)
@@ -1065,8 +1340,13 @@
         [act_pull(grad_hidden * up_part)[0], grad_hidden * gate_act], 1
     ).astype(low)
     h_part = dot(grad_gate_up, in_maps, ((1, 2), (1, 2))).astype(low)
-    grad_h_normed = sum_seq(cut(h_part), ranks)
-    h_blocks, h_part = lax.optimization_barrier((h_blocks, h_part))
+    h_parts = cut(h_part)
+    if ranks == 4:
+        h_parts = [jnp.split(v, 2, axis=1) for v in h_parts]
+    h_blocks, h_parts = lax.optimization_barrier((h_blocks, h_parts))
+    if ranks == 4:
+        h_parts = [jnp.concatenate(v, 1) for v in h_parts]
+    grad_h_normed = sum_seq(h_parts, ranks)
     in_grad = dot(whole_rows(h_blocks), grad_gate_up, ((0,), (0,))).astype(low)
     in_sum = lax.psum_scatter(in_grad, "fsdp", scatter_dimension=0, tiled=True)
 
@@ -1128,76 +1408,35 @@
     head_scale_grad = jnp.pad(
         grad_head_scale.reshape(-1, head_rows, 2), ((0, 0), (0, rows - head_rows), (0, 0))
     ).reshape(width, 2)
-    late_grad = jnp.pad(head_scale_grad, ((0, 0), (1, 125)))
+    late_grad = jnp.pad(head_scale_grad, ((0, 0), (6, 120)))
     last = weight_grad(
         ranks, pairs * 2, [normed_all], grad_qkv, head_all, gain[0][:, None], late_grad
     )
     last, grad_qkv = lax.optimization_barrier((last, grad_qkv))
     x_part = mm_nt(grad_qkv, qkv_map).astype(low)
 
-    half = rows // 2
-    folded = jnp.concatenate(
-        [rest_own[:, :half, 2 * PLE :], rest_own[:, half:, 2 * PLE :]], 2
-    )
-    out_grad = out_grad.reshape(pairs * 2, ranks * rows, q_width)
-    first = [out_grad, rest_own[:, :, : 2 * PLE], folded]
-    if q_width != 2 * PLE:
-        first[0] = out_grad.reshape(pairs * 2, -1, 2 * PLE)
-    first = jnp.concatenate(first, 1)
-    first, last, x_part, in_sum, down_sum = lax.optimization_barrier(
-        (first, last, x_part, in_sum, down_sum)
-    )
-    first_sum = lax.psum_scatter(first, "fsdp", scatter_dimension=0, tiled=False).astype(low)
-    last = last.reshape(width, -1)
-    last_sum = lax.psum_scatter(last, "fsdp", scatter_dimension=0, tiled=True)
-    last_sum = last_sum.reshape(ranks, rows, -1)
-
-    out_end = first.shape[1] - rows - half
-    out_sum = first_sum[:out_end].reshape(ranks, rows, q_width)
-    ple_sum = first_sum[out_end : out_end + rows].astype(full)
-    folded = first_sum[out_end + rows :].astype(full)
-    other_sum = jnp.concatenate([folded[:, : folded.shape[1] // 2], folded[:, folded.shape[1] // 2 :]], 0)
-
-    def across(part):
-        got = jnp.stack(
-            [take(part, 0, rank)]
-            + [permute(take(part, 0, relative[k]), "seq", k) for k in range(1, ranks)]
-        )
-        return [take(got, 0, r ^ rank).astype(full) for r in range(ranks)]
-
-    out_ranks, last_ranks = across(out_sum), across(last_sum)
-
-    grad_x_normed = x_here + sum_seq(cut(x_part), ranks)
-    grad_tokens_norm = norm_back(tokens, x_inverse, gain[0], grad_x_normed)[0]
-    input_grad = grad_mixed * root_half + grad_tokens_norm
-
-    late_sum = sum(part[:, q_width + 2 * HEAD_DIM :] for part in last_ranks)
-    gain_sum = other_sum[:, 2 * LR : 2 * LR + 6]
-    gain_sum = jnp.concatenate([gain_sum[:, :1] + late_sum[:, :1], gain_sum[:, 1:]], 1)
-    scale_sum = late_sum[:head_rows, 1:3]
-
-    def of_kv(parts):
-        return jnp.concatenate(
-            [
-                sum(parts[r] for r in range(ranks) if kv_of[r] == j)
-                for j in range(KEY_VALUE_HEADS)
-            ],
-            1,
-        )
+    if ranks == 4:
+        gain_row = jnp.broadcast_to(gain[0], (8, width))
+        x_parts = x_part.reshape(ranks, block, width)
+        extras = (x_parts, x_here, x_local, grad_mixed, gain_row)
+        *sums, input_grad = finish(sizes, last, out_grad, rest_own, extras)
+    else:
+        sums = finish(sizes, last, out_grad, rest_own)
+        grad_x_normed = x_here + sum_seq(cut(x_part), ranks)
+        grad_tokens_norm = norm_back(tokens, x_inverse, gain[0], grad_x_normed)[0]
+        input_grad = grad_mixed * root_half + grad_tokens_norm
+    small_sum = sums[6]
 
     grad_mlp = jnp.concatenate([in_sum, down_sum[:, None]], 1).astype(full)
     lead = (block, 1, width)
     return (
         hidden_out.reshape(lead),
         input_grad.reshape(lead),
-        jnp.concatenate([part[:, :q_width] for part in last_ranks], 1),
-        of_kv([part[:, q_width : q_width + HEAD_DIM] for part in last_ranks]),
-        of_kv([part[:, q_width + HEAD_DIM : q_width + 2 * HEAD_DIM] for part in last_ranks]),
-        jnp.concatenate(out_ranks, 1),
-        other_sum[:, : 2 * LR],
-        ple_sum,
-        gain_sum,
-        scale_sum,
+        *sums[:4],
+        sums[5],
+        sums[4],
+        small_sum[:, :6],
+        small_sum[:head_rows, 6:8],
         grad_mlp,
     )
 

time: 791 us -> 772 us (0.976)
  Pallas kernels: 185 us -> 275 us
  waiting for transfers between devices: 220 us -> 158 us
  starting transfers between devices: 50.9 us -> 38.3 us
  other arithmetic: 77.1 us -> 65.4 us
  matrix products: 142 us -> 131 us
  local copies, waits for them, and re-layouts: 87.4 us -> 76.4 us
    pallas_call x0 -> x1, Pallas kernels: none -> 90.5 us  [finish(): pl.pallas_call(functools.partial(finish_kernel, sizes, x is not None), ou...]
    ppermute x42 -> x30, waiting for transfers between devices: 168 us -> 128 us  [permute(): return lax.ppermute(v, axis, [(i, i ^ offset) for i in range(size)])]
    reduce_scatter x2 -> x0, waiting for transfers between devices: 37.2 us -> none  [the longest x1 37.2 us: body(): last_sum = lax.psum_scatter(last, 'fsdp', scatter_dimension=0, tiled=True)]
    all_gather x1, waiting for transfers between devices: 13.8 us -> 29 us  [body(): down_map = lax.all_gather(down_rows, 'fsdp', axis=0, tiled=True)]
    ppermute x42 -> x30, starting transfers between devices: 50.5 us -> 38.2 us  [permute(): return lax.ppermute(v, axis, [(i, i ^ offset) for i in range(size)])]
    dot_general x16, matrix products: 137 us -> 126 us  [dot(): lax.dot_general(left, right, (over, ((), ())), preferred_element_type=full)]
    unnamed x232 -> x263, local copies, waits for them, and re-layouts: 30.5 us -> 24.7 us
  transfers between devices with their start and end apart: 48 -> 34, of which waited for: 25 -> 20; matrix products, arithmetic and copies ran while one was open for 35% -> 32% of each run, Pallas kernels for 4% -> 16%
where the time goes in v5:
time: 772 us; the launch traced here: 760 us
  Pallas kernels  275 us (36%)
  waiting for transfers between devices  158 us (20%)
  matrix products  131 us (17%)
  local copies, waits for them, and re-layouts  76.4 us (10%)
  other arithmetic  65.4 us (8%)
  starting transfers between devices  38.3 us (5%)
  between operations  15.9 us (2%)
    ppermute x30, waiting for transfers between devices, permute(): return lax.ppermute(v, axis, [(i, i ^ offset) for i in range(size)])  128 us
    dot_general x16, matrix products, dot(): lax.dot_general(left, right, (over, ((), ())), preferred_element_type=full)  126 us
    pallas_call x1, Pallas kernels, middle(): pl.pallas_call(functools.partial(middle_kernel, block, parts), out_shape=...  95.5 us
    pallas_call x1, Pallas kernels, finish(): pl.pallas_call(functools.partial(finish_kernel, sizes, x is not None), ou...  90.5 us
    pallas_call x1, Pallas kernels, gather_weights(): pl.pallas_call(functools.partial(gather_kernel, sizes), out_shape=(jax.Sh...  56.5 us
    ppermute x30, starting transfers between devices, permute(): return lax.ppermute(v, axis, [(i, i ^ offset) for i in range(size)])  38.2 us
    all_gather x1, waiting for transfers between devices, body(): down_map = lax.all_gather(down_rows, 'fsdp', axis=0, tiled=True)  29 us
    unnamed x263, local copies, waits for them, and re-layouts  24.7 us
  transfers between devices with their start and end apart: 34, of which 20 were waited for; matrix products, arithmetic and copies ran while one was open for 32% of the time, Pallas kernels for 16%

profile of v5, /device:TPU:20, one launch (start us, length us, event | category | flops | bytes accessed | tf_op | source)
XLA Modules:
  0.0 760.2 jit_solution(9991558022897028426)
XLA Ops:
  7.3 3.3 slice.201
  10.6 2.3 slice_bitcast_fusion.2
  15.3 56.5 %shard_map.221 = (bf16[4,4,2,64,1536]{4,3,2,1,0:T(8,128)(2,1)}, bf16[4,4,2,64,256]{4,3,2,1,0:T(8,128)(2,1)}, s32[4,8,256]{2,1,0:T(8,128)}, bf16[4,256,2048]{2,1,0:T(8,128)(2,1)}) custom-call(bf16[4,64,1536]{2,1,0:T(8,128)(2,1)} %pad_maximum_fusion.11.head_ref, bf16[64,256]{1,0:T(8,128)(2,1)} %fusion.85.rest_ref, s32[8,256]{1,0:T(8,128)} %pad.31.mark_ref, ...), custom_call_target="tpu_custom_call" | custom-call | tf_op jit(solution)/shard_map/pallas_call | solution.py:239
  73.7 3.1 slice_reduce_fusion.1
  81.2 4.6 fusion.45
  96.3 4.5 fusion.71
  100.8 2.6 copy.100
  108.4 8.0 %fusion.66 = (f32[1024,1,256]{2,0,1:T(8,128)}, bf16[1024,1,256]{2,0,1:T(8,128)(2,1)S(1)}, f32[1024,1,256]{2,0,1:T(8,128)}) fusion(f32[1024,1,128]{2,0,1:T(8,128)} %get-tuple-element.243, f32[1024,1,128]{2,0,1:T(8,128)} %get-tuple-element.222, f32[1024,1,128]{2,0,1:T(8,128)} %get-tuple-element.221, f32[256]{0:T(256)S(1)} %bitcast.272, ...), kind=kLoop, calls=%fused_computation.126 | loop fusion | flops 2097152 | bytes 5248000 | tf_op jit(solution)/shard_map/sin | solution.py:362
  116.4 2.3 fusion.54
  122.8 3.1 fusion.58
  126.0 4.5 convolution_convert_fusion.1
  133.6 12.1 %collective-permute-done.1 = bf16[256,1024]{1,0:T(8,128)(2,1)S(1)} collective-permute-done((bf16[256,1024]{1,0:T(8,128)(2,1)S(1)}, bf16[256,1024]{1,0:T(8,128)(2,1)S(1)}, u32[]{:S(2)}, u32[]{:S(2)}) %collective-permute-start.1) | collective-permute-done | bytes 524320 | tf_op jit(solution)/shard_map/ppermute | solution.py:266
  148.2 5.4 collective-permute-done
  153.7 7.1 collective-permute-done.2
  163.4 2.9 collective-permute-done.3
  166.4 6.1 collective-permute-done.5
  173.1 2.7 broadcast_multiply_fusion
  179.0 19.6 %collective-permute-done.6 = bf16[256,2048]{1,0:T(8,128)(2,1)S(1)} collective-permute-done((bf16[256,2048]{1,0:T(8,128)(2,1)S(1)}, bf16[256,2048]{1,0:T(8,128)(2,1)S(1)}, u32[]{:S(2)}, u32[]{:S(2)}) %collective-permute-start.6) | collective-permute-done | bytes 1048608 | tf_op jit(solution)/shard_map/ppermute | solution.py:266
  200.6 7.2 collective-permute-done.8
  208.9 8.4 %collective-permute-start.10 = (bf16[64,512]{1,0:T(8,128)(2,1)S(1)}, bf16[64,512]{1,0:T(8,128)(2,1)S(1)}, u32[]{:S(2)}, u32[]{:S(2)}) collective-permute-start(bf16[64,512]{1,0:T(8,128)(2,1)S(1)} %copy-done.85), channel_id=1, source_target_pairs={{0,2},{1,3},{2,0},{3,1},{4,6},{5,7},{6,4},{7,5},{8,10},{9,11},{10,... | collective-permute-start | bytes 196616 | tf_op jit(solution)/shard_map/ppermute | solution.py:266
  221.7 3.6 collective-permute-done.11
  231.2 3.7 collective-permute-done.13
  234.9 6.1 collective-permute-done.14
  242.1 2.6 collective-permute-done.16
  244.7 2.4 fusion.65
  249.5 25.0 %fusion.13 = f32[1024,2,2048]{2,0,1:T(8,128)} fusion(bf16[2048,2,2048]{2,0,1:T(8,128)(2,1)} %all-gather.3.cloned.1.call-done, bf16[256,1024]{1,0:T(8,128)(2,1)} %copy-done.117, bf16[256,1024]{1,0:T(8,128)(2,1)} %copy-done.116, bf16[256,2048]{1,0:T(8,128)(2,1)} %copy-done.64, bf16[256,2048]{1,0:T(8,128)(2,1)S(1)} %copy-done.63, ...), kind=kOutput, calls=%fused_computation.31 | convolution fusion | flops 17200840704 | bytes 37748736 | tf_op jit(solution)/shard_map/dot_general | solution.py:324
  274.5 8.9 %multiply_convert_fusion.1 = bf16[1024,2048]{1,0:T(8,128)(2,1)} fusion(f32[1024,2,2048]{2,0,1:T(8,128)} %fusion.13), kind=kLoop, calls=%fused_computation.19 | loop fusion | flops 20971520 | bytes 20971520 | tf_op jit(solution)/shard_map/convert_element_type | solution.py:1311
  283.4 29.0 %all-gather.5.cloned.1.call-done.map_ref = bf16[2048,2048]{1,0:T(8,128)(2,1)} async-done(((bf16[256,2048]{1,0:T(8,128)(2,1)}), bf16[2048,2048]{1,0:T(8,128)(2,1)}) %all-gather.5.cloned.1.call-update) | async-done | bytes 8388624 | tf_op jit(solution)/shard_map/all_gather | solution.py:1272
  312.4 95.5 %shard_map.222 = (bf16[4,256,2048]{2,1,0:T(8,128)(2,1)}, bf16[2048,2048]{1,0:T(8,128)(2,1)}, bf16[256,2048]{1,0:T(8,128)(2,1)}, bf16[256,2048]{1,0:T(8,128)(2,1)...) custom-call(bf16[4,256,2048]{2,1,0:T(8,128)(2,1)} %bitcast.223, ...), custom_call_target="tpu_custom_call" | custom-call | flops 17179869184 | bytes 104857600 | tf_op jit(solution)/shard_map/pallas_call | solution.py:877
  408.0 22.2 %fusion.43 = (bf16[1024,1,2048]{2,0,1:T(8,128)(2,1)S(1)}, bf16[1024,1,2048]{2,0,1:T(8,128)(2,1)S(1)}) fusion(f32[1024,2,2048]{2,0,1:T(8,128)} %fusion.13, bf16[1024,2048]{1,0:T(8,128)(2,1)} %bitcast.277, bf16[2048,2048]{1,0:T(8,128)(2,1)} %all-gather.5.cloned.1.call-done.map_ref), kind=kOutput, calls=%fused_computation.62 | convolution fusion | flops 8640266240 | bytes 37748736 | tf_op jit(solution)/shard_map/dot_general | solution.py:324
  430.2 23.3 %bitcast_convert_fusion = bf16[1024,2048]{1,0:T(8,128)(2,1)S(1)} fusion(bf16[2048,2,2048]{2,0,1:T(8,128)(2,1)} %all-gather.3.cloned.1.call-done, bf16[1024,1,2048]{2,0,1:T(8,128)(2,1)S(1)} %get-tuple-element.185, bf16[1024,1,2048]{2,0,1:T(8,128)(2,1)S(1)} %get-tuple-element.184), kind=kOutput, calls=%fused_computation.13 | convolution fusion | flops 17186160640 | bytes 29360128 | tf_op jit(solution)/shard_map/dot_general | solution.py:324
  455.6 24.3 %convolution_convert_fusion = bf16[2048,2,2048]{2,0,1:T(8,128)(2,1)} fusion(bf16[1024,1,2048]{2,0,1:T(8,128)(2,1)} %copy-done.119, bf16[1024,1,2048]{2,0,1:T(8,128)(2,1)} %copy-done.118, bf16[256,1024]{1,0:T(8,128)(2,1)} %copy-done.117, bf16[256,1024]{1,0:T(8,128)(2,1)} %copy-done.116, bf16[256,2048]{1,0:T(8,128)(2,1)} %copy-done.64, ...), kind=kOutput, calls=%fused_computation.2 | convolution fusion | flops 17226006528 | bytes 29360128 | tf_op jit(solution)/shard_map/dot_general | solution.py:324
  488.5 9.1 %collective-permute-done.18 = bf16[256,1024]{1,0:T(8,128)(2,1)S(1)} collective-permute-done((bf16[256,1024]{1,0:T(8,128)(2,1)}, bf16[256,1024]{1,0:T(8,128)(2,1)S(1)}, u32[]{:S(2)}, u32[]{:S(2)}) %collective-permute-start.18) | collective-permute-done | bytes 524320 | tf_op jit(solution)/shard_map/ppermute | solution.py:266
  503.6 6.1 copy.109.qkv_ref
  514.8 2.7 copy.121
  517.5 3.2 collective-permute-done.19
  534.0 17.6 %collective-permute-done.23.refs_1_ = bf16[256,2048]{1,0:T(8,128)(2,1)S(1)} collective-permute-done((bf16[256,2048]{1,0:T(8,128)(2,1)S(1)}, bf16[256,2048]{1,0:T(8,128)(2,1)S(1)}, u32[]{:S(2)}, u32[]{:S(2)}) %collective-permute-start.23) | collective-permute-done | bytes 1048608 | tf_op jit(solution)/shard_map/ppermute | solution.py:266
  567.1 6.2 concatenate.148
  573.4 6.5 fusion.59.grad_ref
  580.0 16.7 %shard_map.223 = (bf16[1024,1024]{1,0:T(8,128)(2,1)S(1)}, f32[8,256]{1,0:T(8,128)S(1)}) custom-call(f32[1024,1024]{1,0:T(8,128)S(1)} %copy-done.4, bf16[1024,512]{1,0:T(8,128)(2,1)S(1)} %copy-done.8, bf16[1024,256]{1,0:T(8,128)(2,1)S(1)} %bitcast.214, bf16[1024,256]{1,0:T(8,128)(2,1)S(1)} %copy-done.13, bf16[1024,512]{1,0:T(8,128)(2,1)S(1)} %fusion.59.grad_ref, ...), custom_call_target="tpu_custom_call" | custom-call | flops 3019898880 | bytes 16777216 | tf_op jit(solution)/shard_map/pallas_call | solution.py:526
  599.6 2.9 copy-done.3
  602.5 8.9 %shard_map.224.refs_0_ = bf16[8,4,64,1152]{3,2,1,0:T(8,128)(2,1)S(1)} custom-call(bf16[1024,2048]{1,0:T(8,128)(2,1)S(1)} %copy-done.2, bf16[1024,1024]{1,0:T(8,128)(2,1)S(1)} %get-tuple-element.109.refs_1_, bf16[2048,1536]{1,0:T(8,128)(2,1)S(1)} %bitcast.210, f32[2048,1]{1,0:T(8,128)S(1)} %get-tuple-element.214.refs_3_, f32[2048,128]{1,0:T(8,128)S(1)} %pad.35.refs_4_), custom_call_target="tpu_custom_call" | custom-call | flops 4294967296 | bytes 10485760 | tf_op jit(solution)/shard_map/pallas_call | solution.py:587
  615.2 6.8 shard_map.225.refs_1_
  623.4 6.2 convolution_convert_fusion.2
  629.5 2.6 collective-permute-done.27
  632.2 14.4 %collective-permute-done.28 = bf16[512,768]{1,0:T(8,128)(2,1)S(1)} collective-permute-done((bf16[512,768]{1,0:T(8,128)(2,1)S(1)}, bf16[512,768]{1,0:T(8,128)(2,1)S(1)}, u32[]{:S(2)}, u32[]{:S(2)}) %collective-permute-start.28) | collective-permute-done | bytes 786464 | tf_op jit(solution)/shard_map/ppermute | solution.py:266
  648.5 90.5 %shard_map.226 = (f32[64,2048]{1,0:T(8,128)}, f32[64,512]{1,0:T(8,128)}, f32[64,512]{1,0:T(8,128)}, f32[64,2048]{1,0:T(8,128)}, f32[64,512]{1,0:T(8,128)}, /*ind...) custom-call(bf16[8,4,64,1152]{3,2,1,0:T(8,128)(2,1)} %copy-done, bf16[8,4,64,512]{3,2,1,0:T(8,128)(2,1)} %copy-done.5, ...), custom_call_target="tpu_custom_call" | custom-call | tf_op jit(solution)/shard_map/pallas_call | solution.py:1211
  741.8 5.2 maximum_convert_fusion
  (429 shorter events, 125.9 us)
Async XLA Ops:
  7.3 241.8 %all-gather.3.cloned.1.call-start = ((), (), s32[]{:S(2)}) async-start(), calls=%async_computation.2 | async-start | bytes 18874368 | tf_op jit(solution)/shard_map/all_gather | solution.py:1271
  71.8 240.7 %all-gather.5.cloned.1.call-start = ((), (), s32[]{:S(2)}) async-start(), calls=%async_computation.3 | async-start | bytes 9437184 | tf_op jit(solution)/shard_map/all_gather | solution.py:1272
  72.5 669.3 %reduce-scatter.5.cloned.1.call-start = ((), (), s32[]{:S(2)}) async-start(), calls=%async_computation.5 | async-start | bytes 9437184 | tf_op jit(solution)/shard_map/reduce_scatter | solution.py:1335
  76.8 96.3 %copy-start.76 = (f32[2048]{0:T(1024)}, f32[2048]{0:T(1024)S(1)}, u32[]{:S(2)}) copy-start(f32[2048]{0:T(1024)S(1)} %get-tuple-element.176) | copy-start | bytes 24580
  76.8 96.3 %copy-start.78 = (f32[2048]{0:T(1024)}, f32[2048]{0:T(1024)S(1)}, u32[]{:S(2)}) copy-start(f32[2048]{0:T(1024)S(1)} %get-tuple-element.179) | copy-start | bytes 24580
  76.8 96.2 %copy-start.80 = (f32[2048]{0:T(1024)}, f32[2048]{0:T(1024)S(1)}, u32[]{:S(2)}) copy-start(f32[2048]{0:T(1024)S(1)} %get-tuple-element.180) | copy-start | bytes 24580
  76.8 100.1 %copy-start.67 = (f32[2048]{0:T(1024)}, f32[2048]{0:T(1024)S(1)}, u32[]{:S(2)}) copy-start(f32[2048]{0:T(1024)S(1)} %get-tuple-element.178) | copy-start | bytes 24580
  130.7 31.5 %copy-start.46 = (bf16[4,4,2,64,256]{4,3,2,1,0:T(8,128)(2,1)S(1)}, bf16[4,4,2,64,256]{4,3,2,1,0:T(8,128)(2,1)}, u32[]{:S(2)}) copy-start(bf16[4,4,2,64,256]{4,3,2,1,0:T(8,128)(2,1)} %get-tuple-element.68) | copy-start | bytes 3145732
  130.7 14.9 %collective-permute-start.1 = (bf16[256,1024]{1,0:T(8,128)(2,1)S(1)}, bf16[256,1024]{1,0:T(8,128)(2,1)S(1)}, u32[]{:S(2)}, u32[]{:S(2)}) collective-permute-start(bf16[256,1024]{1,0:T(8,128)(2,1)S(1)} %get-tuple-element.199), channel_id=1, source_target_pairs={{0,8},{8,0},{16,24},{24,16},{1,9},{9,1},{17,25},{25,17},{2,10},{10... | collective-permute-start | bytes 1572872 | tf_op jit(solution)/shard_map/ppermute | solution.py:266
  131.7 22.0 %collective-permute-start = (bf16[256,1024]{1,0:T(8,128)(2,1)S(1)}, bf16[256,1024]{1,0:T(8,128)(2,1)S(1)}, u32[]{:S(2)}, u32[]{:S(2)}) collective-permute-start(bf16[256,1024]{1,0:T(8,128)(2,1)S(1)} %get-tuple-element.196), channel_id=1, source_target_pairs={{0,8},{8,0},{16,24},{24,16},{1,9},{9,1},{17,25},{25,17},{2,10},{10... | collective-permute-start | bytes 1572872 | tf_op jit(solution)/shard_map/ppermute | solution.py:266
  132.8 20.9 %collective-permute-start.4 = (bf16[256,1024]{1,0:T(8,128)(2,1)S(1)}, bf16[256,1024]{1,0:T(8,128)(2,1)S(1)}, u32[]{:S(2)}, u32[]{:S(2)}) collective-permute-start(bf16[256,1024]{1,0:T(8,128)(2,1)S(1)} %get-tuple-element.197), channel_id=1, source_target_pairs={{0,16},{8,24},{16,0},{24,8},{1,17},{9,25},{17,1},{25,9},{2,18},{10... | collective-permute-start | bytes 1572872 | tf_op jit(solution)/shard_map/ppermute | solution.py:266
  145.8 14.9 %collective-permute-start.2 = (bf16[256,1024]{1,0:T(8,128)(2,1)S(1)}, bf16[256,1024]{1,0:T(8,128)(2,1)S(1)}, u32[]{:S(2)}, u32[]{:S(2)}) collective-permute-start(bf16[256,1024]{1,0:T(8,128)(2,1)S(1)} %add_convert_fusion.3), channel_id=1, source_target_pairs={{0,16},{8,24},{16,0},{24,8},{1,17},{9,25},{17,1},{25,9},{2,18},{10... | collective-permute-start | bytes 1572872 | tf_op jit(solution)/shard_map/ppermute | solution.py:266
  146.7 19.7 %collective-permute-start.3 = (bf16[256,1024]{1,0:T(8,128)(2,1)S(1)}, bf16[256,1024]{1,0:T(8,128)(2,1)S(1)}, u32[]{:S(2)}, u32[]{:S(2)}) collective-permute-start(bf16[256,1024]{1,0:T(8,128)(2,1)S(1)} %get-tuple-element.198), channel_id=1, source_target_pairs={{0,16},{8,24},{16,0},{24,8},{1,17},{9,25},{17,1},{25,9},{2,18},{10... | collective-permute-start | bytes 1572872 | tf_op jit(solution)/shard_map/ppermute | solution.py:266
  148.2 24.8 %copy-start.110 = (f32[256]{0:T(256)}, f32[256]{0:T(256)S(1)}, u32[]{:S(2)}) copy-start(f32[256]{0:T(256)S(1)} %add_rsqrt_fusion.5) | copy-start | bytes 3076
  161.2 11.3 %collective-permute-start.5 = (bf16[256,1024]{1,0:T(8,128)(2,1)S(1)}, bf16[256,1024]{1,0:T(8,128)(2,1)S(1)}, u32[]{:S(2)}, u32[]{:S(2)}) collective-permute-start(bf16[256,1024]{1,0:T(8,128)(2,1)S(1)} %get-tuple-element.195), channel_id=1, source_target_pairs={{0,8},{8,0},{16,24},{24,16},{1,9},{9,1},{17,25},{25,17},{2,10},{10... | collective-permute-start | bytes 1572872 | tf_op jit(solution)/shard_map/ppermute | solution.py:266
  175.8 33.1 %copy-start.85 = (bf16[64,512]{1,0:T(8,128)(2,1)S(1)}, bf16[64,512]{1,0:T(8,128)(2,1)}, u32[]{:S(2)}) copy-start(bf16[64,512]{1,0:T(8,128)(2,1)} %param.24) | copy-start | bytes 196612
  176.9 64.2 %copy-start.108 = (f32[256]{0:T(256)}, f32[256]{0:T(256)S(1)}, u32[]{:S(2)}) copy-start(f32[256]{0:T(256)S(1)} %get-tuple-element.248) | copy-start | bytes 3076
  177.4 21.2 %collective-permute-start.6 = (bf16[256,2048]{1,0:T(8,128)(2,1)S(1)}, bf16[256,2048]{1,0:T(8,128)(2,1)S(1)}, u32[]{:S(2)}, u32[]{:S(2)}) collective-permute-start(bf16[256,2048]{1,0:T(8,128)(2,1)S(1)} %multiply_convert_fusion.4), channel_id=1, source_target_pairs={{0,8},{8,0},{16,24},{24,16},{1,9},{9,1},{17,25},{25,17},{2,10},{10... | collective-permute-start | bytes 3145736 | tf_op jit(solution)/shard_map/ppermute | solution.py:266
  178.3 21.2 %collective-permute-start.7 = (bf16[256,2048]{1,0:T(8,128)(2,1)S(1)}, bf16[256,2048]{1,0:T(8,128)(2,1)S(1)}, u32[]{:S(2)}, u32[]{:S(2)}) collective-permute-start(bf16[256,2048]{1,0:T(8,128)(2,1)S(1)} %multiply_convert_fusion.4), channel_id=1, source_target_pairs={{0,16},{8,24},{16,0},{24,8},{1,17},{9,25},{17,1},{25,9},{2,18},{10... | collective-permute-start | bytes 3145736 | tf_op jit(solution)/shard_map/ppermute | solution.py:266
  198.6 9.2 %collective-permute-start.8 = (bf16[256,1024]{1,0:T(8,128)(2,1)S(1)}, bf16[256,1024]{1,0:T(8,128)(2,1)S(1)}, u32[]{:S(2)}, u32[]{:S(2)}) collective-permute-start(bf16[256,1024]{1,0:T(8,128)(2,1)S(1)} %slice.276), channel_id=1, source_target_pairs={{0,16},{8,24},{16,0},{24,8},{1,17},{9,25},{17,1},{25,9},{2,18},{10... | collective-permute-start | bytes 1572872 | tf_op jit(solution)/shard_map/ppermute | solution.py:266
  199.6 9.2 %collective-permute-start.9 = (bf16[256,1024]{1,0:T(8,128)(2,1)S(1)}, bf16[256,1024]{1,0:T(8,128)(2,1)S(1)}, u32[]{:S(2)}, u32[]{:S(2)}) collective-permute-start(bf16[256,1024]{1,0:T(8,128)(2,1)S(1)} %slice.277), channel_id=1, source_target_pairs={{0,8},{8,0},{16,24},{24,16},{1,9},{9,1},{17,25},{25,17},{2,10},{10... | collective-permute-start | bytes 1572872 | tf_op jit(solution)/shard_map/ppermute | solution.py:266
  208.9 12.7 %collective-permute-start.10 = (bf16[64,512]{1,0:T(8,128)(2,1)S(1)}, bf16[64,512]{1,0:T(8,128)(2,1)S(1)}, u32[]{:S(2)}, u32[]{:S(2)}) collective-permute-start(bf16[64,512]{1,0:T(8,128)(2,1)S(1)} %copy-done.85), channel_id=1, source_target_pairs={{0,2},{1,3},{2,0},{3,1},{4,6},{5,7},{6,4},{7,5},{8,10},{9,11},{10,... | collective-permute-start | bytes 196616 | tf_op jit(solution)/shard_map/ppermute | solution.py:266
  217.3 7.9 %collective-permute-start.11 = (bf16[64,512]{1,0:T(8,128)(2,1)S(1)}, bf16[64,512]{1,0:T(8,128)(2,1)S(1)}, u32[]{:S(2)}, u32[]{:S(2)}) collective-permute-start(bf16[64,512]{1,0:T(8,128)(2,1)S(1)} %copy-done.85), channel_id=1, source_target_pairs={{0,4},{1,5},{2,6},{3,7},{4,0},{5,1},{6,2},{7,3},{8,12},{9,13},{10,... | collective-permute-start | bytes 196616 | tf_op jit(solution)/shard_map/ppermute | solution.py:266
  219.3 8.2 %collective-permute-start.12 = (bf16[64,512]{1,0:T(8,128)(2,1)S(1)}, bf16[64,512]{1,0:T(8,128)(2,1)S(1)}, u32[]{:S(2)}, u32[]{:S(2)}) collective-permute-start(bf16[64,512]{1,0:T(8,128)(2,1)S(1)} %copy-done.85), channel_id=1, source_target_pairs={{0,6},{1,7},{2,4},{3,5},{4,2},{5,3},{6,0},{7,1},{8,14},{9,15},{10,... | collective-permute-start | bytes 196616 | tf_op jit(solution)/shard_map/ppermute | solution.py:266
  227.6 7.2 collective-permute-start.13
  229.1 11.8 %collective-permute-start.14 = (bf16[4,64,512]{2,1,0:T(8,128)(2,1)S(1)}, bf16[4,64,512]{2,1,0:T(8,128)(2,1)S(1)}, u32[]{:S(2)}, u32[]{:S(2)}) collective-permute-start(bf16[4,64,512]{2,1,0:T(8,128)(2,1)S(1)} %get-tuple-element.229), channel_id=1, source_target_pairs={{0,16},{8,24},{16,0},{24,8},{1,17},{9,25},{17,1},{25,9},{2,18},{10... | collective-permute-start | bytes 786440 | tf_op jit(solution)/shard_map/ppermute | solution.py:266
  229.7 11.3 %collective-permute-start.15 = (bf16[4,64,512]{2,1,0:T(8,128)(2,1)S(1)}, bf16[4,64,512]{2,1,0:T(8,128)(2,1)S(1)}, u32[]{:S(2)}, u32[]{:S(2)}) collective-permute-start(bf16[4,64,512]{2,1,0:T(8,128)(2,1)S(1)} %get-tuple-element.229), channel_id=1, source_target_pairs={{0,24},{8,16},{16,8},{24,0},{1,25},{9,17},{17,9},{25,1},{2,26},{10... | collective-permute-start | bytes 786440 | tf_op jit(solution)/shard_map/ppermute | solution.py:266
  241.4 3.4 collective-permute-start.16
  408.0 333.8 %reduce-scatter.3.cloned.1.call-start = ((), (), s32[]{:S(2)}) async-start(), calls=%async_computation.4 | async-start | bytes 18874368 | tf_op jit(solution)/shard_map/reduce_scatter | solution.py:1351
  482.6 15.1 %collective-permute-start.18 = (bf16[256,1024]{1,0:T(8,128)(2,1)}, bf16[256,1024]{1,0:T(8,128)(2,1)S(1)}, u32[]{:S(2)}, u32[]{:S(2)}) collective-permute-start(bf16[256,1024]{1,0:T(8,128)(2,1)} %get-tuple-element.94), channel_id=1, source_target_pairs={{0,8},{8,0},{16,24},{24,16},{1,9},{9,1},{17,25},{25,17},{2,10},{10... | collective-permute-start | bytes 1572872 | tf_op jit(solution)/shard_map/ppermute | solution.py:266
  484.9 16.2 %collective-permute-start.21 = (bf16[256,1024]{1,0:T(8,128)(2,1)}, bf16[256,1024]{1,0:T(8,128)(2,1)S(1)}, u32[]{:S(2)}, u32[]{:S(2)}) collective-permute-start(bf16[256,1024]{1,0:T(8,128)(2,1)} %get-tuple-element.98), channel_id=1, source_target_pairs={{0,16},{8,24},{16,0},{24,8},{1,17},{9,25},{17,1},{25,9},{2,18},{10... | collective-permute-start | bytes 1572872 | tf_op jit(solution)/shard_map/ppermute | solution.py:266
  487.4 30.1 %collective-permute-start.17 = (bf16[256,1024]{1,0:T(8,128)(2,1)}, bf16[256,1024]{1,0:T(8,128)(2,1)}, u32[]{:S(2)}, u32[]{:S(2)}) collective-permute-start(bf16[256,1024]{1,0:T(8,128)(2,1)} %get-tuple-element.92), channel_id=1, source_target_pairs={{0,8},{8,0},{16,24},{24,16},{1,9},{9,1},{17,25},{25,17},{2,10},{10... | collective-permute-start | bytes 1572872 | tf_op jit(solution)/shard_map/ppermute | solution.py:266
  488.0 34.4 %collective-permute-start.20 = (bf16[256,1024]{1,0:T(8,128)(2,1)}, bf16[256,1024]{1,0:T(8,128)(2,1)}, u32[]{:S(2)}, u32[]{:S(2)}) collective-permute-start(bf16[256,1024]{1,0:T(8,128)(2,1)} %get-tuple-element.96), channel_id=1, source_target_pairs={{0,16},{8,24},{16,0},{24,8},{1,17},{9,25},{17,1},{25,9},{2,18},{10... | collective-permute-start | bytes 1572872 | tf_op jit(solution)/shard_map/ppermute | solution.py:266
  499.7 21.1 %collective-permute-start.19 = (bf16[256,1024]{1,0:T(8,128)(2,1)}, bf16[256,1024]{1,0:T(8,128)(2,1)}, u32[]{:S(2)}, u32[]{:S(2)}) collective-permute-start(bf16[256,1024]{1,0:T(8,128)(2,1)} %add_convert_fusion.1), channel_id=1, source_target_pairs={{0,16},{8,24},{16,0},{24,8},{1,17},{9,25},{17,1},{25,9},{2,18},{10... | collective-permute-start | bytes 1572872 | tf_op jit(solution)/shard_map/ppermute | solution.py:266
  502.2 20.2 %collective-permute-start.22 = (bf16[256,1024]{1,0:T(8,128)(2,1)}, bf16[256,1024]{1,0:T(8,128)(2,1)}, u32[]{:S(2)}, u32[]{:S(2)}) collective-permute-start(bf16[256,1024]{1,0:T(8,128)(2,1)} %add_convert_fusion), channel_id=1, source_target_pairs={{0,8},{8,0},{16,24},{24,16},{1,9},{9,1},{17,25},{25,17},{2,10},{10... | collective-permute-start | bytes 1572872 | tf_op jit(solution)/shard_map/ppermute | solution.py:266
  526.9 29.7 %copy-start.30 = (f32[256,2048]{1,0:T(8,128)}, f32[256,2048]{1,0:T(8,128)S(1)}, u32[]{:S(2)}) copy-start(f32[256,2048]{1,0:T(8,128)S(1)} %get-tuple-element.181.refs_6_) | copy-start | bytes 6291460
  528.1 30.6 %copy-start.41 = (bf16[256,2048]{1,0:T(8,128)(2,1)}, bf16[256,2048]{1,0:T(8,128)(2,1)S(1)}, u32[]{:S(2)}) copy-start(bf16[256,2048]{1,0:T(8,128)(2,1)S(1)} %get-tuple-element.206) | copy-start | bytes 3145732
  528.1 45.2 %copy-start.9 = (bf16[256,2048]{1,0:T(8,128)(2,1)}, bf16[256,2048]{1,0:T(8,128)(2,1)S(1)}, u32[]{:S(2)}) copy-start(bf16[256,2048]{1,0:T(8,128)(2,1)S(1)} %get-tuple-element.100.refs_0_) | copy-start | bytes 3145732
  528.2 28.5 %copy-start.32 = (bf16[256,1,2048]{2,0,1:T(8,128)(2,1)S(1)}, bf16[256,1,2048]{2,0,1:T(8,128)(2,1)}, u32[]{:S(2)}) copy-start(bf16[256,1,2048]{2,0,1:T(8,128)(2,1)} %param.14) | copy-start | bytes 3145732
  528.2 28.5 %copy-start.111 = (f32[256]{0:T(256)S(1)}, f32[256]{0:T(256)}, u32[]{:S(2)}) copy-start(f32[256]{0:T(256)} %copy-done.110) | copy-start | bytes 3076
  528.2 23.4 %collective-permute-start.23 = (bf16[256,2048]{1,0:T(8,128)(2,1)S(1)}, bf16[256,2048]{1,0:T(8,128)(2,1)S(1)}, u32[]{:S(2)}, u32[]{:S(2)}) collective-permute-start(bf16[256,2048]{1,0:T(8,128)(2,1)S(1)} %get-tuple-element.100.refs_0_), channel_id=1, source_target_pairs={{0,8},{8,0},{16,24},{24,16},{1,9},{9,1},{17,25},{25,17},{2,10},{10... | collective-permute-start | bytes 3145736 | tf_op jit(solution)/shard_map/ppermute | solution.py:266
  528.6 25.9 %collective-permute-start.24 = (bf16[256,2048]{1,0:T(8,128)(2,1)S(1)}, bf16[256,2048]{1,0:T(8,128)(2,1)S(1)}, u32[]{:S(2)}, u32[]{:S(2)}) collective-permute-start(bf16[256,2048]{1,0:T(8,128)(2,1)S(1)} %get-tuple-element.100.refs_0_), channel_id=1, source_target_pairs={{0,16},{8,24},{16,0},{24,8},{1,17},{9,25},{17,1},{25,9},{2,18},{10... | collective-permute-start | bytes 3145736 | tf_op jit(solution)/shard_map/ppermute | solution.py:266
  534.0 25.9 %copy-start.72 = (bf16[256,64]{0,1:T(8,128)(2,1)S(1)}, bf16[256,64]{0,1:T(8,128)(2,1)}, u32[]{:S(2)}) copy-start(bf16[256,64]{0,1:T(8,128)(2,1)} %copy-done.71) | copy-start | bytes 98308
  552.5 20.8 %collective-permute-start.25 = (bf16[256,1024]{1,0:T(8,128)(2,1)}, bf16[256,1024]{1,0:T(8,128)(2,1)}, u32[]{:S(2)}, u32[]{:S(2)}) collective-permute-start(bf16[256,1024]{1,0:T(8,128)(2,1)} %slice.286), channel_id=1, source_target_pairs={{0,16},{8,24},{16,0},{24,8},{1,17},{9,25},{17,1},{25,9},{2,18},{10... | collective-permute-start | bytes 1572872 | tf_op jit(solution)/shard_map/ppermute | solution.py:266
  556.4 17.0 %collective-permute-start.26 = (bf16[256,1024]{1,0:T(8,128)(2,1)}, bf16[256,1024]{1,0:T(8,128)(2,1)}, u32[]{:S(2)}, u32[]{:S(2)}) collective-permute-start(bf16[256,1024]{1,0:T(8,128)(2,1)} %slice.287), channel_id=1, source_target_pairs={{0,8},{8,0},{16,24},{24,16},{1,9},{9,1},{17,25},{25,17},{2,10},{10... | collective-permute-start | bytes 1572872 | tf_op jit(solution)/shard_map/ppermute | solution.py:266
  611.6 20.5 %collective-permute-start.27 = (bf16[512,768]{1,0:T(8,128)(2,1)S(1)}, bf16[512,768]{1,0:T(8,128)(2,1)S(1)}, u32[]{:S(2)}, u32[]{:S(2)}) collective-permute-start(bf16[512,768]{1,0:T(8,128)(2,1)S(1)} %get-tuple-element.202), channel_id=1, source_target_pairs={{0,8},{8,0},{16,24},{24,16},{1,9},{9,1},{17,25},{25,17},{2,10},{10... | collective-permute-start | bytes 2359304 | tf_op jit(solution)/shard_map/ppermute | solution.py:266
  613.4 33.2 %collective-permute-start.28 = (bf16[512,768]{1,0:T(8,128)(2,1)S(1)}, bf16[512,768]{1,0:T(8,128)(2,1)S(1)}, u32[]{:S(2)}, u32[]{:S(2)}) collective-permute-start(bf16[512,768]{1,0:T(8,128)(2,1)S(1)} %get-tuple-element.204), channel_id=1, source_target_pairs={{0,16},{8,24},{16,0},{24,8},{1,17},{9,25},{17,1},{25,9},{2,18},{10... | collective-permute-start | bytes 2359304 | tf_op jit(solution)/shard_map/ppermute | solution.py:266
  613.5 33.1 %collective-permute-start.29 = (bf16[512,768]{1,0:T(8,128)(2,1)S(1)}, bf16[512,768]{1,0:T(8,128)(2,1)S(1)}, u32[]{:S(2)}, u32[]{:S(2)}) collective-permute-start(bf16[512,768]{1,0:T(8,128)(2,1)S(1)} %get-tuple-element.203), channel_id=1, source_target_pairs={{0,24},{8,16},{16,8},{24,0},{1,25},{9,17},{17,9},{25,1},{2,26},{10... | collective-permute-start | bytes 2359304 | tf_op jit(solution)/shard_map/ppermute | solution.py:266
  (110 other events, 744.2 us)
Sparse Core Ops, SparseCore 0:
  71.9 156.9 all-gather.2
  230.5 81.9 all-gather.4
  408.1 87.0 reduce-scatter.4
  497.4 165.6 reduce-scatter.2

commit v6 on v5

--- a/solution.py
+++ b/solution.py
@@ -358,45 +358,135 @@
     half_width = HEAD_DIM // 2
     frequency = theta ** (-jnp.arange(half_width).astype(full) * 2.0 / HEAD_DIM)
     angles = places.astype(full)[:, None] * frequency
-    angles = jnp.concatenate([angles, angles], -1)[:, None, :]
     return (jnp.cos(angles), jnp.sin(angles))
 
 
-def rotate(v, cos_table, sin_table):
-    half_width = v.shape[-1] // 2
-    turned = jnp.concatenate([-v[..., half_width:], v[..., :half_width]], -1)
-    return v * cos_table + turned * sin_table
-
-
-def head_prep(qkv, head_scale, cos_table, sin_table):
-    per_head = qkv.reshape(qkv.shape[0], -1, HEAD_DIM)
-    queries = rotate(norm_rows(per_head[:, :-2], head_scale[:, 0])[0], cos_table, sin_table)
-    keys = rotate(norm_rows(per_head[:, -2:-1], head_scale[:, 1])[0], cos_table, sin_table)
-    values = norm_rows(per_head[:, -1:], 1.0)[0]
-    return (queries, keys, values)
-
-
-def allowed_mask(segments, indices):
-    offset = indices[:, None] - indices[None, :]
-    nearby = (offset >= 0) & (offset < WIN)
-    return (segments[:, None] == segments[None, :]) & nearby
-
-
-def scores_of(q_heads, keys, allowed):
-    raw_scores = jnp.einsum("qhd,kd->hqk", q_heads, keys, preferred_element_type=full)
-    return jnp.where(allowed[None], raw_scores * HEAD_DIM ** (-0.5), -1000000000.0)
-
-
-def attend_heads(q_heads, keys, values, allowed):
-    scores = scores_of(q_heads, keys, allowed)
-    row_peak = jnp.max(scores, -1, keepdims=True)
-    exp_scores = jnp.exp(scores - row_peak)
-    row_total = jnp.sum(exp_scores, -1, keepdims=True)
-    attn_probs = exp_scores / row_total
-    head_out = jnp.einsum(
-        "hqk,kd->qhd", attn_probs.astype(low), values, preferred_element_type=full
-    )
-    return (head_out, row_peak + jnp.log(row_total))
+def reaches(rank, mine, other, block):
+    apart = (rank ^ mine) - (rank ^ other)
+    return (apart >= 0) & (apart * block - (block - 1) < WIN)
+
+
+def attend_kernel(
+    ranks,
+    block,
+    qkv_ref,
+    code_col_ref,
+    code_row_ref,
+    cos_ref,
+    sin_ref,
+    gain_ref,
+    q_ref,
+    k_ref,
+    v_ref,
+    out_ref,
+    total_ref,
+    scores_ref,
+    peak_acc,
+    sum_acc,
+    out_acc,
+):
+    head, mine = pl.program_id(0), pl.program_id(1)
+    rank = lax.axis_index("seq")
+    half = HEAD_DIM // 2
+    base = qkv_ref.shape[1] - 2 * HEAD_DIM
+
+    def normed(v):
+        return v * lax.rsqrt(jnp.mean(v * v, -1, keepdims=True) + eps)
+
+    def turned(v, cos_table, sin_table):
+        first, second = v[:, :half], v[:, half:]
+        return jnp.concatenate(
+            [
+                first * cos_table - second * sin_table,
+                second * cos_table + first * sin_table,
+            ],
+            1,
+        )
+
+    @pl.when((head == 0) & (mine == 0))
+    def _():
+        for other in range(ranks):
+            span = slice(other * block, (other + 1) * block)
+            keys = normed(qkv_ref[span, base : base + HEAD_DIM]) * gain_ref[1:2, :]
+            k_ref[span, :] = turned(keys, cos_ref[span, :], sin_ref[span, :]).astype(low)
+            v_ref[span, :] = normed(qkv_ref[span, base + HEAD_DIM :]).astype(low)
+
+    rows = pl.ds(pl.multiple_of(mine * block, block), block)
+    columns = pl.ds(pl.multiple_of(head * HEAD_DIM, HEAD_DIM), HEAD_DIM)
+    queries = normed(qkv_ref[rows, columns]) * gain_ref[0:1, :]
+    q = turned(queries, cos_ref[rows, :], sin_ref[rows, :]).astype(low)
+    q_ref[rows, columns] = q
+    code = code_col_ref[rows, :]
+    peak_acc[...] = jnp.full_like(peak_acc, -1000000000.0)
+    sum_acc[...] = jnp.zeros_like(sum_acc)
+    out_acc[...] = jnp.zeros_like(out_acc)
+    for other in range(ranks):
+        span = slice(other * block, (other + 1) * block)
+
+        @pl.when(reaches(rank, mine, other, block))
+        def _():
+            scores = mm_nt(q, k_ref[span, :]) * HEAD_DIM ** (-0.5)
+            offset = code - code_row_ref[:, span]
+            scores = jnp.where((offset >= 0) & (offset < WIN), scores, -1000000000.0)
+            scores_ref[other] = scores
+            peak_acc[...] = jnp.maximum(peak_acc[...], jnp.max(scores, -1, keepdims=True))
+
+    peak = peak_acc[...]
+    for other in range(ranks):
+
+        @pl.when(reaches(rank, mine, other, block))
+        def _():
+            weights = jnp.exp(scores_ref[other] - peak)
+            scores_ref[other] = weights
+            sum_acc[...] += jnp.sum(weights, -1, keepdims=True)
+
+    row_total = sum_acc[...]
+    for other in range(ranks):
+        span = slice(other * block, (other + 1) * block)
+
+        @pl.when(reaches(rank, mine, other, block))
+        def _():
+            probs = (scores_ref[other] / row_total).astype(low)
+            out_acc[...] += mm(probs, v_ref[span, :])
+
+    out_ref[rows, columns] = out_acc[...].astype(low)
+    total_ref[head, rows, :] = peak + jnp.log(row_total)
+
+
+def attend(ranks, qkv, codes, cos_table, sin_table, gains):
+    length = qkv.shape[0]
+    block = length // ranks
+    heads = qkv.shape[1] // HEAD_DIM - 2
+    whole = lambda v: pl.BlockSpec(
+        v.shape, lambda i, j, n=len(v.shape): (0,) * n, pipeline_mode=pl.Buffered(1)
+    )
+    operands = (qkv, codes[:, None], codes[None], cos_table, sin_table, gains)
+    results = (
+        jax.ShapeDtypeStruct((length, heads * HEAD_DIM), low),
+        jax.ShapeDtypeStruct((length, HEAD_DIM), low),
+        jax.ShapeDtypeStruct((length, HEAD_DIM), low),
+        jax.ShapeDtypeStruct((length, heads * HEAD_DIM), low),
+        jax.ShapeDtypeStruct((heads, length, 1), full),
+    )
+    return pl.pallas_call(
+        functools.partial(attend_kernel, ranks, block),
+        grid=(heads, ranks),
+        out_shape=results,
+        in_specs=[whole(v) for v in operands],
+        out_specs=tuple(whole(v) for v in results),
+        scratch_shapes=[
+            pltpu.VMEM((ranks, block, block), full),
+            pltpu.VMEM((block, 1), full),
+            pltpu.VMEM((block, 1), full),
+            pltpu.VMEM((block, HEAD_DIM), full),
+        ],
+        compiler_params=pltpu.CompilerParams(vmem_limit_bytes=40 << 20),
+        cost_estimate=pl.CostEstimate(
+            flops=4 * heads * length * length * HEAD_DIM * 9 // 16,
+            bytes_accessed=12 * length * HEAD_DIM * (heads + 2),
+            transcendentals=heads * length * length,
+        ),
+    )(*operands)
 
 
 def norm_rope_back(lin, gain, incoming):
@@ -452,14 +542,10 @@
     row_acc[...] = jnp.zeros_like(row_acc)
     query_acc[...] = jnp.zeros_like(query_acc)
 
-    def reaches(other):
-        apart = (rank ^ mine) - (rank ^ other)
-        return (apart >= 0) & (apart * block - (block - 1) < WIN)
-
     for other in range(ranks):
         span = slice(other * block, (other + 1) * block)
 
-        @pl.when(reaches(other))
+        @pl.when(reaches(rank, mine, other, block))
         def _():
             scores = mm_nt(q, k_ref[span, :]) * scale
             offset = code - code_row_ref[:, span]
@@ -473,7 +559,7 @@
     for other in range(ranks):
         span = slice(other * block, (other + 1) * block)
 
-        @pl.when(reaches(other))
+        @pl.when(reaches(rank, mine, other, block))
         def _():
             probs = probs_ref[other]
             grad_scores = (probs * (grad_probs_ref[other] - inner) * scale).astype(low)
@@ -592,7 +678,7 @@
         + [pl.BlockSpec((length, columns), lambda i: (0, 0))]
         + [pl.BlockSpec((tile, v.shape[1]), lambda i: (i, 0)) for v in extras],
         out_specs=pl.BlockSpec((each, 1, rows, wide), place),
-        compiler_params=pltpu.CompilerParams(vmem_limit_bytes=32 << 20),
+        compiler_params=pltpu.CompilerParams(vmem_limit_bytes=60 << 20),
         cost_estimate=pl.CostEstimate(
             flops=2 * length * width * columns,
             bytes_accessed=2 * (length * (width + columns) + width * columns),
@@ -602,18 +688,27 @@
 
 
 def middle_kernel(
+    pairs,
     block,
     parts,
-    hidden_ref,
-    map_ref,
+    rows_own,
+    rows_x_in,
+    rows_y_in,
+    rows_left_in,
+    rows_right_in,
+    in_maps_ref,
+    shard_ref,
     mixed_ref,
     gain_ref,
     ple_gate_ref,
     ple_proj_ref,
     ple_input_ref,
     cotangent_ref,
-    rows_ref,
+    rows_out_ref,
     grad_map_ref,
+    map_ref,
+    gate_part_ref,
+    up_part_ref,
     out_ref,
     second_ref,
     grad_second_ref,
@@ -621,58 +716,286 @@
     ple_mixed_ref,
     grad_gate_ref,
     gain_out_ref,
+    rows_ref,
+    in_tiles,
+    wide_stage,
+    hidden_ref,
     maps,
+    product_ref,
     own,
-    keep_left,
-    keep_right,
-    send_x,
-    send_y,
-    got_x,
-    got_y,
-    relay_x,
-    relay_y,
-    far_x,
-    far_y,
+    keep,
+    send,
+    got,
+    relay,
+    far,
     stage,
+    load_sem,
+    tile_sem,
+    wide_sem,
+    stage_sem,
     map_sem,
-    stage_sem,
-    *sems,
+    right_s,
+    right_r,
+    left_s,
+    left_r,
+    core_s,
+    core_r,
+    near_s,
+    near_r,
+    far_s,
+    far_r,
+    gx_s,
+    gx_r,
+    gy_s,
+    gy_r,
+    fx_s,
+    fx_r,
+    fy_s,
+    fy_r,
 ):
-    (sx_s, sx_r, sy_s, sy_r, rx_s, rx_r, ry_s, ry_r) = sems[:8]
-    (gx_s, gx_r, gy_s, gy_r, fx_s, fx_r, fy_s, fy_r) = sems[8:]
     rank = lax.axis_index("seq")
     fsdp_index = lax.axis_index("fsdp")
-    by_x, by_y = (flip(rank, 1, 4), fsdp_index), (flip(rank, 2, 4), fsdp_index)
+    pair, core = fsdp_index // 2, fsdp_index % 2
+    sibling = (rank, pair * 2 + 1 - core)
+    rank_x, rank_y = flip(rank, 1, 4), flip(rank, 2, 4)
+    by_x, by_y = (rank_x, fsdp_index), (rank_y, fsdp_index)
     size = block // parts
-    width = map_ref.shape[0]
+    width, span = in_maps_ref.shape[1], in_maps_ref.shape[2]
     half = width // 2
     tile = 256
-    tiles = width // tile
+    tiles = span // tile
+    shard = shard_ref.shape[0]
+    cut = shard // 2
     left, right = slice(0, half), slice(half, width)
     up = lambda v: v.astype(full)
 
-    def remote(source, target, send, recv, device):
+    def remote(source, target, send_sem, recv_sem, device):
         return pltpu.make_async_remote_copy(
             src_ref=source,
             dst_ref=target,
-            send_sem=send,
-            recv_sem=recv,
+            send_sem=send_sem,
+            recv_sem=recv_sem,
             device_id=device,
             device_id_type=MESH,
         )
 
+    def columns_of(i):
+        return pl.ds(pl.multiple_of(i * tile, tile), tile)
+
+    loads = [
+        pltpu.make_async_copy(source, target, load_sem.at[i])
+        for i, (source, target) in enumerate(
+            (
+                (rows_own, rows_ref.at[0]),
+                (rows_x_in, rows_ref.at[1]),
+                (rows_y_in, rows_ref.at[2]),
+                (rows_left_in, rows_ref.at[3, :, left]),
+                (rows_right_in, rows_ref.at[3, :, right]),
+                (shard_ref, maps.at[pair, core]),
+            )
+        )
+    ]
+
+    def tile_copy(i, slot):
+        return pltpu.make_async_copy(
+            in_maps_ref.at[:, :, columns_of(i)], in_tiles.at[slot], tile_sem.at[slot]
+        )
+
+    for copy in loads:
+        copy.start()
+    tile_copy(0, 0).start()
+
+    barrier = pltpu.get_barrier_semaphore()
+    devices = [by_x, by_y, sibling]
+    devices += [(rank, ((pair + i) % pairs) * 2 + core) for i in range(1, pairs)]
+    for device in devices:
+        pl.semaphore_signal(barrier, inc=1, device_id=device, device_id_type=MESH)
+    pl.semaphore_wait(barrier, len(devices))
+
+    def piece(at, k):
+        return maps.at[at, core, pl.ds(k * cut, cut), :]
+
+    def source_of(at, k, t):
+        return shard_ref.at[pl.ds(k * cut, cut), :] if t == 0 else piece(at, k)
+
+    def pass_right(t, k):
+        at, slot = pair - (t - 1), (t - 1) * 2 + k
+        return remote(
+            source_of(at, k, t - 1),
+            piece(at, k),
+            right_s.at[slot],
+            right_r.at[slot],
+            (rank, fsdp_index + 2),
+        )
+
+    def pass_left(t, k):
+        at, slot = pair + (t - 1), (t - 1) * 2 + k
+        return remote(
+            source_of(at, k, t - 1),
+            piece(at, k),
+            left_s.at[slot],
+            left_r.at[slot],
+            (rank, fsdp_index - 2),
+        )
+
+    def to_sibling(at, k, own_shard=False):
+        slot = at * 2 + k
+        return remote(
+            source_of(at, k, 0 if own_shard else 1),
+            piece(at, k),
+            core_s.at[slot],
+            core_r.at[slot],
+            sibling,
+        )
+
+    sends_right = lambda t: (pair - (t - 1) >= 0) & (pair + 1 < pairs)
+    sends_left = lambda t: (pair + (t - 1) < pairs) & (pair - 1 >= 0)
+    for k in range(2):
+        pl.when(sends_right(1))(lambda k=k: pass_right(1, k).start())
+        pl.when(sends_left(1))(lambda k=k: pass_left(1, k).start())
+        to_sibling(pair, k, True).start()
+
+    def chain_step(t, k):
+        slot = (t - 1) * 2 + k
+
+        def from_left():
+            target = piece(pair - t, k)
+            remote(target, target, right_s.at[slot], right_r.at[slot], sibling).wait_recv()
+            if t + 1 < pairs:
+                pl.when(pair + 1 < pairs)(lambda: pass_right(t + 1, k).start())
+            to_sibling(pair - t, k).start()
+
+        def from_right():
+            target = piece(pair + t, k)
+            remote(target, target, left_s.at[slot], left_r.at[slot], sibling).wait_recv()
+            if t + 1 < pairs:
+                pl.when(pair - 1 >= 0)(lambda: pass_left(t + 1, k).start())
+            to_sibling(pair + t, k).start()
+
+        pl.when(pair - t >= 0)(from_left)
+        pl.when(pair + t < pairs)(from_right)
+
+    for copy in loads:
+        copy.wait()
+
+    def wide_copies(i, slot):
+        return [
+            pltpu.make_async_copy(
+                wide_stage.at[slot, n], target.at[:, columns_of(i)], wide_sem.at[slot, n]
+            )
+            for n, target in enumerate((gate_part_ref, up_part_ref))
+        ]
+
+    slope, cubic = math.sqrt(2.0 / math.pi), 0.044715
+
+    def gate_up_tile(i, carry):
+        slot = i % 2
+        tile_copy(i, slot).wait()
+        pl.when(i + 1 < tiles)(lambda: tile_copy(i + 1, 1 - slot).start())
+
+        @pl.when(i >= 2)
+        def _():
+            for copy in wide_copies(i - 2, slot):
+                copy.wait()
+
+        v = rows_ref[...].reshape(4 * block, width)
+        gate = mm(v, in_tiles[slot, 0])
+        wide_stage[slot, 0] = gate
+        upper = mm(v, in_tiles[slot, 1])
+        wide_stage[slot, 1] = upper
+        bend = jnp.tanh(slope * (gate + cubic * gate * gate * gate))
+        hidden_ref[:, columns_of(i)] = (0.5 * gate * (1.0 + bend) * upper).astype(low)
+        for copy in wide_copies(i, slot):
+            copy.start()
+        return carry
+
+    steps = [(t, k) for t in range(1, pairs) for k in range(2)]
+    early = min(len(steps), 4)
+    at_tile = [tiles * (n + 1) // early for n in range(early)]
+    done = 0
+    for n in range(early):
+        lax.fori_loop(done, at_tile[n], gate_up_tile, 0)
+        done = at_tile[n]
+        chain_step(*steps[n])
+    for i in (tiles - 2, tiles - 1):
+        for copy in wide_copies(i, i % 2):
+            copy.wait()
+
+    def chip_of(j):
+        orders = [sorted(range(pairs), key=lambda p: (abs(p - z), p)) for z in range(pairs)]
+        return sum(jnp.where(pair == z, orders[z][j], 0) for z in range(pairs))
+
+    def shard_of(j):
+        chip = chip_of(j // 2)
+        at_core = core if j % 2 == 0 else 1 - core
+        return chip, at_core, chip * 2 + at_core, 1 - chip // (pairs // 2)
+
+    def near_copy(j):
+        chip, at_core, place, is_left = shard_of(j)
+        to = rank_x * is_left + rank_y * (1 - is_left)
+        return remote(
+            send.at[place], got.at[place], near_s.at[place], near_r.at[place], (to, fsdp_index)
+        )
+
+    def far_copy(j):
+        chip, at_core, place, is_left = shard_of(j)
+        to = rank_y * is_left + rank_x * (1 - is_left)
+        return remote(
+            relay.at[place], far.at[place], far_s.at[place], far_r.at[place], (to, fsdp_index)
+        )
+
+    def product(j):
+        chip, at_core, place, is_left = shard_of(j)
+        if j % 2:
+            for k in range(2):
+                target = maps.at[chip, at_core, pl.ds(k * cut, cut), :]
+                remote(
+                    target, target, core_s.at[0], core_r.at[chip * 2 + k], sibling
+                ).wait_recv()
+        v = mm_nt(hidden_ref[...], maps[chip, at_core])
+        product_ref[...] = v.reshape(4, block, shard)
+        near = 2 - is_left
+        own[:, columns_of(place)] = product_ref[0]
+        send[place, 0] = product_ref[3].astype(low)
+        send[place, 1] = product_ref[near].astype(low)
+        keep[place] = product_ref[3 - near]
+        near_copy(j).start()
+
+    def pass_on(j):
+        place = shard_of(j)[2]
+        near_copy(j).wait_recv()
+        relay[place] = (keep[place] + up(got[place, 0])).astype(low)
+        far_copy(j).start()
+
+    def collect(j):
+        place = shard_of(j)[2]
+        far_copy(j).wait_recv()
+        columns = columns_of(place)
+        own[:, columns] += up(got[place, 1]) + up(far[place])
+
+    count = 2 * pairs
+    rest = steps[early:]
+    for j in range(count):
+        need = j // 2
+        while rest and rest[0][0] <= need:
+            chain_step(*rest.pop(0))
+        product(j)
+        if j >= 2:
+            pass_on(j - 2)
+        if j >= 4:
+            collect(j - 4)
+    for j in (count - 2, count - 1):
+        pass_on(j)
+    for j in range(count - 4, count):
+        collect(j)
+
     def map_copy(i):
-        at = pl.ds(pl.multiple_of(i * tile, tile), tile)
-        return pltpu.make_async_copy(map_ref.at[at, :], maps.at[at, :], map_sem.at[i])
-
-    for i in range(tiles):
+        return pltpu.make_async_copy(
+            maps.at[i // 2, i % 2], map_ref.at[pl.ds(i * shard, shard), :], map_sem.at[i]
+        )
+
+    for i in range(count):
         map_copy(i).start()
-
-    barrier = pltpu.get_barrier_semaphore()
-    for device in (by_x, by_y):
-        pl.semaphore_signal(barrier, inc=1, device_id=device, device_id_type=MESH)
-    pl.semaphore_wait(barrier, 2)
-
     sent = []
 
     def go(copy):
@@ -683,62 +1006,13 @@
     def rows_of(u):
         return pl.ds(u * size, size)
 
-    near_x, near_y = [], []
-    for u in range(parts):
-        at = rows_of(u)
-
-        def product(i):
-            if u == 0:
-                map_copy(i).wait()
-            rows = pl.ds(pl.multiple_of(i * tile, tile), tile)
-            v = hidden_ref[:, at, :].reshape(4 * size, hidden_ref.shape[2])
-            return mm_nt(v, maps[rows, :]).reshape(4, size, tile)
-
-        def left_tile(i, carry):
-            v = product(i)
-            columns = pl.ds(pl.multiple_of(i * tile, tile), tile)
-            own[at, columns] = v[0]
-            keep_left[at, columns] = v[2]
-            send_x[u, 0, :, columns] = v[3].astype(low)
-            send_x[u, 1, :, columns] = v[1].astype(low)
-            return carry
-
-        def right_tile(i, carry):
-            v = product(i + tiles // 2)
-            columns = pl.ds(pl.multiple_of(i * tile, tile), tile)
-            own[at, pl.ds(pl.multiple_of(half + i * tile, tile), tile)] = v[0]
-            keep_right[at, columns] = v[1]
-            send_y[u, 0, :, columns] = v[3].astype(low)
-            send_y[u, 1, :, columns] = v[2].astype(low)
-            return carry
-
-        lax.fori_loop(0, tiles // 2, left_tile, 0)
-        near_x.append(go(remote(send_x.at[u], got_x.at[u], sx_s.at[u], sx_r.at[u], by_x)))
-        lax.fori_loop(0, tiles // 2, right_tile, 0)
-        near_y.append(go(remote(send_y.at[u], got_y.at[u], sy_s.at[u], sy_r.at[u], by_y)))
-
-    last_x, last_y = [], []
-    for u in range(parts):
-        at = rows_of(u)
-        near_x[u].wait_recv()
-        relay_y[u] = (keep_left[at, :] + up(got_x[u, 0])).astype(low)
-        last_y.append(go(remote(relay_y.at[u], far_y.at[u], ry_s.at[u], ry_r.at[u], by_y)))
-        near_y[u].wait_recv()
-        relay_x[u] = (keep_right[at, :] + up(got_y[u, 0])).astype(low)
-        last_x.append(go(remote(relay_x.at[u], far_x.at[u], rx_s.at[u], rx_r.at[u], by_x)))
-
     gain_out_ref[...] = jnp.zeros_like(gain_out_ref)
     ffn_gain, ple_gain = gain_ref[0:1, :], gain_ref[1:2, :]
     mean = lambda v: jnp.mean(v, -1, keepdims=True)
     total = lambda v: jnp.sum(v, 0, keepdims=True)
-    slope, cubic = math.sqrt(2.0 / math.pi), 0.044715
     rows_x, rows_y = [], []
     for u in range(parts):
         at = rows_of(u)
-        last_y[u].wait_recv()
-        last_x[u].wait_recv()
-        own[at, left] = own[at, left] + up(got_x[u, 1]) + up(far_y[u])
-        own[at, right] = own[at, right] + up(got_y[u, 1]) + up(far_x[u])
         f = own[at, :]
         f_inverse = lax.rsqrt(mean(f * f) + eps)
         second = (mixed_ref[at, :] + f * f_inverse * ffn_gain).astype(low)
@@ -773,17 +1047,17 @@
         rows_ref[0, at, :] = grad_f.astype(low)
         pair_x, pair_y = [], []
         for order in range(2):
-            for pairs, device, send, recv, index, part in (
+            for copies, device, send_sem, recv_sem, index, part in (
                 (pair_x, by_x, gx_s, gx_r, 1, (left, right)[order]),
                 (pair_y, by_y, gy_s, gy_r, 2, (right, left)[order]),
             ):
-                pairs.append(
+                copies.append(
                     go(
                         remote(
                             rows_ref.at[0, at, part],
                             rows_ref.at[index, at, part],
-                            send.at[u, order],
-                            recv.at[u, order],
+                            send_sem.at[u, order],
+                            recv_sem.at[u, order],
                             device,
                         )
                     )
@@ -791,11 +1065,11 @@
         rows_x.append(pair_x)
         rows_y.append(pair_y)
 
-    far = []
+    forwards = []
     for u in range(parts):
         at = rows_of(u)
         rows_x[u][0].wait_recv()
-        far.append(
+        forwards.append(
             go(
                 remote(
                     rows_ref.at[1, at, left],
@@ -807,7 +1081,7 @@
             )
         )
         rows_y[u][0].wait_recv()
-        far.append(
+        forwards.append(
             go(
                 remote(
                     rows_ref.at[2, at, right],
@@ -821,14 +1095,15 @@
     for u in range(parts):
         rows_x[u][1].wait_recv()
         rows_y[u][1].wait_recv()
-    for copy in far:
+    for copy in forwards:
         copy.wait_recv()
 
     def stage_copy(i, slot):
         at = pl.ds(pl.multiple_of(i * tile, tile), tile)
         return pltpu.make_async_copy(stage.at[slot], grad_map_ref.at[at, :], stage_sem.at[slot])
 
-    span = hidden_ref.shape[2]
+    rows_copy = pltpu.make_async_copy(rows_ref, rows_out_ref, load_sem.at[0])
+    rows_copy.start()
 
     def grad_tile(i, carry):
         slot = i % 2
@@ -840,32 +1115,45 @@
         columns = pl.ds(pl.multiple_of(i * tile, tile), tile)
         v = rows_ref[:, :, columns].reshape(4 * block, tile)
         for j in range(0, span, span // 2):
-            w = hidden_ref[:, :, j : j + span // 2].reshape(4 * block, span // 2)
-            stage[slot, :, j : j + span // 2] = mm_tn(v, w).astype(low)
+            stage[slot, :, j : j + span // 2] = mm_tn(v, hidden_ref[:, j : j + span // 2]).astype(low)
         stage_copy(i, slot).start()
         return carry
 
-    lax.fori_loop(0, tiles, grad_tile, 0)
-    stage_copy(tiles - 2, 0).wait()
-    stage_copy(tiles - 1, 1).wait()
+    lax.fori_loop(0, count, grad_tile, 0)
+    stage_copy(count - 2, 0).wait()
+    stage_copy(count - 1, 1).wait()
     for copy in sent:
         copy.wait_send()
-
-
-def middle(hidden, down_map, mixed, gains, ple, ple_input, cotangent):
+    rows_copy.wait()
+    for i in range(count):
+        map_copy(i).wait()
+    for j in range(count):
+        near_copy(j).wait_send()
+        far_copy(j).wait_send()
+    for k in range(2):
+        to_sibling(pair, k, True).wait_send()
+        for t in range(1, pairs):
+            pl.when(pair - t >= 0)(lambda t=t, k=k: to_sibling(pair - t, k).wait_send())
+            pl.when(pair + t < pairs)(lambda t=t, k=k: to_sibling(pair + t, k).wait_send())
+            pl.when(sends_right(t))(lambda t=t, k=k: pass_right(t, k).wait_send())
+            pl.when(sends_left(t))(lambda t=t, k=k: pass_left(t, k).wait_send())
+
+
+def middle(pairs, h_blocks, in_maps, down_rows, mixed, gains, ple, ple_input, cotangent):
     block, width = mixed.shape
-    span = hidden.shape[1]
-    parts, half = 2, width // 2
-    size = block // parts
-    hidden = hidden.reshape(4, block, span)
-    dma = pltpu.SemaphoreType.DMA
+    span = in_maps.shape[2]
+    shard = down_rows.shape[0]
+    parts, length = 2, 4 * block
+    count = 2 * pairs
+    dma = lambda *n: pltpu.SemaphoreType.DMA(n)
     vmem = pl.BlockSpec(memory_space=pltpu.VMEM)
     anywhere = pl.BlockSpec(memory_space=pl.ANY)
-    pieces = pltpu.VMEM((parts, 2, size, half), low)
-    singles = pltpu.VMEM((parts, size, half), low)
     shapes = (
         ((4, block, width), low),
         ((width, span), low),
+        ((width, span), low),
+        ((length, span), full),
+        ((length, span), full),
         ((block, width), low),
         ((block, width), low),
         ((block, width), full),
@@ -875,33 +1163,45 @@
         ((8, width), full),
     )
     return pl.pallas_call(
-        functools.partial(middle_kernel, block, parts),
+        functools.partial(middle_kernel, pairs, block, parts),
         out_shape=tuple(jax.ShapeDtypeStruct(*v) for v in shapes),
-        in_specs=[vmem, anywhere] + [vmem] * 6,
-        out_specs=tuple(anywhere if i == 1 else vmem for i in range(len(shapes))),
+        in_specs=[anywhere] * 7 + [vmem] * 6,
+        out_specs=tuple(anywhere if i < 5 else vmem for i in range(len(shapes))),
         scratch_shapes=[
-            pltpu.VMEM((width, span), low),
+            pltpu.VMEM((4, block, width), low),
+            pltpu.VMEM((2, 2, width, 256), low),
+            pltpu.VMEM((2, 2, length, 256), full),
+            pltpu.VMEM((length, span), low),
+            pltpu.VMEM((pairs, 2, shard, span), low),
+            pltpu.VMEM((4, block, shard), full),
             pltpu.VMEM((block, width), full),
-            pltpu.VMEM((block, half), full),
-            pltpu.VMEM((block, half), full),
-            *[pieces] * 4,
-            *[singles] * 4,
+            pltpu.VMEM((count, block, shard), full),
+            pltpu.VMEM((count, 2, block, shard), low),
+            pltpu.VMEM((count, 2, block, shard), low),
+            pltpu.VMEM((count, block, shard), low),
+            pltpu.VMEM((count, block, shard), low),
             pltpu.VMEM((2, 256, span), low),
-            dma((width // 256,)),
-            dma((2,)),
-            *[dma((parts,))] * 8,
-            *[dma((parts, 2))] * 4,
-            *[dma((parts,))] * 4,
+            dma(6),
+            dma(2),
+            dma(2, 2),
+            dma(2),
+            dma(count),
+            *[dma(2 * (pairs - 1))] * 4,
+            *[dma(count)] * 2,
+            *[dma(count)] * 4,
+            *[dma(parts, 2)] * 4,
+            *[dma(parts)] * 4,
         ],
         compiler_params=pltpu.CompilerParams(
-            collective_id=1, has_side_effects=True, vmem_limit_bytes=56 << 20
+            collective_id=1, has_side_effects=True, vmem_limit_bytes=62 << 20
         ),
         cost_estimate=pl.CostEstimate(
             flops=16 * block * width * span, bytes_accessed=100 << 20, transcendentals=0
         ),
     )(
-        hidden,
-        down_map,
+        *h_blocks,
+        in_maps,
+        down_rows,
         mixed,
         jnp.pad(jnp.stack(gains), ((0, 6), (0, 0))),
         ple[:, :PLE],
@@ -911,8 +1211,12 @@
     )
 
 
-def middle_plain(ranks, hidden, down_map, mixed, gains, ple, ple_input, cotangent):
+def middle_plain(ranks, h_blocks, in_maps, down_rows, mixed, gains, ple, ple_input, cotangent):
     block = mixed.shape[0]
+    down_map = lax.all_gather(down_rows, "fsdp", axis=0, tiled=True)
+    gate_up = dot(whole_rows(h_blocks), in_maps, ((1,), (1,)))
+    gate_part, up_part = gate_up[:, 0], gate_up[:, 1]
+    hidden = (gelu_tanh(gate_part) * up_part).astype(low)
     parts = mm_nt(hidden, down_map).astype(low)
     ffn_out = sum_seq([parts[k * block : (k + 1) * block] for k in range(ranks)], ranks)
     ffn_normed, ffn_inverse = norm_rows(ffn_out, gains[0])
@@ -935,6 +1239,9 @@
     return (
         rows,
         mm_tn(rows, hidden).astype(low),
+        down_map,
+        gate_part,
+        up_part,
         hidden_out,
         h_second,
         grad_second,
@@ -943,6 +1250,199 @@
         grad_ple_gate,
         jnp.stack([gain_grad_four, gain_grad_five]),
     )
+
+
+def back_kernel(
+    block,
+    gate_ref,
+    up_ref,
+    maps_ref,
+    rows_own,
+    rows_x,
+    rows_y,
+    rows_left,
+    rows_right,
+    grad_maps_ref,
+    sum_ref,
+    maps,
+    keep_left,
+    keep_right,
+    send_x,
+    send_y,
+    got_x,
+    got_y,
+    relay_x,
+    relay_y,
+    far_x,
+    far_y,
+    stage,
+    map_sem,
+    stage_sem,
+    sx_s,
+    sx_r,
+    sy_s,
+    sy_r,
+    rx_s,
+    rx_r,
+    ry_s,
+    ry_r,
+):
+    rank = lax.axis_index("seq")
+    fsdp_index = lax.axis_index("fsdp")
+    by_x, by_y = (flip(rank, 1, 4), fsdp_index), (flip(rank, 2, 4), fsdp_index)
+    width, span = maps_ref.shape[1], maps_ref.shape[2]
+    tile = 256
+    tiles = width // tile
+    each = tiles // 2
+    up = lambda v: v.astype(full)
+
+    def columns_of(i):
+        return pl.ds(pl.multiple_of(i * tile, tile), tile)
+
+    def remote(source, target, send, recv, device):
+        return pltpu.make_async_remote_copy(
+            src_ref=source,
+            dst_ref=target,
+            send_sem=send,
+            recv_sem=recv,
+            device_id=device,
+            device_id_type=MESH,
+        )
+
+    def map_copy(i):
+        return pltpu.make_async_copy(
+            maps_ref.at[:, columns_of(i), :], maps.at[:, columns_of(i), :], map_sem.at[i]
+        )
+
+    def near_x(j):
+        return remote(send_x.at[j], got_x.at[j], sx_s.at[j], sx_r.at[j], by_x)
+
+    def near_y(j):
+        return remote(send_y.at[j], got_y.at[j], sy_s.at[j], sy_r.at[j], by_y)
+
+    def last_x(j):
+        return remote(relay_x.at[j], far_x.at[j], rx_s.at[j], rx_r.at[j], by_x)
+
+    def last_y(j):
+        return remote(relay_y.at[j], far_y.at[j], ry_s.at[j], ry_r.at[j], by_y)
+
+    for j in range(each):
+        map_copy(j).start()
+        map_copy(j + each).start()
+
+    barrier = pltpu.get_barrier_semaphore()
+    for device in (by_x, by_y):
+        pl.semaphore_signal(barrier, inc=1, device_id=device, device_id_type=MESH)
+    pl.semaphore_wait(barrier, 2)
+
+    def product(i):
+        map_copy(i).wait()
+        v = mm_nt(gate_ref[...], maps[0, columns_of(i), :])
+        v = v + mm_nt(up_ref[...], maps[1, columns_of(i), :])
+        return v.reshape(4, block, tile)
+
+    def send_tiles(j, carry):
+        v = product(j)
+        sum_ref[:, columns_of(j)] = v[0]
+        keep_left[j] = v[2]
+        send_x[j, 0] = v[3].astype(low)
+        send_x[j, 1] = v[1].astype(low)
+        near_x(j).start()
+        v = product(j + each)
+        sum_ref[:, columns_of(j + each)] = v[0]
+        keep_right[j] = v[1]
+        send_y[j, 0] = v[3].astype(low)
+        send_y[j, 1] = v[2].astype(low)
+        near_y(j).start()
+        return carry
+
+    lax.fori_loop(0, each, send_tiles, 0)
+
+    def stage_copy(i, slot):
+        return pltpu.make_async_copy(
+            stage.at[slot], grad_maps_ref.at[:, columns_of(i), :], stage_sem.at[slot]
+        )
+
+    def grad_tile(i, j, far_ref):
+        slot = j % 2
+        pl.when(i >= 2)(lambda: stage_copy(i - 2, slot).wait())
+        near = columns_of(i)
+        v = jnp.concatenate(
+            [rows_own[:, near], rows_x[:, near], rows_y[:, near], far_ref[:, columns_of(j)]], 0
+        )
+        for k in range(0, span, span // 2):
+            part = slice(k, k + span // 2)
+            stage[slot, 0, :, part] = mm_tn(v, gate_ref[:, part]).astype(low)
+            stage[slot, 1, :, part] = mm_tn(v, up_ref[:, part]).astype(low)
+        stage_copy(i, slot).start()
+
+    def left_tile(j, carry):
+        grad_tile(j, j, rows_left)
+        near_x(j).wait_recv()
+        relay_y[j] = (keep_left[j] + up(got_x[j, 0])).astype(low)
+        last_y(j).start()
+        near_y(j).wait_recv()
+        relay_x[j] = (keep_right[j] + up(got_y[j, 0])).astype(low)
+        last_x(j).start()
+        return carry
+
+    def right_tile(j, carry):
+        grad_tile(j + each, j, rows_right)
+        last_y(j).wait_recv()
+        sum_ref[:, columns_of(j)] += up(got_x[j, 1]) + up(far_y[j])
+        last_x(j).wait_recv()
+        sum_ref[:, columns_of(j + each)] += up(got_y[j, 1]) + up(far_x[j])
+        return carry
+
+    lax.fori_loop(0, each, left_tile, 0)
+    lax.fori_loop(0, each, right_tile, 0)
+    stage_copy(tiles - 2, 0).wait()
+    stage_copy(tiles - 1, 1).wait()
+
+    def sent(j, carry):
+        for copy in (near_x(j), near_y(j), last_x(j), last_y(j)):
+            copy.wait_send()
+        return carry
+
+    lax.fori_loop(0, each, sent, 0)
+
+
+def back(grad_gate, grad_up, in_maps, h_blocks):
+    length, span = grad_gate.shape
+    block, width = h_blocks[0].shape
+    each = width // 512
+    dma = pltpu.SemaphoreType.DMA
+    vmem = pl.BlockSpec(memory_space=pltpu.VMEM)
+    anywhere = pl.BlockSpec(memory_space=pl.ANY)
+    keep = pltpu.VMEM((each, block, 256), full)
+    pieces = pltpu.VMEM((each, 2, block, 256), low)
+    singles = pltpu.VMEM((each, block, 256), low)
+    return pl.pallas_call(
+        functools.partial(back_kernel, block),
+        out_shape=(
+            jax.ShapeDtypeStruct((2, width, span), low),
+            jax.ShapeDtypeStruct((block, width), full),
+        ),
+        in_specs=[vmem, vmem, anywhere] + [vmem] * 5,
+        out_specs=(anywhere, vmem),
+        scratch_shapes=[
+            pltpu.VMEM((2, width, span), low),
+            keep,
+            keep,
+            *[pieces] * 4,
+            *[singles] * 4,
+            pltpu.VMEM((2, 2, 256, span), low),
+            dma((width // 256,)),
+            dma((2,)),
+            *[dma((each,))] * 8,
+        ],
+        compiler_params=pltpu.CompilerParams(
+            collective_id=3, has_side_effects=True, vmem_limit_bytes=58 << 20
+        ),
+        cost_estimate=pl.CostEstimate(
+            flops=8 * length * width * span, bytes_accessed=50 << 20, transcendentals=0
+        ),
+    )(grad_gate, grad_up, in_maps, *h_blocks)
 
 
 def finish_kernel(sizes, with_x, *refs):
@@ -1266,10 +1766,9 @@
         sizes, head_pack, rest_pack, marks, x_local
     )
     in_rows, down_rows, head_all = lax.optimization_barrier(
-        (w_mlp[:, :2], w_mlp[:, 2], head_all)
-    )
-    in_maps = lax.all_gather(in_rows, "fsdp", axis=0, tiled=True)
-    down_map = lax.all_gather(down_rows, "fsdp", axis=0, tiled=True)
+        (jnp.moveaxis(w_mlp[:, :2], 1, 0), w_mlp[:, 2], head_all)
+    )
+    in_maps = lax.all_gather(in_rows, "fsdp", axis=1, tiled=True)
     x_all = x_all.reshape(length, width)
     head_all = head_all.reshape(width, -1)
     rest_all = rest_all.reshape(width, -1)
@@ -1286,15 +1785,11 @@
     normed = x_normed_f.astype(low)
     indices = jnp.concatenate([r * block + jnp.arange(block) for r in relative])
     cos_table, sin_table = rope_tables(marks_all[:, 1].reshape(length))
-    allowed = allowed_mask(marks_all[:, 0].reshape(length), indices)
-
+    codes = marks_all[:, 0].reshape(length) * (4 * length) + indices
     qkv = mm(normed_all, qkv_map)
-    queries, keys, values = head_prep(qkv, head_scale, cos_table, sin_table)
-    q_heads = queries.astype(low)
-    k_head = keys[:, 0].astype(low)
-    v_head = values[:, 0].astype(low)
-    head_out, log_total = attend_heads(q_heads, k_head, v_head, allowed)
-    attn_in = head_out.astype(low).reshape(length, q_width)
+    q_heads, k_head, v_head, attn_in, log_total = attend(
+        ranks, qkv, codes, cos_table, sin_table, head_scale.T
+    )
     attn_lin = sum_seq(cut(mm_nt(attn_in, out_map).astype(low)), ranks)
 
     attn_normed, attn_inverse = norm_rows(attn_lin, gain[1])
@@ -1306,14 +1801,15 @@
     h_blocks = gather_seq(h_normed_f.astype(low), ranks)
     h_blocks, per_layer_maps = lax.optimization_barrier((h_blocks, per_layer_maps))
     ple = gather_everywhere(per_layer_maps, ranks, pairs)
-    gate_up = dot(whole_rows(h_blocks), in_maps, ((1,), (0,)))
-    gate_part, up_part = gate_up[:, 0], gate_up[:, 1]
-    hidden = (gelu_tanh(gate_part) * up_part).astype(low)
-    hidden, down_map = lax.optimization_barrier((hidden, down_map))
-    run_middle = middle if ranks == 4 else functools.partial(middle_plain, ranks)
+    run_middle = functools.partial(
+        *((middle, pairs) if ranks == 4 else (middle_plain, ranks))
+    )
     (
         grad_ffn_rows,
         down_grad,
+        down_map,
+        gate_part,
+        up_part,
         hidden_out,
         h_second,
         grad_second,
@@ -1322,8 +1818,9 @@
         grad_ple_gate,
         ffn_gain_grads,
     ) = run_middle(
-        hidden,
-        down_map,
+        h_blocks,
+        in_maps,
+        down_rows,
         mixed,
         gain[4:6],
         ple,
@@ -1336,19 +1833,18 @@
     grad_ffn_rows, down_grad = lax.optimization_barrier((grad_ffn_rows, down_grad))
     grad_hidden = mm(grad_ffn_rows, down_map)
     gate_act, act_pull = jax.vjp(gelu_tanh, gate_part)
-    grad_gate_up = jnp.stack(
-        [act_pull(grad_hidden * up_part)[0], grad_hidden * gate_act], 1
-    ).astype(low)
-    h_part = dot(grad_gate_up, in_maps, ((1, 2), (1, 2))).astype(low)
-    h_parts = cut(h_part)
+    grad_gate = act_pull(grad_hidden * up_part)[0].astype(low)
+    grad_up = (grad_hidden * gate_act).astype(low)
     if ranks == 4:
-        h_parts = [jnp.split(v, 2, axis=1) for v in h_parts]
-    h_blocks, h_parts = lax.optimization_barrier((h_blocks, h_parts))
-    if ranks == 4:
-        h_parts = [jnp.concatenate(v, 1) for v in h_parts]
-    grad_h_normed = sum_seq(h_parts, ranks)
-    in_grad = dot(whole_rows(h_blocks), grad_gate_up, ((0,), (0,))).astype(low)
-    in_sum = lax.psum_scatter(in_grad, "fsdp", scatter_dimension=0, tiled=True)
+        in_grad, grad_h_normed = back(grad_gate, grad_up, in_maps, h_blocks)
+    else:
+        h_part = mm_nt(grad_gate, in_maps[0]) + mm_nt(grad_up, in_maps[1])
+        h_part = h_part.astype(low)
+        grad_h_normed = sum_seq(cut(h_part), ranks)
+        h_rows = whole_rows(h_blocks)
+        in_grad = jnp.stack([mm_tn(h_rows, grad_gate), mm_tn(h_rows, grad_up)]).astype(low)
+    in_sum = lax.psum_scatter(in_grad, "fsdp", scatter_dimension=1, tiled=True)
+    in_sum = jnp.moveaxis(in_sum, 0, 1)
 
     grad_ple_up = mm_tn(grad_ple_low, ple_mixed)
     grad_ple_down = mm_tn(h_second, grad_ple_gate)
@@ -1384,27 +1880,26 @@
     ).astype(low)
     rest_grad = rest_grad.reshape(ranks, -1, rest_grad.shape[1])
     rest_grad, grad_attn_blocks = lax.optimization_barrier((rest_grad, grad_attn_blocks))
-    rest_own = take(rest_grad, 0, rank).astype(full) + sum(
-        permute(take(rest_grad, 0, relative[k]), "seq", k).astype(full) for k in range(1, ranks)
-    )
-    rest_own = rest_own.astype(low).reshape(pairs * 2, rows, -1)
+    rest_others = [permute(take(rest_grad, 0, relative[k]), "seq", k) for k in range(1, ranks)]
     out_grad = weight_grad(ranks, pairs * 2, grad_attn_blocks, attn_in)
     grad_heads = mm(whole_rows(grad_attn_blocks), out_map).astype(low)
-    codes = marks_all[:, 0].reshape(length) * (4 * length) + indices
     grad_qkv, grad_gains = attend_back(
         ranks,
         qkv,
-        q_heads.reshape(length, q_width),
+        q_heads,
         k_head,
         v_head,
         grad_heads,
         log_total,
         codes,
-        cos_table[:, 0, : HEAD_DIM // 2],
-        sin_table[:, 0, : HEAD_DIM // 2],
+        cos_table,
+        sin_table,
         head_scale.T,
     )
     grad_head_scale = grad_gains[:2].T
+    rest_others, grad_qkv = lax.optimization_barrier((rest_others, grad_qkv))
+    rest_own = sum((v.astype(full) for v in rest_others), take(rest_grad, 0, rank).astype(full))
+    rest_own = rest_own.astype(low).reshape(pairs * 2, rows, -1)
     head_scale_grad = jnp.pad(
         grad_head_scale.reshape(-1, head_rows, 2), ((0, 0), (0, rows - head_rows), (0, 0))
     ).reshape(width, 2)

time: 772 us -> 749 us (0.970)
  Pallas kernels: 275 us -> 463 us
  matrix products: 131 us -> 43.3 us
  waiting for transfers between devices: 158 us -> 92.7 us
  local copies, waits for them, and re-layouts: 76.4 us -> 46.7 us
  other arithmetic: 65.4 us -> 42.8 us
    pallas_call x1 -> x3, Pallas kernels: 95.5 us -> 232 us  [the longest x1 151 us: middle(): pl.pallas_call(functools.partial(middle_kernel, pairs, block, parts), out...]
    dot_general x16 -> x13, matrix products: 126 us -> 43.3 us  [dot(): lax.dot_general(left, right, (over, ((), ())), preferred_element_type=full)]
    pallas_call x1, Pallas kernels: 90.5 us -> 135 us  [finish(): pl.pallas_call(functools.partial(finish_kernel, sizes, x is not None), ou...]
    ppermute x30 -> x24, waiting for transfers between devices: 128 us -> 88.5 us  [permute(): return lax.ppermute(v, axis, [(i, i ^ offset) for i in range(size)])]
    all_gather x2 -> x1, waiting for transfers between devices: 29 us -> 4.22 us  [body(): in_maps = lax.all_gather(in_rows, 'fsdp', axis=1, tiled=True)]
    unnamed x263 -> x143, local copies, waits for them, and re-layouts: 24.7 us -> 14 us
    ppermute x30 -> x24, starting transfers between devices: 38.2 us -> 34 us  [permute(): return lax.ppermute(v, axis, [(i, i ^ offset) for i in range(size)])]
  transfers between devices with their start and end apart: 34 -> 27, of which waited for: 20 -> 16; matrix products, arithmetic and copies ran while one was open for 32% -> 15% of each run, Pallas kernels for 16% -> 35%
where the time goes in v6:
time: 749 us; the launch traced here: 738 us
  Pallas kernels  463 us (62%)
  waiting for transfers between devices  92.7 us (12%)
  local copies, waits for them, and re-layouts  46.7 us (6%)
  matrix products  43.3 us (6%)
  other arithmetic  42.8 us (6%)
  starting transfers between devices  34.1 us (5%)
  between operations  15.3 us (2%)
    pallas_call x1, Pallas kernels, middle(): pl.pallas_call(functools.partial(middle_kernel, pairs, block, parts), out...  151 us
    pallas_call x1, Pallas kernels, finish(): pl.pallas_call(functools.partial(finish_kernel, sizes, x is not None), ou...  135 us
    ppermute x24, waiting for transfers between devices, permute(): return lax.ppermute(v, axis, [(i, i ^ offset) for i in range(size)])  88.5 us
    pallas_call x1, Pallas kernels, back(): pl.pallas_call(functools.partial(back_kernel, block), out_shape=(jax.Shap...  65.1 us
    pallas_call x1, Pallas kernels, gather_weights(): pl.pallas_call(functools.partial(gather_kernel, sizes), out_shape=(jax.Sh...  56.5 us
    dot_general x13, matrix products, dot(): lax.dot_general(left, right, (over, ((), ())), preferred_element_type=full)  43.3 us
    ppermute x24, starting transfers between devices, permute(): return lax.ppermute(v, axis, [(i, i ^ offset) for i in range(size)])  34 us
    pallas_call x2, Pallas kernels, weight_grad(): pl.pallas_call(functools.partial(weight_grad_kernel, len(lefts), half_til...  21.9 us
  transfers between devices with their start and end apart: 27, of which 16 were waited for; matrix products, arithmetic and copies ran while one was open for 15% of the time, Pallas kernels for 35%

profile of v6, /device:TPU:20, one launch (start us, length us, event | category | flops | bytes accessed | tf_op | source)
XLA Modules:
  0.0 738.2 jit_solution(17601254266614937130)
XLA Ops:
  7.2 3.2 slice_bitcast_fusion
  10.5 2.4 slice_bitcast_fusion.1.shard_ref
  15.3 56.5 %shard_map.221 = (bf16[4,4,2,64,1536]{4,3,2,1,0:T(8,128)(2,1)}, bf16[4,4,2,64,256]{4,3,2,1,0:T(8,128)(2,1)}, s32[4,8,256]{2,1,0:T(8,128)}, bf16[4,256,2048]{2,1,0:T(8,128)(2,1)}) custom-call(bf16[4,64,1536]{2,1,0:T(8,128)(2,1)} %pad_maximum_fusion.3.head_ref, bf16[64,256]{1,0:T(8,128)(2,1)} %fusion.49.rest_ref, s32[8,256]{1,0:T(8,128)} %pad.31.mark_ref, ...), custom_call_target="tpu_custom_call" | custom-call | tf_op jit(solution)/shard_map/pallas_call | solution.py:239
  71.9 3.2 multiply_reduce_fusion
  76.8 1.9 multiply_sine_fusion
  78.7 3.1 slice_reduce_fusion.1
  83.9 4.5 fusion.20.qkv_ref
  88.4 16.3 %shard_map.222 = (bf16[1024,512]{1,0:T(8,128)(2,1)S(1)}, bf16[1024,256]{1,0:T(8,128)(2,1)S(1)}, bf16[1024,256]{1,0:T(8,128)(2,1)S(1)}, bf16[1024,512]{1,0:T(8,128)(2,1)S(1)}, f32[2,1024,1]{2,1,0:T(8,128)S(1)}) custom-call(f32[1024,1024]{1,0:T(8,128)S(1)} %fusion.20.qkv_ref, s32[1024,1]{1,0:T(8,128)S(1)} %copy.71.code_col_ref, ...), custom_call_target="tpu_custom_call" | custom-call | flops 1207959552 | bytes 12582912 | tf_op jit(solution)/shard_map/pallas_call | solution.py:471
  104.7 2.4 convolution_convert_fusion
  110.3 12.0 %collective-permute-done.1 = bf16[256,1024]{1,0:T(8,128)(2,1)S(1)} collective-permute-done((bf16[256,1024]{1,0:T(8,128)(2,1)S(1)}, bf16[256,1024]{1,0:T(8,128)(2,1)S(1)}, u32[]{:S(2)}, u32[]{:S(2)}) %collective-permute-start.1) | collective-permute-done | bytes 524320 | tf_op jit(solution)/shard_map/ppermute | solution.py:266
  124.9 5.5 collective-permute-done
  130.5 7.0 collective-permute-done.2
  140.1 3.1 collective-permute-done.3
  143.2 6.1 collective-permute-done.5
  149.8 2.6 broadcast_multiply_fusion
  155.5 19.7 %collective-permute-done.6.rows_x_in.rows_x = bf16[256,2048]{1,0:T(8,128)(2,1)S(1)} collective-permute-done((bf16[256,2048]{1,0:T(8,128)(2,1)S(1)}, bf16[256,2048]{1,0:T(8,128)(2,1)S(1)}, u32[]{:S(2)}, u32[]{:S(2)}) %collective-permute-start.6) | collective-permute-done | bytes 1048608 | tf_op jit(solution)/shard_map/ppermute | solution.py:266
  177.3 7.3 collective-permute-done.8.rows_left_in.rows_left
  186.5 10.3 %collective-permute-start.11 = (bf16[64,512]{1,0:T(8,128)(2,1)S(1)}, bf16[64,512]{1,0:T(8,128)(2,1)S(1)}, u32[]{:S(2)}, u32[]{:S(2)}) collective-permute-start(bf16[64,512]{1,0:T(8,128)(2,1)S(1)} %copy-done.50), channel_id=1, source_target_pairs={{0,4},{1,5},{2,6},{3,7},{4,0},{5,1},{6,2},{7,3},{8,12},{9,13},{10,... | collective-permute-start | bytes 196616 | tf_op jit(solution)/shard_map/ppermute | solution.py:266
  197.1 6.2 collective-permute-done.11
  203.3 1.9 collective-permute-done.10
  209.0 5.2 collective-permute-done.15
  214.1 2.2 collective-permute-done.14
  218.4 2.4 collective-permute-done.16
  220.7 2.0 fusion.39
  224.7 4.2 all-gather.2.cloned.1.call-done.in_maps_ref.maps_ref
  228.9 151.1 %shard_map.223 = (bf16[4,256,2048]{2,1,0:T(8,128)(2,1)}, bf16[2048,2048]{1,0:T(8,128)(2,1)}, bf16[2048,2048]{1,0:T(8,128)(2,1)}, f32[1024,2048]{1,0:T(8,128)}, f...) custom-call(bf16[256,2048]{1,0:T(8,128)(2,1)} %copy-done.32, ...), custom_call_target="tpu_custom_call" | custom-call | flops 17179869184 | bytes 104857600 | tf_op jit(solution)/shard_map/pallas_call | solution.py:1165
  380.1 12.6 %fusion.60 = f32[1024,2048]{1,0:T(8,128)S(1)} fusion(bf16[1024,2048]{1,0:T(8,128)(2,1)} %bitcast.190, bf16[2048,2048]{1,0:T(8,128)(2,1)} %get-tuple-element.89), kind=kOutput, calls=%fused_computation.160 | convolution fusion | flops 8589934592 | bytes 20971520 | tf_op jit(solution)/shard_map/dot_general | solution.py:324
  392.8 8.2 %multiply_convert_fusion = (bf16[1024,2048]{1,0:T(8,128)(2,1)}, bf16[1024,2048]{1,0:T(8,128)(2,1)}) fusion(f32[1024,2048]{1,0:T(8,128)S(1)} %fusion.60, f32[1024,2048]{1,0:T(8,128)S(1)} %bitcast.134, f32[1024,2048]{1,0:T(8,128)S(1)} %bitcast.136), kind=kLoop, calls=%fused_computation.12 | loop fusion | flops 50331648 | bytes 33554432 | tf_op jit(solution)/shard_map/convert_element_type | solution.py:1837
  401.0 65.1 %shard_map.224 = (bf16[2,2048,2048]{2,1,0:T(8,128)(2,1)}, f32[256,2048]{1,0:T(8,128)}) custom-call(bf16[1024,2048]{1,0:T(8,128)(2,1)} %get-tuple-element.183.gate_ref, bf16[1024,2048]{1,0:T(8,128)(2,1)} %get-tuple-element.182.up_ref, bf16[2,2048,2048]{2,1,0:T(8,128)(2,1)} %all-gather.2.cloned.1.call-done.in_maps_ref.maps_ref, bf16[256,2048]{1,0:T(8,128)(2,1)} %copy-done.32, ...), custom_call_target="tpu_custom_call" | custom-call | flops 34359738368 | bytes 52428800 | tf_op jit(solution)/shard_map/pallas_call | solution.py:1420
  466.2 2.3 copy.81
  468.5 2.9 multiply_reduce_fusion.2
  472.1 4.0 multiply_reduce_fusion.1
  476.1 2.1 multiply_convert_fusion.1
  484.8 3.8 fusion.27
  490.0 8.6 %collective-permute-done.17.refs_1_ = bf16[256,2048]{1,0:T(8,128)(2,1)} collective-permute-done((bf16[256,2048]{1,0:T(8,128)(2,1)}, bf16[256,2048]{1,0:T(8,128)(2,1)}, u32[]{:S(2)}, u32[]{:S(2)}) %collective-permute-start.17) | collective-permute-done | bytes 1048608 | tf_op jit(solution)/shard_map/ppermute | solution.py:266
  498.7 1.9 slice.210
  502.0 1.9 slice.211
  507.3 6.1 concatenate.91
  513.5 3.1 dynamic-slice_bitcast_fusion
  516.6 1.9 collective-permute-start.21
  520.7 5.9 fusion.33.grad_ref
  526.6 17.1 %shard_map.225 = (bf16[1024,1024]{1,0:T(8,128)(2,1)S(1)}, f32[8,256]{1,0:T(8,128)S(1)}) custom-call(f32[1024,1024]{1,0:T(8,128)S(1)} %copy-done.1, bf16[1024,512]{1,0:T(8,128)(2,1)S(1)} %copy-done.6, bf16[1024,256]{1,0:T(8,128)(2,1)S(1)} %copy-done.10, bf16[1024,256]{1,0:T(8,128)(2,1)S(1)} %copy-done.12, bf16[1024,512]{1,0:T(8,128)(2,1)S(1)} %fusion.33.grad_ref, ...), custom_call_target="tpu_custom_call" | custom-call | flops 3019898880 | bytes 16777216 | tf_op jit(solution)/shard_map/pallas_call | solution.py:612
  546.7 8.6 %shard_map.227.refs_1_ = bf16[8,4,64,512]{3,2,1,0:T(8,128)(2,1)} custom-call(bf16[256,2048]{1,0:T(8,128)(2,1)} %get-tuple-element.98.refs_0_, bf16[256,2048]{1,0:T(8,128)(2,1)} %collective-permute-done.17.refs_1_, bf16[256,2048]{1,0:T(8,128)(2,1)} %collective-permute-done.18.refs_2_, bf16[256,1024]{1,0:T(8,128)(2,1)} %collective-permute-done.19.refs_3_, ...), custom_call_target="tpu_custom_call" | custom-call | flops 2147483648 | bytes 7340032 | tf_op jit(solution)/shard_map/pallas_call | solution.py:673
  555.3 13.4 %shard_map.226.refs_0_ = bf16[8,4,64,1152]{3,2,1,0:T(8,128)(2,1)} custom-call(bf16[1024,2048]{1,0:T(8,128)(2,1)} %copy-done.24, bf16[1024,1024]{1,0:T(8,128)(2,1)} %copy-done.2, bf16[2048,1536]{1,0:T(8,128)(2,1)} %bitcast.138, f32[2048,1]{1,0:T(8,128)} %get-tuple-element.200.refs_3_, f32[2048,128]{1,0:T(8,128)} %pad.35.refs_4_), custom_call_target="tpu_custom_call" | custom-call | flops 4294967296 | bytes 10485760 | tf_op jit(solution)/shard_map/pallas_call | solution.py:673
  568.7 2.9 fusion.32
  571.5 8.4 %convolution_convert_fusion.1 = bf16[1024,2048]{1,0:T(8,128)(2,1)} fusion(bf16[1024,1024]{1,0:T(8,128)(2,1)S(1)} %copy-done.3, bf16[2048,1536]{1,0:T(8,128)(2,1)} %bitcast.139), kind=kOutput, calls=%fused_computation.25 | convolution fusion | flops 4297064448 | bytes 10485760 | tf_op jit(solution)/shard_map/dot_general | solution.py:324
  580.6 135.2 %shard_map.228 = (f32[64,2048]{1,0:T(8,128)}, f32[64,512]{1,0:T(8,128)}, f32[64,512]{1,0:T(8,128)}, f32[64,2048]{1,0:T(8,128)}, f32[64,512]{1,0:T(8,128)}, /*ind...) custom-call(bf16[8,4,64,1152]{3,2,1,0:T(8,128)(2,1)} %shard_map.226.refs_0_, ...), custom_call_target="tpu_custom_call" | custom-call | tf_op jit(solution)/shard_map/pallas_call | solution.py:1711
  718.6 5.1 maximum_convert_fusion
  (261 shorter events, 59.5 us)
Async XLA Ops:
  7.2 221.7 %all-gather.2.cloned.1.call-start = ((), (), s32[]{:S(2)}) async-start(), calls=%async_computation.2 | async-start | bytes 18874368 | tf_op jit(solution)/shard_map/all_gather | solution.py:1771
  71.8 646.7 %reduce-scatter.5.cloned.1.call-start = ((), (), s32[]{:S(2)}) async-start(), calls=%async_computation.4 | async-start | bytes 9437184 | tf_op jit(solution)/shard_map/reduce_scatter | solution.py:1832
  88.4 16.3 %copy-start = (f32[1024,1024]{1,0:T(8,128)}, f32[1024,1024]{1,0:T(8,128)S(1)}, u32[]{:S(2)}) copy-start(f32[1024,1024]{1,0:T(8,128)S(1)} %fusion.20.qkv_ref) | copy-start | bytes 12582916
  107.1 17.5 %copy-start.18 = (bf16[256,1,2048]{2,0,1:T(8,128)(2,1)S(1)}, bf16[256,1,2048]{2,0,1:T(8,128)(2,1)}, u32[]{:S(2)}) copy-start(bf16[256,1,2048]{2,0,1:T(8,128)(2,1)} %param.14) | copy-start | bytes 3145732
  107.4 14.9 %collective-permute-start.1 = (bf16[256,1024]{1,0:T(8,128)(2,1)S(1)}, bf16[256,1024]{1,0:T(8,128)(2,1)S(1)}, u32[]{:S(2)}, u32[]{:S(2)}) collective-permute-start(bf16[256,1024]{1,0:T(8,128)(2,1)S(1)} %get-tuple-element.189), channel_id=1, source_target_pairs={{0,8},{8,0},{16,24},{24,16},{1,9},{9,1},{17,25},{25,17},{2,10},{10... | collective-permute-start | bytes 1572872 | tf_op jit(solution)/shard_map/ppermute | solution.py:266
  108.4 22.1 %collective-permute-start = (bf16[256,1024]{1,0:T(8,128)(2,1)S(1)}, bf16[256,1024]{1,0:T(8,128)(2,1)S(1)}, u32[]{:S(2)}, u32[]{:S(2)}) collective-permute-start(bf16[256,1024]{1,0:T(8,128)(2,1)S(1)} %get-tuple-element.186), channel_id=1, source_target_pairs={{0,8},{8,0},{16,24},{24,16},{1,9},{9,1},{17,25},{25,17},{2,10},{10... | collective-permute-start | bytes 1572872 | tf_op jit(solution)/shard_map/ppermute | solution.py:266
  109.5 21.0 %collective-permute-start.4 = (bf16[256,1024]{1,0:T(8,128)(2,1)S(1)}, bf16[256,1024]{1,0:T(8,128)(2,1)S(1)}, u32[]{:S(2)}, u32[]{:S(2)}) collective-permute-start(bf16[256,1024]{1,0:T(8,128)(2,1)S(1)} %get-tuple-element.187), channel_id=1, source_target_pairs={{0,16},{8,24},{16,0},{24,8},{1,17},{9,25},{17,1},{25,9},{2,18},{10... | collective-permute-start | bytes 1572872 | tf_op jit(solution)/shard_map/ppermute | solution.py:266
  122.5 14.9 %collective-permute-start.2 = (bf16[256,1024]{1,0:T(8,128)(2,1)S(1)}, bf16[256,1024]{1,0:T(8,128)(2,1)S(1)}, u32[]{:S(2)}, u32[]{:S(2)}) collective-permute-start(bf16[256,1024]{1,0:T(8,128)(2,1)S(1)} %add_convert_fusion.1), channel_id=1, source_target_pairs={{0,16},{8,24},{16,0},{24,8},{1,17},{9,25},{17,1},{25,9},{2,18},{10... | collective-permute-start | bytes 1572872 | tf_op jit(solution)/shard_map/ppermute | solution.py:266
  123.4 19.8 %collective-permute-start.3 = (bf16[256,1024]{1,0:T(8,128)(2,1)S(1)}, bf16[256,1024]{1,0:T(8,128)(2,1)S(1)}, u32[]{:S(2)}, u32[]{:S(2)}) collective-permute-start(bf16[256,1024]{1,0:T(8,128)(2,1)S(1)} %get-tuple-element.188), channel_id=1, source_target_pairs={{0,16},{8,24},{16,0},{24,8},{1,17},{9,25},{17,1},{25,9},{2,18},{10... | collective-permute-start | bytes 1572872 | tf_op jit(solution)/shard_map/ppermute | solution.py:266
  124.9 14.0 %copy-start.28 = (bf16[4,4,2,64,256]{4,3,2,1,0:T(8,128)(2,1)S(1)}, bf16[4,4,2,64,256]{4,3,2,1,0:T(8,128)(2,1)}, u32[]{:S(2)}) copy-start(bf16[4,4,2,64,256]{4,3,2,1,0:T(8,128)(2,1)} %get-tuple-element.67) | copy-start | bytes 3145732
  137.9 11.9 %copy-start.22 = (f32[256,1024]{1,0:T(8,128)}, f32[256,1024]{1,0:T(8,128)S(1)}, u32[]{:S(2)}) copy-start(f32[256,1024]{1,0:T(8,128)S(1)} %get-tuple-element.184) | copy-start | bytes 3145732
  137.9 11.4 %collective-permute-start.5 = (bf16[256,1024]{1,0:T(8,128)(2,1)S(1)}, bf16[256,1024]{1,0:T(8,128)(2,1)S(1)}, u32[]{:S(2)}, u32[]{:S(2)}) collective-permute-start(bf16[256,1024]{1,0:T(8,128)(2,1)S(1)} %get-tuple-element.185), channel_id=1, source_target_pairs={{0,8},{8,0},{16,24},{24,16},{1,9},{9,1},{17,25},{25,17},{2,10},{10... | collective-permute-start | bytes 1572872 | tf_op jit(solution)/shard_map/ppermute | solution.py:266
  140.1 9.7 %copy-start.15 = (f32[256,2048]{1,0:T(8,128)}, f32[256,2048]{1,0:T(8,128)S(1)}, u32[]{:S(2)}) copy-start(f32[256,2048]{1,0:T(8,128)S(1)} %get-tuple-element.226) | copy-start | bytes 6291460
  152.7 32.8 %copy-start.50 = (bf16[64,512]{1,0:T(8,128)(2,1)S(1)}, bf16[64,512]{1,0:T(8,128)(2,1)}, u32[]{:S(2)}) copy-start(bf16[64,512]{1,0:T(8,128)(2,1)} %param.24) | copy-start | bytes 196612
  153.8 21.5 %collective-permute-start.6 = (bf16[256,2048]{1,0:T(8,128)(2,1)S(1)}, bf16[256,2048]{1,0:T(8,128)(2,1)S(1)}, u32[]{:S(2)}, u32[]{:S(2)}) collective-permute-start(bf16[256,2048]{1,0:T(8,128)(2,1)S(1)} %multiply_convert_fusion.3.rows_own), channel_id=1, source_target_pairs={{0,8},{8,0},{16,24},{24,16},{1,9},{9,1},{17,25},{25,17},{2,10},{10... | collective-permute-start | bytes 3145736 | tf_op jit(solution)/shard_map/ppermute | solution.py:266
  154.8 21.4 %collective-permute-start.7 = (bf16[256,2048]{1,0:T(8,128)(2,1)S(1)}, bf16[256,2048]{1,0:T(8,128)(2,1)S(1)}, u32[]{:S(2)}, u32[]{:S(2)}) collective-permute-start(bf16[256,2048]{1,0:T(8,128)(2,1)S(1)} %multiply_convert_fusion.3.rows_own), channel_id=1, source_target_pairs={{0,16},{8,24},{16,0},{24,8},{1,17},{9,25},{17,1},{25,9},{2,18},{10... | collective-permute-start | bytes 3145736 | tf_op jit(solution)/shard_map/ppermute | solution.py:266
  175.3 9.2 %collective-permute-start.8 = (bf16[256,1024]{1,0:T(8,128)(2,1)S(1)}, bf16[256,1024]{1,0:T(8,128)(2,1)S(1)}, u32[]{:S(2)}, u32[]{:S(2)}) collective-permute-start(bf16[256,1024]{1,0:T(8,128)(2,1)S(1)} %slice.202), channel_id=1, source_target_pairs={{0,16},{8,24},{16,0},{24,8},{1,17},{9,25},{17,1},{25,9},{2,18},{10... | collective-permute-start | bytes 1572872 | tf_op jit(solution)/shard_map/ppermute | solution.py:266
  176.2 9.3 %copy-start.39 = (bf16[256,2048]{1,0:T(8,128)(2,1)}, bf16[256,2048]{1,0:T(8,128)(2,1)S(1)}, u32[]{:S(2)}) copy-start(bf16[256,2048]{1,0:T(8,128)(2,1)S(1)} %collective-permute-done.7.rows_y_in.rows_y) | copy-start | bytes 3145732
  176.3 9.2 %collective-permute-start.9 = (bf16[256,1024]{1,0:T(8,128)(2,1)S(1)}, bf16[256,1024]{1,0:T(8,128)(2,1)S(1)}, u32[]{:S(2)}, u32[]{:S(2)}) collective-permute-start(bf16[256,1024]{1,0:T(8,128)(2,1)S(1)} %slice.203), channel_id=1, source_target_pairs={{0,8},{8,0},{16,24},{24,16},{1,9},{9,1},{17,25},{25,17},{2,10},{10... | collective-permute-start | bytes 1572872 | tf_op jit(solution)/shard_map/ppermute | solution.py:266
  185.5 11.3 %copy-start.58 = (bf16[256,1024]{1,0:T(8,128)(2,1)}, bf16[256,1024]{1,0:T(8,128)(2,1)S(1)}, u32[]{:S(2)}) copy-start(bf16[256,1024]{1,0:T(8,128)(2,1)S(1)} %collective-permute-done.9.rows_right_in.rows_right) | copy-start | bytes 1572868
  185.5 11.6 %collective-permute-start.12 = (bf16[64,512]{1,0:T(8,128)(2,1)S(1)}, bf16[64,512]{1,0:T(8,128)(2,1)S(1)}, u32[]{:S(2)}, u32[]{:S(2)}) collective-permute-start(bf16[64,512]{1,0:T(8,128)(2,1)S(1)} %copy-done.50), channel_id=1, source_target_pairs={{0,6},{1,7},{2,4},{3,5},{4,2},{5,3},{6,0},{7,1},{8,14},{9,15},{10,... | collective-permute-start | bytes 196616 | tf_op jit(solution)/shard_map/ppermute | solution.py:266
  186.5 16.8 %collective-permute-start.11 = (bf16[64,512]{1,0:T(8,128)(2,1)S(1)}, bf16[64,512]{1,0:T(8,128)(2,1)S(1)}, u32[]{:S(2)}, u32[]{:S(2)}) collective-permute-start(bf16[64,512]{1,0:T(8,128)(2,1)S(1)} %copy-done.50), channel_id=1, source_target_pairs={{0,4},{1,5},{2,6},{3,7},{4,0},{5,1},{6,2},{7,3},{8,12},{9,13},{10,... | collective-permute-start | bytes 196616 | tf_op jit(solution)/shard_map/ppermute | solution.py:266
  196.9 8.4 %collective-permute-start.10 = (bf16[64,512]{1,0:T(8,128)(2,1)S(1)}, bf16[64,512]{1,0:T(8,128)(2,1)S(1)}, u32[]{:S(2)}, u32[]{:S(2)}) collective-permute-start(bf16[64,512]{1,0:T(8,128)(2,1)S(1)} %copy-done.50), channel_id=1, source_target_pairs={{0,2},{1,3},{2,0},{3,1},{4,6},{5,7},{6,4},{7,5},{8,10},{9,11},{10,... | collective-permute-start | bytes 196616 | tf_op jit(solution)/shard_map/ppermute | solution.py:266
  205.4 8.7 %collective-permute-start.15 = (bf16[4,64,512]{2,1,0:T(8,128)(2,1)S(1)}, bf16[4,64,512]{2,1,0:T(8,128)(2,1)S(1)}, u32[]{:S(2)}, u32[]{:S(2)}) collective-permute-start(bf16[4,64,512]{2,1,0:T(8,128)(2,1)S(1)} %get-tuple-element.208), channel_id=1, source_target_pairs={{0,24},{8,16},{16,8},{24,0},{1,25},{9,17},{17,9},{25,1},{2,26},{10... | collective-permute-start | bytes 786440 | tf_op jit(solution)/shard_map/ppermute | solution.py:266
  206.2 10.1 %collective-permute-start.14 = (bf16[4,64,512]{2,1,0:T(8,128)(2,1)S(1)}, bf16[4,64,512]{2,1,0:T(8,128)(2,1)S(1)}, u32[]{:S(2)}, u32[]{:S(2)}) collective-permute-start(bf16[4,64,512]{2,1,0:T(8,128)(2,1)S(1)} %get-tuple-element.208), channel_id=1, source_target_pairs={{0,16},{8,24},{16,0},{24,8},{1,17},{9,25},{17,1},{25,9},{2,18},{10... | collective-permute-start | bytes 786440 | tf_op jit(solution)/shard_map/ppermute | solution.py:266
  207.8 8.5 %collective-permute-start.13 = (bf16[4,64,512]{2,1,0:T(8,128)(2,1)S(1)}, bf16[4,64,512]{2,1,0:T(8,128)(2,1)S(1)}, u32[]{:S(2)}, u32[]{:S(2)}) collective-permute-start(bf16[4,64,512]{2,1,0:T(8,128)(2,1)S(1)} %get-tuple-element.208), channel_id=1, source_target_pairs={{0,8},{8,0},{16,24},{24,16},{1,9},{9,1},{17,25},{25,17},{2,10},{10... | collective-permute-start | bytes 786440 | tf_op jit(solution)/shard_map/ppermute | solution.py:266
  217.7 3.0 collective-permute-start.16
  380.0 338.6 %reduce-scatter.3.cloned.1.call-start = ((), (), s32[]{:S(2)}) async-start(), calls=%async_computation.3 | async-start | bytes 18874368 | tf_op jit(solution)/shard_map/reduce_scatter | solution.py:1846
  380.1 12.7 %slice-start = ((s8[8388608]{0:T(1024)(128)(4,1)}), s8[4194304]{0:T(1024)(128)(4,1)S(1)}, s32[]{:S(2)}) async-start(s8[8388608]{0:T(1024)(128)(4,1)} %bitcast.133), calls=%async_computation.5 | async-start | bytes 8388608
  380.1 12.7 %slice-start.2 = ((s8[8388608]{0:T(1024)(128)(4,1)}), s8[4194304]{0:T(1024)(128)(4,1)S(1)}, s32[]{:S(2)}) async-start(s8[8388608]{0:T(1024)(128)(4,1)} %bitcast.135), calls=%async_computation.7 | async-start | bytes 8388608
  380.1 12.7 %slice-start.1 = ((s8[8388608]{0:T(1024)(128)(4,1)}), s8[4194304]{0:T(1024)(128)(4,1)S(1)}, s32[]{:S(2)}) async-start(s8[8388608]{0:T(1024)(128)(4,1)} %bitcast.133), calls=%async_computation.6 | async-start | bytes 8388608
  380.1 12.7 %slice-start.3 = ((s8[8388608]{0:T(1024)(128)(4,1)}), s8[4194304]{0:T(1024)(128)(4,1)S(1)}, s32[]{:S(2)}) async-start(s8[8388608]{0:T(1024)(128)(4,1)} %bitcast.135), calls=%async_computation.8 | async-start | bytes 8388608
  478.3 20.4 %collective-permute-start.17 = (bf16[256,2048]{1,0:T(8,128)(2,1)}, bf16[256,2048]{1,0:T(8,128)(2,1)}, u32[]{:S(2)}, u32[]{:S(2)}) collective-permute-start(bf16[256,2048]{1,0:T(8,128)(2,1)} %get-tuple-element.98.refs_0_), channel_id=1, source_target_pairs={{0,8},{8,0},{16,24},{24,16},{1,9},{9,1},{17,25},{25,17},{2,10},{10... | collective-permute-start | bytes 3145736 | tf_op jit(solution)/shard_map/ppermute | solution.py:266
  479.8 22.2 %collective-permute-start.18 = (bf16[256,2048]{1,0:T(8,128)(2,1)}, bf16[256,2048]{1,0:T(8,128)(2,1)}, u32[]{:S(2)}, u32[]{:S(2)}) collective-permute-start(bf16[256,2048]{1,0:T(8,128)(2,1)} %get-tuple-element.98.refs_0_), channel_id=1, source_target_pairs={{0,16},{8,24},{16,0},{24,8},{1,17},{9,25},{17,1},{25,9},{2,18},{10... | collective-permute-start | bytes 3145736 | tf_op jit(solution)/shard_map/ppermute | solution.py:266
  488.6 16.8 %copy-start.43 = (bf16[256,256]{1,0:T(8,128)(2,1)S(1)}, bf16[256,256]{1,0:T(8,128)(2,1)}, u32[]{:S(2)}) copy-start(bf16[256,256]{1,0:T(8,128)(2,1)} %get-tuple-element.82) | copy-start | bytes 393220
  489.1 16.3 %copy-start.35 = (bf16[256,2048]{1,0:T(8,128)(2,1)S(1)}, bf16[256,2048]{1,0:T(8,128)(2,1)}, u32[]{:S(2)}) copy-start(bf16[256,2048]{1,0:T(8,128)(2,1)} %get-tuple-element.81) | copy-start | bytes 3145732
  490.0 15.8 %copy-start.34 = (bf16[256,2048]{1,0:T(8,128)(2,1)S(1)}, bf16[256,2048]{1,0:T(8,128)(2,1)}, u32[]{:S(2)}) copy-start(bf16[256,2048]{1,0:T(8,128)(2,1)} %get-tuple-element.83) | copy-start | bytes 3145732
  490.0 15.8 %copy-start.42 = (bf16[256,256]{1,0:T(8,128)(2,1)S(1)}, bf16[256,256]{1,0:T(8,128)(2,1)}, u32[]{:S(2)}) copy-start(bf16[256,256]{1,0:T(8,128)(2,1)} %get-tuple-element.84) | copy-start | bytes 393220
  500.5 12.9 %collective-permute-start.19 = (bf16[256,1024]{1,0:T(8,128)(2,1)}, bf16[256,1024]{1,0:T(8,128)(2,1)}, u32[]{:S(2)}, u32[]{:S(2)}) collective-permute-start(bf16[256,1024]{1,0:T(8,128)(2,1)} %slice.210), channel_id=1, source_target_pairs={{0,16},{8,24},{16,0},{24,8},{1,17},{9,25},{17,1},{25,9},{2,18},{10... | collective-permute-start | bytes 1572872 | tf_op jit(solution)/shard_map/ppermute | solution.py:266
  503.9 9.6 %collective-permute-start.20 = (bf16[256,1024]{1,0:T(8,128)(2,1)}, bf16[256,1024]{1,0:T(8,128)(2,1)}, u32[]{:S(2)}, u32[]{:S(2)}) collective-permute-start(bf16[256,1024]{1,0:T(8,128)(2,1)} %slice.211), channel_id=1, source_target_pairs={{0,8},{8,0},{16,24},{24,16},{1,9},{9,1},{17,25},{25,17},{2,10},{10... | collective-permute-start | bytes 1572872 | tf_op jit(solution)/shard_map/ppermute | solution.py:266
  516.6 38.7 %collective-permute-start.21 = (bf16[512,768]{1,0:T(8,128)(2,1)}, bf16[512,768]{1,0:T(8,128)(2,1)S(1)}, u32[]{:S(2)}, u32[]{:S(2)}) collective-permute-start(bf16[512,768]{1,0:T(8,128)(2,1)} %get-tuple-element.192), channel_id=1, source_target_pairs={{0,8},{8,0},{16,24},{24,16},{1,9},{9,1},{17,25},{25,17},{2,10},{10... | collective-permute-start | bytes 2359304 | tf_op jit(solution)/shard_map/ppermute | solution.py:266
  518.4 36.8 %collective-permute-start.22 = (bf16[512,768]{1,0:T(8,128)(2,1)}, bf16[512,768]{1,0:T(8,128)(2,1)S(1)}, u32[]{:S(2)}, u32[]{:S(2)}) collective-permute-start(bf16[512,768]{1,0:T(8,128)(2,1)} %get-tuple-element.191), channel_id=1, source_target_pairs={{0,16},{8,24},{16,0},{24,8},{1,17},{9,25},{17,1},{25,9},{2,18},{10... | collective-permute-start | bytes 2359304 | tf_op jit(solution)/shard_map/ppermute | solution.py:266
  519.1 7.5 %copy-start.1 = (f32[1024,1024]{1,0:T(8,128)S(1)}, f32[1024,1024]{1,0:T(8,128)}, u32[]{:S(2)}) copy-start(f32[1024,1024]{1,0:T(8,128)} %copy-done) | copy-start | bytes 12582916
  519.1 7.5 %copy-start.6 = (bf16[1024,512]{1,0:T(8,128)(2,1)S(1)}, bf16[1024,512]{1,0:T(8,128)(2,1)}, u32[]{:S(2)}) copy-start(bf16[1024,512]{1,0:T(8,128)(2,1)} %copy-done.5) | copy-start | bytes 3145732
  519.1 7.5 %copy-start.8 = (f32[2,1024,1]{2,1,0:T(8,128)S(1)}, f32[2,1024,1]{2,1,0:T(8,128)}, u32[]{:S(2)}) copy-start(f32[2,1024,1]{2,1,0:T(8,128)} %copy-done.7) | copy-start | bytes 24580
  519.1 7.5 %copy-start.10 = (bf16[1024,256]{1,0:T(8,128)(2,1)S(1)}, bf16[1024,256]{1,0:T(8,128)(2,1)}, u32[]{:S(2)}) copy-start(bf16[1024,256]{1,0:T(8,128)(2,1)} %copy-done.9) | copy-start | bytes 1572868
  519.1 7.5 %copy-start.12 = (bf16[1024,256]{1,0:T(8,128)(2,1)S(1)}, bf16[1024,256]{1,0:T(8,128)(2,1)}, u32[]{:S(2)}) copy-start(bf16[1024,256]{1,0:T(8,128)(2,1)} %copy-done.11) | copy-start | bytes 1572868
  519.1 36.1 %collective-permute-start.23 = (bf16[512,768]{1,0:T(8,128)(2,1)}, bf16[512,768]{1,0:T(8,128)(2,1)}, u32[]{:S(2)}, u32[]{:S(2)}) collective-permute-start(bf16[512,768]{1,0:T(8,128)(2,1)} %get-tuple-element.190), channel_id=1, source_target_pairs={{0,24},{8,16},{16,8},{24,0},{1,25},{9,17},{17,9},{25,1},{2,26},{10... | collective-permute-start | bytes 2359304 | tf_op jit(solution)/shard_map/ppermute | solution.py:266
  (44 other events, 130.3 us)
Sparse Core Ops, SparseCore 0:
  72.0 156.8 all-gather.1
  380.1 91.6 reduce-scatter.4
  474.2 190.5 reduce-scatter.2

commit v7 on v6

--- a/solution.py
+++ b/solution.py
@@ -33,7 +33,19 @@
 
 
 def gather_kernel(
-    sizes, head_ref, rest_ref, mark_ref, x_ref, head_out, rest_out, mark_out, x_out, *sems
+    sizes,
+    head_ref,
+    rest_ref,
+    mark_ref,
+    x_ref,
+    planes_ref,
+    head_out,
+    rest_out,
+    mark_out,
+    x_out,
+    planes_out,
+    planes,
+    *sems,
 ):
     (local, head_s1, head_r1, right_s, right_r, left_s, left_r, head_s3, head_r3) = sems[:9]
     (rest_s1, rest_r1, rest_s2, rest_r2, rest_s3, rest_r3, mark_s, mark_r, x_s, x_r) = sems[9:]
@@ -59,6 +71,8 @@
             device_id_type=MESH,
         )
 
+    load = pltpu.make_async_copy(planes_ref.at[pl.ds(0, 2)], planes, local.at[4])
+    load.start()
     barrier = pltpu.get_barrier_semaphore()
     devices = [on_seq(i) for i in range(1, ranks)] + [on_pair(i) for i in range(1, pairs)]
     for device in devices + [sibling]:
@@ -165,6 +179,9 @@
                 go(remote(x_ref, x_out.at[i], x_s.at[i - 1], x_r.at[i - 1], on_seq(i)))
             )
 
+    load.wait()
+    store = pltpu.make_async_copy(planes, planes_out, local.at[4])
+    store.start()
     owns[1].wait()
     for copy in rest_pair:
         copy.wait_recv()
@@ -217,6 +234,7 @@
         row = rest_out.at[flip(rank, i, ranks), :, core]
         rest_core.append(go(remote(row, row, rest_s3.at[i], rest_r3.at[i], sibling)))
     owns[0].wait()
+    store.wait()
     for copy in owns[2:]:
         copy.wait()
     for copy in marks + x_seq[2 if ranks == 4 else 0 :] + relays + rest_core:
@@ -232,7 +250,7 @@
         copy.wait_send()
 
 
-def gather_weights(sizes, head, rest, marks, x):
+def gather_weights(sizes, head, rest, marks, x, planes):
     ranks, pairs = sizes["seq"], sizes["pair"]
     dma = lambda n: pltpu.SemaphoreType.DMA((n,))
     anywhere = pl.BlockSpec(memory_space=pl.ANY)
@@ -243,11 +261,13 @@
             jax.ShapeDtypeStruct((ranks, pairs, 2) + rest.shape, rest.dtype),
             jax.ShapeDtypeStruct((ranks,) + marks.shape, marks.dtype),
             jax.ShapeDtypeStruct((ranks,) + x.shape, x.dtype),
+            jax.ShapeDtypeStruct((2,) + planes.shape[1:], planes.dtype),
         ),
-        in_specs=[anywhere] * 4,
-        out_specs=(anywhere,) * 4,
+        in_specs=[anywhere] * 5,
+        out_specs=(anywhere,) * 5,
         scratch_shapes=[
-            dma(4),
+            pltpu.VMEM((2,) + planes.shape[1:], planes.dtype),
+            dma(5),
             *[dma(ranks - 1)] * 2,
             *[dma((pairs - 1) * ranks)] * 4,
             *[dma((2 * pairs - 1) * ranks)] * 2,
@@ -258,7 +278,7 @@
             *[dma(2 * ranks - 2)] * 2,
         ],
         compiler_params=pltpu.CompilerParams(collective_id=0, has_side_effects=True),
-    )(head, rest, marks, x)
+    )(head, rest, marks, x, planes)
 
 
 def permute(v, axis, offset):
@@ -633,7 +653,8 @@
 
 
 def weight_grad_kernel(count, half_tiles, *refs):
-    lefts, right_ref, out_ref = refs[:count], refs[count], refs[-1]
+    lefts, right_ref = refs[:count], refs[count]
+    out_ref = refs[-1] if len(refs) == count + 2 else refs[-2]
     pieces = [ref[...] for ref in lefts]
     if half_tiles:
         pieces[-2:] = [jnp.where(pl.program_id(0) < half_tiles, pieces[-2], pieces[-1])]
@@ -648,7 +669,9 @@
         of_gain = jnp.sum(maps * result, -1, keepdims=True) / gain_ref[...]
         late = late_ref[...]
         lane = lax.broadcasted_iota(jnp.int32, late.shape, 1)
-        result = jnp.concatenate([result, jnp.where(lane == 0, of_gain, late)], 1)
+        split = result.shape[1] - 2 * HEAD_DIM
+        refs[-1][...] = result[:, split:].astype(low).reshape(refs[-1].shape)
+        result = jnp.concatenate([result[:, :split], jnp.where(lane == 0, of_gain, late)], 1)
     out_ref[...] = result.astype(low).reshape(out_ref.shape)
 
 
@@ -658,7 +681,7 @@
     rows = width // (ranks * parts)
     tile = max(min(256, rows * parts), rows)
     each = tile // rows
-    wide = columns + (128 if extras else 0)
+    wides = [columns + 128 - 2 * HEAD_DIM, 2 * HEAD_DIM] if extras else [columns]
     half_tiles = lefts[-1].shape[1] // tile if lefts[-1].shape[1] < width else 0
 
     def place(i):
@@ -670,14 +693,14 @@
             pl.BlockSpec((lefts[-1].shape[0], tile), lambda i: (0, jnp.minimum(i, half_tiles - 1))),
             pl.BlockSpec((lefts[-1].shape[0], tile), lambda i: (0, jnp.maximum(i - half_tiles, 0))),
         ]
-    return pl.pallas_call(
+    results = pl.pallas_call(
         functools.partial(weight_grad_kernel, len(lefts), half_tiles),
         grid=(width // tile,),
-        out_shape=jax.ShapeDtypeStruct((parts, ranks, rows, wide), low),
+        out_shape=tuple(jax.ShapeDtypeStruct((parts, ranks, rows, n), low) for n in wides),
         in_specs=left_specs
         + [pl.BlockSpec((length, columns), lambda i: (0, 0))]
         + [pl.BlockSpec((tile, v.shape[1]), lambda i: (i, 0)) for v in extras],
-        out_specs=pl.BlockSpec((each, 1, rows, wide), place),
+        out_specs=tuple(pl.BlockSpec((each, 1, rows, n), place) for n in wides),
         compiler_params=pltpu.CompilerParams(vmem_limit_bytes=60 << 20),
         cost_estimate=pl.CostEstimate(
             flops=2 * length * width * columns,
@@ -685,6 +708,7 @@
             transcendentals=0,
         ),
     )(*lefts, right, *extras)
+    return results if extras else results[0]
 
 
 def middle_kernel(
@@ -764,7 +788,8 @@
     half = width // 2
     tile = 256
     tiles = span // tile
-    shard = shard_ref.shape[0]
+    shard = shard_ref.shape[1]
+    shard_ref = shard_ref.at[2]
     cut = shard // 2
     left, right = slice(0, half), slice(half, width)
     up = lambda v: v.astype(full)
@@ -1139,10 +1164,10 @@
             pl.when(sends_left(t))(lambda t=t, k=k: pass_left(t, k).wait_send())
 
 
-def middle(pairs, h_blocks, in_maps, down_rows, mixed, gains, ple, ple_input, cotangent):
+def middle(pairs, h_blocks, in_maps, planes, mixed, gains, ple, ple_input, cotangent):
     block, width = mixed.shape
     span = in_maps.shape[2]
-    shard = down_rows.shape[0]
+    shard = planes.shape[1]
     parts, length = 2, 4 * block
     count = 2 * pairs
     dma = lambda *n: pltpu.SemaphoreType.DMA(n)
@@ -1201,7 +1226,7 @@
     )(
         *h_blocks,
         in_maps,
-        down_rows,
+        planes,
         mixed,
         jnp.pad(jnp.stack(gains), ((0, 6), (0, 0))),
         ple[:, :PLE],
@@ -1211,9 +1236,9 @@
     )
 
 
-def middle_plain(ranks, h_blocks, in_maps, down_rows, mixed, gains, ple, ple_input, cotangent):
+def middle_plain(ranks, h_blocks, in_maps, planes, mixed, gains, ple, ple_input, cotangent):
     block = mixed.shape[0]
-    down_map = lax.all_gather(down_rows, "fsdp", axis=0, tiled=True)
+    down_map = lax.all_gather(planes[2], "fsdp", axis=0, tiled=True)
     gate_up = dot(whole_rows(h_blocks), in_maps, ((1,), (1,)))
     gate_part, up_part = gate_up[:, 0], gate_up[:, 1]
     hidden = (gelu_tanh(gate_part) * up_part).astype(low)
@@ -1454,17 +1479,21 @@
         del refs[:count]
         return head
 
-    owns = some(3)
+    shared = ranks == 4
+    owns = some(3 + shared)
     x_ref, branch_ref, tokens_ref, base_ref, gain_ref = some(5) if with_x else [None] * 5
     query_ref, key_ref, value_ref, out_ref, ple_ref, laurel_ref, small_ref = some(7)
     (input_ref,) = some(1) if with_x else [None]
-    sums, from_left, from_right = some(3), some(3), some(3)
+    sums, from_left, from_right = some(3 + shared), some(3 + shared), some(3 + shared)
     got_last, got_out = some(2)
+    (got_pair,) = some(1) if shared else [None]
     if with_x:
         got_x, got_y, relay_x, relay_y, far_x, far_y = some(6)
     core_s, core_r, right_s, right_r, left_s, left_r, last_s, last_r, out_s, out_r = some(10)
     if with_x:
         x_s, x_r = some(2)
+    if shared:
+        pair_s, pair_r = some(2)
 
     rank = lax.axis_index("seq")
     fsdp_index = lax.axis_index("fsdp")
@@ -1503,7 +1532,7 @@
         (2, None),
         (0, slice(0, half_ranks)),
         (0, slice(half_ranks, ranks)),
-    ]
+    ] + [(3, None)] * shared
     count = len(pieces)
 
     def view(group, lead, piece):
@@ -1639,7 +1668,7 @@
         pl.when(pair > 0)(lambda: add_left(pairs - 1, piece, target))
         pl.when(mirrored > 0)(lambda: add_right(pairs - 1, piece, target))
 
-    last_sum, out_sum, rest_sum = [ref.at[pair] for ref in sums]
+    last_sum, out_sum, rest_sum = [ref.at[pair] for ref in sums[:3]]
     across = []
     for k in range(1, ranks):
         peer = flip(rank, k, ranks)
@@ -1649,11 +1678,31 @@
                 go(remote(out_sum.at[peer], got_out.at[k], out_s.at[k], out_r.at[k], on_seq(k))),
             )
         )
+    def put_pair(group, v):
+        head = pl.ds(pl.multiple_of(group * HEAD_DIM, HEAD_DIM), HEAD_DIM)
+        key_ref[:, head] = v[:, :HEAD_DIM]
+        value_ref[:, head] = v[:, HEAD_DIM:]
+
+    def pair_copy(k):
+        to = flip(rank, k, ranks)
+        return remote(
+            sums[3].at[pair, to % 2],
+            got_pair.at[rank // 2],
+            pair_s.at[k],
+            pair_r.at[k],
+            on_seq(k),
+        )
+
+    goes = lambda k: flip(rank, k, ranks) // 2 == rank % 2
+    if shared:
+        for k in range(1, ranks):
+            pl.when(goes(k))(lambda k=k: pair_copy(k).start())
     ple_ref[...] = up(rest_sum[:, : 2 * PLE])
     laurel_ref[...] = up(rest_sum[:, 2 * PLE : 2 * PLE + 2 * LR])
     small_ref[...] = up(rest_sum[:, 2 * PLE + 2 * LR :])
-    key_ref[...] = jnp.zeros_like(key_ref)
-    value_ref[...] = jnp.zeros_like(value_ref)
+    if not shared:
+        key_ref[...] = jnp.zeros_like(key_ref)
+        value_ref[...] = jnp.zeros_like(value_ref)
     q_width = out_sum.shape[2]
     for k in range(ranks):
         if k:
@@ -1668,9 +1717,25 @@
         head = pl.ds(pl.multiple_of(group * HEAD_DIM, HEAD_DIM), HEAD_DIM)
         query_ref[:, columns] = last[:, :q_width]
         out_ref[:, columns] = out
-        key_ref[:, head] += last[:, q_width : q_width + HEAD_DIM]
-        value_ref[:, head] += last[:, q_width + HEAD_DIM : q_width + 2 * HEAD_DIM]
-        small_ref[...] += last[:, q_width + 2 * HEAD_DIM :]
+        small_ref[...] += last[:, q_width : q_width + small_ref.shape[1]]
+        if not shared:
+            key_ref[:, head] += last[:, -2 * HEAD_DIM : -HEAD_DIM]
+            value_ref[:, head] += last[:, -HEAD_DIM:]
+    if shared:
+        pl.when(rank // 2 == rank % 2)(
+            lambda: put_pair(rank // 2, up(sums[3][pair, rank % 2]))
+        )
+        for k in range(1, ranks):
+
+            def arrived(k=k):
+                sender = flip(rank, k, ranks)
+                target = got_pair.at[sender // 2]
+                remote(target, target, pair_s.at[k], pair_r.at[k], sibling).wait_recv()
+                put_pair(sender // 2, up(got_pair[sender // 2]))
+
+            pl.when(flip(rank, k, ranks) % 2 == rank // 2)(arrived)
+        for k in range(1, ranks):
+            pl.when(goes(k))(lambda k=k: pair_copy(k).wait_send())
 
     for t in range(1, pairs):
         for piece in range(count):
@@ -1680,10 +1745,14 @@
         copy.wait_send()
 
 
-def finish(sizes, last, out, rest, x=None):
+def finish(sizes, last, out, rest, key_value, x=None):
     ranks, pairs = sizes["seq"], sizes["pair"]
     rows = last.shape[2]
-    arrays = [last, out, rest]
+    shared = ranks == 4
+    if shared:
+        arrays = [last, out, rest, key_value]
+    else:
+        arrays = [jnp.concatenate([last, key_value], 3), out, rest]
     vmem = pl.BlockSpec(memory_space=pltpu.VMEM)
     dma = lambda n: pltpu.SemaphoreType.DMA((n,))
     width = KEY_VALUE_HEADS * HEAD_DIM
@@ -1699,14 +1768,19 @@
     scratch = [pltpu.VMEM((pairs,) + v.shape[1:], low) for v in arrays]
     scratch += [pltpu.VMEM((pairs - 1,) + v.shape[1:], low) for v in arrays] * 2
     scratch += [pltpu.VMEM((ranks,) + v.shape[2:], low) for v in arrays[:2]]
+    if shared:
+        scratch.append(pltpu.VMEM((KEY_VALUE_HEADS,) + key_value.shape[2:], low))
     if x is not None:
         block, columns = x[0].shape[1], x[0].shape[2] // 2
         shapes.append((block, 1, 2 * columns))
         scratch += [pltpu.VMEM((2, block, columns), low)] * 2
         scratch += [pltpu.VMEM((block, columns), low)] * 4
-    scratch += [dma(4 * pairs)] * 2 + [dma(4 * (pairs - 1))] * 4 + [dma(ranks)] * 4
+    count = 4 + shared
+    scratch += [dma(count * pairs)] * 2 + [dma(count * (pairs - 1))] * 4 + [dma(ranks)] * 4
     if x is not None:
         scratch += [dma(6)] * 2
+    if shared:
+        scratch += [dma(ranks)] * 2
     operands = arrays + list(x or ())
     return pl.pallas_call(
         functools.partial(finish_kernel, sizes, x is not None),
@@ -1762,11 +1836,9 @@
     marks = jnp.pad(jnp.concatenate([segment_ids.T, positions.T], 0), ((0, 6), (0, 0)))
     x_local = hidden_in.reshape(block, width)
 
-    head_all, rest_all, marks_all, x_all = gather_weights(
-        sizes, head_pack, rest_pack, marks, x_local
-    )
-    in_rows, down_rows, head_all = lax.optimization_barrier(
-        (jnp.moveaxis(w_mlp[:, :2], 1, 0), w_mlp[:, 2], head_all)
+    planes = jnp.moveaxis(w_mlp, 1, 0)
+    head_all, rest_all, marks_all, x_all, in_rows = gather_weights(
+        sizes, head_pack, rest_pack, marks, x_local, planes
     )
     in_maps = lax.all_gather(in_rows, "fsdp", axis=1, tiled=True)
     x_all = x_all.reshape(length, width)
@@ -1820,7 +1892,7 @@
     ) = run_middle(
         h_blocks,
         in_maps,
-        down_rows,
+        planes,
         mixed,
         gain[4:6],
         ple,
@@ -1904,19 +1976,23 @@
         grad_head_scale.reshape(-1, head_rows, 2), ((0, 0), (0, rows - head_rows), (0, 0))
     ).reshape(width, 2)
     late_grad = jnp.pad(head_scale_grad, ((0, 0), (6, 120)))
-    last = weight_grad(
+    last, pair_grad = weight_grad(
         ranks, pairs * 2, [normed_all], grad_qkv, head_all, gain[0][:, None], late_grad
     )
-    last, grad_qkv = lax.optimization_barrier((last, grad_qkv))
+    last, pair_grad, grad_qkv = lax.optimization_barrier((last, pair_grad, grad_qkv))
     x_part = mm_nt(grad_qkv, qkv_map).astype(low)
 
     if ranks == 4:
         gain_row = jnp.broadcast_to(gain[0], (8, width))
         x_parts = x_part.reshape(ranks, block, width)
         extras = (x_parts, x_here, x_local, grad_mixed, gain_row)
-        *sums, input_grad = finish(sizes, last, out_grad, rest_own, extras)
+        side = rank % 2 * 2
+        mine = lax.dynamic_slice_in_dim(pair_grad, side, 2, 1)
+        other = permute(lax.dynamic_slice_in_dim(pair_grad, 2 - side, 2, 1), "seq", 1)
+        pair_grad = (mine.astype(full) + other.astype(full)).astype(low)
+        *sums, input_grad = finish(sizes, last, out_grad, rest_own, pair_grad, extras)
     else:
-        sums = finish(sizes, last, out_grad, rest_own)
+        sums = finish(sizes, last, out_grad, rest_own, pair_grad)
         grad_x_normed = x_here + sum_seq(cut(x_part), ranks)
         grad_tokens_norm = norm_back(tokens, x_inverse, gain[0], grad_x_normed)[0]
         input_grad = grad_mixed * root_half + grad_tokens_norm

time: 749 us -> 736 us (0.983)
  Pallas kernels: 463 us -> 445 us
    pallas_call x1, Pallas kernels: 135 us -> 117 us  [finish(): pl.pallas_call(functools.partial(finish_kernel, sizes, x is not None), ou...]
    ppermute x24 -> x25, waiting for transfers between devices: 88.5 us -> 93 us  [permute(): return lax.ppermute(v, axis, [(i, i ^ offset) for i in range(size)])]
    ppermute x24 -> x25, starting transfers between devices: 34 us -> 35.3 us  [permute(): return lax.ppermute(v, axis, [(i, i ^ offset) for i in range(size)])]
  transfers between devices with their start and end apart: 27 -> 28, of which waited for: 16 -> 16; matrix products, arithmetic and copies ran while one was open for 15% -> 15% of each run, Pallas kernels for 35% -> 33%
where the time goes in v7:
time: 736 us; the launch traced here: 727 us
  Pallas kernels  445 us (60%)
  waiting for transfers between devices  97.2 us (13%)
  other arithmetic  46.1 us (6%)
  local copies, waits for them, and re-layouts  44.2 us (6%)
  matrix products  43.5 us (6%)
  starting transfers between devices  35.4 us (5%)
  between operations  15.2 us (2%)
    pallas_call x1, Pallas kernels, middle(): pl.pallas_call(functools.partial(middle_kernel, pairs, block, parts), out...  151 us
    pallas_call x1, Pallas kernels, finish(): pl.pallas_call(functools.partial(finish_kernel, sizes, x is not None), ou...  117 us
    ppermute x25, waiting for transfers between devices, permute(): return lax.ppermute(v, axis, [(i, i ^ offset) for i in range(size)])  93 us
    pallas_call x1, Pallas kernels, back(): pl.pallas_call(functools.partial(back_kernel, block), out_shape=(jax.Shap...  65.1 us
    pallas_call x1, Pallas kernels, gather_weights(): pl.pallas_call(functools.partial(gather_kernel, sizes), out_shape=(jax.Sh...  56.5 us
    dot_general x13, matrix products, dot(): lax.dot_general(left, right, (over, ((), ())), preferred_element_type=full)  43.5 us
    ppermute x25, starting transfers between devices, permute(): return lax.ppermute(v, axis, [(i, i ^ offset) for i in range(size)])  35.3 us
    pallas_call x2, Pallas kernels, weight_grad(): pl.pallas_call(functools.partial(weight_grad_kernel, len(lefts), half_til...  22 us
  transfers between devices with their start and end apart: 28, of which 16 were waited for; matrix products, arithmetic and copies ran while one was open for 15% of the time, Pallas kernels for 33%

profile of v7, /device:TPU:20, one launch (start us, length us, event | category | flops | bytes accessed | tf_op | source)
XLA Modules:
  0.0 727.0 jit_solution(6220483274477701339)
XLA Ops:
  13.5 56.5 %shard_map.221 = (bf16[4,4,2,64,1536]{4,3,2,1,0:T(8,128)(2,1)}, bf16[4,4,2,64,256]{4,3,2,1,0:T(8,128)(2,1)}, s32[4,8,256]{2,1,0:T(8,128)}, bf16[4,256,2048]{2,1,0:T(8,128)(2,1)}, bf16[2,256,2048]{2,1,0:T(8,128)(2,1)}) custom-call(bf16[4,64,1536]{2,1,0:T(8,128)(2,1)} %pad_maximum_fusion.3.head_ref, bf16[64,256]{1,0:T(8,128)(2,1)} %fusion.49.rest_ref, ...), custom_call_target="tpu_custom_call" | custom-call | tf_op jit(solution)/shard_map/pallas_call | solution.py:257
  70.1 3.2 multiply_reduce_fusion
  75.0 1.9 multiply_sine_fusion
  76.9 3.1 slice_reduce_fusion.1
  82.1 4.5 fusion.20.qkv_ref
  86.6 16.3 %shard_map.222 = (bf16[1024,512]{1,0:T(8,128)(2,1)S(1)}, bf16[1024,256]{1,0:T(8,128)(2,1)S(1)}, bf16[1024,256]{1,0:T(8,128)(2,1)S(1)}, bf16[1024,512]{1,0:T(8,128)(2,1)S(1)}, f32[2,1024,1]{2,1,0:T(8,128)S(1)}) custom-call(f32[1024,1024]{1,0:T(8,128)S(1)} %fusion.20.qkv_ref, s32[1024,1]{1,0:T(8,128)S(1)} %copy.71.code_col_ref, ...), custom_call_target="tpu_custom_call" | custom-call | flops 1207959552 | bytes 12582912 | tf_op jit(solution)/shard_map/pallas_call | solution.py:491
  102.9 2.4 convolution_convert_fusion
  108.5 12.0 %collective-permute-done.1 = bf16[256,1024]{1,0:T(8,128)(2,1)S(1)} collective-permute-done((bf16[256,1024]{1,0:T(8,128)(2,1)S(1)}, bf16[256,1024]{1,0:T(8,128)(2,1)S(1)}, u32[]{:S(2)}, u32[]{:S(2)}) %collective-permute-start.1) | collective-permute-done | bytes 524320 | tf_op jit(solution)/shard_map/ppermute | solution.py:286
  123.1 5.5 collective-permute-done
  128.6 7.0 collective-permute-done.2
  138.3 3.1 collective-permute-done.3
  141.3 6.1 collective-permute-done.5
  148.0 2.6 broadcast_multiply_fusion
  153.7 19.7 %collective-permute-done.6.rows_x_in.rows_x = bf16[256,2048]{1,0:T(8,128)(2,1)S(1)} collective-permute-done((bf16[256,2048]{1,0:T(8,128)(2,1)S(1)}, bf16[256,2048]{1,0:T(8,128)(2,1)S(1)}, u32[]{:S(2)}, u32[]{:S(2)}) %collective-permute-start.6) | collective-permute-done | bytes 1048608 | tf_op jit(solution)/shard_map/ppermute | solution.py:286
  175.5 7.3 collective-permute-done.8.rows_left_in.rows_left
  184.7 10.4 %collective-permute-start.11 = (bf16[64,512]{1,0:T(8,128)(2,1)S(1)}, bf16[64,512]{1,0:T(8,128)(2,1)S(1)}, u32[]{:S(2)}, u32[]{:S(2)}) collective-permute-start(bf16[64,512]{1,0:T(8,128)(2,1)S(1)} %copy-done.47), channel_id=1, source_target_pairs={{0,4},{1,5},{2,6},{3,7},{4,0},{5,1},{6,2},{7,3},{8,12},{9,13},{10,... | collective-permute-start | bytes 196616 | tf_op jit(solution)/shard_map/ppermute | solution.py:286
  195.2 6.4 collective-permute-done.11
  201.6 1.9 collective-permute-done.10
  204.5 1.6 collective-permute-start.14
  207.2 5.3 collective-permute-done.15
  212.4 2.1 collective-permute-done.14
  216.6 2.4 collective-permute-done.16
  219.0 2.0 fusion.39
  222.9 4.2 all-gather.2.cloned.1.call-done.in_maps_ref.maps_ref
  227.1 151.2 %shard_map.223 = (bf16[4,256,2048]{2,1,0:T(8,128)(2,1)}, bf16[2048,2048]{1,0:T(8,128)(2,1)}, bf16[2048,2048]{1,0:T(8,128)(2,1)}, f32[1024,2048]{1,0:T(8,128)}, f...) custom-call(bf16[256,2048]{1,0:T(8,128)(2,1)} %copy-done.34, ...), custom_call_target="tpu_custom_call" | custom-call | flops 17179869184 | bytes 104857600 | tf_op jit(solution)/shard_map/pallas_call | solution.py:1190
  378.4 12.6 %fusion.60 = f32[1024,2048]{1,0:T(8,128)S(1)} fusion(bf16[1024,2048]{1,0:T(8,128)(2,1)} %bitcast.189, bf16[2048,2048]{1,0:T(8,128)(2,1)} %get-tuple-element.88), kind=kOutput, calls=%fused_computation.160 | convolution fusion | flops 8589934592 | bytes 20971520 | tf_op jit(solution)/shard_map/dot_general | solution.py:344
  391.0 8.2 %multiply_convert_fusion = (bf16[1024,2048]{1,0:T(8,128)(2,1)}, bf16[1024,2048]{1,0:T(8,128)(2,1)}) fusion(f32[1024,2048]{1,0:T(8,128)S(1)} %fusion.60, f32[1024,2048]{1,0:T(8,128)S(1)} %bitcast.131, f32[1024,2048]{1,0:T(8,128)S(1)} %bitcast.133), kind=kLoop, calls=%fused_computation.12 | loop fusion | flops 50331648 | bytes 33554432 | tf_op jit(solution)/shard_map/convert_element_type | solution.py:1909
  399.3 65.1 %shard_map.224 = (bf16[2,2048,2048]{2,1,0:T(8,128)(2,1)}, f32[256,2048]{1,0:T(8,128)}) custom-call(bf16[1024,2048]{1,0:T(8,128)(2,1)} %get-tuple-element.185.gate_ref, bf16[1024,2048]{1,0:T(8,128)(2,1)} %get-tuple-element.184.up_ref, bf16[2,2048,2048]{2,1,0:T(8,128)(2,1)} %all-gather.2.cloned.1.call-done.in_maps_ref.maps_ref, bf16[256,2048]{1,0:T(8,128)(2,1)} %copy-done.34, ...), custom_call_target="tpu_custom_call" | custom-call | flops 34359738368 | bytes 52428800 | tf_op jit(solution)/shard_map/pallas_call | solution.py:1445
  464.4 2.3 copy.81
  466.8 2.9 multiply_reduce_fusion.2
  470.3 4.0 multiply_reduce_fusion.1
  474.4 2.2 multiply_convert_fusion.1
  483.0 3.8 fusion.27
  488.3 8.6 %collective-permute-done.17.refs_1_ = bf16[256,2048]{1,0:T(8,128)(2,1)} collective-permute-done((bf16[256,2048]{1,0:T(8,128)(2,1)}, bf16[256,2048]{1,0:T(8,128)(2,1)}, u32[]{:S(2)}, u32[]{:S(2)}) %collective-permute-start.17) | collective-permute-done | bytes 1048608 | tf_op jit(solution)/shard_map/ppermute | solution.py:286
  497.0 1.9 slice.202
  500.3 1.9 slice.203
  505.6 6.1 concatenate.91
  511.8 3.1 dynamic-slice_bitcast_fusion
  514.9 1.8 collective-permute-start.21
  518.8 5.9 fusion.33.grad_ref
  524.7 17.1 %shard_map.225 = (bf16[1024,1024]{1,0:T(8,128)(2,1)S(1)}, f32[8,256]{1,0:T(8,128)S(1)}) custom-call(f32[1024,1024]{1,0:T(8,128)S(1)} %copy-done.1, bf16[1024,512]{1,0:T(8,128)(2,1)S(1)} %copy-done.4, bf16[1024,256]{1,0:T(8,128)(2,1)S(1)} %copy-done.8, bf16[1024,256]{1,0:T(8,128)(2,1)S(1)} %copy-done.10, bf16[1024,512]{1,0:T(8,128)(2,1)S(1)} %fusion.33.grad_ref, ...), custom_call_target="tpu_custom_call" | custom-call | flops 3019898880 | bytes 16777216 | tf_op jit(solution)/shard_map/pallas_call | solution.py:632
  544.8 8.5 %shard_map.227.refs_1_ = bf16[8,4,64,512]{3,2,1,0:T(8,128)(2,1)} custom-call(bf16[256,2048]{1,0:T(8,128)(2,1)} %get-tuple-element.97.refs_0_, bf16[256,2048]{1,0:T(8,128)(2,1)} %collective-permute-done.17.refs_1_, bf16[256,2048]{1,0:T(8,128)(2,1)} %collective-permute-done.18.refs_2_, bf16[256,1024]{1,0:T(8,128)(2,1)} %collective-permute-done.19.refs_3_, ...), custom_call_target="tpu_custom_call" | custom-call | flops 2147483648 | bytes 7340032 | tf_op jit(solution)/shard_map/pallas_call | solution.py:696
  553.4 13.4 %shard_map.226 = (bf16[8,4,64,640]{3,2,1,0:T(8,128)(2,1)}, bf16[8,4,64,512]{3,2,1,0:T(8,128)(2,1)}) custom-call(bf16[1024,2048]{1,0:T(8,128)(2,1)} %copy-done.26, bf16[1024,1024]{1,0:T(8,128)(2,1)} %copy-done.11, bf16[2048,1536]{1,0:T(8,128)(2,1)} %bitcast.181, f32[2048,1]{1,0:T(8,128)} %get-tuple-element.202.refs_3_, f32[2048,128]{1,0:T(8,128)} %pad.35.refs_4_), custom_call_target="tpu_custom_call" | custom-call | flops 4294967296 | bytes 10485760 | tf_op jit(solution)/shard_map/pallas_call | solution.py:696
  569.6 2.7 fusion.32
  572.3 8.6 %convolution_convert_fusion.1 = bf16[1024,2048]{1,0:T(8,128)(2,1)} fusion(bf16[1024,1024]{1,0:T(8,128)(2,1)S(1)} %copy-done.12, bf16[2048,1536]{1,0:T(8,128)(2,1)} %bitcast.182), kind=kOutput, calls=%fused_computation.25 | convolution fusion | flops 4297064448 | bytes 10485760 | tf_op jit(solution)/shard_map/dot_general | solution.py:344
  580.9 4.6 collective-permute-done.24
  587.4 117.2 %shard_map.228 = (f32[64,2048]{1,0:T(8,128)}, f32[64,512]{1,0:T(8,128)}, f32[64,512]{1,0:T(8,128)}, f32[64,2048]{1,0:T(8,128)}, f32[64,512]{1,0:T(8,128)}, /*ind...) custom-call(bf16[8,4,64,640]{3,2,1,0:T(8,128)(2,1)} %get-tuple-element.108.refs_0_, ...), custom_call_target="tpu_custom_call" | custom-call | tf_op jit(solution)/shard_map/pallas_call | solution.py:1785
  707.4 5.1 maximum_convert_fusion
  (247 shorter events, 65.5 us)
Async XLA Ops:
  7.2 219.9 %all-gather.2.cloned.1.call-start = ((), (), s32[]{:S(2)}) async-start(), calls=%async_computation.2 | async-start | bytes 18874368 | tf_op jit(solution)/shard_map/all_gather | solution.py:1843
  70.0 637.3 %reduce-scatter.5.cloned.1.call-start = ((), (), s32[]{:S(2)}) async-start(), calls=%async_computation.4 | async-start | bytes 9437184 | tf_op jit(solution)/shard_map/reduce_scatter | solution.py:1904
  86.5 16.3 %copy-start = (f32[1024,1024]{1,0:T(8,128)}, f32[1024,1024]{1,0:T(8,128)S(1)}, u32[]{:S(2)}) copy-start(f32[1024,1024]{1,0:T(8,128)S(1)} %fusion.20.qkv_ref) | copy-start | bytes 12582916
  105.3 17.5 %copy-start.22 = (bf16[256,1,2048]{2,0,1:T(8,128)(2,1)S(1)}, bf16[256,1,2048]{2,0,1:T(8,128)(2,1)}, u32[]{:S(2)}) copy-start(bf16[256,1,2048]{2,0,1:T(8,128)(2,1)} %param.14) | copy-start | bytes 3145732
  105.6 14.9 %collective-permute-start.1 = (bf16[256,1024]{1,0:T(8,128)(2,1)S(1)}, bf16[256,1024]{1,0:T(8,128)(2,1)S(1)}, u32[]{:S(2)}, u32[]{:S(2)}) collective-permute-start(bf16[256,1024]{1,0:T(8,128)(2,1)S(1)} %get-tuple-element.191), channel_id=1, source_target_pairs={{0,8},{8,0},{16,24},{24,16},{1,9},{9,1},{17,25},{25,17},{2,10},{10... | collective-permute-start | bytes 1572872 | tf_op jit(solution)/shard_map/ppermute | solution.py:286
  106.5 22.1 %collective-permute-start = (bf16[256,1024]{1,0:T(8,128)(2,1)S(1)}, bf16[256,1024]{1,0:T(8,128)(2,1)S(1)}, u32[]{:S(2)}, u32[]{:S(2)}) collective-permute-start(bf16[256,1024]{1,0:T(8,128)(2,1)S(1)} %get-tuple-element.188), channel_id=1, source_target_pairs={{0,8},{8,0},{16,24},{24,16},{1,9},{9,1},{17,25},{25,17},{2,10},{10... | collective-permute-start | bytes 1572872 | tf_op jit(solution)/shard_map/ppermute | solution.py:286
  107.7 21.0 %collective-permute-start.4 = (bf16[256,1024]{1,0:T(8,128)(2,1)S(1)}, bf16[256,1024]{1,0:T(8,128)(2,1)S(1)}, u32[]{:S(2)}, u32[]{:S(2)}) collective-permute-start(bf16[256,1024]{1,0:T(8,128)(2,1)S(1)} %get-tuple-element.189), channel_id=1, source_target_pairs={{0,16},{8,24},{16,0},{24,8},{1,17},{9,25},{17,1},{25,9},{2,18},{10... | collective-permute-start | bytes 1572872 | tf_op jit(solution)/shard_map/ppermute | solution.py:286
  120.7 14.9 %collective-permute-start.2 = (bf16[256,1024]{1,0:T(8,128)(2,1)S(1)}, bf16[256,1024]{1,0:T(8,128)(2,1)S(1)}, u32[]{:S(2)}, u32[]{:S(2)}) collective-permute-start(bf16[256,1024]{1,0:T(8,128)(2,1)S(1)} %add_convert_fusion.2), channel_id=1, source_target_pairs={{0,16},{8,24},{16,0},{24,8},{1,17},{9,25},{17,1},{25,9},{2,18},{10... | collective-permute-start | bytes 1572872 | tf_op jit(solution)/shard_map/ppermute | solution.py:286
  121.6 19.8 %collective-permute-start.3 = (bf16[256,1024]{1,0:T(8,128)(2,1)S(1)}, bf16[256,1024]{1,0:T(8,128)(2,1)S(1)}, u32[]{:S(2)}, u32[]{:S(2)}) collective-permute-start(bf16[256,1024]{1,0:T(8,128)(2,1)S(1)} %get-tuple-element.190), channel_id=1, source_target_pairs={{0,16},{8,24},{16,0},{24,8},{1,17},{9,25},{17,1},{25,9},{2,18},{10... | collective-permute-start | bytes 1572872 | tf_op jit(solution)/shard_map/ppermute | solution.py:286
  123.1 14.0 %copy-start.28 = (bf16[4,4,2,64,256]{4,3,2,1,0:T(8,128)(2,1)S(1)}, bf16[4,4,2,64,256]{4,3,2,1,0:T(8,128)(2,1)}, u32[]{:S(2)}) copy-start(bf16[4,4,2,64,256]{4,3,2,1,0:T(8,128)(2,1)} %get-tuple-element.68) | copy-start | bytes 3145732
  136.1 11.9 %copy-start.20 = (f32[256,1024]{1,0:T(8,128)}, f32[256,1024]{1,0:T(8,128)S(1)}, u32[]{:S(2)}) copy-start(f32[256,1024]{1,0:T(8,128)S(1)} %get-tuple-element.186) | copy-start | bytes 3145732
  136.1 11.4 %collective-permute-start.5 = (bf16[256,1024]{1,0:T(8,128)(2,1)S(1)}, bf16[256,1024]{1,0:T(8,128)(2,1)S(1)}, u32[]{:S(2)}, u32[]{:S(2)}) collective-permute-start(bf16[256,1024]{1,0:T(8,128)(2,1)S(1)} %get-tuple-element.187), channel_id=1, source_target_pairs={{0,8},{8,0},{16,24},{24,16},{1,9},{9,1},{17,25},{25,17},{2,10},{10... | collective-permute-start | bytes 1572872 | tf_op jit(solution)/shard_map/ppermute | solution.py:286
  138.2 9.7 %copy-start.15 = (f32[256,2048]{1,0:T(8,128)}, f32[256,2048]{1,0:T(8,128)S(1)}, u32[]{:S(2)}) copy-start(f32[256,2048]{1,0:T(8,128)S(1)} %get-tuple-element.228) | copy-start | bytes 6291460
  150.9 32.8 %copy-start.47 = (bf16[64,512]{1,0:T(8,128)(2,1)S(1)}, bf16[64,512]{1,0:T(8,128)(2,1)}, u32[]{:S(2)}) copy-start(bf16[64,512]{1,0:T(8,128)(2,1)} %param.24) | copy-start | bytes 196612
  152.0 21.5 %collective-permute-start.6 = (bf16[256,2048]{1,0:T(8,128)(2,1)S(1)}, bf16[256,2048]{1,0:T(8,128)(2,1)S(1)}, u32[]{:S(2)}, u32[]{:S(2)}) collective-permute-start(bf16[256,2048]{1,0:T(8,128)(2,1)S(1)} %multiply_convert_fusion.3.rows_own), channel_id=1, source_target_pairs={{0,8},{8,0},{16,24},{24,16},{1,9},{9,1},{17,25},{25,17},{2,10},{10... | collective-permute-start | bytes 3145736 | tf_op jit(solution)/shard_map/ppermute | solution.py:286
  153.0 21.4 %collective-permute-start.7 = (bf16[256,2048]{1,0:T(8,128)(2,1)S(1)}, bf16[256,2048]{1,0:T(8,128)(2,1)S(1)}, u32[]{:S(2)}, u32[]{:S(2)}) collective-permute-start(bf16[256,2048]{1,0:T(8,128)(2,1)S(1)} %multiply_convert_fusion.3.rows_own), channel_id=1, source_target_pairs={{0,16},{8,24},{16,0},{24,8},{1,17},{9,25},{17,1},{25,9},{2,18},{10... | collective-permute-start | bytes 3145736 | tf_op jit(solution)/shard_map/ppermute | solution.py:286
  173.5 9.2 %collective-permute-start.8 = (bf16[256,1024]{1,0:T(8,128)(2,1)S(1)}, bf16[256,1024]{1,0:T(8,128)(2,1)S(1)}, u32[]{:S(2)}, u32[]{:S(2)}) collective-permute-start(bf16[256,1024]{1,0:T(8,128)(2,1)S(1)} %slice.194), channel_id=1, source_target_pairs={{0,16},{8,24},{16,0},{24,8},{1,17},{9,25},{17,1},{25,9},{2,18},{10... | collective-permute-start | bytes 1572872 | tf_op jit(solution)/shard_map/ppermute | solution.py:286
  174.4 9.3 %copy-start.40 = (bf16[256,2048]{1,0:T(8,128)(2,1)}, bf16[256,2048]{1,0:T(8,128)(2,1)S(1)}, u32[]{:S(2)}) copy-start(bf16[256,2048]{1,0:T(8,128)(2,1)S(1)} %collective-permute-done.7.rows_y_in.rows_y) | copy-start | bytes 3145732
  174.5 9.2 %collective-permute-start.9 = (bf16[256,1024]{1,0:T(8,128)(2,1)S(1)}, bf16[256,1024]{1,0:T(8,128)(2,1)S(1)}, u32[]{:S(2)}, u32[]{:S(2)}) collective-permute-start(bf16[256,1024]{1,0:T(8,128)(2,1)S(1)} %slice.195), channel_id=1, source_target_pairs={{0,8},{8,0},{16,24},{24,16},{1,9},{9,1},{17,25},{25,17},{2,10},{10... | collective-permute-start | bytes 1572872 | tf_op jit(solution)/shard_map/ppermute | solution.py:286
  183.7 11.4 %copy-start.50 = (bf16[256,1024]{1,0:T(8,128)(2,1)}, bf16[256,1024]{1,0:T(8,128)(2,1)S(1)}, u32[]{:S(2)}) copy-start(bf16[256,1024]{1,0:T(8,128)(2,1)S(1)} %collective-permute-done.9.rows_right_in.rows_right) | copy-start | bytes 1572868
  183.7 11.5 %collective-permute-start.12 = (bf16[64,512]{1,0:T(8,128)(2,1)S(1)}, bf16[64,512]{1,0:T(8,128)(2,1)S(1)}, u32[]{:S(2)}, u32[]{:S(2)}) collective-permute-start(bf16[64,512]{1,0:T(8,128)(2,1)S(1)} %copy-done.47), channel_id=1, source_target_pairs={{0,6},{1,7},{2,4},{3,5},{4,2},{5,3},{6,0},{7,1},{8,14},{9,15},{10,... | collective-permute-start | bytes 196616 | tf_op jit(solution)/shard_map/ppermute | solution.py:286
  184.7 16.9 %collective-permute-start.11 = (bf16[64,512]{1,0:T(8,128)(2,1)S(1)}, bf16[64,512]{1,0:T(8,128)(2,1)S(1)}, u32[]{:S(2)}, u32[]{:S(2)}) collective-permute-start(bf16[64,512]{1,0:T(8,128)(2,1)S(1)} %copy-done.47), channel_id=1, source_target_pairs={{0,4},{1,5},{2,6},{3,7},{4,0},{5,1},{6,2},{7,3},{8,12},{9,13},{10,... | collective-permute-start | bytes 196616 | tf_op jit(solution)/shard_map/ppermute | solution.py:286
  195.2 8.3 %collective-permute-start.10 = (bf16[64,512]{1,0:T(8,128)(2,1)S(1)}, bf16[64,512]{1,0:T(8,128)(2,1)S(1)}, u32[]{:S(2)}, u32[]{:S(2)}) collective-permute-start(bf16[64,512]{1,0:T(8,128)(2,1)S(1)} %copy-done.47), channel_id=1, source_target_pairs={{0,2},{1,3},{2,0},{3,1},{4,6},{5,7},{6,4},{7,5},{8,10},{9,11},{10,... | collective-permute-start | bytes 196616 | tf_op jit(solution)/shard_map/ppermute | solution.py:286
  203.6 8.8 %collective-permute-start.15 = (bf16[4,64,512]{2,1,0:T(8,128)(2,1)S(1)}, bf16[4,64,512]{2,1,0:T(8,128)(2,1)S(1)}, u32[]{:S(2)}, u32[]{:S(2)}) collective-permute-start(bf16[4,64,512]{2,1,0:T(8,128)(2,1)S(1)} %get-tuple-element.210), channel_id=1, source_target_pairs={{0,24},{8,16},{16,8},{24,0},{1,25},{9,17},{17,9},{25,1},{2,26},{10... | collective-permute-start | bytes 786440 | tf_op jit(solution)/shard_map/ppermute | solution.py:286
  204.5 10.1 %collective-permute-start.14 = (bf16[4,64,512]{2,1,0:T(8,128)(2,1)S(1)}, bf16[4,64,512]{2,1,0:T(8,128)(2,1)S(1)}, u32[]{:S(2)}, u32[]{:S(2)}) collective-permute-start(bf16[4,64,512]{2,1,0:T(8,128)(2,1)S(1)} %get-tuple-element.210), channel_id=1, source_target_pairs={{0,16},{8,24},{16,0},{24,8},{1,17},{9,25},{17,1},{25,9},{2,18},{10... | collective-permute-start | bytes 786440 | tf_op jit(solution)/shard_map/ppermute | solution.py:286
  206.1 8.5 %collective-permute-start.13 = (bf16[4,64,512]{2,1,0:T(8,128)(2,1)S(1)}, bf16[4,64,512]{2,1,0:T(8,128)(2,1)S(1)}, u32[]{:S(2)}, u32[]{:S(2)}) collective-permute-start(bf16[4,64,512]{2,1,0:T(8,128)(2,1)S(1)} %get-tuple-element.210), channel_id=1, source_target_pairs={{0,8},{8,0},{16,24},{24,16},{1,9},{9,1},{17,25},{25,17},{2,10},{10... | collective-permute-start | bytes 786440 | tf_op jit(solution)/shard_map/ppermute | solution.py:286
  216.0 3.0 collective-permute-start.16
  378.3 329.1 %reduce-scatter.3.cloned.1.call-start = ((), (), s32[]{:S(2)}) async-start(), calls=%async_computation.3 | async-start | bytes 18874368 | tf_op jit(solution)/shard_map/reduce_scatter | solution.py:1918
  378.3 12.7 %slice-start = ((s8[8388608]{0:T(1024)(128)(4,1)}), s8[4194304]{0:T(1024)(128)(4,1)S(1)}, s32[]{:S(2)}) async-start(s8[8388608]{0:T(1024)(128)(4,1)} %bitcast.130), calls=%async_computation.5 | async-start | bytes 8388608
  378.3 12.7 %slice-start.2 = ((s8[8388608]{0:T(1024)(128)(4,1)}), s8[4194304]{0:T(1024)(128)(4,1)S(1)}, s32[]{:S(2)}) async-start(s8[8388608]{0:T(1024)(128)(4,1)} %bitcast.132), calls=%async_computation.7 | async-start | bytes 8388608
  378.3 12.7 %slice-start.1 = ((s8[8388608]{0:T(1024)(128)(4,1)}), s8[4194304]{0:T(1024)(128)(4,1)S(1)}, s32[]{:S(2)}) async-start(s8[8388608]{0:T(1024)(128)(4,1)} %bitcast.130), calls=%async_computation.6 | async-start | bytes 8388608
  378.4 12.7 %slice-start.3 = ((s8[8388608]{0:T(1024)(128)(4,1)}), s8[4194304]{0:T(1024)(128)(4,1)S(1)}, s32[]{:S(2)}) async-start(s8[8388608]{0:T(1024)(128)(4,1)} %bitcast.132), calls=%async_computation.8 | async-start | bytes 8388608
  476.6 20.4 %collective-permute-start.17 = (bf16[256,2048]{1,0:T(8,128)(2,1)}, bf16[256,2048]{1,0:T(8,128)(2,1)}, u32[]{:S(2)}, u32[]{:S(2)}) collective-permute-start(bf16[256,2048]{1,0:T(8,128)(2,1)} %get-tuple-element.97.refs_0_), channel_id=1, source_target_pairs={{0,8},{8,0},{16,24},{24,16},{1,9},{9,1},{17,25},{25,17},{2,10},{10... | collective-permute-start | bytes 3145736 | tf_op jit(solution)/shard_map/ppermute | solution.py:286
  478.0 22.3 %collective-permute-start.18 = (bf16[256,2048]{1,0:T(8,128)(2,1)}, bf16[256,2048]{1,0:T(8,128)(2,1)}, u32[]{:S(2)}, u32[]{:S(2)}) collective-permute-start(bf16[256,2048]{1,0:T(8,128)(2,1)} %get-tuple-element.97.refs_0_), channel_id=1, source_target_pairs={{0,16},{8,24},{16,0},{24,8},{1,17},{9,25},{17,1},{25,9},{2,18},{10... | collective-permute-start | bytes 3145736 | tf_op jit(solution)/shard_map/ppermute | solution.py:286
  486.9 16.8 %copy-start.42 = (bf16[256,256]{1,0:T(8,128)(2,1)S(1)}, bf16[256,256]{1,0:T(8,128)(2,1)}, u32[]{:S(2)}) copy-start(bf16[256,256]{1,0:T(8,128)(2,1)} %get-tuple-element.81) | copy-start | bytes 393220
  487.4 16.3 %copy-start.36 = (bf16[256,2048]{1,0:T(8,128)(2,1)S(1)}, bf16[256,2048]{1,0:T(8,128)(2,1)}, u32[]{:S(2)}) copy-start(bf16[256,2048]{1,0:T(8,128)(2,1)} %get-tuple-element.80) | copy-start | bytes 3145732
  488.3 15.8 %copy-start.35 = (bf16[256,2048]{1,0:T(8,128)(2,1)S(1)}, bf16[256,2048]{1,0:T(8,128)(2,1)}, u32[]{:S(2)}) copy-start(bf16[256,2048]{1,0:T(8,128)(2,1)} %get-tuple-element.82) | copy-start | bytes 3145732
  488.3 15.8 %copy-start.41 = (bf16[256,256]{1,0:T(8,128)(2,1)S(1)}, bf16[256,256]{1,0:T(8,128)(2,1)}, u32[]{:S(2)}) copy-start(bf16[256,256]{1,0:T(8,128)(2,1)} %get-tuple-element.83) | copy-start | bytes 393220
  498.8 12.9 %collective-permute-start.19 = (bf16[256,1024]{1,0:T(8,128)(2,1)}, bf16[256,1024]{1,0:T(8,128)(2,1)}, u32[]{:S(2)}, u32[]{:S(2)}) collective-permute-start(bf16[256,1024]{1,0:T(8,128)(2,1)} %slice.202), channel_id=1, source_target_pairs={{0,16},{8,24},{16,0},{24,8},{1,17},{9,25},{17,1},{25,9},{2,18},{10... | collective-permute-start | bytes 1572872 | tf_op jit(solution)/shard_map/ppermute | solution.py:286
  502.2 9.6 %collective-permute-start.20 = (bf16[256,1024]{1,0:T(8,128)(2,1)}, bf16[256,1024]{1,0:T(8,128)(2,1)}, u32[]{:S(2)}, u32[]{:S(2)}) collective-permute-start(bf16[256,1024]{1,0:T(8,128)(2,1)} %slice.203), channel_id=1, source_target_pairs={{0,8},{8,0},{16,24},{24,16},{1,9},{9,1},{17,25},{25,17},{2,10},{10... | collective-permute-start | bytes 1572872 | tf_op jit(solution)/shard_map/ppermute | solution.py:286
  514.9 38.5 %collective-permute-start.21 = (bf16[512,768]{1,0:T(8,128)(2,1)}, bf16[512,768]{1,0:T(8,128)(2,1)S(1)}, u32[]{:S(2)}, u32[]{:S(2)}) collective-permute-start(bf16[512,768]{1,0:T(8,128)(2,1)} %get-tuple-element.194), channel_id=1, source_target_pairs={{0,8},{8,0},{16,24},{24,16},{1,9},{9,1},{17,25},{25,17},{2,10},{10... | collective-permute-start | bytes 2359304 | tf_op jit(solution)/shard_map/ppermute | solution.py:286
  516.7 36.7 %collective-permute-start.22 = (bf16[512,768]{1,0:T(8,128)(2,1)}, bf16[512,768]{1,0:T(8,128)(2,1)S(1)}, u32[]{:S(2)}, u32[]{:S(2)}) collective-permute-start(bf16[512,768]{1,0:T(8,128)(2,1)} %get-tuple-element.193), channel_id=1, source_target_pairs={{0,16},{8,24},{16,0},{24,8},{1,17},{9,25},{17,1},{25,9},{2,18},{10... | collective-permute-start | bytes 2359304 | tf_op jit(solution)/shard_map/ppermute | solution.py:286
  517.2 7.5 %copy-start.6 = (f32[2,1024,1]{2,1,0:T(8,128)S(1)}, f32[2,1024,1]{2,1,0:T(8,128)}, u32[]{:S(2)}) copy-start(f32[2,1024,1]{2,1,0:T(8,128)} %copy-done.5) | copy-start | bytes 24580
  517.2 7.5 %copy-start.8 = (bf16[1024,256]{1,0:T(8,128)(2,1)S(1)}, bf16[1024,256]{1,0:T(8,128)(2,1)}, u32[]{:S(2)}) copy-start(bf16[1024,256]{1,0:T(8,128)(2,1)} %copy-done.7) | copy-start | bytes 1572868
  517.2 7.5 %copy-start.10 = (bf16[1024,256]{1,0:T(8,128)(2,1)S(1)}, bf16[1024,256]{1,0:T(8,128)(2,1)}, u32[]{:S(2)}) copy-start(bf16[1024,256]{1,0:T(8,128)(2,1)} %copy-done.9) | copy-start | bytes 1572868
  517.2 36.1 %collective-permute-start.23 = (bf16[512,768]{1,0:T(8,128)(2,1)}, bf16[512,768]{1,0:T(8,128)(2,1)}, u32[]{:S(2)}, u32[]{:S(2)}) collective-permute-start(bf16[512,768]{1,0:T(8,128)(2,1)} %get-tuple-element.192), channel_id=1, source_target_pairs={{0,24},{8,16},{16,8},{24,0},{1,25},{9,17},{17,9},{25,1},{2,26},{10... | collective-permute-start | bytes 2359304 | tf_op jit(solution)/shard_map/ppermute | solution.py:286
  568.1 17.3 %collective-permute-start.24 = (bf16[8,2,64,512]{3,2,1,0:T(8,128)(2,1)S(1)}, bf16[8,2,64,512]{3,2,1,0:T(8,128)(2,1)S(1)}, u32[]{:S(2)}, u32[]{:S(2)}) collective-permute-start(bf16[8,2,64,512]{3,2,1,0:T(8,128)(2,1)S(1)} %constant_dynamic-slice_fusion), channel_id=1, source_target_pairs={{0,8},{8,0},{16,24},{24,16},{1,9},{9,1},{17,25},{25,17},{2,10},{10... | collective-permute-start | bytes 3145736 | tf_op jit(solution)/shard_map/ppermute | solution.py:286
  572.3 13.1 %copy-start.31 = (bf16[8,4,64,512]{3,2,1,0:T(8,128)(2,1)S(1)}, bf16[8,4,64,512]{3,2,1,0:T(8,128)(2,1)}, u32[]{:S(2)}) copy-start(bf16[8,4,64,512]{3,2,1,0:T(8,128)(2,1)} %get-tuple-element.112) | copy-start | bytes 6291460
  (37 other events, 121.8 us)
Sparse Core Ops, SparseCore 0:
  70.2 156.8 all-gather.1
  378.4 91.6 reduce-scatter.4
  472.4 181.6 reduce-scatter.2

commit v8 on v7

--- a/solution.py
+++ b/solution.py
@@ -654,7 +654,7 @@
 
 def weight_grad_kernel(count, half_tiles, *refs):
     lefts, right_ref = refs[:count], refs[count]
-    out_ref = refs[-1] if len(refs) == count + 2 else refs[-2]
+    out_ref = refs[-1] if len(refs) == count + 2 else refs[-3]
     pieces = [ref[...] for ref in lefts]
     if half_tiles:
         pieces[-2:] = [jnp.where(pl.program_id(0) < half_tiles, pieces[-2], pieces[-1])]
@@ -670,8 +670,10 @@
         late = late_ref[...]
         lane = lax.broadcasted_iota(jnp.int32, late.shape, 1)
         split = result.shape[1] - 2 * HEAD_DIM
-        refs[-1][...] = result[:, split:].astype(low).reshape(refs[-1].shape)
-        result = jnp.concatenate([result[:, :split], jnp.where(lane == 0, of_gain, late)], 1)
+        refs[-2][...] = result[:, split:].astype(low).reshape(refs[-2].shape)
+        late = jnp.where(lane == 0, of_gain, late)
+        refs[-1][...] = late.astype(low).reshape(refs[-1].shape)
+        result = result[:, :split]
     out_ref[...] = result.astype(low).reshape(out_ref.shape)
 
 
@@ -681,7 +683,7 @@
     rows = width // (ranks * parts)
     tile = max(min(256, rows * parts), rows)
     each = tile // rows
-    wides = [columns + 128 - 2 * HEAD_DIM, 2 * HEAD_DIM] if extras else [columns]
+    wides = [columns - 2 * HEAD_DIM, 2 * HEAD_DIM, 128] if extras else [columns]
     half_tiles = lefts[-1].shape[1] // tile if lefts[-1].shape[1] < width else 0
 
     def place(i):
@@ -1717,7 +1719,6 @@
         head = pl.ds(pl.multiple_of(group * HEAD_DIM, HEAD_DIM), HEAD_DIM)
         query_ref[:, columns] = last[:, :q_width]
         out_ref[:, columns] = out
-        small_ref[...] += last[:, q_width : q_width + small_ref.shape[1]]
         if not shared:
             key_ref[:, head] += last[:, -2 * HEAD_DIM : -HEAD_DIM]
             value_ref[:, head] += last[:, -HEAD_DIM:]
@@ -1976,10 +1977,23 @@
         grad_head_scale.reshape(-1, head_rows, 2), ((0, 0), (0, rows - head_rows), (0, 0))
     ).reshape(width, 2)
     late_grad = jnp.pad(head_scale_grad, ((0, 0), (6, 120)))
-    last, pair_grad = weight_grad(
+    last, pair_grad, late_grad = weight_grad(
         ranks, pairs * 2, [normed_all], grad_qkv, head_all, gain[0][:, None], late_grad
     )
-    last, pair_grad, grad_qkv = lax.optimization_barrier((last, pair_grad, grad_qkv))
+    last, pair_grad, late_grad, grad_qkv = lax.optimization_barrier(
+        (last, pair_grad, late_grad, grad_qkv)
+    )
+    late_sum = take(late_grad, 1, rank).astype(full)
+    for k in range(1, ranks):
+        late_sum = late_sum + permute(take(late_grad, 1, relative[k]), "seq", k).astype(full)
+    small_at = rest_own.shape[2] - 128
+    rest_own = jnp.concatenate(
+        [
+            rest_own[:, :, :small_at],
+            (rest_own[:, :, small_at:].astype(full) + late_sum).astype(low),
+        ],
+        2,
+    )
     x_part = mm_nt(grad_qkv, qkv_map).astype(low)
 
     if ranks == 4:

time: 736 us -> 732 us (level)
  Pallas kernels: 445 us -> 434 us
    pallas_call x1, Pallas kernels: 117 us -> 106 us  [finish(): pl.pallas_call(functools.partial(finish_kernel, sizes, x is not None), ou...]
    ppermute x25 -> x28, starting transfers between devices: 35.3 us -> 38.9 us  [permute(): return lax.ppermute(v, axis, [(i, i ^ offset) for i in range(size)])]
    ppermute x25 -> x28, waiting for transfers between devices: 93 us -> 93.8 us  [permute(): return lax.ppermute(v, axis, [(i, i ^ offset) for i in range(size)])]
  transfers between devices with their start and end apart: 28 -> 31, of which waited for: 16 -> 16; matrix products, arithmetic and copies ran while one was open for 15% -> 16% of each run, Pallas kernels for 33% -> 31%
where the time goes in v8:
time: 732 us; the launch traced here: 722 us
  Pallas kernels  434 us (59%)
  waiting for transfers between devices  98 us (13%)
  other arithmetic  47.3 us (6%)
  local copies, waits for them, and re-layouts  45.4 us (6%)
  matrix products  43.3 us (6%)
  starting transfers between devices  39 us (5%)
  between operations  15.3 us (2%)
    pallas_call x1, Pallas kernels, middle(): pl.pallas_call(functools.partial(middle_kernel, pairs, block, parts), out...  151 us
    pallas_call x1, Pallas kernels, finish(): pl.pallas_call(functools.partial(finish_kernel, sizes, x is not None), ou...  106 us
    ppermute x28, waiting for transfers between devices, permute(): return lax.ppermute(v, axis, [(i, i ^ offset) for i in range(size)])  93.8 us
    pallas_call x1, Pallas kernels, back(): pl.pallas_call(functools.partial(back_kernel, block), out_shape=(jax.Shap...  65.1 us
    pallas_call x1, Pallas kernels, gather_weights(): pl.pallas_call(functools.partial(gather_kernel, sizes), out_shape=(jax.Sh...  56.5 us
    dot_general x13, matrix products, dot(): lax.dot_general(left, right, (over, ((), ())), preferred_element_type=full)  43.3 us
    ppermute x28, starting transfers between devices, permute(): return lax.ppermute(v, axis, [(i, i ^ offset) for i in range(size)])  38.9 us
    pallas_call x2, Pallas kernels, weight_grad(): pl.pallas_call(functools.partial(weight_grad_kernel, len(lefts), half_til...  22 us
  transfers between devices with their start and end apart: 31, of which 16 were waited for; matrix products, arithmetic and copies ran while one was open for 16% of the time, Pallas kernels for 31%

profile of v8, /device:TPU:20, one launch (start us, length us, event | category | flops | bytes accessed | tf_op | source)
XLA Modules:
  0.0 722.1 jit_solution(8716026622283929200)
XLA Ops:
  13.5 56.5 %shard_map.221 = (bf16[4,4,2,64,1536]{4,3,2,1,0:T(8,128)(2,1)}, bf16[4,4,2,64,256]{4,3,2,1,0:T(8,128)(2,1)}, s32[4,8,256]{2,1,0:T(8,128)}, bf16[4,256,2048]{2,1,0:T(8,128)(2,1)}, bf16[2,256,2048]{2,1,0:T(8,128)(2,1)}) custom-call(bf16[4,64,1536]{2,1,0:T(8,128)(2,1)} %pad_maximum_fusion.3.head_ref, bf16[64,256]{1,0:T(8,128)(2,1)} %fusion.53.rest_ref, ...), custom_call_target="tpu_custom_call" | custom-call | tf_op jit(solution)/shard_map/pallas_call | solution.py:257
  70.1 3.2 multiply_reduce_fusion
  75.0 1.9 multiply_sine_fusion
  76.9 3.1 slice_reduce_fusion.1
  82.1 4.5 fusion.20.qkv_ref
  86.6 16.3 %shard_map.222 = (bf16[1024,512]{1,0:T(8,128)(2,1)S(1)}, bf16[1024,256]{1,0:T(8,128)(2,1)S(1)}, bf16[1024,256]{1,0:T(8,128)(2,1)S(1)}, bf16[1024,512]{1,0:T(8,128)(2,1)S(1)}, f32[2,1024,1]{2,1,0:T(8,128)S(1)}) custom-call(f32[1024,1024]{1,0:T(8,128)S(1)} %fusion.20.qkv_ref, s32[1024,1]{1,0:T(8,128)S(1)} %copy.74.code_col_ref, ...), custom_call_target="tpu_custom_call" | custom-call | flops 1207959552 | bytes 12582912 | tf_op jit(solution)/shard_map/pallas_call | solution.py:491
  102.9 2.4 convolution_convert_fusion
  108.5 12.0 %collective-permute-done.1 = bf16[256,1024]{1,0:T(8,128)(2,1)S(1)} collective-permute-done((bf16[256,1024]{1,0:T(8,128)(2,1)S(1)}, bf16[256,1024]{1,0:T(8,128)(2,1)S(1)}, u32[]{:S(2)}, u32[]{:S(2)}) %collective-permute-start.1) | collective-permute-done | bytes 524320 | tf_op jit(solution)/shard_map/ppermute | solution.py:286
  123.1 5.5 collective-permute-done
  128.6 7.0 collective-permute-done.2
  138.3 3.1 collective-permute-done.3
  141.3 6.1 collective-permute-done.5
  148.0 2.6 broadcast_multiply_fusion
  153.7 19.7 %collective-permute-done.6.rows_x_in.rows_x = bf16[256,2048]{1,0:T(8,128)(2,1)S(1)} collective-permute-done((bf16[256,2048]{1,0:T(8,128)(2,1)S(1)}, bf16[256,2048]{1,0:T(8,128)(2,1)S(1)}, u32[]{:S(2)}, u32[]{:S(2)}) %collective-permute-start.6) | collective-permute-done | bytes 1048608 | tf_op jit(solution)/shard_map/ppermute | solution.py:286
  175.5 7.3 %collective-permute-done.8.rows_left_in.rows_left = bf16[256,1024]{1,0:T(8,128)(2,1)S(1)} collective-permute-done((bf16[256,1024]{1,0:T(8,128)(2,1)S(1)}, bf16[256,1024]{1,0:T(8,128)(2,1)S(1)}, u32[]{:S(2)}, u32[]{:S(2)}) %collective-permute-start.8) | collective-permute-done | bytes 524320 | tf_op jit(solution)/shard_map/ppermute | solution.py:286
  184.7 10.4 %collective-permute-start.11 = (bf16[64,512]{1,0:T(8,128)(2,1)S(1)}, bf16[64,512]{1,0:T(8,128)(2,1)S(1)}, u32[]{:S(2)}, u32[]{:S(2)}) collective-permute-start(bf16[64,512]{1,0:T(8,128)(2,1)S(1)} %copy-done.47), channel_id=1, source_target_pairs={{0,4},{1,5},{2,6},{3,7},{4,0},{5,1},{6,2},{7,3},{8,12},{9,13},{10,... | collective-permute-start | bytes 196616 | tf_op jit(solution)/shard_map/ppermute | solution.py:286
  195.2 6.4 collective-permute-done.11
  201.6 1.9 collective-permute-done.10
  204.5 1.6 collective-permute-start.14
  207.2 5.3 collective-permute-done.15
  212.4 2.1 collective-permute-done.14
  216.6 2.4 collective-permute-done.16
  219.0 2.0 fusion.39
  222.9 4.2 all-gather.2.cloned.1.call-done.in_maps_ref.maps_ref
  227.1 151.2 %shard_map.223 = (bf16[4,256,2048]{2,1,0:T(8,128)(2,1)}, bf16[2048,2048]{1,0:T(8,128)(2,1)}, bf16[2048,2048]{1,0:T(8,128)(2,1)}, f32[1024,2048]{1,0:T(8,128)}, f...) custom-call(bf16[256,2048]{1,0:T(8,128)(2,1)} %copy-done.34, ...), custom_call_target="tpu_custom_call" | custom-call | flops 17179869184 | bytes 104857600 | tf_op jit(solution)/shard_map/pallas_call | solution.py:1192
  378.4 12.6 %fusion.64 = f32[1024,2048]{1,0:T(8,128)S(1)} fusion(bf16[1024,2048]{1,0:T(8,128)(2,1)} %bitcast.199, bf16[2048,2048]{1,0:T(8,128)(2,1)} %get-tuple-element.90), kind=kOutput, calls=%fused_computation.169 | convolution fusion | flops 8589934592 | bytes 20971520 | tf_op jit(solution)/shard_map/dot_general | solution.py:344
  391.1 8.2 %multiply_convert_fusion = (bf16[1024,2048]{1,0:T(8,128)(2,1)}, bf16[1024,2048]{1,0:T(8,128)(2,1)}) fusion(f32[1024,2048]{1,0:T(8,128)S(1)} %fusion.64, f32[1024,2048]{1,0:T(8,128)S(1)} %bitcast.140, f32[1024,2048]{1,0:T(8,128)S(1)} %bitcast.142), kind=kLoop, calls=%fused_computation.12 | loop fusion | flops 50331648 | bytes 33554432 | tf_op jit(solution)/shard_map/convert_element_type | solution.py:1910
  399.3 65.1 %shard_map.224 = (bf16[2,2048,2048]{2,1,0:T(8,128)(2,1)}, f32[256,2048]{1,0:T(8,128)}) custom-call(bf16[1024,2048]{1,0:T(8,128)(2,1)} %get-tuple-element.189.gate_ref, bf16[1024,2048]{1,0:T(8,128)(2,1)} %get-tuple-element.188.up_ref, bf16[2,2048,2048]{2,1,0:T(8,128)(2,1)} %all-gather.2.cloned.1.call-done.in_maps_ref.maps_ref, bf16[256,2048]{1,0:T(8,128)(2,1)} %copy-done.34, ...), custom_call_target="tpu_custom_call" | custom-call | flops 34359738368 | bytes 52428800 | tf_op jit(solution)/shard_map/pallas_call | solution.py:1447
  464.4 2.3 copy.85
  466.8 2.9 multiply_reduce_fusion.2
  470.3 4.0 multiply_reduce_fusion.1
  474.4 2.1 multiply_convert_fusion.1
  483.0 3.8 fusion.27
  488.2 8.7 %collective-permute-done.17.refs_1_ = bf16[256,2048]{1,0:T(8,128)(2,1)} collective-permute-done((bf16[256,2048]{1,0:T(8,128)(2,1)}, bf16[256,2048]{1,0:T(8,128)(2,1)}, u32[]{:S(2)}, u32[]{:S(2)}) %collective-permute-start.17) | collective-permute-done | bytes 1048608 | tf_op jit(solution)/shard_map/ppermute | solution.py:286
  496.9 1.9 slice.210
  500.2 1.9 slice.211
  505.6 6.1 concatenate.94
  511.7 3.1 dynamic-slice_bitcast_fusion
  514.8 1.9 collective-permute-start.21
  518.8 5.9 fusion.33.grad_ref
  524.7 17.1 %shard_map.225 = (bf16[1024,1024]{1,0:T(8,128)(2,1)S(1)}, f32[8,256]{1,0:T(8,128)S(1)}) custom-call(f32[1024,1024]{1,0:T(8,128)S(1)} %copy-done.1, bf16[1024,512]{1,0:T(8,128)(2,1)S(1)} %copy-done.4, bf16[1024,256]{1,0:T(8,128)(2,1)S(1)} %copy-done.8, bf16[1024,256]{1,0:T(8,128)(2,1)S(1)} %copy-done.10, bf16[1024,512]{1,0:T(8,128)(2,1)S(1)} %fusion.33.grad_ref, ...), custom_call_target="tpu_custom_call" | custom-call | flops 3019898880 | bytes 16777216 | tf_op jit(solution)/shard_map/pallas_call | solution.py:632
  544.8 8.6 %shard_map.227.refs_1_ = bf16[8,4,64,512]{3,2,1,0:T(8,128)(2,1)} custom-call(bf16[256,2048]{1,0:T(8,128)(2,1)} %get-tuple-element.99.refs_0_, bf16[256,2048]{1,0:T(8,128)(2,1)} %collective-permute-done.17.refs_1_, bf16[256,2048]{1,0:T(8,128)(2,1)} %collective-permute-done.18.refs_2_, bf16[256,1024]{1,0:T(8,128)(2,1)} %collective-permute-done.19.refs_3_, ...), custom_call_target="tpu_custom_call" | custom-call | flops 2147483648 | bytes 7340032 | tf_op jit(solution)/shard_map/pallas_call | solution.py:698
  553.4 13.4 %shard_map.226 = (bf16[8,4,64,512]{3,2,1,0:T(8,128)(2,1)}, bf16[8,4,64,512]{3,2,1,0:T(8,128)(2,1)}, bf16[8,4,64,128]{3,2,1,0:T(8,128)(2,1)}) custom-call(bf16[1024,2048]{1,0:T(8,128)(2,1)} %copy-done.26, bf16[1024,1024]{1,0:T(8,128)(2,1)} %copy-done.11, bf16[2048,1536]{1,0:T(8,128)(2,1)} %bitcast.191, f32[2048,1]{1,0:T(8,128)} %get-tuple-element.206.refs_3_, ...), custom_call_target="tpu_custom_call" | custom-call | flops 4294967296 | bytes 10485760 | tf_op jit(solution)/shard_map/pallas_call | solution.py:698
  574.3 8.4 %convolution_convert_fusion.1 = bf16[1024,2048]{1,0:T(8,128)(2,1)} fusion(bf16[1024,1024]{1,0:T(8,128)(2,1)S(1)} %copy-done.12, bf16[2048,1536]{1,0:T(8,128)(2,1)} %bitcast.192), kind=kOutput, calls=%fused_computation.25 | convolution fusion | flops 4297064448 | bytes 10485760 | tf_op jit(solution)/shard_map/dot_general | solution.py:344
  582.7 1.8 fusion.32
  586.7 5.4 collective-permute-done.27
  594.0 105.6 %shard_map.228 = (f32[64,2048]{1,0:T(8,128)}, f32[64,512]{1,0:T(8,128)}, f32[64,512]{1,0:T(8,128)}, f32[64,2048]{1,0:T(8,128)}, f32[64,512]{1,0:T(8,128)}, /*ind...) custom-call(bf16[8,4,64,512]{3,2,1,0:T(8,128)(2,1)} %get-tuple-element.111.refs_0_, ...), custom_call_target="tpu_custom_call" | custom-call | tf_op jit(solution)/shard_map/pallas_call | solution.py:1786
  702.5 5.1 maximum_convert_fusion
  (257 shorter events, 72.4 us)
Async XLA Ops:
  7.2 219.9 %all-gather.2.cloned.1.call-start = ((), (), s32[]{:S(2)}) async-start(), calls=%async_computation.2 | async-start | bytes 18874368 | tf_op jit(solution)/shard_map/all_gather | solution.py:1844
  70.0 632.4 %reduce-scatter.5.cloned.1.call-start = ((), (), s32[]{:S(2)}) async-start(), calls=%async_computation.4 | async-start | bytes 9437184 | tf_op jit(solution)/shard_map/reduce_scatter | solution.py:1905
  86.5 16.3 %copy-start = (f32[1024,1024]{1,0:T(8,128)}, f32[1024,1024]{1,0:T(8,128)S(1)}, u32[]{:S(2)}) copy-start(f32[1024,1024]{1,0:T(8,128)S(1)} %fusion.20.qkv_ref) | copy-start | bytes 12582916
  105.3 17.5 %copy-start.22 = (bf16[256,1,2048]{2,0,1:T(8,128)(2,1)S(1)}, bf16[256,1,2048]{2,0,1:T(8,128)(2,1)}, u32[]{:S(2)}) copy-start(bf16[256,1,2048]{2,0,1:T(8,128)(2,1)} %param.14) | copy-start | bytes 3145732
  105.6 14.9 %collective-permute-start.1 = (bf16[256,1024]{1,0:T(8,128)(2,1)S(1)}, bf16[256,1024]{1,0:T(8,128)(2,1)S(1)}, u32[]{:S(2)}, u32[]{:S(2)}) collective-permute-start(bf16[256,1024]{1,0:T(8,128)(2,1)S(1)} %get-tuple-element.195), channel_id=1, source_target_pairs={{0,8},{8,0},{16,24},{24,16},{1,9},{9,1},{17,25},{25,17},{2,10},{10... | collective-permute-start | bytes 1572872 | tf_op jit(solution)/shard_map/ppermute | solution.py:286
  106.5 22.1 %collective-permute-start = (bf16[256,1024]{1,0:T(8,128)(2,1)S(1)}, bf16[256,1024]{1,0:T(8,128)(2,1)S(1)}, u32[]{:S(2)}, u32[]{:S(2)}) collective-permute-start(bf16[256,1024]{1,0:T(8,128)(2,1)S(1)} %get-tuple-element.192), channel_id=1, source_target_pairs={{0,8},{8,0},{16,24},{24,16},{1,9},{9,1},{17,25},{25,17},{2,10},{10... | collective-permute-start | bytes 1572872 | tf_op jit(solution)/shard_map/ppermute | solution.py:286
  107.7 21.0 %collective-permute-start.4 = (bf16[256,1024]{1,0:T(8,128)(2,1)S(1)}, bf16[256,1024]{1,0:T(8,128)(2,1)S(1)}, u32[]{:S(2)}, u32[]{:S(2)}) collective-permute-start(bf16[256,1024]{1,0:T(8,128)(2,1)S(1)} %get-tuple-element.193), channel_id=1, source_target_pairs={{0,16},{8,24},{16,0},{24,8},{1,17},{9,25},{17,1},{25,9},{2,18},{10... | collective-permute-start | bytes 1572872 | tf_op jit(solution)/shard_map/ppermute | solution.py:286
  120.7 14.9 %collective-permute-start.2 = (bf16[256,1024]{1,0:T(8,128)(2,1)S(1)}, bf16[256,1024]{1,0:T(8,128)(2,1)S(1)}, u32[]{:S(2)}, u32[]{:S(2)}) collective-permute-start(bf16[256,1024]{1,0:T(8,128)(2,1)S(1)} %add_convert_fusion.2), channel_id=1, source_target_pairs={{0,16},{8,24},{16,0},{24,8},{1,17},{9,25},{17,1},{25,9},{2,18},{10... | collective-permute-start | bytes 1572872 | tf_op jit(solution)/shard_map/ppermute | solution.py:286
  121.6 19.8 %collective-permute-start.3 = (bf16[256,1024]{1,0:T(8,128)(2,1)S(1)}, bf16[256,1024]{1,0:T(8,128)(2,1)S(1)}, u32[]{:S(2)}, u32[]{:S(2)}) collective-permute-start(bf16[256,1024]{1,0:T(8,128)(2,1)S(1)} %get-tuple-element.194), channel_id=1, source_target_pairs={{0,16},{8,24},{16,0},{24,8},{1,17},{9,25},{17,1},{25,9},{2,18},{10... | collective-permute-start | bytes 1572872 | tf_op jit(solution)/shard_map/ppermute | solution.py:286
  123.1 14.0 %copy-start.28 = (bf16[4,4,2,64,256]{4,3,2,1,0:T(8,128)(2,1)S(1)}, bf16[4,4,2,64,256]{4,3,2,1,0:T(8,128)(2,1)}, u32[]{:S(2)}) copy-start(bf16[4,4,2,64,256]{4,3,2,1,0:T(8,128)(2,1)} %get-tuple-element.70) | copy-start | bytes 3145732
  136.1 11.9 %copy-start.20 = (f32[256,1024]{1,0:T(8,128)}, f32[256,1024]{1,0:T(8,128)S(1)}, u32[]{:S(2)}) copy-start(f32[256,1024]{1,0:T(8,128)S(1)} %get-tuple-element.190) | copy-start | bytes 3145732
  136.1 11.4 %collective-permute-start.5 = (bf16[256,1024]{1,0:T(8,128)(2,1)S(1)}, bf16[256,1024]{1,0:T(8,128)(2,1)S(1)}, u32[]{:S(2)}, u32[]{:S(2)}) collective-permute-start(bf16[256,1024]{1,0:T(8,128)(2,1)S(1)} %get-tuple-element.191), channel_id=1, source_target_pairs={{0,8},{8,0},{16,24},{24,16},{1,9},{9,1},{17,25},{25,17},{2,10},{10... | collective-permute-start | bytes 1572872 | tf_op jit(solution)/shard_map/ppermute | solution.py:286
  138.2 9.7 %copy-start.15 = (f32[256,2048]{1,0:T(8,128)}, f32[256,2048]{1,0:T(8,128)S(1)}, u32[]{:S(2)}) copy-start(f32[256,2048]{1,0:T(8,128)S(1)} %get-tuple-element.235) | copy-start | bytes 6291460
  150.9 32.8 %copy-start.47 = (bf16[64,512]{1,0:T(8,128)(2,1)S(1)}, bf16[64,512]{1,0:T(8,128)(2,1)}, u32[]{:S(2)}) copy-start(bf16[64,512]{1,0:T(8,128)(2,1)} %param.24) | copy-start | bytes 196612
  152.0 21.5 %collective-permute-start.6 = (bf16[256,2048]{1,0:T(8,128)(2,1)S(1)}, bf16[256,2048]{1,0:T(8,128)(2,1)S(1)}, u32[]{:S(2)}, u32[]{:S(2)}) collective-permute-start(bf16[256,2048]{1,0:T(8,128)(2,1)S(1)} %multiply_convert_fusion.3.rows_own), channel_id=1, source_target_pairs={{0,8},{8,0},{16,24},{24,16},{1,9},{9,1},{17,25},{25,17},{2,10},{10... | collective-permute-start | bytes 3145736 | tf_op jit(solution)/shard_map/ppermute | solution.py:286
  153.0 21.4 %collective-permute-start.7 = (bf16[256,2048]{1,0:T(8,128)(2,1)S(1)}, bf16[256,2048]{1,0:T(8,128)(2,1)S(1)}, u32[]{:S(2)}, u32[]{:S(2)}) collective-permute-start(bf16[256,2048]{1,0:T(8,128)(2,1)S(1)} %multiply_convert_fusion.3.rows_own), channel_id=1, source_target_pairs={{0,16},{8,24},{16,0},{24,8},{1,17},{9,25},{17,1},{25,9},{2,18},{10... | collective-permute-start | bytes 3145736 | tf_op jit(solution)/shard_map/ppermute | solution.py:286
  173.5 9.2 %collective-permute-start.8 = (bf16[256,1024]{1,0:T(8,128)(2,1)S(1)}, bf16[256,1024]{1,0:T(8,128)(2,1)S(1)}, u32[]{:S(2)}, u32[]{:S(2)}) collective-permute-start(bf16[256,1024]{1,0:T(8,128)(2,1)S(1)} %slice.202), channel_id=1, source_target_pairs={{0,16},{8,24},{16,0},{24,8},{1,17},{9,25},{17,1},{25,9},{2,18},{10... | collective-permute-start | bytes 1572872 | tf_op jit(solution)/shard_map/ppermute | solution.py:286
  174.4 9.3 %copy-start.40 = (bf16[256,2048]{1,0:T(8,128)(2,1)}, bf16[256,2048]{1,0:T(8,128)(2,1)S(1)}, u32[]{:S(2)}) copy-start(bf16[256,2048]{1,0:T(8,128)(2,1)S(1)} %collective-permute-done.7.rows_y_in.rows_y) | copy-start | bytes 3145732
  174.5 9.2 %collective-permute-start.9 = (bf16[256,1024]{1,0:T(8,128)(2,1)S(1)}, bf16[256,1024]{1,0:T(8,128)(2,1)S(1)}, u32[]{:S(2)}, u32[]{:S(2)}) collective-permute-start(bf16[256,1024]{1,0:T(8,128)(2,1)S(1)} %slice.203), channel_id=1, source_target_pairs={{0,8},{8,0},{16,24},{24,16},{1,9},{9,1},{17,25},{25,17},{2,10},{10... | collective-permute-start | bytes 1572872 | tf_op jit(solution)/shard_map/ppermute | solution.py:286
  183.7 11.4 %copy-start.50 = (bf16[256,1024]{1,0:T(8,128)(2,1)}, bf16[256,1024]{1,0:T(8,128)(2,1)S(1)}, u32[]{:S(2)}) copy-start(bf16[256,1024]{1,0:T(8,128)(2,1)S(1)} %collective-permute-done.9.rows_right_in.rows_right) | copy-start | bytes 1572868
  183.7 11.5 %collective-permute-start.12 = (bf16[64,512]{1,0:T(8,128)(2,1)S(1)}, bf16[64,512]{1,0:T(8,128)(2,1)S(1)}, u32[]{:S(2)}, u32[]{:S(2)}) collective-permute-start(bf16[64,512]{1,0:T(8,128)(2,1)S(1)} %copy-done.47), channel_id=1, source_target_pairs={{0,6},{1,7},{2,4},{3,5},{4,2},{5,3},{6,0},{7,1},{8,14},{9,15},{10,... | collective-permute-start | bytes 196616 | tf_op jit(solution)/shard_map/ppermute | solution.py:286
  184.7 16.9 %collective-permute-start.11 = (bf16[64,512]{1,0:T(8,128)(2,1)S(1)}, bf16[64,512]{1,0:T(8,128)(2,1)S(1)}, u32[]{:S(2)}, u32[]{:S(2)}) collective-permute-start(bf16[64,512]{1,0:T(8,128)(2,1)S(1)} %copy-done.47), channel_id=1, source_target_pairs={{0,4},{1,5},{2,6},{3,7},{4,0},{5,1},{6,2},{7,3},{8,12},{9,13},{10,... | collective-permute-start | bytes 196616 | tf_op jit(solution)/shard_map/ppermute | solution.py:286
  195.2 8.3 %collective-permute-start.10 = (bf16[64,512]{1,0:T(8,128)(2,1)S(1)}, bf16[64,512]{1,0:T(8,128)(2,1)S(1)}, u32[]{:S(2)}, u32[]{:S(2)}) collective-permute-start(bf16[64,512]{1,0:T(8,128)(2,1)S(1)} %copy-done.47), channel_id=1, source_target_pairs={{0,2},{1,3},{2,0},{3,1},{4,6},{5,7},{6,4},{7,5},{8,10},{9,11},{10,... | collective-permute-start | bytes 196616 | tf_op jit(solution)/shard_map/ppermute | solution.py:286
  203.6 8.8 %collective-permute-start.15 = (bf16[4,64,512]{2,1,0:T(8,128)(2,1)S(1)}, bf16[4,64,512]{2,1,0:T(8,128)(2,1)S(1)}, u32[]{:S(2)}, u32[]{:S(2)}) collective-permute-start(bf16[4,64,512]{2,1,0:T(8,128)(2,1)S(1)} %get-tuple-element.217), channel_id=1, source_target_pairs={{0,24},{8,16},{16,8},{24,0},{1,25},{9,17},{17,9},{25,1},{2,26},{10... | collective-permute-start | bytes 786440 | tf_op jit(solution)/shard_map/ppermute | solution.py:286
  204.5 10.1 %collective-permute-start.14 = (bf16[4,64,512]{2,1,0:T(8,128)(2,1)S(1)}, bf16[4,64,512]{2,1,0:T(8,128)(2,1)S(1)}, u32[]{:S(2)}, u32[]{:S(2)}) collective-permute-start(bf16[4,64,512]{2,1,0:T(8,128)(2,1)S(1)} %get-tuple-element.217), channel_id=1, source_target_pairs={{0,16},{8,24},{16,0},{24,8},{1,17},{9,25},{17,1},{25,9},{2,18},{10... | collective-permute-start | bytes 786440 | tf_op jit(solution)/shard_map/ppermute | solution.py:286
  206.1 8.5 %collective-permute-start.13 = (bf16[4,64,512]{2,1,0:T(8,128)(2,1)S(1)}, bf16[4,64,512]{2,1,0:T(8,128)(2,1)S(1)}, u32[]{:S(2)}, u32[]{:S(2)}) collective-permute-start(bf16[4,64,512]{2,1,0:T(8,128)(2,1)S(1)} %get-tuple-element.217), channel_id=1, source_target_pairs={{0,8},{8,0},{16,24},{24,16},{1,9},{9,1},{17,25},{25,17},{2,10},{10... | collective-permute-start | bytes 786440 | tf_op jit(solution)/shard_map/ppermute | solution.py:286
  216.0 3.0 collective-permute-start.16
  378.3 324.2 %reduce-scatter.3.cloned.1.call-start = ((), (), s32[]{:S(2)}) async-start(), calls=%async_computation.3 | async-start | bytes 18874368 | tf_op jit(solution)/shard_map/reduce_scatter | solution.py:1919
  378.4 12.7 %slice-start = ((s8[8388608]{0:T(1024)(128)(4,1)}), s8[4194304]{0:T(1024)(128)(4,1)S(1)}, s32[]{:S(2)}) async-start(s8[8388608]{0:T(1024)(128)(4,1)} %bitcast.139), calls=%async_computation.5 | async-start | bytes 8388608
  378.4 12.7 %slice-start.2 = ((s8[8388608]{0:T(1024)(128)(4,1)}), s8[4194304]{0:T(1024)(128)(4,1)S(1)}, s32[]{:S(2)}) async-start(s8[8388608]{0:T(1024)(128)(4,1)} %bitcast.141), calls=%async_computation.7 | async-start | bytes 8388608
  378.4 12.7 %slice-start.1 = ((s8[8388608]{0:T(1024)(128)(4,1)}), s8[4194304]{0:T(1024)(128)(4,1)S(1)}, s32[]{:S(2)}) async-start(s8[8388608]{0:T(1024)(128)(4,1)} %bitcast.139), calls=%async_computation.6 | async-start | bytes 8388608
  378.4 12.7 %slice-start.3 = ((s8[8388608]{0:T(1024)(128)(4,1)}), s8[4194304]{0:T(1024)(128)(4,1)S(1)}, s32[]{:S(2)}) async-start(s8[8388608]{0:T(1024)(128)(4,1)} %bitcast.141), calls=%async_computation.8 | async-start | bytes 8388608
  476.5 20.4 %collective-permute-start.17 = (bf16[256,2048]{1,0:T(8,128)(2,1)}, bf16[256,2048]{1,0:T(8,128)(2,1)}, u32[]{:S(2)}, u32[]{:S(2)}) collective-permute-start(bf16[256,2048]{1,0:T(8,128)(2,1)} %get-tuple-element.99.refs_0_), channel_id=1, source_target_pairs={{0,8},{8,0},{16,24},{24,16},{1,9},{9,1},{17,25},{25,17},{2,10},{10... | collective-permute-start | bytes 3145736 | tf_op jit(solution)/shard_map/ppermute | solution.py:286
  478.0 22.2 %collective-permute-start.18 = (bf16[256,2048]{1,0:T(8,128)(2,1)}, bf16[256,2048]{1,0:T(8,128)(2,1)}, u32[]{:S(2)}, u32[]{:S(2)}) collective-permute-start(bf16[256,2048]{1,0:T(8,128)(2,1)} %get-tuple-element.99.refs_0_), channel_id=1, source_target_pairs={{0,16},{8,24},{16,0},{24,8},{1,17},{9,25},{17,1},{25,9},{2,18},{10... | collective-permute-start | bytes 3145736 | tf_op jit(solution)/shard_map/ppermute | solution.py:286
  486.8 16.8 %copy-start.42 = (bf16[256,256]{1,0:T(8,128)(2,1)S(1)}, bf16[256,256]{1,0:T(8,128)(2,1)}, u32[]{:S(2)}) copy-start(bf16[256,256]{1,0:T(8,128)(2,1)} %get-tuple-element.83) | copy-start | bytes 393220
  487.3 16.3 %copy-start.36 = (bf16[256,2048]{1,0:T(8,128)(2,1)S(1)}, bf16[256,2048]{1,0:T(8,128)(2,1)}, u32[]{:S(2)}) copy-start(bf16[256,2048]{1,0:T(8,128)(2,1)} %get-tuple-element.82) | copy-start | bytes 3145732
  488.2 15.9 %copy-start.35 = (bf16[256,2048]{1,0:T(8,128)(2,1)S(1)}, bf16[256,2048]{1,0:T(8,128)(2,1)}, u32[]{:S(2)}) copy-start(bf16[256,2048]{1,0:T(8,128)(2,1)} %get-tuple-element.84) | copy-start | bytes 3145732
  488.2 15.9 %copy-start.41 = (bf16[256,256]{1,0:T(8,128)(2,1)S(1)}, bf16[256,256]{1,0:T(8,128)(2,1)}, u32[]{:S(2)}) copy-start(bf16[256,256]{1,0:T(8,128)(2,1)} %get-tuple-element.85) | copy-start | bytes 393220
  498.8 12.9 %collective-permute-start.19 = (bf16[256,1024]{1,0:T(8,128)(2,1)}, bf16[256,1024]{1,0:T(8,128)(2,1)}, u32[]{:S(2)}, u32[]{:S(2)}) collective-permute-start(bf16[256,1024]{1,0:T(8,128)(2,1)} %slice.210), channel_id=1, source_target_pairs={{0,16},{8,24},{16,0},{24,8},{1,17},{9,25},{17,1},{25,9},{2,18},{10... | collective-permute-start | bytes 1572872 | tf_op jit(solution)/shard_map/ppermute | solution.py:286
  502.1 9.6 %collective-permute-start.20 = (bf16[256,1024]{1,0:T(8,128)(2,1)}, bf16[256,1024]{1,0:T(8,128)(2,1)}, u32[]{:S(2)}, u32[]{:S(2)}) collective-permute-start(bf16[256,1024]{1,0:T(8,128)(2,1)} %slice.211), channel_id=1, source_target_pairs={{0,8},{8,0},{16,24},{24,16},{1,9},{9,1},{17,25},{25,17},{2,10},{10... | collective-permute-start | bytes 1572872 | tf_op jit(solution)/shard_map/ppermute | solution.py:286
  514.8 38.6 %collective-permute-start.21 = (bf16[512,768]{1,0:T(8,128)(2,1)}, bf16[512,768]{1,0:T(8,128)(2,1)S(1)}, u32[]{:S(2)}, u32[]{:S(2)}) collective-permute-start(bf16[512,768]{1,0:T(8,128)(2,1)} %get-tuple-element.198), channel_id=1, source_target_pairs={{0,8},{8,0},{16,24},{24,16},{1,9},{9,1},{17,25},{25,17},{2,10},{10... | collective-permute-start | bytes 2359304 | tf_op jit(solution)/shard_map/ppermute | solution.py:286
  516.7 36.8 %collective-permute-start.22 = (bf16[512,768]{1,0:T(8,128)(2,1)}, bf16[512,768]{1,0:T(8,128)(2,1)S(1)}, u32[]{:S(2)}, u32[]{:S(2)}) collective-permute-start(bf16[512,768]{1,0:T(8,128)(2,1)} %get-tuple-element.197), channel_id=1, source_target_pairs={{0,16},{8,24},{16,0},{24,8},{1,17},{9,25},{17,1},{25,9},{2,18},{10... | collective-permute-start | bytes 2359304 | tf_op jit(solution)/shard_map/ppermute | solution.py:286
  517.3 36.2 %collective-permute-start.23 = (bf16[512,768]{1,0:T(8,128)(2,1)}, bf16[512,768]{1,0:T(8,128)(2,1)}, u32[]{:S(2)}, u32[]{:S(2)}) collective-permute-start(bf16[512,768]{1,0:T(8,128)(2,1)} %get-tuple-element.196), channel_id=1, source_target_pairs={{0,24},{8,16},{16,8},{24,0},{1,25},{9,17},{17,9},{25,1},{2,26},{10... | collective-permute-start | bytes 2359304 | tf_op jit(solution)/shard_map/ppermute | solution.py:286
  568.1 16.6 %collective-permute-start.26 = (bf16[8,64,128]{2,1,0:T(8,128)(2,1)S(1)}, bf16[8,64,128]{2,1,0:T(8,128)(2,1)S(1)}, u32[]{:S(2)}, u32[]{:S(2)}) collective-permute-start(bf16[8,64,128]{2,1,0:T(8,128)(2,1)S(1)} %get-tuple-element.214), channel_id=1, source_target_pairs={{0,24},{8,16},{16,8},{24,0},{1,25},{9,17},{17,9},{25,1},{2,26},{10... | collective-permute-start | bytes 393224 | tf_op jit(solution)/shard_map/ppermute | solution.py:286
  569.5 15.1 %collective-permute-start.25 = (bf16[8,64,128]{2,1,0:T(8,128)(2,1)S(1)}, bf16[8,64,128]{2,1,0:T(8,128)(2,1)S(1)}, u32[]{:S(2)}, u32[]{:S(2)}) collective-permute-start(bf16[8,64,128]{2,1,0:T(8,128)(2,1)S(1)} %get-tuple-element.215), channel_id=1, source_target_pairs={{0,16},{8,24},{16,0},{24,8},{1,17},{9,25},{17,1},{25,9},{2,18},{10... | collective-permute-start | bytes 393224 | tf_op jit(solution)/shard_map/ppermute | solution.py:286
  570.9 13.7 %collective-permute-start.24 = (bf16[8,64,128]{2,1,0:T(8,128)(2,1)S(1)}, bf16[8,64,128]{2,1,0:T(8,128)(2,1)S(1)}, u32[]{:S(2)}, u32[]{:S(2)}) collective-permute-start(bf16[8,64,128]{2,1,0:T(8,128)(2,1)S(1)} %get-tuple-element.213), channel_id=1, source_target_pairs={{0,8},{8,0},{16,24},{24,16},{1,9},{9,1},{17,25},{25,17},{2,10},{10... | collective-permute-start | bytes 393224 | tf_op jit(solution)/shard_map/ppermute | solution.py:286
  572.9 19.2 %collective-permute-start.27 = (bf16[8,2,64,512]{3,2,1,0:T(8,128)(2,1)S(1)}, bf16[8,2,64,512]{3,2,1,0:T(8,128)(2,1)S(1)}, u32[]{:S(2)}, u32[]{:S(2)}) collective-permute-start(bf16[8,2,64,512]{3,2,1,0:T(8,128)(2,1)S(1)} %constant_dynamic-slice_fusion), channel_id=1, source_target_pairs={{0,8},{8,0},{16,24},{24,16},{1,9},{9,1},{17,25},{25,17},{2,10},{10... | collective-permute-start | bytes 3145736 | tf_op jit(solution)/shard_map/ppermute | solution.py:286
  584.5 7.6 %copy-start.31 = (bf16[8,4,64,512]{3,2,1,0:T(8,128)(2,1)S(1)}, bf16[8,4,64,512]{3,2,1,0:T(8,128)(2,1)}, u32[]{:S(2)}) copy-start(bf16[8,4,64,512]{3,2,1,0:T(8,128)(2,1)} %get-tuple-element.116) | copy-start | bytes 6291460
  (40 other events, 147.3 us)
Sparse Core Ops, SparseCore 0:
  70.2 156.8 all-gather.1
  378.4 91.6 reduce-scatter.4
  472.5 175.3 reduce-scatter.2
